TPU v7x, 32 devices: a whole 2x2x4 slice. The times are simulated.
32 devices in a mesh: row: 4 (over x, core), col: 8 (over z, y).
Axes of the slice: x: 2, y: 2, z: 4, core: 2. Of those that a mesh axis runs over, the one named last changes fastest.
Arguments:
- inputs: bfloat16 [512, 12288], P('row', 'col'), may hold values from -6 to 6
- out_grad: bfloat16 [512, 12288], P('row', 'col'), may hold values from -1.5 to 1.5
- first_vals: bfloat16 [4, 8, 512, 128, 128], P('row', 'col'), may hold values from -0.109375 to 0.109375
- first_rows: int32 [4, 8, 512], P('row', 'col'), may hold values from 0 to 11, as said below
- first_cols: int32 [4, 8, 512], P('row', 'col'), may hold values from 0 to 95
- first_count: int32 [4, 8], P('row', 'col'), may hold values from 64 to 512, as said below
- second_vals: bfloat16 [4, 8, 512, 128, 128], P('row', 'col'), may hold values from -0.0546875 to 0.0546875
- second_rows: int32 [4, 8, 512], P('row', 'col'), may hold values from 0 to 95, as said below
- second_cols: int32 [4, 8, 512], P('row', 'col'), may hold values from 0 to 11
- second_count: int32 [4, 8], P('row', 'col'), may hold values from 64 to 512, as said below
Outputs:
- layer_out: bfloat16 [512, 12288], P('row', 'col')
- input_grad: bfloat16 [512, 12288], P('row', 'col')
- first_grad: bfloat16 [4, 8, 512, 128, 128], P('row', 'col')
- second_grad: bfloat16 [4, 8, 512, 128, 128], P('row', 'col')
Inputs may be any that keep to these rules, and one draw needn't show every extreme that they name: Within one tile the slots name distinct blocks; slot s of tile (i, j) holds block (first_rows, first_cols) of that tile's 12 x 96 grid. The live slots are slots 0 to first_count - 1; some tile has all 512 slots live in every draw. `second_rows`: within one tile the slots name distinct blocks of that tile's 96 x 12 grid. The live slots are slots 0 to second_count - 1; some tile has all 512 slots live in every draw.
All inputs are finite; a program needn't handle non-finite values.
Results may differ from a plain program's by a relative error of at most 0.018.
Values may be sent and summed in bfloat16 or wider, within the bound.
No kernel may reach another device: no remote copies, remote signals or barrier semaphores. Data moves between devices by JAX's collectives and lax.ppermute only.
A program may use at most 640 MiB of HBM per device.

v0:
```python
import jax
import jax.numpy as jnp
from jax import lax
from jax.sharding import PartitionSpec as P

FF = 49152
BLK = 128


def activate(value):
    return jax.nn.gelu(value, approximate=True)


def live_slots(count, slots):
    return jnp.arange(slots, dtype=jnp.int32) < count


def dense_tile(vals, first, second, count, n_first, n_second):
    kept = jnp.where(live_slots(count, vals.shape[0])[:, None, None], vals, jnp.zeros_like(vals))
    layout = jnp.zeros((n_first, n_second, BLK, BLK), vals.dtype).at[first, second].set(kept)
    return layout.transpose(0, 2, 1, 3).reshape(n_first * BLK, n_second * BLK)


def slot_grad(left, left_idx, right, right_idx):
    rows = left.shape[0]
    left_pick = jnp.take(left.reshape(rows, -1, BLK), left_idx, axis=1)
    right_pick = jnp.take(right.reshape(rows, -1, BLK), right_idx, axis=1)
    return jnp.einsum("tsk,tsn->skn", left_pick, right_pick, preferred_element_type=jnp.float32)


def back_product(left, weight):
    return lax.dot_general(
        left, weight, (((1,), (1,)), ((), ())), preferred_element_type=jnp.float32
    )


def total_sum(term):
    return lax.psum(term.astype(jnp.bfloat16), "col").astype(jnp.float32)


def width_sum(partial_value):
    return lax.psum_scatter(
        partial_value.astype(jnp.bfloat16), "row", scatter_dimension=0, tiled=True
    ).astype(jnp.float32)


def shards(
    inputs,
    out_grad,
    first_vals,
    first_rows,
    first_cols,
    first_count,
    second_vals,
    second_rows,
    second_cols,
    second_count,
):
    full_x, full_dy = (
        lax.all_gather(inputs, "row", axis=0, tiled=True),
        lax.all_gather(out_grad, "row", axis=0, tiled=True),
    )
    width_cols = full_x.shape[1]
    d_blocks = width_cols // BLK
    f_blocks = FF // (BLK * lax.axis_size("row"))
    slots = first_vals.shape[2]
    up_rows = first_rows[0, 0]
    up_cols = first_cols[0, 0]
    up_count = first_count[0, 0]
    down_rows = second_rows[0, 0]
    down_cols = second_cols[0, 0]
    down_count = second_count[0, 0]
    w_first = dense_tile(first_vals[0, 0], up_rows, up_cols, up_count, d_blocks, f_blocks)
    w_second = dense_tile(second_vals[0, 0], down_rows, down_cols, down_count, f_blocks, d_blocks)
    hidden = total_sum(jnp.dot(full_x, w_first, preferred_element_type=jnp.float32))
    activated = activate(hidden).astype(jnp.bfloat16)
    out_part = jnp.dot(activated, w_second, preferred_element_type=jnp.float32)
    second_acc = slot_grad(activated, down_rows, full_dy, down_cols)
    act_grad = total_sum(back_product(full_dy, w_second))
    _, pullback = jax.vjp(activate, hidden)
    hid_grad = pullback(act_grad)[0].astype(jnp.bfloat16)
    in_part = back_product(hid_grad, w_first)
    first_acc = slot_grad(full_x, up_rows, hid_grad, up_cols)
    out_sum = width_sum(out_part)
    in_sum = width_sum(in_part)
    first_grad = jnp.where(live_slots(up_count, slots)[:, None, None], first_acc, 0.0).astype(
        jnp.bfloat16
    )
    second_grad = jnp.where(live_slots(down_count, slots)[:, None, None], second_acc, 0.0).astype(
        jnp.bfloat16
    )
    return (
        out_sum.astype(jnp.bfloat16),
        in_sum.astype(jnp.bfloat16),
        first_grad[None, None],
        second_grad[None, None],
    )


def solution(mesh):
    placed = (
        P("row", "col"),
        P("row", "col"),
        P("row", "col", None, None, None),
        P("row", "col", None),
        P("row", "col", None),
        P("row", "col"),
        P("row", "col", None, None, None),
        P("row", "col", None),
        P("row", "col", None),
        P("row", "col"),
    )
    return jax.shard_map(
        shards,
        mesh=mesh,
        in_specs=placed,
        out_specs=(
            P("row", "col"),
            P("row", "col"),
            P("row", "col", None, None, None),
            P("row", "col", None, None, None),
        ),
        check_vma=False,
    )
```

profile of v0, /device:TPU:0, one launch (start us, length us, event | category | flops | bytes accessed | tf_op | source)
XLA Modules:
  0.0 1425.5 jit_solution(4931404374228830329)
XLA Ops:
  7.2 0.0 all-gather.3.cloned.1.call-start
  7.2 1.9 copy.21
  9.1 0.0 all-gather.3.cloned.1.call-update
  9.1 0.0 all-gather.5.cloned.1.call-start
  9.2 1.9 copy.23
  11.1 0.0 all-gather.5.cloned.1.call-update
  11.1 0.0 all-reduce.3.cloned.1.call-start
  11.8 0.0 copy-start.7
  11.9 0.7 or_select_fusion
  12.6 0.0 copy-done.7
  12.6 14.5 %bitcast_select_fusion = bf16[512,128,128]{2,1,0:T(8,128)(2,1)} fusion(bf16[1,1,512,128,128]{4,3,2,1,0:T(8,128)(2,1)} %param.20, pred[512]{0:T(512)(128)(4,1)S(1)} %iota_compare_fusion), kind=kLoop, calls=%fused_computation.58 | loop fusion | flops 8388608 | bytes 33554944 | tf_op jit(solution)/shard_map/jit(_where)/select_n | solution.py:19
  27.1 12.6 broadcast_in_dim.67
  39.7 80.6 %scatter_fusion.1 = bf16[96,12,128,128]{3,2,1,0:T(8,128)(2,1)} fusion(bf16[96,12,128,128]{3,2,1,0:T(8,128)(2,1)} %broadcast_in_dim.67, s32[512]{0:T(512)S(1)} %bitcast.112, bf16[512,128,128]{2,1,0:T(8,128)(2,1)} %bitcast_select_fusion), kind=kCustom, calls=%fused_computation.5 | custom fusion | bytes 50335744 | tf_op jit(solution)/shard_map/scatter | solution.py:20
  120.3 46.2 %copy.22 = bf16[96,128,12,128]{1,0,3,2:T(8,128)(2,1)} copy(bf16[96,128,12,128]{3,1,2,0:T(8,128)(2,1)} %bitcast.105) | data formatting | bytes 75497472 | tf_op jit(solution)/shard_map/transpose | solution.py:21
  167.2 0.0 copy-done.1
  167.2 0.0 copy-done.2
  167.2 0.0 copy-start.9
  167.2 0.5 copy-done.9
  167.7 14.4 %bitcast_select_fusion.1 = bf16[512,128,128]{2,1,0:T(8,128)(2,1)} fusion(bf16[1,1,512,128,128]{4,3,2,1,0:T(8,128)(2,1)} %param.16, pred[512]{0:T(512)(128)(4,1)S(1)} %iota_compare_fusion.1), kind=kLoop, calls=%fused_computation.59 | loop fusion | flops 8388608 | bytes 33554944 | tf_op jit(solution)/shard_map/jit(_where)/select_n | solution.py:19
  182.1 12.6 broadcast_in_dim.65
  194.8 80.4 %scatter_fusion = bf16[12,96,128,128]{3,2,1,0:T(8,128)(2,1)} fusion(bf16[12,96,128,128]{3,2,1,0:T(8,128)(2,1)} %broadcast_in_dim.65, s32[512]{0:T(512)S(1)} %bitcast.111, bf16[512,128,128]{2,1,0:T(8,128)(2,1)} %bitcast_select_fusion.1), kind=kCustom, calls=%fused_computation.4 | custom fusion | bytes 50335744 | tf_op jit(solution)/shard_map/scatter | solution.py:20
  275.2 35.2 %copy.20 = bf16[12,128,96,128]{3,2,1,0:T(8,128)(2,1)} copy(bf16[12,128,96,128]{3,1,2,0:T(8,128)(2,1)} %bitcast.104) | data formatting | bytes 75497472 | tf_op jit(solution)/shard_map/transpose | solution.py:21
  310.4 46.8 %fusion.51 = bf16[512,12288]{0,1:T(8,128)(2,1)} fusion(bf16[512,1536]{0,1:T(8,128)(2,1)} %all-gather.3.cloned.1.call-done, bf16[192,8,96,128]{3,2,1,0:T(8,128)(2,1)} %bitcast.107), kind=kOutput, calls=%fused_computation.61 | convolution fusion | flops 19333644288 | bytes 51904512 | tf_op jit(solution)/shard_map/dot_general | solution.py:75
  357.2 47.2 %fusion.48 = bf16[512,12288]{0,1:T(8,128)(2,1)} fusion(bf16[512,1536]{0,1:T(8,128)(2,1)} %all-gather.5.cloned.1.call-done, bf16[192,8,96,128]{3,2,1,0:T(8,128)(2,1)} %bitcast.109), kind=kOutput, calls=%fused_computation.60 | convolution fusion | flops 19333644288 | bytes 51904512 | tf_op jit(solution)/shard_map/dot_general | solution.py:32
  404.4 0.0 copy-start.3
  404.4 0.0 copy-start.4
  404.4 0.0 copy-start
  404.4 0.0 all-reduce.3.cloned.1.call-update
  404.5 0.0 reduce-scatter.3.cloned.1.call-start
  404.5 0.6 pad_clamp_fusion.2
  405.1 0.0 copy-done.3
  405.2 0.0 copy-done.4
  405.2 0.6 pad_clamp_fusion.1
  405.8 0.5 compare_and_fusion.2
  406.3 0.6 compare_and_fusion
  406.9 0.0 copy-done
  406.9 0.9 copy.24
  407.8 1.9 copy.27
  409.7 25.6 %gather_fusion = bf16[512,512,128]{2,1,0:T(8,128)(2,1)} fusion(bf16[512,12,128]{2,0,1:T(8,128)(2,1)S(1)} %copy.24, s32[1024]{0:T(1024)S(1)} %pad_clamp_fusion.3), kind=kCustom, calls=%fused_computation.clone | custom fusion | bytes 134219776 | tf_op jit(solution)/shard_map/jit(_take)/gather | solution.py:26
  435.3 25.0 %gather_fusion.3 = bf16[512,512,128]{2,1,0:T(8,128)(2,1)} fusion(bf16[512,12,128]{2,0,1:T(8,128)(2,1)S(1)} %copy.27, s32[1024]{0:T(1024)S(1)} %pad_clamp_fusion), kind=kCustom, calls=%fused_computation.2.clone | custom fusion | bytes 134219776 | tf_op jit(solution)/shard_map/jit(_take)/gather | solution.py:27
  460.3 694.8 %all-reduce.3.cloned.1.call-done = (bf16[512,12288]{0,1:T(8,128)(2,1)}, bf16[512,12288]{0,1:T(8,128)(2,1)}) async-done(((bf16[512,12288]{0,1:T(8,128)(2,1)}, bf16[512,12288]{0,1:T(8,128)(2,1)}), (bf16[512,12288]{0,1:T(8,128)(2,1)}, bf16[512,12288]{0,1:T(8,128)(2,1)})) %all-reduce.3.cloned.1.call-update) | async-done | bytes 25165840 | tf_op jit(solution)/shard_map/psum | solution.py:38
  1155.1 35.0 %fusion.65 = bf16[512,1536]{1,0:T(8,128)(2,1)} fusion(bf16[192,8,96,128]{3,2,1,0:T(8,128)(2,1)} %bitcast.110, bf16[512,12288]{0,1:T(8,128)(2,1)} %get-tuple-element.6), kind=kOutput, calls=%fused_computation.63 | convolution fusion | flops 19391053824 | bytes 51904512 | tf_op jit(solution)/shard_map/dot_general | solution.py:77
  1190.1 0.0 reduce-scatter.3.cloned.1.call-update
  1190.1 0.0 reduce-scatter.5.cloned.1.call-start
  1190.2 25.6 %fusion.37 = (bf16[512,12288]{0,1:T(8,128)(2,1)}, bf16[512,12288]{0,1:T(8,128)(2,1)}) fusion(bf16[512,12288]{0,1:T(8,128)(2,1)} %get-tuple-element.6, bf16[512,12288]{0,1:T(8,128)(2,1)} %get-tuple-element.7), kind=kLoop, calls=%fused_computation.51 | loop fusion | flops 150994944 | bytes 50331648 | tf_op jit(solution)/shard_map/convert_element_type | solution.py:76
  1215.8 15.9 %copy.25 = bf16[512,96,128]{2,0,1:T(8,128)(2,1)} copy(bf16[512,96,128]{0,2,1:T(8,128)(2,1)} %bitcast.106) | data formatting | bytes 25165824 | tf_op jit(solution)/shard_map/reshape | solution.py:27
  1231.7 28.9 %fusion.62 = bf16[512,1536]{1,0:T(8,128)(2,1)} fusion(bf16[512,12288]{0,1:T(8,128)(2,1)} %get-tuple-element.9, bf16[192,8,96,128]{3,2,1,0:T(8,128)(2,1)} %bitcast.108), kind=kOutput, calls=%fused_computation.62 | convolution fusion | flops 19328139264 | bytes 51904512 | tf_op jit(solution)/shard_map/dot_general | solution.py:32
  1260.6 0.0 reduce-scatter.5.cloned.1.call-update
  1260.6 0.0 copy-done.5
  1260.6 0.0 copy-start.6
  1260.6 29.8 %gather_fusion.1 = bf16[512,512,128]{2,1,0:T(8,128)(2,1)} fusion(bf16[512,96,128]{2,0,1:T(8,128)(2,1)} %copy.25, s32[1024]{0:T(1024)S(1)} %copy-done.5), kind=kCustom, calls=%fused_computation.1.clone | custom fusion | bytes 134219776 | tf_op jit(solution)/shard_map/jit(_take)/gather | solution.py:27
  1290.4 0.0 copy-done.6
  1290.4 29.7 %gather_fusion.2 = bf16[512,512,128]{1,2,0:T(8,128)(2,1)} fusion(bf16[512,96,128]{0,2,1:T(8,128)(2,1)} %bitcast.103, s32[1024]{0:T(1024)S(1)} %copy-done.6), kind=kCustom, calls=%fused_computation.3.clone | custom fusion | bytes 134219776 | tf_op jit(solution)/shard_map/jit(_take)/gather | solution.py:26
  1320.2 0.0 copy-done.8
  1320.2 0.0 copy-done.13
  1320.2 0.0 copy-done.14
  1320.2 0.0 copy-start.10
  1320.2 0.0 copy-start.11
  1320.2 0.0 copy-start.12
  1320.2 48.7 %fusion.47 = bf16[1,1,512,128,128]{4,3,2,1,0:T(8,128)(2,1)} fusion(pred[512]{0:T(512)(128)(4,1)S(1)} %copy-done.8, bf16[512,512,128]{2,1,0:T(8,128)(2,1)} %gather_fusion.3, pred[512]{0:T(512)(128)(4,1)S(1)} %copy-done.13, bf16[512,512,128]{1,2,0:T(8,128)(2,1)} %gather_fusion.2, pred[512]{0:T(512)(128)(4,1)S(1)} %copy-done.14), kind=kOutput, calls=%fused_computation.57 | convolution fusion | flops 8673820672 | bytes 150996480 | tf_op jit(solution)/shard_map/tsk,tsn->skn/dot_general | solution.py:28
  1368.9 0.0 copy-done.10
  1368.9 0.0 copy-done.11
  1368.9 0.0 copy-done.12
  1368.9 49.8 %fusion.46 = bf16[1,1,512,128,128]{4,3,2,1,0:T(8,128)(2,1)} fusion(pred[512]{0:T(512)(128)(4,1)S(1)} %copy-done.10, bf16[512,512,128]{2,1,0:T(8,128)(2,1)} %gather_fusion.1, pred[512]{0:T(512)(128)(4,1)S(1)} %copy-done.11, bf16[512,512,128]{2,1,0:T(8,128)(2,1)} %gather_fusion, pred[512]{0:T(512)(128)(4,1)S(1)} %copy-done.12), kind=kOutput, calls=%fused_computation.56 | convolution fusion | flops 8673820672 | bytes 150996480 | tf_op jit(solution)/shard_map/tsk,tsn->skn/dot_general | solution.py:28
  (19 shorter events, 0.1 us)
Async XLA Ops:
  7.2 303.2 %all-gather.3.cloned.1.call-start = ((), (), s32[]{:S(2)}) async-start(), calls=%async_computation.2 | async-start | bytes 1966080 | tf_op jit(solution)/shard_map/all_gather | solution.py:60
  9.1 348.1 %all-gather.5.cloned.1.call-start = ((), (), s32[]{:S(2)}) async-start(), calls=%async_computation.4 | async-start | bytes 1966080 | tf_op jit(solution)/shard_map/all_gather | solution.py:61
  11.1 1144.0 %all-reduce.3.cloned.1.call-start = ((), (), s32[]{:S(2)}) async-start(), calls=%async_computation.6 | async-start | bytes 50331648 | tf_op jit(solution)/shard_map/psum | solution.py:38
  11.8 0.7 copy-start.7
  120.3 46.9 %copy-start.1 = (s32[1,1,512]{2,1,0:T(1,128)S(1)}, s32[1,1,512]{2,1,0:T(1,128)}, u32[]{:S(2)}) copy-start(s32[1,1,512]{2,1,0:T(1,128)} %param.18) | copy-start | bytes 6148
  120.3 46.9 %copy-start.2 = (s32[1,1,512]{2,1,0:T(1,128)S(1)}, s32[1,1,512]{2,1,0:T(1,128)}, u32[]{:S(2)}) copy-start(s32[1,1,512]{2,1,0:T(1,128)} %param.17) | copy-start | bytes 6148
  167.2 0.5 copy-start.9
  404.4 0.7 copy-start.3
  404.4 0.8 copy-start.4
  404.4 2.5 copy-start
  404.5 1014.3 %reduce-scatter.3.cloned.1.call-start = ((), (), s32[]{:S(2)}) async-start(), calls=%async_computation.3 | async-start | bytes 1966080 | tf_op jit(solution)/shard_map/reduce_scatter | solution.py:42
  1190.1 228.6 %reduce-scatter.5.cloned.1.call-start = ((), (), s32[]{:S(2)}) async-start(), calls=%async_computation.5 | async-start | bytes 1966080 | tf_op jit(solution)/shard_map/reduce_scatter | solution.py:42
  1231.7 28.9 %copy-start.5 = (s32[1024]{0:T(1024)S(1)}, s32[1024]{0:T(1024)}, u32[]{:S(2)}) copy-start(s32[1024]{0:T(1024)} %pad_clamp_fusion.2) | copy-start | bytes 12292
  1260.6 29.8 %copy-start.6 = (s32[1024]{0:T(1024)S(1)}, s32[1024]{0:T(1024)}, u32[]{:S(2)}) copy-start(s32[1024]{0:T(1024)} %pad_clamp_fusion.1) | copy-start | bytes 12292
  1290.4 29.7 %copy-start.8 = (pred[512]{0:T(512)(128)(4,1)S(1)}, pred[512]{0:T(512)(128)(4,1)}, u32[]{:S(2)}) copy-start(pred[512]{0:T(512)(128)(4,1)} %copy-done.7) | copy-start | bytes 1540
  1290.4 29.7 %copy-start.13 = (pred[512]{0:T(512)(128)(4,1)S(1)}, pred[512]{0:T(512)(128)(4,1)}, u32[]{:S(2)}) copy-start(pred[512]{0:T(512)(128)(4,1)} %get-tuple-element.12) | copy-start | bytes 1540
  1290.4 29.7 %copy-start.14 = (pred[512]{0:T(512)(128)(4,1)S(1)}, pred[512]{0:T(512)(128)(4,1)}, u32[]{:S(2)}) copy-start(pred[512]{0:T(512)(128)(4,1)} %get-tuple-element.13) | copy-start | bytes 1540
  1320.2 48.8 %copy-start.10 = (pred[512]{0:T(512)(128)(4,1)S(1)}, pred[512]{0:T(512)(128)(4,1)}, u32[]{:S(2)}) copy-start(pred[512]{0:T(512)(128)(4,1)} %copy-done.9) | copy-start | bytes 1540
  1320.2 48.8 %copy-start.11 = (pred[512]{0:T(512)(128)(4,1)S(1)}, pred[512]{0:T(512)(128)(4,1)}, u32[]{:S(2)}) copy-start(pred[512]{0:T(512)(128)(4,1)} %get-tuple-element.10) | copy-start | bytes 1540
  1320.2 48.8 %copy-start.12 = (pred[512]{0:T(512)(128)(4,1)S(1)}, pred[512]{0:T(512)(128)(4,1)}, u32[]{:S(2)}) copy-start(pred[512]{0:T(512)(128)(4,1)} %get-tuple-element.11) | copy-start | bytes 1540
Sparse Core Ops, SparseCore 0:
  10.1 22.5 all-gather.2
  34.8 19.8 all-gather.4
  404.6 750.4 all-reduce.2
  1190.3 27.2 reduce-scatter.2
  1260.7 27.1 reduce-scatter.4
where the time goes:
time: 1430 us
  waiting for transfers between devices  695 us (49%)
  local copies, waits for them, and re-layouts  401 us (28%)
  matrix products  256 us (18%)
  other arithmetic  57.6 us (4%)
  between operations  15.5 us (1%)
    psum x1, waiting for transfers between devices, total_sum(): return lax.psum(term.astype(jnp.bfloat16), 'col').astype(jnp.float32)  695 us
    scatter x2, local copies, waits for them, and re-layouts, dense_tile(): jnp.zeros((n_first, n_second, BLK, BLK), vals.dtype).at[first, second]  161 us
    dot_general x2, matrix products, slot_grad(): jnp.einsum('tsk,tsn->skn', left_pick, right_pick, preferred_element_type=...  98.5 us
    transpose x2, local copies, waits for them, and re-layouts, dense_tile(): return layout.transpose(0, 2, 1, 3).reshape(n_first * BLK, n_second * BLK)  81.4 us
    dot_general x2, matrix products, back_product(): lax.dot_general(left, weight, (((1,), (1,)), ((), ())), preferred_element...  76 us
    gather x2, local copies, waits for them, and re-layouts, slot_grad(): left_pick = jnp.take(left.reshape(rows, -1, BLK), left_idx, axis=1)  55.3 us
    gather x2, local copies, waits for them, and re-layouts, slot_grad(): right_pick = jnp.take(right.reshape(rows, -1, BLK), right_idx, axis=1)  54.8 us
    dot_general x1, matrix products, shards(): jnp.dot(full_x, w_first, preferred_element_type=jnp.float32)  46.8 us
  transfers between devices with their start and end apart: 5, of which 1 were waited for; matrix products, arithmetic and copies ran while one was open for 44% of the time, Pallas kernels for 0%

commit v1 on v0

v1 whole, which is shorter than its diff:
```python
import functools

import jax
import jax.numpy as jnp
from jax import lax
from jax.experimental import pallas as pl
from jax.experimental.pallas import tpu as pltpu
from jax.sharding import PartitionSpec as P

BLK = 128
Z_CHIPS = 4
ROOT_2_PI = 0.7978845608028654
CUBIC = 0.044715
VMEM_LIMIT = 40 << 20


def ring_of(n):
    if n % Z_CHIPS or n // Z_CHIPS < 2:
        return list(range(n))
    wide = n // Z_CHIPS
    order = [z * wide for z in range(Z_CHIPS)]
    for k, z in enumerate(reversed(range(Z_CHIPS))):
        ys = range(1, wide) if k % 2 == 0 else range(wide - 1, 0, -1)
        order += [z * wide + y for y in ys]
    return order


def gelu_pair(value, grad):
    inner = ROOT_2_PI * (value + CUBIC * (value * value * value))
    th = jnp.tanh(inner)
    half = 0.5 * (1.0 + th)
    slope = half + 0.5 * value * (1.0 - th * th) * (ROOT_2_PI * (1.0 + (3.0 * CUBIC) * (value * value)))
    return value * half, grad * slope


def block_table(first, second, count, n_second, n_total):
    slots = first.shape[0]
    ids = jnp.arange(slots, dtype=jnp.int32)
    key = jnp.where(ids < count, first * n_second + second, -1)
    hit = key[None, :] == jnp.arange(n_total, dtype=jnp.int32)[:, None]
    return jnp.max(jnp.where(hit, ids[None, :], -1), axis=1)


class Tiles:
    def __init__(self, base, tab1, tab2, vals1, vals2, buf1, buf2, sems, sizes, width):
        self.args = (tab1, tab2, vals1, vals2, buf1, buf2, sems)
        self.width = width
        self.blocks = []
        for g, size in enumerate(sizes):
            for k in range(size):
                self.blocks.append((base[g] + k) * width)

    def place(self, which, b, r):
        tab1, tab2, vals1, vals2, buf1, buf2, sems = self.args
        wide = pl.ds(pl.multiple_of(r * BLK, BLK), BLK)
        if which == 0:
            return tab1, vals1, buf1.at[wide, pl.ds(b * BLK, BLK)], sems.at[0, b, r]
        return tab2, vals2, buf2.at[pl.ds(b * BLK, BLK), wide], sems.at[1, b, r]

    def start(self):
        def step(r, carry):
            for which in (0, 1):
                for b, row in enumerate(self.blocks):
                    tab, vals, dst, sem = self.place(which, b, r)
                    slot = tab[row + r]

                    @pl.when(slot >= 0)
                    def _():
                        pltpu.make_async_copy(vals.at[jnp.maximum(slot, 0)], dst, sem).start()

                    @pl.when(slot < 0)
                    def _():
                        dst[...] = jnp.zeros((BLK, BLK), dst.dtype)
            return carry

        lax.fori_loop(0, self.width, step, 0)

    def wait(self):
        def step(r, carry):
            for which in (0, 1):
                for b, row in enumerate(self.blocks):
                    tab, vals, dst, sem = self.place(which, b, r)

                    @pl.when(tab[row + r] >= 0)
                    def _():
                        pltpu.make_async_copy(vals.at[0], dst, sem).wait()
            return carry

        lax.fori_loop(0, self.width, step, 0)


def dot_nn(a, b):
    return jnp.dot(a, b, preferred_element_type=jnp.float32)


def dot_nt(a, b):
    return lax.dot_general(a, b, (((1,), (1,)), ((), ())), preferred_element_type=jnp.float32)


def dot_tn(a, b):
    return lax.dot_general(a, b, (((0,), (0,)), ((), ())), preferred_element_type=jnp.float32)


def up_kernel(sizes, width, has_in, last, *refs):
    base, tab1, tab2, x, dy, vals1, vals2 = refs[:7]
    refs = refs[7:]
    n = len(sizes)
    ins = refs[:n] if has_in else [None] * n
    refs = refs[n:] if has_in else refs
    outs, refs = refs[:n], refs[n:]
    buf1, buf2, sems = refs
    tiles = Tiles(base, tab1, tab2, vals1, vals2, buf1, buf2, sems, sizes, width)
    tiles.start()
    tiles.wait()
    where = [(g, k) for g, size in enumerate(sizes) for k in range(size)]
    total = len(where)
    for lo in range(0, total, 2):
        cnt = min(2, total - lo)
        span = pl.ds(lo * BLK, cnt * BLK)
        hid = dot_nn(x[...], buf1[:, span])
        grd = dot_nt(dy[...], buf2[span, :])
        for i in range(cnt):
            g, k = where[lo + i]
            at = pl.ds(k * BLK, BLK)
            h = hid[:, i * BLK : (i + 1) * BLK]
            d = grd[:, i * BLK : (i + 1) * BLK]
            if has_in:
                h = h + ins[g][0, :, at].astype(jnp.float32)
                d = d + ins[g][1, :, at].astype(jnp.float32)
            if last:
                h, d = gelu_pair(h, d)
            outs[g][0, :, at] = h.astype(jnp.bfloat16)
            outs[g][1, :, at] = d.astype(jnp.bfloat16)


def smem():
    return pl.BlockSpec(memory_space=pltpu.SMEM)


def vmem():
    return pl.BlockSpec(memory_space=pltpu.VMEM)


def hbm():
    return pl.BlockSpec(memory_space=pl.ANY)


def tile_scratch(total, width):
    return [
        pltpu.VMEM((width * BLK, total * BLK), jnp.bfloat16),
        pltpu.VMEM((total * BLK, width * BLK), jnp.bfloat16),
        pltpu.SemaphoreType.DMA((2, total, width)),
    ]


def up_call(sizes, width, base, tabs, x, dy, vals, ins, last):
    total = sum(sizes)
    tokens = x.shape[0]
    has_in = ins is not None
    return pl.pallas_call(
        functools.partial(up_kernel, sizes, width, has_in, last),
        out_shape=[jax.ShapeDtypeStruct((2, tokens, s * BLK), jnp.bfloat16) for s in sizes],
        in_specs=[smem()] * 3 + [vmem()] * 2 + [hbm()] * 2 + [vmem()] * (len(sizes) if has_in else 0),
        out_specs=[vmem()] * len(sizes),
        scratch_shapes=tile_scratch(total, width),
        compiler_params=pltpu.CompilerParams(vmem_limit_bytes=VMEM_LIMIT),
        cost_estimate=pl.CostEstimate(
            flops=4 * tokens * width * total * BLK * BLK,
            bytes_accessed=4 * width * total * BLK * BLK + 8 * tokens * total * BLK,
            transcendentals=0,
        ),
        name="up_last" if last else "up",
    )(base, *tabs, x, dy, *vals, *(ins if has_in else ()))


def down_kernel(sizes, width, first, last, *refs):
    base, tab1, tab2, vals1, vals2 = refs[:5]
    refs = refs[5:]
    n = len(sizes)
    acts, refs = refs[:n], refs[n:]
    if not first:
        out_in, in_in = refs[:2]
        refs = refs[2:]
    out_o, in_o, buf1, buf2, sems = refs
    step = pl.program_id(0)

    @pl.when(step == 0)
    def _():
        tiles = Tiles(base, tab1, tab2, vals1, vals2, buf1, buf2, sems, sizes, width)
        tiles.start()
        tiles.wait()

    wide = out_o.shape[1]
    span = pl.ds(pl.multiple_of(step * wide, BLK), wide)
    act = jnp.concatenate([a[0] for a in acts], axis=1)
    grd = jnp.concatenate([a[1] for a in acts], axis=1)
    out = dot_nn(act, buf2[:, span])
    inp = dot_nt(grd, buf1[span, :])
    if not first:
        out = out + out_in[...]
        inp = inp + in_in[...]
    out_o[...] = out.astype(out_o.dtype)
    in_o[...] = inp.astype(in_o.dtype)


def down_call(sizes, width, base, tabs, vals, acts, sums, last):
    total = sum(sizes)
    tokens = acts[0].shape[1]
    first = sums is None
    pair = 2 if width % 2 == 0 else 1
    dtype = jnp.bfloat16 if last else jnp.float32
    acc = pl.BlockSpec((tokens, pair * BLK), lambda i: (0, i))
    shape = jax.ShapeDtypeStruct((tokens, width * BLK), dtype)
    return pl.pallas_call(
        functools.partial(down_kernel, sizes, width, first, last),
        grid=(width // pair,),
        out_shape=[shape, shape],
        in_specs=[smem()] * 3 + [hbm()] * 2 + [vmem()] * len(sizes) + ([] if first else [acc, acc]),
        out_specs=[acc, acc],
        scratch_shapes=tile_scratch(total, width),
        compiler_params=pltpu.CompilerParams(
            vmem_limit_bytes=VMEM_LIMIT, dimension_semantics=("arbitrary",)
        ),
        cost_estimate=pl.CostEstimate(
            flops=4 * tokens * width * total * BLK * BLK,
            bytes_accessed=4 * width * total * BLK * BLK + 16 * tokens * width * BLK,
            transcendentals=0,
        ),
        name="down",
    )(base, *tabs, *vals, *acts, *(() if first else sums))


def grad_kernel(sizes, width, *refs):
    base, tab1, tab2, x_t, dy = refs[:5]
    refs = refs[5:]
    n = len(sizes)
    acts, refs = refs[:n], refs[n:]
    _, _, first_o, second_o, act_t, stage1, stage2, sems = refs
    total = sum(sizes)
    rows = []
    for g, size in enumerate(sizes):
        for k in range(size):
            rows.append((base[g] + k) * width)
    act = jnp.concatenate([a[0] for a in acts], axis=1)
    act_t[...] = act.T
    pairs = (total + 1) // 2
    where = [(g, k) for g, size in enumerate(sizes) for k in range(size)]

    def copies(part, which, b, at, r, go):
        tab = tab1 if which == 0 else tab2
        out = first_o if which == 0 else second_o
        stage = stage1 if which == 0 else stage2
        slot = tab[rows[b] + r]

        @pl.when(slot >= 0)
        def _():
            copy = pltpu.make_async_copy(
                stage.at[part, at], out.at[jnp.maximum(slot, 0)], sems.at[which, part, at]
            )
            if go:
                copy.start()
            else:
                copy.wait()

    plan1 = []
    for p in range(pairs):
        plan1.append([b for b in (2 * p, 2 * p + 1) if b < total])

    def sweep1(p, go):
        for i, b in enumerate(plan1[p]):
            for r in range(width):
                copies(p % 2, 0, b, i * width + r, r, go)

    for p in range(pairs):
        blocks = plan1[p]
        hid = jnp.concatenate(
            [acts[where[b][0]][1, :, where[b][1] * BLK : (where[b][1] + 1) * BLK] for b in blocks], axis=1
        )
        res = dot_nn(x_t[...], hid).astype(jnp.bfloat16)
        if p >= 2:
            sweep1(p - 2, False)
        for i in range(len(blocks)):
            for r in range(width):
                stage1[p % 2, i * width + r] = res[r * BLK : (r + 1) * BLK, i * BLK : (i + 1) * BLK]
        sweep1(p, True)
    span = 2 if width % 2 == 0 else 1
    steps = width // span

    def sweep2(p, go):
        for b in range(total):
            for i in range(span):
                copies(p % 2, 1, b, b * span + i, p * span + i, go)

    for p in range(steps):
        res = dot_nn(act_t[...], dy[:, p * span * BLK : (p + 1) * span * BLK]).astype(jnp.bfloat16)
        if p >= 2:
            sweep2(p - 2, False)
        for b in range(total):
            for i in range(span):
                stage2[p % 2, b * span + i] = res[b * BLK : (b + 1) * BLK, i * BLK : (i + 1) * BLK]
        sweep2(p, True)
    for p in range(max(0, pairs - 2), pairs):
        sweep1(p, False)
    for p in range(max(0, steps - 2), steps):
        sweep2(p, False)


def grad_call(sizes, width, base, tabs, x_t, dy, acts, grads):
    total = sum(sizes)
    tokens = dy.shape[0]
    span = 2 if width % 2 == 0 else 1
    n_stage = max(2 * width, total * span)
    shape = jax.ShapeDtypeStruct(grads[0].shape, jnp.bfloat16)
    n = len(sizes)
    return pl.pallas_call(
        functools.partial(grad_kernel, sizes, width),
        out_shape=[shape, shape],
        in_specs=[smem()] * 3 + [vmem()] * (2 + n) + [hbm()] * 2,
        out_specs=[hbm(), hbm()],
        scratch_shapes=[
            pltpu.VMEM((total * BLK, tokens), jnp.bfloat16),
            pltpu.VMEM((2, n_stage, BLK, BLK), jnp.bfloat16),
            pltpu.VMEM((2, n_stage, BLK, BLK), jnp.bfloat16),
            pltpu.SemaphoreType.DMA((2, 2, n_stage)),
        ],
        input_output_aliases={5 + n: 0, 6 + n: 1},
        compiler_params=pltpu.CompilerParams(vmem_limit_bytes=VMEM_LIMIT),
        cost_estimate=pl.CostEstimate(
            flops=4 * tokens * width * total * BLK * BLK,
            bytes_accessed=4 * width * total * BLK * BLK // 2 + 8 * tokens * width * BLK,
            transcendentals=0,
        ),
        name="grads",
    )(base, *tabs, x_t, dy, *acts, *grads)


def shards(
    inputs,
    out_grad,
    first_vals,
    first_rows,
    first_cols,
    first_count,
    second_vals,
    second_rows,
    second_cols,
    second_count,
    *,
    hidden_blocks,
):
    n = lax.axis_size("col")
    ring = ring_of(n)
    ahead = [(ring[k], ring[(k + 1) % n]) for k in range(n)]
    back = [(b, a) for a, b in ahead]
    place = [0] * n
    for k, dev in enumerate(ring):
        place[dev] = k
    me = jnp.asarray(place, jnp.int32)[lax.axis_index("col")]

    x = lax.all_gather(inputs, "row", axis=0, tiled=True)
    dy = lax.all_gather(out_grad, "row", axis=0, tiled=True)
    width = x.shape[1] // BLK
    per = hidden_blocks // n
    vals = (first_vals[0, 0], second_vals[0, 0])
    n_blocks = hidden_blocks * width
    tabs = (
        block_table(first_cols[0, 0], first_rows[0, 0], first_count[0, 0], width, n_blocks),
        block_table(second_rows[0, 0], second_cols[0, 0], second_count[0, 0], width, n_blocks),
    )

    n_ahead = (per + 1) // 2
    parts = []
    for lo, cnt, sign in ((0, n_ahead, 1), (n_ahead, per - n_ahead, -1)):
        half = (cnt + 1) // 2
        parts.append([(lo, half, sign), (lo + half, cnt - half, sign)])
    streams = [[part[s] for part in parts if part[s][1] > 0] for s in range(2)]
    streams = [s for s in streams if s]

    def bases(stream, shift):
        return jnp.stack([((me - sign * shift) % n) * per + lo for lo, _, sign in stream])

    def hop(stream, arrays):
        return [
            lax.ppermute(a, "col", ahead if sign > 0 else back) for a, (_, _, sign) in zip(arrays, stream)
        ]

    held = [None] * len(streams)
    for t in range(n):
        for s, stream in enumerate(streams):
            sizes = tuple(c for _, c, _ in stream)
            ins = None if t == 0 else hop(stream, held[s])
            held[s] = up_call(sizes, width, bases(stream, t + 1), tabs, x, dy, vals, ins, t == n - 1)

    x_t = x.T
    grads = (jnp.zeros_like(vals[0]), jnp.zeros_like(vals[1]))
    sums = None
    for t in range(n):
        for s, stream in enumerate(streams):
            sizes = tuple(c for _, c, _ in stream)
            if t > 0:
                held[s] = hop(stream, held[s])
            base = bases(stream, t)
            last = t == n - 1 and s == len(streams) - 1
            sums = down_call(sizes, width, base, tabs, vals, held[s], sums, last)
            grads = grad_call(sizes, width, base, tabs, x_t, dy, held[s], grads)

    out_sum = lax.psum_scatter(sums[0], "row", scatter_dimension=0, tiled=True)
    in_sum = lax.psum_scatter(sums[1], "row", scatter_dimension=0, tiled=True)
    return out_sum, in_sum, grads[0][None, None], grads[1][None, None]


def solution(mesh):
    hidden_blocks = 49152 // BLK // mesh.shape["row"]
    placed = (
        P("row", "col"),
        P("row", "col"),
        P("row", "col", None, None, None),
        P("row", "col", None),
        P("row", "col", None),
        P("row", "col"),
        P("row", "col", None, None, None),
        P("row", "col", None),
        P("row", "col", None),
        P("row", "col"),
    )
    return jax.shard_map(
        functools.partial(shards, hidden_blocks=hidden_blocks),
        mesh=mesh,
        in_specs=placed,
        out_specs=(
            P("row", "col"),
            P("row", "col"),
            P("row", "col", None, None, None),
            P("row", "col", None, None, None),
        ),
        check_vma=False,
    )
```

time: 1430 us -> 729 us (0.51)
  the two profiles are of different devices: /device:TPU:0 before, /device:TPU:4 now
where the time goes in v1:
time: 729 us; the launch traced here: 716 us
  Pallas kernels  406 us (56%)
  waiting for transfers between devices  186 us (26%)
  starting transfers between devices  59.3 us (8%)
  local copies, waits for them, and re-layouts  31.6 us (4%)
  between operations  29.7 us (4%)
    ppermute x56, waiting for transfers between devices, hop(): lax.ppermute(a, 'col', ahead if sign > 0 else back)  150 us
    pallas_call x16, Pallas kernels, down_call(): pl.pallas_call(functools.partial(down_kernel, sizes, width, first, last),...  144 us
    pallas_call x16, Pallas kernels, up_call(): pl.pallas_call(functools.partial(up_kernel, sizes, width, has_in, last),...  136 us
    pallas_call x16, Pallas kernels, grad_call(): pl.pallas_call(functools.partial(grad_kernel, sizes, width), out_shape=[s...  125 us
    ppermute x56, starting transfers between devices, hop(): lax.ppermute(a, 'col', ahead if sign > 0 else back)  59.2 us
    all_gather x1, waiting for transfers between devices, shards(): dy = lax.all_gather(out_grad, 'row', axis=0, tiled=True)  19.5 us
    unnamed x209, local copies, waits for them, and re-layouts  15.7 us
    all_gather x1, waiting for transfers between devices, shards(): x = lax.all_gather(inputs, 'row', axis=0, tiled=True)  15.1 us
  transfers between devices with their start and end apart: 60, of which 37 were waited for; matrix products, arithmetic and copies ran while one was open for 3% of the time, Pallas kernels for 54%

profile of v1, /device:TPU:4, one launch (start us, length us, event | category | flops | bytes accessed | tf_op | source)
XLA Modules:
  0.0 715.6 jit_solution(10075251161246580966)
XLA Ops:
  16.1 15.1 %all-gather.3.cloned.1.call-done = bf16[512,1536]{0,1:T(8,128)(2,1)} async-done(((bf16[128,1536]{0,1:T(8,128)(2,1)}), bf16[512,1536]{0,1:T(8,128)(2,1)}) %all-gather.3.cloned.1.call-update) | async-done | bytes 1572880 | tf_op jit(solution)/shard_map/all_gather | solution.py:360
  32.9 19.5 %all-gather.5.cloned.1.call-done.refs_4_ = bf16[512,1536]{1,0:T(8,128)(2,1)} async-done(((bf16[128,1536]{1,0:T(8,128)(2,1)}), bf16[512,1536]{1,0:T(8,128)(2,1)}) %all-gather.5.cloned.1.call-update) | async-done | bytes 1572880 | tf_op jit(solution)/shard_map/all_gather | solution.py:361
  53.9 8.0 %up.21 = (bf16[2,512,384]{2,1,0:T(8,128)(2,1)}, bf16[2,512,384]{2,1,0:T(8,128)(2,1)}) custom-call(s32[2]{0:T(128)S(1)} %pad_add_fusion.15.refs_0_, s32[1152]{0:T(1024)S(1)} %get-tuple-element.197.refs_1_, s32[1152]{0:T(1024)S(1)} %get-tuple-element.196.refs_2_, bf16[512,1536]{1,0:T(8,128)(2,1)S(1)} %copy.72.refs_3_, bf16[512,1536]{1,0:T(8,128)(2,1)S(1)} %copy-done, ...), custom_call_target="tpu_custom_call" | custom-call | flops 2415919104 | bytes 7864320 | tf_op jit(solution)/shard_map/up/pallas_call | solution.py:160
  64.0 7.9 %up.14 = (bf16[2,512,384]{2,1,0:T(8,128)(2,1)}, bf16[2,512,384]{2,1,0:T(8,128)(2,1)}) custom-call(s32[2]{0:T(128)S(1)} %pad_add_fusion.7.refs_0_, s32[1152]{0:T(1024)S(1)} %get-tuple-element.197.refs_1_, s32[1152]{0:T(1024)S(1)} %get-tuple-element.196.refs_2_, bf16[512,1536]{1,0:T(8,128)(2,1)S(1)} %copy.72.refs_3_, bf16[512,1536]{1,0:T(8,128)(2,1)S(1)} %copy-done.1, ...), custom_call_target="tpu_custom_call" | custom-call | flops 2415919104 | bytes 7864320 | tf_op jit(solution)/shard_map/up/pallas_call | solution.py:160
  75.5 7.1 collective-permute-done.28.refs_7_
  83.2 8.7 %up.22 = (bf16[2,512,384]{2,1,0:T(8,128)(2,1)}, bf16[2,512,384]{2,1,0:T(8,128)(2,1)}) custom-call(s32[2]{0:T(128)S(1)} %pad_add_fusion.14.refs_0_, s32[1152]{0:T(1024)S(1)} %get-tuple-element.197.refs_1_, s32[1152]{0:T(1024)S(1)} %get-tuple-element.196.refs_2_, bf16[512,1536]{1,0:T(8,128)(2,1)S(1)} %copy.72.refs_3_, bf16[512,1536]{1,0:T(8,128)(2,1)S(1)} %copy-done.1, ...), custom_call_target="tpu_custom_call" | custom-call | flops 2415919104 | bytes 7864320 | tf_op jit(solution)/shard_map/up/pallas_call | solution.py:160
  94.0 5.4 collective-permute-done.refs_7_
  100.1 8.6 %up.15 = (bf16[2,512,384]{2,1,0:T(8,128)(2,1)}, bf16[2,512,384]{2,1,0:T(8,128)(2,1)}) custom-call(s32[2]{0:T(128)S(1)} %pad_add_fusion.6.refs_0_, s32[1152]{0:T(1024)S(1)} %get-tuple-element.197.refs_1_, s32[1152]{0:T(1024)S(1)} %get-tuple-element.196.refs_2_, bf16[512,1536]{1,0:T(8,128)(2,1)S(1)} %copy.72.refs_3_, bf16[512,1536]{1,0:T(8,128)(2,1)S(1)} %copy-done.1, ...), custom_call_target="tpu_custom_call" | custom-call | flops 2415919104 | bytes 7864320 | tf_op jit(solution)/shard_map/up/pallas_call | solution.py:160
  116.9 8.7 %up.23 = (bf16[2,512,384]{2,1,0:T(8,128)(2,1)}, bf16[2,512,384]{2,1,0:T(8,128)(2,1)}) custom-call(s32[2]{0:T(128)S(1)} %pad_add_fusion.13.refs_0_, s32[1152]{0:T(1024)S(1)} %get-tuple-element.197.refs_1_, s32[1152]{0:T(1024)S(1)} %get-tuple-element.196.refs_2_, bf16[512,1536]{1,0:T(8,128)(2,1)S(1)} %copy.72.refs_3_, bf16[512,1536]{1,0:T(8,128)(2,1)S(1)} %copy-done.1, ...), custom_call_target="tpu_custom_call" | custom-call | flops 2415919104 | bytes 7864320 | tf_op jit(solution)/shard_map/up/pallas_call | solution.py:160
  133.8 8.6 %up.16 = (bf16[2,512,384]{2,1,0:T(8,128)(2,1)}, bf16[2,512,384]{2,1,0:T(8,128)(2,1)}) custom-call(s32[2]{0:T(128)S(1)} %pad_add_fusion.5.refs_0_, s32[1152]{0:T(1024)S(1)} %get-tuple-element.197.refs_1_, s32[1152]{0:T(1024)S(1)} %get-tuple-element.196.refs_2_, bf16[512,1536]{1,0:T(8,128)(2,1)S(1)} %copy.72.refs_3_, bf16[512,1536]{1,0:T(8,128)(2,1)S(1)} %copy-done.1, ...), custom_call_target="tpu_custom_call" | custom-call | flops 2415919104 | bytes 7864320 | tf_op jit(solution)/shard_map/up/pallas_call | solution.py:160
  150.6 8.7 %up.24 = (bf16[2,512,384]{2,1,0:T(8,128)(2,1)}, bf16[2,512,384]{2,1,0:T(8,128)(2,1)}) custom-call(s32[2]{0:T(128)S(1)} %pad_add_fusion.12.refs_0_, s32[1152]{0:T(1024)S(1)} %get-tuple-element.197.refs_1_, s32[1152]{0:T(1024)S(1)} %get-tuple-element.196.refs_2_, bf16[512,1536]{1,0:T(8,128)(2,1)S(1)} %copy.72.refs_3_, bf16[512,1536]{1,0:T(8,128)(2,1)S(1)} %copy-done.1, ...), custom_call_target="tpu_custom_call" | custom-call | flops 2415919104 | bytes 7864320 | tf_op jit(solution)/shard_map/up/pallas_call | solution.py:160
  161.4 5.4 collective-permute-done.4.refs_7_
  167.5 8.6 %up.17 = (bf16[2,512,384]{2,1,0:T(8,128)(2,1)}, bf16[2,512,384]{2,1,0:T(8,128)(2,1)}) custom-call(s32[2]{0:T(128)S(1)} %pad_add_fusion.4.refs_0_, s32[1152]{0:T(1024)S(1)} %get-tuple-element.197.refs_1_, s32[1152]{0:T(1024)S(1)} %get-tuple-element.196.refs_2_, bf16[512,1536]{1,0:T(8,128)(2,1)S(1)} %copy.72.refs_3_, bf16[512,1536]{1,0:T(8,128)(2,1)S(1)} %copy-done.1, ...), custom_call_target="tpu_custom_call" | custom-call | flops 2415919104 | bytes 7864320 | tf_op jit(solution)/shard_map/up/pallas_call | solution.py:160
  184.3 8.7 %up.25 = (bf16[2,512,384]{2,1,0:T(8,128)(2,1)}, bf16[2,512,384]{2,1,0:T(8,128)(2,1)}) custom-call(s32[2]{0:T(128)S(1)} %pad_add_fusion.11.refs_0_, s32[1152]{0:T(1024)S(1)} %get-tuple-element.197.refs_1_, s32[1152]{0:T(1024)S(1)} %get-tuple-element.196.refs_2_, bf16[512,1536]{1,0:T(8,128)(2,1)S(1)} %copy.72.refs_3_, bf16[512,1536]{1,0:T(8,128)(2,1)S(1)} %copy-done.1, ...), custom_call_target="tpu_custom_call" | custom-call | flops 2415919104 | bytes 7864320 | tf_op jit(solution)/shard_map/up/pallas_call | solution.py:160
  195.2 5.4 collective-permute-done.6.refs_7_
  201.2 8.6 %up.18 = (bf16[2,512,384]{2,1,0:T(8,128)(2,1)}, bf16[2,512,384]{2,1,0:T(8,128)(2,1)}) custom-call(s32[2]{0:T(128)S(1)} %pad_add_fusion.3.refs_0_, s32[1152]{0:T(1024)S(1)} %get-tuple-element.197.refs_1_, s32[1152]{0:T(1024)S(1)} %get-tuple-element.196.refs_2_, bf16[512,1536]{1,0:T(8,128)(2,1)S(1)} %copy.72.refs_3_, bf16[512,1536]{1,0:T(8,128)(2,1)S(1)} %copy-done.1, ...), custom_call_target="tpu_custom_call" | custom-call | flops 2415919104 | bytes 7864320 | tf_op jit(solution)/shard_map/up/pallas_call | solution.py:160
  218.0 8.7 %up.26 = (bf16[2,512,384]{2,1,0:T(8,128)(2,1)}, bf16[2,512,384]{2,1,0:T(8,128)(2,1)}) custom-call(s32[2]{0:T(128)S(1)} %pad_add_fusion.10.refs_0_, s32[1152]{0:T(1024)S(1)} %get-tuple-element.197.refs_1_, s32[1152]{0:T(1024)S(1)} %get-tuple-element.196.refs_2_, bf16[512,1536]{1,0:T(8,128)(2,1)S(1)} %copy.72.refs_3_, bf16[512,1536]{1,0:T(8,128)(2,1)S(1)} %copy-done.1, ...), custom_call_target="tpu_custom_call" | custom-call | flops 2415919104 | bytes 7864320 | tf_op jit(solution)/shard_map/up/pallas_call | solution.py:160
  228.8 5.4 collective-permute-done.8.refs_7_
  234.9 8.6 %up.19 = (bf16[2,512,384]{2,1,0:T(8,128)(2,1)}, bf16[2,512,384]{2,1,0:T(8,128)(2,1)}) custom-call(s32[2]{0:T(128)S(1)} %pad_add_fusion.2.refs_0_, s32[1152]{0:T(1024)S(1)} %get-tuple-element.197.refs_1_, s32[1152]{0:T(1024)S(1)} %get-tuple-element.196.refs_2_, bf16[512,1536]{1,0:T(8,128)(2,1)S(1)} %copy.72.refs_3_, bf16[512,1536]{1,0:T(8,128)(2,1)S(1)} %copy-done.1, ...), custom_call_target="tpu_custom_call" | custom-call | flops 2415919104 | bytes 7864320 | tf_op jit(solution)/shard_map/up/pallas_call | solution.py:160
  251.7 8.7 %up.27 = (bf16[2,512,384]{2,1,0:T(8,128)(2,1)}, bf16[2,512,384]{2,1,0:T(8,128)(2,1)}) custom-call(s32[2]{0:T(128)S(1)} %pad_add_fusion.8.refs_0_, s32[1152]{0:T(1024)S(1)} %get-tuple-element.197.refs_1_, s32[1152]{0:T(1024)S(1)} %get-tuple-element.196.refs_2_, bf16[512,1536]{1,0:T(8,128)(2,1)S(1)} %copy.72.refs_3_, bf16[512,1536]{1,0:T(8,128)(2,1)S(1)} %copy-done.1, ...), custom_call_target="tpu_custom_call" | custom-call | flops 2415919104 | bytes 7864320 | tf_op jit(solution)/shard_map/up/pallas_call | solution.py:160
  262.5 5.4 collective-permute-done.10.refs_7_
  268.6 8.6 %up.20 = (bf16[2,512,384]{2,1,0:T(8,128)(2,1)}, bf16[2,512,384]{2,1,0:T(8,128)(2,1)}) custom-call(s32[2]{0:T(128)S(1)} %pad_add_fusion.refs_0_, s32[1152]{0:T(1024)S(1)} %get-tuple-element.197.refs_1_, s32[1152]{0:T(1024)S(1)} %get-tuple-element.196.refs_2_, bf16[512,1536]{1,0:T(8,128)(2,1)S(1)} %copy.72.refs_3_, bf16[512,1536]{1,0:T(8,128)(2,1)S(1)} %copy-done.1, ...), custom_call_target="tpu_custom_call" | custom-call | flops 2415919104 | bytes 7864320 | tf_op jit(solution)/shard_map/up/pallas_call | solution.py:160
  285.4 8.3 %up_last.3 = (bf16[2,512,384]{2,1,0:T(8,128)(2,1)S(1)}, bf16[2,512,384]{2,1,0:T(8,128)(2,1)S(1)}) custom-call(s32[2]{0:T(128)S(1)} %pad_add_fusion.9.refs_0_, s32[1152]{0:T(1024)S(1)} %get-tuple-element.197.refs_1_, s32[1152]{0:T(1024)S(1)} %get-tuple-element.196.refs_2_, bf16[512,1536]{1,0:T(8,128)(2,1)S(1)} %copy.72.refs_3_, ...), custom_call_target="tpu_custom_call" | custom-call | flops 2415919104 | bytes 7864320 | tf_op jit(solution)/shard_map/up_last/pallas_call | solution.py:160
  295.8 5.8 collective-permute-done.12.refs_7_
  302.3 8.3 %up_last.2 = (bf16[2,512,384]{2,1,0:T(8,128)(2,1)S(1)}, bf16[2,512,384]{2,1,0:T(8,128)(2,1)S(1)}) custom-call(s32[2]{0:T(128)S(1)} %pad_add_fusion.1.refs_0_, s32[1152]{0:T(1024)S(1)} %get-tuple-element.197.refs_1_, s32[1152]{0:T(1024)S(1)} %get-tuple-element.196.refs_2_, bf16[512,1536]{1,0:T(8,128)(2,1)S(1)} %copy.72.refs_3_, ...), custom_call_target="tpu_custom_call" | custom-call | flops 2415919104 | bytes 7864320 | tf_op jit(solution)/shard_map/up_last/pallas_call | solution.py:160
  322.3 13.0 %collective-permute-done.14.refs_5_ = bf16[2,512,384]{2,1,0:T(8,128)(2,1)S(1)} collective-permute-done((bf16[2,512,384]{2,1,0:T(8,128)(2,1)S(1)}, bf16[2,512,384]{2,1,0:T(8,128)(2,1)S(1)}, u32[]{:S(2)}, u32[]{:S(2)}) %collective-permute-start.14) | collective-permute-done | bytes 786464 | tf_op jit(solution)/shard_map/ppermute | solution.py:384
  338.5 13.6 %collective-permute-done.43.refs_5_ = bf16[2,512,384]{2,1,0:T(8,128)(2,1)S(1)} collective-permute-done((bf16[2,512,384]{2,1,0:T(8,128)(2,1)S(1)}, bf16[2,512,384]{2,1,0:T(8,128)(2,1)S(1)}, u32[]{:S(2)}, u32[]{:S(2)}) %collective-permute-start.43) | collective-permute-done | bytes 786464 | tf_op jit(solution)/shard_map/ppermute | solution.py:384
  356.0 13.1 %collective-permute-done.15.refs_5_ = bf16[2,512,384]{2,1,0:T(8,128)(2,1)} collective-permute-done((bf16[2,512,384]{2,1,0:T(8,128)(2,1)S(1)}, bf16[2,512,384]{2,1,0:T(8,128)(2,1)}, u32[]{:S(2)}, u32[]{:S(2)}) %collective-permute-start.15) | collective-permute-done | bytes 786464 | tf_op jit(solution)/shard_map/ppermute | solution.py:384
  371.2 14.8 %collective-permute-done.44.refs_5_ = bf16[2,512,384]{2,1,0:T(8,128)(2,1)} collective-permute-done((bf16[2,512,384]{2,1,0:T(8,128)(2,1)S(1)}, bf16[2,512,384]{2,1,0:T(8,128)(2,1)}, u32[]{:S(2)}, u32[]{:S(2)}) %collective-permute-start.44) | collective-permute-done | bytes 786464 | tf_op jit(solution)/shard_map/ppermute | solution.py:384
  390.1 12.7 %collective-permute-done.16.refs_5_ = bf16[2,512,384]{2,1,0:T(8,128)(2,1)} collective-permute-done((bf16[2,512,384]{2,1,0:T(8,128)(2,1)}, bf16[2,512,384]{2,1,0:T(8,128)(2,1)}, u32[]{:S(2)}, u32[]{:S(2)}) %collective-permute-start.16) | collective-permute-done | bytes 786464 | tf_op jit(solution)/shard_map/ppermute | solution.py:384
  407.2 8.4 %down.16 = (f32[512,1536]{1,0:T(8,128)S(1)}, f32[512,1536]{1,0:T(8,128)S(1)}) custom-call(s32[2]{0:T(128)S(1)} %pad_add_fusion.17.refs_0_, s32[1152]{0:T(1024)S(1)} %get-tuple-element.197.refs_1_, s32[1152]{0:T(1024)S(1)} %get-tuple-element.196.refs_2_, bf16[512,128,128]{2,1,0:T(8,128)(2,1)} %bitcast.80, bf16[512,128,128]{2,1,0:T(8,128)(2,1)} %bitcast.112, ...), custom_call_target="tpu_custom_call" | custom-call | flops 2415919104 | bytes 17301504 | tf_op jit(solution)/shard_map/down/pallas_call | solution.py:214
  415.7 8.9 %down.17 = (f32[512,1536]{1,0:T(8,128)S(1)}, f32[512,1536]{1,0:T(8,128)S(1)}) custom-call(s32[2]{0:T(128)S(1)} %pad_add_fusion.16.refs_0_, s32[1152]{0:T(1024)S(1)} %get-tuple-element.197.refs_1_, s32[1152]{0:T(1024)S(1)} %get-tuple-element.196.refs_2_, bf16[512,128,128]{2,1,0:T(8,128)(2,1)} %bitcast.81, bf16[512,128,128]{2,1,0:T(8,128)(2,1)} %bitcast.113, ...), custom_call_target="tpu_custom_call" | custom-call | flops 2415919104 | bytes 17301504 | tf_op jit(solution)/shard_map/down/pallas_call | solution.py:214
  426.6 8.8 %down.18 = (f32[512,1536]{1,0:T(8,128)S(1)}, f32[512,1536]{1,0:T(8,128)S(1)}) custom-call(s32[2]{0:T(128)S(1)} %pad_add_fusion.15.refs_0_, s32[1152]{0:T(1024)S(1)} %get-tuple-element.197.refs_1_, s32[1152]{0:T(1024)S(1)} %get-tuple-element.196.refs_2_, bf16[512,128,128]{2,1,0:T(8,128)(2,1)} %bitcast.82, bf16[512,128,128]{2,1,0:T(8,128)(2,1)} %bitcast.114, ...), custom_call_target="tpu_custom_call" | custom-call | flops 2415919104 | bytes 17301504 | tf_op jit(solution)/shard_map/down/pallas_call | solution.py:214
  438.5 8.8 %down.19 = (f32[512,1536]{1,0:T(8,128)S(1)}, f32[512,1536]{1,0:T(8,128)S(1)}) custom-call(s32[2]{0:T(128)S(1)} %copy-done.62, s32[1152]{0:T(1024)S(1)} %get-tuple-element.197.refs_1_, s32[1152]{0:T(1024)S(1)} %get-tuple-element.196.refs_2_, bf16[512,128,128]{2,1,0:T(8,128)(2,1)} %bitcast.83, bf16[512,128,128]{2,1,0:T(8,128)(2,1)} %bitcast.115, ...), custom_call_target="tpu_custom_call" | custom-call | flops 2415919104 | bytes 17301504 | tf_op jit(solution)/shard_map/down/pallas_call | solution.py:214
  447.4 8.8 %down.20 = (f32[512,1536]{1,0:T(8,128)S(1)}, f32[512,1536]{1,0:T(8,128)S(1)}) custom-call(s32[2]{0:T(128)S(1)} %copy-done.68, s32[1152]{0:T(1024)S(1)} %get-tuple-element.197.refs_1_, s32[1152]{0:T(1024)S(1)} %get-tuple-element.196.refs_2_, bf16[512,128,128]{2,1,0:T(8,128)(2,1)} %bitcast.84, bf16[512,128,128]{2,1,0:T(8,128)(2,1)} %bitcast.116, ...), custom_call_target="tpu_custom_call" | custom-call | flops 2415919104 | bytes 17301504 | tf_op jit(solution)/shard_map/down/pallas_call | solution.py:214
  456.3 9.6 %down.21 = (f32[512,1536]{1,0:T(8,128)S(1)}, f32[512,1536]{1,0:T(8,128)S(1)}) custom-call(s32[2]{0:T(128)S(1)} %copy-done.65, s32[1152]{0:T(1024)S(1)} %get-tuple-element.197.refs_1_, s32[1152]{0:T(1024)S(1)} %get-tuple-element.196.refs_2_, bf16[512,128,128]{2,1,0:T(8,128)(2,1)} %bitcast.85, bf16[512,128,128]{2,1,0:T(8,128)(2,1)} %bitcast.117, ...), custom_call_target="tpu_custom_call" | custom-call | flops 2415919104 | bytes 17301504 | tf_op jit(solution)/shard_map/down/pallas_call | solution.py:214
  467.9 9.6 %down.22 = (f32[512,1536]{1,0:T(8,128)S(1)}, f32[512,1536]{1,0:T(8,128)S(1)}) custom-call(s32[2]{0:T(128)S(1)} %copy-done.74, s32[1152]{0:T(1024)S(1)} %get-tuple-element.197.refs_1_, s32[1152]{0:T(1024)S(1)} %get-tuple-element.196.refs_2_, bf16[512,128,128]{2,1,0:T(8,128)(2,1)} %bitcast.86, bf16[512,128,128]{2,1,0:T(8,128)(2,1)} %bitcast.118, ...), custom_call_target="tpu_custom_call" | custom-call | flops 2415919104 | bytes 17301504 | tf_op jit(solution)/shard_map/down/pallas_call | solution.py:214
  480.0 9.5 %down.23 = (f32[512,1536]{1,0:T(8,128)S(1)}, f32[512,1536]{1,0:T(8,128)S(1)}) custom-call(s32[2]{0:T(128)S(1)} %copy-done.71, s32[1152]{0:T(1024)S(1)} %get-tuple-element.197.refs_1_, s32[1152]{0:T(1024)S(1)} %get-tuple-element.196.refs_2_, bf16[512,128,128]{2,1,0:T(8,128)(2,1)} %bitcast.87, bf16[512,128,128]{2,1,0:T(8,128)(2,1)} %bitcast.119, ...), custom_call_target="tpu_custom_call" | custom-call | flops 2415919104 | bytes 17301504 | tf_op jit(solution)/shard_map/down/pallas_call | solution.py:214
  489.6 9.6 %down.24 = (f32[512,1536]{1,0:T(8,128)S(1)}, f32[512,1536]{1,0:T(8,128)S(1)}) custom-call(s32[2]{0:T(128)S(1)} %copy-done.80, s32[1152]{0:T(1024)S(1)} %get-tuple-element.197.refs_1_, s32[1152]{0:T(1024)S(1)} %get-tuple-element.196.refs_2_, bf16[512,128,128]{2,1,0:T(8,128)(2,1)} %bitcast.88, bf16[512,128,128]{2,1,0:T(8,128)(2,1)} %bitcast.120, ...), custom_call_target="tpu_custom_call" | custom-call | flops 2415919104 | bytes 17301504 | tf_op jit(solution)/shard_map/down/pallas_call | solution.py:214
  499.2 8.9 %down.25 = (f32[512,1536]{1,0:T(8,128)S(1)}, f32[512,1536]{1,0:T(8,128)S(1)}) custom-call(s32[2]{0:T(128)S(1)} %copy-done.77, s32[1152]{0:T(1024)S(1)} %get-tuple-element.197.refs_1_, s32[1152]{0:T(1024)S(1)} %get-tuple-element.196.refs_2_, bf16[512,128,128]{2,1,0:T(8,128)(2,1)} %bitcast.89, bf16[512,128,128]{2,1,0:T(8,128)(2,1)} %bitcast.121, ...), custom_call_target="tpu_custom_call" | custom-call | flops 2415919104 | bytes 17301504 | tf_op jit(solution)/shard_map/down/pallas_call | solution.py:214
  510.2 8.9 %down.26 = (f32[512,1536]{1,0:T(8,128)S(1)}, f32[512,1536]{1,0:T(8,128)S(1)}) custom-call(s32[2]{0:T(128)S(1)} %copy-done.86, s32[1152]{0:T(1024)S(1)} %get-tuple-element.197.refs_1_, s32[1152]{0:T(1024)S(1)} %get-tuple-element.196.refs_2_, bf16[512,128,128]{2,1,0:T(8,128)(2,1)} %bitcast.90, bf16[512,128,128]{2,1,0:T(8,128)(2,1)} %bitcast.122, ...), custom_call_target="tpu_custom_call" | custom-call | flops 2415919104 | bytes 17301504 | tf_op jit(solution)/shard_map/down/pallas_call | solution.py:214
  521.2 8.9 %down.27 = (f32[512,1536]{1,0:T(8,128)S(1)}, f32[512,1536]{1,0:T(8,128)S(1)}) custom-call(s32[2]{0:T(128)S(1)} %copy-done.83, s32[1152]{0:T(1024)S(1)} %get-tuple-element.197.refs_1_, s32[1152]{0:T(1024)S(1)} %get-tuple-element.196.refs_2_, bf16[512,128,128]{2,1,0:T(8,128)(2,1)} %bitcast.91, bf16[512,128,128]{2,1,0:T(8,128)(2,1)} %bitcast.123, ...), custom_call_target="tpu_custom_call" | custom-call | flops 2415919104 | bytes 17301504 | tf_op jit(solution)/shard_map/down/pallas_call | solution.py:214
  530.1 8.9 %down.28 = (f32[512,1536]{1,0:T(8,128)S(1)}, f32[512,1536]{1,0:T(8,128)S(1)}) custom-call(s32[2]{0:T(128)S(1)} %copy-done.92, s32[1152]{0:T(1024)S(1)} %get-tuple-element.197.refs_1_, s32[1152]{0:T(1024)S(1)} %get-tuple-element.196.refs_2_, bf16[512,128,128]{2,1,0:T(8,128)(2,1)} %bitcast.92, bf16[512,128,128]{2,1,0:T(8,128)(2,1)} %bitcast.124, ...), custom_call_target="tpu_custom_call" | custom-call | flops 2415919104 | bytes 17301504 | tf_op jit(solution)/shard_map/down/pallas_call | solution.py:214
  539.0 8.9 %down.29 = (f32[512,1536]{1,0:T(8,128)S(1)}, f32[512,1536]{1,0:T(8,128)S(1)}) custom-call(s32[2]{0:T(128)S(1)} %copy-done.89, s32[1152]{0:T(1024)S(1)} %get-tuple-element.197.refs_1_, s32[1152]{0:T(1024)S(1)} %get-tuple-element.196.refs_2_, bf16[512,128,128]{2,1,0:T(8,128)(2,1)} %bitcast.93, bf16[512,128,128]{2,1,0:T(8,128)(2,1)} %bitcast.125, ...), custom_call_target="tpu_custom_call" | custom-call | flops 2415919104 | bytes 17301504 | tf_op jit(solution)/shard_map/down/pallas_call | solution.py:214
  548.0 8.9 %down.30 = (f32[512,1536]{1,0:T(8,128)S(1)}, f32[512,1536]{1,0:T(8,128)S(1)}) custom-call(s32[2]{0:T(128)S(1)} %copy-done.98, s32[1152]{0:T(1024)S(1)} %get-tuple-element.197.refs_1_, s32[1152]{0:T(1024)S(1)} %get-tuple-element.196.refs_2_, bf16[512,128,128]{2,1,0:T(8,128)(2,1)} %bitcast.94, bf16[512,128,128]{2,1,0:T(8,128)(2,1)} %bitcast.126, ...), custom_call_target="tpu_custom_call" | custom-call | flops 2415919104 | bytes 17301504 | tf_op jit(solution)/shard_map/down/pallas_call | solution.py:214
  556.9 9.2 %down.31 = (bf16[512,1536]{1,0:T(8,128)(2,1)}, bf16[512,1536]{1,0:T(8,128)(2,1)S(1)}) custom-call(s32[2]{0:T(128)S(1)} %copy-done.95, s32[1152]{0:T(1024)S(1)} %get-tuple-element.197.refs_1_, s32[1152]{0:T(1024)S(1)} %get-tuple-element.196.refs_2_, bf16[512,128,128]{2,1,0:T(8,128)(2,1)} %bitcast.95, bf16[512,128,128]{2,1,0:T(8,128)(2,1)} %bitcast.127, ...), custom_call_target="tpu_custom_call" | custom-call | flops 2415919104 | bytes 17301504 | tf_op jit(solution)/shard_map/down/pallas_call | solution.py:214
  567.4 6.4 broadcast_2_refs_7__refs_8_.2.refs_7_
  573.7 6.7 broadcast_2_refs_7__refs_8_.2.clone.refs_8_
  580.5 7.6 %grads.16 = (bf16[512,128,128]{2,1,0:T(8,128)(2,1)}, bf16[512,128,128]{2,1,0:T(8,128)(2,1)}) custom-call(s32[2]{0:T(128)S(1)} %copy-done.101, s32[1152]{0:T(1024)S(1)} %get-tuple-element.197.refs_1_, s32[1152]{0:T(1024)S(1)} %get-tuple-element.196.refs_2_, bf16[1536,512]{1,0:T(8,128)(2,1)S(1)} %bitcast.48, ...), custom_call_target="tpu_custom_call", output_to_operand_aliasing={{0}: (7, {}), {1}: (8, {})} | custom-call | flops 2415919104 | bytes 8650752 | tf_op jit(solution)/shard_map/grads/pallas_call | solution.py:315
  588.1 7.6 %grads.17 = (bf16[512,128,128]{2,1,0:T(8,128)(2,1)}, bf16[512,128,128]{2,1,0:T(8,128)(2,1)}) custom-call(s32[2]{0:T(128)S(1)} %copy-done.103, s32[1152]{0:T(1024)S(1)} %get-tuple-element.197.refs_1_, s32[1152]{0:T(1024)S(1)} %get-tuple-element.196.refs_2_, bf16[1536,512]{1,0:T(8,128)(2,1)S(1)} %bitcast.49, ...), custom_call_target="tpu_custom_call", output_to_operand_aliasing={{0}: (7, {}), {1}: (8, {})} | custom-call | flops 2415919104 | bytes 8650752 | tf_op jit(solution)/shard_map/grads/pallas_call | solution.py:315
  598.0 7.6 %grads.18 = (bf16[512,128,128]{2,1,0:T(8,128)(2,1)}, bf16[512,128,128]{2,1,0:T(8,128)(2,1)}) custom-call(s32[2]{0:T(128)S(1)} %pad_add_fusion.15.refs_0_, s32[1152]{0:T(1024)S(1)} %get-tuple-element.197.refs_1_, s32[1152]{0:T(1024)S(1)} %get-tuple-element.196.refs_2_, bf16[1536,512]{1,0:T(8,128)(2,1)S(1)} %bitcast.50, ...), custom_call_target="tpu_custom_call", output_to_operand_aliasing={{0}: (7, {}), {1}: (8, {})} | custom-call | flops 2415919104 | bytes 8650752 | tf_op jit(solution)/shard_map/grads/pallas_call | solution.py:315
  605.6 7.7 %grads.19 = (bf16[512,128,128]{2,1,0:T(8,128)(2,1)}, bf16[512,128,128]{2,1,0:T(8,128)(2,1)}) custom-call(s32[2]{0:T(128)S(1)} %copy-done.63, s32[1152]{0:T(1024)S(1)} %get-tuple-element.197.refs_1_, s32[1152]{0:T(1024)S(1)} %get-tuple-element.196.refs_2_, bf16[1536,512]{1,0:T(8,128)(2,1)S(1)} %bitcast.51, ...), custom_call_target="tpu_custom_call", output_to_operand_aliasing={{0}: (7, {}), {1}: (8, {})} | custom-call | flops 2415919104 | bytes 8650752 | tf_op jit(solution)/shard_map/grads/pallas_call | solution.py:315
  613.4 7.6 %grads.20 = (bf16[512,128,128]{2,1,0:T(8,128)(2,1)}, bf16[512,128,128]{2,1,0:T(8,128)(2,1)}) custom-call(s32[2]{0:T(128)S(1)} %copy-done.69, s32[1152]{0:T(1024)S(1)} %get-tuple-element.197.refs_1_, s32[1152]{0:T(1024)S(1)} %get-tuple-element.196.refs_2_, bf16[1536,512]{1,0:T(8,128)(2,1)S(1)} %bitcast.52, ...), custom_call_target="tpu_custom_call", output_to_operand_aliasing={{0}: (7, {}), {1}: (8, {})} | custom-call | flops 2415919104 | bytes 8650752 | tf_op jit(solution)/shard_map/grads/pallas_call | solution.py:315
  621.0 8.2 %grads.21 = (bf16[512,128,128]{2,1,0:T(8,128)(2,1)}, bf16[512,128,128]{2,1,0:T(8,128)(2,1)}) custom-call(s32[2]{0:T(128)S(1)} %copy-done.66, s32[1152]{0:T(1024)S(1)} %get-tuple-element.197.refs_1_, s32[1152]{0:T(1024)S(1)} %get-tuple-element.196.refs_2_, bf16[1536,512]{1,0:T(8,128)(2,1)S(1)} %bitcast.53, ...), custom_call_target="tpu_custom_call", output_to_operand_aliasing={{0}: (7, {}), {1}: (8, {})} | custom-call | flops 2415919104 | bytes 8650752 | tf_op jit(solution)/shard_map/grads/pallas_call | solution.py:315
  629.3 8.7 %grads.22 = (bf16[512,128,128]{2,1,0:T(8,128)(2,1)}, bf16[512,128,128]{2,1,0:T(8,128)(2,1)}) custom-call(s32[2]{0:T(128)S(1)} %copy-done.75, s32[1152]{0:T(1024)S(1)} %get-tuple-element.197.refs_1_, s32[1152]{0:T(1024)S(1)} %get-tuple-element.196.refs_2_, bf16[1536,512]{1,0:T(8,128)(2,1)S(1)} %bitcast.54, ...), custom_call_target="tpu_custom_call", output_to_operand_aliasing={{0}: (7, {}), {1}: (8, {})} | custom-call | flops 2415919104 | bytes 8650752 | tf_op jit(solution)/shard_map/grads/pallas_call | solution.py:315
  638.0 8.2 %grads.23 = (bf16[512,128,128]{2,1,0:T(8,128)(2,1)}, bf16[512,128,128]{2,1,0:T(8,128)(2,1)}) custom-call(s32[2]{0:T(128)S(1)} %copy-done.72, s32[1152]{0:T(1024)S(1)} %get-tuple-element.197.refs_1_, s32[1152]{0:T(1024)S(1)} %get-tuple-element.196.refs_2_, bf16[1536,512]{1,0:T(8,128)(2,1)S(1)} %bitcast.55, ...), custom_call_target="tpu_custom_call", output_to_operand_aliasing={{0}: (7, {}), {1}: (8, {})} | custom-call | flops 2415919104 | bytes 8650752 | tf_op jit(solution)/shard_map/grads/pallas_call | solution.py:315
  646.2 8.4 %grads.24 = (bf16[512,128,128]{2,1,0:T(8,128)(2,1)}, bf16[512,128,128]{2,1,0:T(8,128)(2,1)}) custom-call(s32[2]{0:T(128)S(1)} %copy-done.81, s32[1152]{0:T(1024)S(1)} %get-tuple-element.197.refs_1_, s32[1152]{0:T(1024)S(1)} %get-tuple-element.196.refs_2_, bf16[1536,512]{1,0:T(8,128)(2,1)S(1)} %bitcast.56, ...), custom_call_target="tpu_custom_call", output_to_operand_aliasing={{0}: (7, {}), {1}: (8, {})} | custom-call | flops 2415919104 | bytes 8650752 | tf_op jit(solution)/shard_map/grads/pallas_call | solution.py:315
  654.6 7.7 %grads.25 = (bf16[512,128,128]{2,1,0:T(8,128)(2,1)}, bf16[512,128,128]{2,1,0:T(8,128)(2,1)}) custom-call(s32[2]{0:T(128)S(1)} %copy-done.78, s32[1152]{0:T(1024)S(1)} %get-tuple-element.197.refs_1_, s32[1152]{0:T(1024)S(1)} %get-tuple-element.196.refs_2_, bf16[1536,512]{1,0:T(8,128)(2,1)S(1)} %bitcast.57, ...), custom_call_target="tpu_custom_call", output_to_operand_aliasing={{0}: (7, {}), {1}: (8, {})} | custom-call | flops 2415919104 | bytes 8650752 | tf_op jit(solution)/shard_map/grads/pallas_call | solution.py:315
  662.4 7.6 %grads.26 = (bf16[512,128,128]{2,1,0:T(8,128)(2,1)}, bf16[512,128,128]{2,1,0:T(8,128)(2,1)}) custom-call(s32[2]{0:T(128)S(1)} %copy-done.87, s32[1152]{0:T(1024)S(1)} %get-tuple-element.197.refs_1_, s32[1152]{0:T(1024)S(1)} %get-tuple-element.196.refs_2_, bf16[1536,512]{1,0:T(8,128)(2,1)S(1)} %bitcast.58, ...), custom_call_target="tpu_custom_call", output_to_operand_aliasing={{0}: (7, {}), {1}: (8, {})} | custom-call | flops 2415919104 | bytes 8650752 | tf_op jit(solution)/shard_map/grads/pallas_call | solution.py:315
  670.1 7.6 %grads.27 = (bf16[512,128,128]{2,1,0:T(8,128)(2,1)}, bf16[512,128,128]{2,1,0:T(8,128)(2,1)}) custom-call(s32[2]{0:T(128)S(1)} %copy-done.84, s32[1152]{0:T(1024)S(1)} %get-tuple-element.197.refs_1_, s32[1152]{0:T(1024)S(1)} %get-tuple-element.196.refs_2_, bf16[1536,512]{1,0:T(8,128)(2,1)S(1)} %bitcast.59, ...), custom_call_target="tpu_custom_call", output_to_operand_aliasing={{0}: (7, {}), {1}: (8, {})} | custom-call | flops 2415919104 | bytes 8650752 | tf_op jit(solution)/shard_map/grads/pallas_call | solution.py:315
  677.7 7.8 %grads.28 = (bf16[512,128,128]{2,1,0:T(8,128)(2,1)}, bf16[512,128,128]{2,1,0:T(8,128)(2,1)}) custom-call(s32[2]{0:T(128)S(1)} %copy-done.93, s32[1152]{0:T(1024)S(1)} %get-tuple-element.197.refs_1_, s32[1152]{0:T(1024)S(1)} %get-tuple-element.196.refs_2_, bf16[1536,512]{1,0:T(8,128)(2,1)S(1)} %bitcast.60, ...), custom_call_target="tpu_custom_call", output_to_operand_aliasing={{0}: (7, {}), {1}: (8, {})} | custom-call | flops 2415919104 | bytes 8650752 | tf_op jit(solution)/shard_map/grads/pallas_call | solution.py:315
  685.6 7.5 %grads.29 = (bf16[512,128,128]{2,1,0:T(8,128)(2,1)}, bf16[512,128,128]{2,1,0:T(8,128)(2,1)}) custom-call(s32[2]{0:T(128)S(1)} %copy-done.90, s32[1152]{0:T(1024)S(1)} %get-tuple-element.197.refs_1_, s32[1152]{0:T(1024)S(1)} %get-tuple-element.196.refs_2_, bf16[1536,512]{1,0:T(8,128)(2,1)S(1)} %bitcast.61, ...), custom_call_target="tpu_custom_call", output_to_operand_aliasing={{0}: (7, {}), {1}: (8, {})} | custom-call | flops 2415919104 | bytes 8650752 | tf_op jit(solution)/shard_map/grads/pallas_call | solution.py:315
  693.2 7.5 %grads.30 = (bf16[512,128,128]{2,1,0:T(8,128)(2,1)}, bf16[512,128,128]{2,1,0:T(8,128)(2,1)}) custom-call(s32[2]{0:T(128)S(1)} %copy-done.99, s32[1152]{0:T(1024)S(1)} %get-tuple-element.197.refs_1_, s32[1152]{0:T(1024)S(1)} %get-tuple-element.196.refs_2_, bf16[1536,512]{1,0:T(8,128)(2,1)S(1)} %bitcast.62, ...), custom_call_target="tpu_custom_call", output_to_operand_aliasing={{0}: (7, {}), {1}: (8, {})} | custom-call | flops 2415919104 | bytes 8650752 | tf_op jit(solution)/shard_map/grads/pallas_call | solution.py:315
  700.8 7.8 %grads.31 = (bf16[512,128,128]{2,1,0:T(8,128)(2,1)}, bf16[512,128,128]{2,1,0:T(8,128)(2,1)}) custom-call(s32[2]{0:T(128)S(1)} %copy-done.96, s32[1152]{0:T(1024)S(1)} %get-tuple-element.197.refs_1_, s32[1152]{0:T(1024)S(1)} %get-tuple-element.196.refs_2_, bf16[1536,512]{1,0:T(8,128)(2,1)S(1)} %bitcast.63, ...), custom_call_target="tpu_custom_call", output_to_operand_aliasing={{0}: (7, {}), {1}: (8, {})} | custom-call | flops 2415919104 | bytes 8650752 | tf_op jit(solution)/shard_map/grads/pallas_call | solution.py:315
  (344 shorter events, 124.9 us)
Async XLA Ops:
  7.2 24.0 %all-gather.3.cloned.1.call-start = ((), (), s32[]{:S(2)}) async-start(), calls=%async_computation.2 | async-start | bytes 1966080 | tf_op jit(solution)/shard_map/all_gather | solution.py:360
  9.1 43.3 %all-gather.5.cloned.1.call-start = ((), (), s32[]{:S(2)}) async-start(), calls=%async_computation.3 | async-start | bytes 1966080 | tf_op jit(solution)/shard_map/all_gather | solution.py:361
  9.9 698.7 %reduce-scatter.3.cloned.1.call-start = ((), (), s32[]{:S(2)}) async-start(), calls=%async_computation.4 | async-start | bytes 1966080 | tf_op jit(solution)/shard_map/reduce_scatter | solution.py:407
  61.9 20.7 %collective-permute-start.28 = (bf16[2,512,384]{2,1,0:T(8,128)(2,1)}, bf16[2,512,384]{2,1,0:T(8,128)(2,1)}, u32[]{:S(2)}, u32[]{:S(2)}) collective-permute-start(bf16[2,512,384]{2,1,0:T(8,128)(2,1)} %get-tuple-element.116), channel_id=1, source_target_pairs={{0,2},{2,4},{4,6},{6,7},{7,5},{5,3},{3,1},{1,0},{8,10},{10,12},{12... | collective-permute-start | bytes 2359304 | tf_op jit(solution)/shard_map/ppermute | solution.py:384
  62.5 20.7 %collective-permute-start.29 = (bf16[2,512,384]{2,1,0:T(8,128)(2,1)}, bf16[2,512,384]{2,1,0:T(8,128)(2,1)}, u32[]{:S(2)}, u32[]{:S(2)}) collective-permute-start(bf16[2,512,384]{2,1,0:T(8,128)(2,1)} %get-tuple-element.117), channel_id=1, source_target_pairs={{2,0},{4,2},{6,4},{7,6},{5,7},{3,5},{1,3},{0,1},{10,8},{12,10},{14... | collective-permute-start | bytes 2359304 | tf_op jit(solution)/shard_map/ppermute | solution.py:384
  71.9 27.5 %collective-permute-start = (bf16[2,512,384]{2,1,0:T(8,128)(2,1)}, bf16[2,512,384]{2,1,0:T(8,128)(2,1)}, u32[]{:S(2)}, u32[]{:S(2)}) collective-permute-start(bf16[2,512,384]{2,1,0:T(8,128)(2,1)} %get-tuple-element.100), channel_id=1, source_target_pairs={{0,2},{2,4},{4,6},{6,7},{7,5},{5,3},{3,1},{1,0},{8,10},{10,12},{12... | collective-permute-start | bytes 2359304 | tf_op jit(solution)/shard_map/ppermute | solution.py:384
  72.6 27.5 %collective-permute-start.1 = (bf16[2,512,384]{2,1,0:T(8,128)(2,1)}, bf16[2,512,384]{2,1,0:T(8,128)(2,1)}, u32[]{:S(2)}, u32[]{:S(2)}) collective-permute-start(bf16[2,512,384]{2,1,0:T(8,128)(2,1)} %get-tuple-element.101), channel_id=1, source_target_pairs={{2,0},{4,2},{6,4},{7,6},{5,7},{3,5},{1,3},{0,1},{10,8},{12,10},{14... | collective-permute-start | bytes 2359304 | tf_op jit(solution)/shard_map/ppermute | solution.py:384
  91.9 24.4 %collective-permute-start.30 = (bf16[2,512,384]{2,1,0:T(8,128)(2,1)}, bf16[2,512,384]{2,1,0:T(8,128)(2,1)}, u32[]{:S(2)}, u32[]{:S(2)}) collective-permute-start(bf16[2,512,384]{2,1,0:T(8,128)(2,1)} %get-tuple-element.118), channel_id=1, source_target_pairs={{0,2},{2,4},{4,6},{6,7},{7,5},{5,3},{3,1},{1,0},{8,10},{10,12},{12... | collective-permute-start | bytes 2359304 | tf_op jit(solution)/shard_map/ppermute | solution.py:384
  93.5 23.4 %collective-permute-start.31 = (bf16[2,512,384]{2,1,0:T(8,128)(2,1)}, bf16[2,512,384]{2,1,0:T(8,128)(2,1)}, u32[]{:S(2)}, u32[]{:S(2)}) collective-permute-start(bf16[2,512,384]{2,1,0:T(8,128)(2,1)} %get-tuple-element.119), channel_id=1, source_target_pairs={{2,0},{4,2},{6,4},{7,6},{5,7},{3,5},{1,3},{0,1},{10,8},{12,10},{14... | collective-permute-start | bytes 2359304 | tf_op jit(solution)/shard_map/ppermute | solution.py:384
  108.7 24.5 %collective-permute-start.2 = (bf16[2,512,384]{2,1,0:T(8,128)(2,1)}, bf16[2,512,384]{2,1,0:T(8,128)(2,1)}, u32[]{:S(2)}, u32[]{:S(2)}) collective-permute-start(bf16[2,512,384]{2,1,0:T(8,128)(2,1)} %get-tuple-element.102), channel_id=1, source_target_pairs={{0,2},{2,4},{4,6},{6,7},{7,5},{5,3},{3,1},{1,0},{8,10},{10,12},{12... | collective-permute-start | bytes 2359304 | tf_op jit(solution)/shard_map/ppermute | solution.py:384
  110.3 23.5 %collective-permute-start.3 = (bf16[2,512,384]{2,1,0:T(8,128)(2,1)}, bf16[2,512,384]{2,1,0:T(8,128)(2,1)}, u32[]{:S(2)}, u32[]{:S(2)}) collective-permute-start(bf16[2,512,384]{2,1,0:T(8,128)(2,1)} %get-tuple-element.103), channel_id=1, source_target_pairs={{2,0},{4,2},{6,4},{7,6},{5,7},{3,5},{1,3},{0,1},{10,8},{12,10},{14... | collective-permute-start | bytes 2359304 | tf_op jit(solution)/shard_map/ppermute | solution.py:384
  125.7 24.3 %collective-permute-start.32 = (bf16[2,512,384]{2,1,0:T(8,128)(2,1)}, bf16[2,512,384]{2,1,0:T(8,128)(2,1)}, u32[]{:S(2)}, u32[]{:S(2)}) collective-permute-start(bf16[2,512,384]{2,1,0:T(8,128)(2,1)} %get-tuple-element.120), channel_id=1, source_target_pairs={{0,2},{2,4},{4,6},{6,7},{7,5},{5,3},{3,1},{1,0},{8,10},{10,12},{12... | collective-permute-start | bytes 2359304 | tf_op jit(solution)/shard_map/ppermute | solution.py:384
  127.2 23.4 %collective-permute-start.33 = (bf16[2,512,384]{2,1,0:T(8,128)(2,1)}, bf16[2,512,384]{2,1,0:T(8,128)(2,1)}, u32[]{:S(2)}, u32[]{:S(2)}) collective-permute-start(bf16[2,512,384]{2,1,0:T(8,128)(2,1)} %get-tuple-element.121), channel_id=1, source_target_pairs={{2,0},{4,2},{6,4},{7,6},{5,7},{3,5},{1,3},{0,1},{10,8},{12,10},{14... | collective-permute-start | bytes 2359304 | tf_op jit(solution)/shard_map/ppermute | solution.py:384
  142.3 24.5 %collective-permute-start.4 = (bf16[2,512,384]{2,1,0:T(8,128)(2,1)}, bf16[2,512,384]{2,1,0:T(8,128)(2,1)}, u32[]{:S(2)}, u32[]{:S(2)}) collective-permute-start(bf16[2,512,384]{2,1,0:T(8,128)(2,1)} %get-tuple-element.104), channel_id=1, source_target_pairs={{0,2},{2,4},{4,6},{6,7},{7,5},{5,3},{3,1},{1,0},{8,10},{10,12},{12... | collective-permute-start | bytes 2359304 | tf_op jit(solution)/shard_map/ppermute | solution.py:384
  144.0 23.5 %collective-permute-start.5 = (bf16[2,512,384]{2,1,0:T(8,128)(2,1)}, bf16[2,512,384]{2,1,0:T(8,128)(2,1)}, u32[]{:S(2)}, u32[]{:S(2)}) collective-permute-start(bf16[2,512,384]{2,1,0:T(8,128)(2,1)} %get-tuple-element.105), channel_id=1, source_target_pairs={{2,0},{4,2},{6,4},{7,6},{5,7},{3,5},{1,3},{0,1},{10,8},{12,10},{14... | collective-permute-start | bytes 2359304 | tf_op jit(solution)/shard_map/ppermute | solution.py:384
  159.3 24.4 %collective-permute-start.34 = (bf16[2,512,384]{2,1,0:T(8,128)(2,1)}, bf16[2,512,384]{2,1,0:T(8,128)(2,1)}, u32[]{:S(2)}, u32[]{:S(2)}) collective-permute-start(bf16[2,512,384]{2,1,0:T(8,128)(2,1)} %get-tuple-element.122), channel_id=1, source_target_pairs={{0,2},{2,4},{4,6},{6,7},{7,5},{5,3},{3,1},{1,0},{8,10},{10,12},{12... | collective-permute-start | bytes 2359304 | tf_op jit(solution)/shard_map/ppermute | solution.py:384
  160.9 23.4 %collective-permute-start.35 = (bf16[2,512,384]{2,1,0:T(8,128)(2,1)}, bf16[2,512,384]{2,1,0:T(8,128)(2,1)}, u32[]{:S(2)}, u32[]{:S(2)}) collective-permute-start(bf16[2,512,384]{2,1,0:T(8,128)(2,1)} %get-tuple-element.123), channel_id=1, source_target_pairs={{2,0},{4,2},{6,4},{7,6},{5,7},{3,5},{1,3},{0,1},{10,8},{12,10},{14... | collective-permute-start | bytes 2359304 | tf_op jit(solution)/shard_map/ppermute | solution.py:384
  176.1 24.5 %collective-permute-start.6 = (bf16[2,512,384]{2,1,0:T(8,128)(2,1)}, bf16[2,512,384]{2,1,0:T(8,128)(2,1)}, u32[]{:S(2)}, u32[]{:S(2)}) collective-permute-start(bf16[2,512,384]{2,1,0:T(8,128)(2,1)} %get-tuple-element.106), channel_id=1, source_target_pairs={{0,2},{2,4},{4,6},{6,7},{7,5},{5,3},{3,1},{1,0},{8,10},{10,12},{12... | collective-permute-start | bytes 2359304 | tf_op jit(solution)/shard_map/ppermute | solution.py:384
  177.7 23.5 %collective-permute-start.7 = (bf16[2,512,384]{2,1,0:T(8,128)(2,1)}, bf16[2,512,384]{2,1,0:T(8,128)(2,1)}, u32[]{:S(2)}, u32[]{:S(2)}) collective-permute-start(bf16[2,512,384]{2,1,0:T(8,128)(2,1)} %get-tuple-element.107), channel_id=1, source_target_pairs={{2,0},{4,2},{6,4},{7,6},{5,7},{3,5},{1,3},{0,1},{10,8},{12,10},{14... | collective-permute-start | bytes 2359304 | tf_op jit(solution)/shard_map/ppermute | solution.py:384
  193.1 24.3 %collective-permute-start.36 = (bf16[2,512,384]{2,1,0:T(8,128)(2,1)}, bf16[2,512,384]{2,1,0:T(8,128)(2,1)}, u32[]{:S(2)}, u32[]{:S(2)}) collective-permute-start(bf16[2,512,384]{2,1,0:T(8,128)(2,1)} %get-tuple-element.124), channel_id=1, source_target_pairs={{0,2},{2,4},{4,6},{6,7},{7,5},{5,3},{3,1},{1,0},{8,10},{10,12},{12... | collective-permute-start | bytes 2359304 | tf_op jit(solution)/shard_map/ppermute | solution.py:384
  194.6 23.4 %collective-permute-start.37 = (bf16[2,512,384]{2,1,0:T(8,128)(2,1)}, bf16[2,512,384]{2,1,0:T(8,128)(2,1)}, u32[]{:S(2)}, u32[]{:S(2)}) collective-permute-start(bf16[2,512,384]{2,1,0:T(8,128)(2,1)} %get-tuple-element.125), channel_id=1, source_target_pairs={{2,0},{4,2},{6,4},{7,6},{5,7},{3,5},{1,3},{0,1},{10,8},{12,10},{14... | collective-permute-start | bytes 2359304 | tf_op jit(solution)/shard_map/ppermute | solution.py:384
  209.8 24.5 %collective-permute-start.8 = (bf16[2,512,384]{2,1,0:T(8,128)(2,1)}, bf16[2,512,384]{2,1,0:T(8,128)(2,1)}, u32[]{:S(2)}, u32[]{:S(2)}) collective-permute-start(bf16[2,512,384]{2,1,0:T(8,128)(2,1)} %get-tuple-element.108), channel_id=1, source_target_pairs={{0,2},{2,4},{4,6},{6,7},{7,5},{5,3},{3,1},{1,0},{8,10},{10,12},{12... | collective-permute-start | bytes 2359304 | tf_op jit(solution)/shard_map/ppermute | solution.py:384
  211.4 23.5 %collective-permute-start.9 = (bf16[2,512,384]{2,1,0:T(8,128)(2,1)}, bf16[2,512,384]{2,1,0:T(8,128)(2,1)}, u32[]{:S(2)}, u32[]{:S(2)}) collective-permute-start(bf16[2,512,384]{2,1,0:T(8,128)(2,1)} %get-tuple-element.109), channel_id=1, source_target_pairs={{2,0},{4,2},{6,4},{7,6},{5,7},{3,5},{1,3},{0,1},{10,8},{12,10},{14... | collective-permute-start | bytes 2359304 | tf_op jit(solution)/shard_map/ppermute | solution.py:384
  226.8 24.4 %collective-permute-start.38 = (bf16[2,512,384]{2,1,0:T(8,128)(2,1)}, bf16[2,512,384]{2,1,0:T(8,128)(2,1)}, u32[]{:S(2)}, u32[]{:S(2)}) collective-permute-start(bf16[2,512,384]{2,1,0:T(8,128)(2,1)} %get-tuple-element.126), channel_id=1, source_target_pairs={{0,2},{2,4},{4,6},{6,7},{7,5},{5,3},{3,1},{1,0},{8,10},{10,12},{12... | collective-permute-start | bytes 2359304 | tf_op jit(solution)/shard_map/ppermute | solution.py:384
  228.3 23.4 %collective-permute-start.39 = (bf16[2,512,384]{2,1,0:T(8,128)(2,1)}, bf16[2,512,384]{2,1,0:T(8,128)(2,1)}, u32[]{:S(2)}, u32[]{:S(2)}) collective-permute-start(bf16[2,512,384]{2,1,0:T(8,128)(2,1)} %get-tuple-element.127), channel_id=1, source_target_pairs={{2,0},{4,2},{6,4},{7,6},{5,7},{3,5},{1,3},{0,1},{10,8},{12,10},{14... | collective-permute-start | bytes 2359304 | tf_op jit(solution)/shard_map/ppermute | solution.py:384
  243.5 24.4 %collective-permute-start.10 = (bf16[2,512,384]{2,1,0:T(8,128)(2,1)}, bf16[2,512,384]{2,1,0:T(8,128)(2,1)}, u32[]{:S(2)}, u32[]{:S(2)}) collective-permute-start(bf16[2,512,384]{2,1,0:T(8,128)(2,1)} %get-tuple-element.110), channel_id=1, source_target_pairs={{0,2},{2,4},{4,6},{6,7},{7,5},{5,3},{3,1},{1,0},{8,10},{10,12},{12... | collective-permute-start | bytes 2359304 | tf_op jit(solution)/shard_map/ppermute | solution.py:384
  245.1 23.5 %collective-permute-start.11 = (bf16[2,512,384]{2,1,0:T(8,128)(2,1)}, bf16[2,512,384]{2,1,0:T(8,128)(2,1)}, u32[]{:S(2)}, u32[]{:S(2)}) collective-permute-start(bf16[2,512,384]{2,1,0:T(8,128)(2,1)} %get-tuple-element.111), channel_id=1, source_target_pairs={{2,0},{4,2},{6,4},{7,6},{5,7},{3,5},{1,3},{0,1},{10,8},{12,10},{14... | collective-permute-start | bytes 2359304 | tf_op jit(solution)/shard_map/ppermute | solution.py:384
  260.5 24.4 %collective-permute-start.40 = (bf16[2,512,384]{2,1,0:T(8,128)(2,1)}, bf16[2,512,384]{2,1,0:T(8,128)(2,1)}, u32[]{:S(2)}, u32[]{:S(2)}) collective-permute-start(bf16[2,512,384]{2,1,0:T(8,128)(2,1)} %get-tuple-element.128), channel_id=1, source_target_pairs={{0,2},{2,4},{4,6},{6,7},{7,5},{5,3},{3,1},{1,0},{8,10},{10,12},{12... | collective-permute-start | bytes 2359304 | tf_op jit(solution)/shard_map/ppermute | solution.py:384
  262.1 23.4 %collective-permute-start.41 = (bf16[2,512,384]{2,1,0:T(8,128)(2,1)}, bf16[2,512,384]{2,1,0:T(8,128)(2,1)}, u32[]{:S(2)}, u32[]{:S(2)}) collective-permute-start(bf16[2,512,384]{2,1,0:T(8,128)(2,1)} %get-tuple-element.129), channel_id=1, source_target_pairs={{2,0},{4,2},{6,4},{7,6},{5,7},{3,5},{1,3},{0,1},{10,8},{12,10},{14... | collective-permute-start | bytes 2359304 | tf_op jit(solution)/shard_map/ppermute | solution.py:384
  277.2 24.5 %collective-permute-start.12 = (bf16[2,512,384]{2,1,0:T(8,128)(2,1)}, bf16[2,512,384]{2,1,0:T(8,128)(2,1)}, u32[]{:S(2)}, u32[]{:S(2)}) collective-permute-start(bf16[2,512,384]{2,1,0:T(8,128)(2,1)} %get-tuple-element.112), channel_id=1, source_target_pairs={{0,2},{2,4},{4,6},{6,7},{7,5},{5,3},{3,1},{1,0},{8,10},{10,12},{12... | collective-permute-start | bytes 2359304 | tf_op jit(solution)/shard_map/ppermute | solution.py:384
  278.8 23.5 %collective-permute-start.13 = (bf16[2,512,384]{2,1,0:T(8,128)(2,1)}, bf16[2,512,384]{2,1,0:T(8,128)(2,1)}, u32[]{:S(2)}, u32[]{:S(2)}) collective-permute-start(bf16[2,512,384]{2,1,0:T(8,128)(2,1)} %get-tuple-element.113), channel_id=1, source_target_pairs={{2,0},{4,2},{6,4},{7,6},{5,7},{3,5},{1,3},{0,1},{10,8},{12,10},{14... | collective-permute-start | bytes 2359304 | tf_op jit(solution)/shard_map/ppermute | solution.py:384
  293.8 24.7 %collective-permute-start.42 = (bf16[2,512,384]{2,1,0:T(8,128)(2,1)S(1)}, bf16[2,512,384]{2,1,0:T(8,128)(2,1)S(1)}, u32[]{:S(2)}, u32[]{:S(2)}) collective-permute-start(bf16[2,512,384]{2,1,0:T(8,128)(2,1)S(1)} %get-tuple-element.130.refs_5_), channel_id=1, source_target_pairs={{0,2},{2,4},{4,6},{6,7},{7,5},{5,3},{3,1},{1,0},{8,10},{10,12},{12... | collective-permute-start | bytes 2359304 | tf_op jit(solution)/shard_map/ppermute | solution.py:384
  295.4 24.5 %collective-permute-start.49 = (bf16[2,512,384]{2,1,0:T(8,128)(2,1)S(1)}, bf16[2,512,384]{2,1,0:T(8,128)(2,1)S(1)}, u32[]{:S(2)}, u32[]{:S(2)}) collective-permute-start(bf16[2,512,384]{2,1,0:T(8,128)(2,1)S(1)} %get-tuple-element.131.refs_6_), channel_id=1, source_target_pairs={{2,0},{4,2},{6,4},{7,6},{5,7},{3,5},{1,3},{0,1},{10,8},{12,10},{14... | collective-permute-start | bytes 2359304 | tf_op jit(solution)/shard_map/ppermute | solution.py:384
  310.6 24.6 %collective-permute-start.14 = (bf16[2,512,384]{2,1,0:T(8,128)(2,1)S(1)}, bf16[2,512,384]{2,1,0:T(8,128)(2,1)S(1)}, u32[]{:S(2)}, u32[]{:S(2)}) collective-permute-start(bf16[2,512,384]{2,1,0:T(8,128)(2,1)S(1)} %get-tuple-element.114.refs_5_), channel_id=1, source_target_pairs={{0,2},{2,4},{4,6},{6,7},{7,5},{5,3},{3,1},{1,0},{8,10},{10,12},{12... | collective-permute-start | bytes 2359304 | tf_op jit(solution)/shard_map/ppermute | solution.py:384
  313.1 22.8 %collective-permute-start.21 = (bf16[2,512,384]{2,1,0:T(8,128)(2,1)S(1)}, bf16[2,512,384]{2,1,0:T(8,128)(2,1)S(1)}, u32[]{:S(2)}, u32[]{:S(2)}) collective-permute-start(bf16[2,512,384]{2,1,0:T(8,128)(2,1)S(1)} %get-tuple-element.115.refs_6_), channel_id=1, source_target_pairs={{2,0},{4,2},{6,4},{7,6},{5,7},{3,5},{1,3},{0,1},{10,8},{12,10},{14... | collective-permute-start | bytes 2359304 | tf_op jit(solution)/shard_map/ppermute | solution.py:384
  318.4 33.7 %collective-permute-start.43 = (bf16[2,512,384]{2,1,0:T(8,128)(2,1)S(1)}, bf16[2,512,384]{2,1,0:T(8,128)(2,1)S(1)}, u32[]{:S(2)}, u32[]{:S(2)}) collective-permute-start(bf16[2,512,384]{2,1,0:T(8,128)(2,1)S(1)} %collective-permute-done.42.refs_5_), channel_id=1, source_target_pairs={{0,2},{2,4},{4,6},{6,7},{7,5},{5,3},{3,1},{1,0},{8,10},{10,12},{12... | collective-permute-start | bytes 2359304 | tf_op jit(solution)/shard_map/ppermute | solution.py:384
  319.9 33.7 %collective-permute-start.50 = (bf16[2,512,384]{2,1,0:T(8,128)(2,1)S(1)}, bf16[2,512,384]{2,1,0:T(8,128)(2,1)S(1)}, u32[]{:S(2)}, u32[]{:S(2)}) collective-permute-start(bf16[2,512,384]{2,1,0:T(8,128)(2,1)S(1)} %collective-permute-done.49.refs_6_), channel_id=1, source_target_pairs={{2,0},{4,2},{6,4},{7,6},{5,7},{3,5},{1,3},{0,1},{10,8},{12,10},{14... | collective-permute-start | bytes 2359304 | tf_op jit(solution)/shard_map/ppermute | solution.py:384
  335.3 103.2 %copy-start.9 = (bf16[2,512,384]{2,1,0:T(8,128)(2,1)}, bf16[2,512,384]{2,1,0:T(8,128)(2,1)S(1)}, u32[]{:S(2)}) copy-start(bf16[2,512,384]{2,1,0:T(8,128)(2,1)S(1)} %collective-permute-done.14.refs_5_) | copy-start | bytes 2359300
  335.3 33.8 %collective-permute-start.15 = (bf16[2,512,384]{2,1,0:T(8,128)(2,1)S(1)}, bf16[2,512,384]{2,1,0:T(8,128)(2,1)}, u32[]{:S(2)}, u32[]{:S(2)}) collective-permute-start(bf16[2,512,384]{2,1,0:T(8,128)(2,1)S(1)} %collective-permute-done.14.refs_5_), channel_id=1, source_target_pairs={{0,2},{2,4},{4,6},{6,7},{7,5},{5,3},{3,1},{1,0},{8,10},{10,12},{12... | collective-permute-start | bytes 2359304 | tf_op jit(solution)/shard_map/ppermute | solution.py:384
  335.9 33.8 %collective-permute-start.22 = (bf16[2,512,384]{2,1,0:T(8,128)(2,1)S(1)}, bf16[2,512,384]{2,1,0:T(8,128)(2,1)}, u32[]{:S(2)}, u32[]{:S(2)}) collective-permute-start(bf16[2,512,384]{2,1,0:T(8,128)(2,1)S(1)} %collective-permute-done.21.refs_6_), channel_id=1, source_target_pairs={{2,0},{4,2},{6,4},{7,6},{5,7},{3,5},{1,3},{0,1},{10,8},{12,10},{14... | collective-permute-start | bytes 2359304 | tf_op jit(solution)/shard_map/ppermute | solution.py:384
  352.1 33.8 %collective-permute-start.44 = (bf16[2,512,384]{2,1,0:T(8,128)(2,1)S(1)}, bf16[2,512,384]{2,1,0:T(8,128)(2,1)}, u32[]{:S(2)}, u32[]{:S(2)}) collective-permute-start(bf16[2,512,384]{2,1,0:T(8,128)(2,1)S(1)} %collective-permute-done.43.refs_5_), channel_id=1, source_target_pairs={{0,2},{2,4},{4,6},{6,7},{7,5},{5,3},{3,1},{1,0},{8,10},{10,12},{12... | collective-permute-start | bytes 2359304 | tf_op jit(solution)/shard_map/ppermute | solution.py:384
  353.6 33.0 %collective-permute-start.51 = (bf16[2,512,384]{2,1,0:T(8,128)(2,1)S(1)}, bf16[2,512,384]{2,1,0:T(8,128)(2,1)}, u32[]{:S(2)}, u32[]{:S(2)}) collective-permute-start(bf16[2,512,384]{2,1,0:T(8,128)(2,1)S(1)} %collective-permute-done.50.refs_6_), channel_id=1, source_target_pairs={{2,0},{4,2},{6,4},{7,6},{5,7},{3,5},{1,3},{0,1},{10,8},{12,10},{14... | collective-permute-start | bytes 2359304 | tf_op jit(solution)/shard_map/ppermute | solution.py:384
  369.1 33.7 %collective-permute-start.16 = (bf16[2,512,384]{2,1,0:T(8,128)(2,1)}, bf16[2,512,384]{2,1,0:T(8,128)(2,1)}, u32[]{:S(2)}, u32[]{:S(2)}) collective-permute-start(bf16[2,512,384]{2,1,0:T(8,128)(2,1)} %collective-permute-done.15.refs_5_), channel_id=1, source_target_pairs={{0,2},{2,4},{4,6},{6,7},{7,5},{5,3},{3,1},{1,0},{8,10},{10,12},{12... | collective-permute-start | bytes 2359304 | tf_op jit(solution)/shard_map/ppermute | solution.py:384
  369.7 33.7 %collective-permute-start.23 = (bf16[2,512,384]{2,1,0:T(8,128)(2,1)}, bf16[2,512,384]{2,1,0:T(8,128)(2,1)}, u32[]{:S(2)}, u32[]{:S(2)}) collective-permute-start(bf16[2,512,384]{2,1,0:T(8,128)(2,1)} %collective-permute-done.22.refs_6_), channel_id=1, source_target_pairs={{2,0},{4,2},{6,4},{7,6},{5,7},{3,5},{1,3},{0,1},{10,8},{12,10},{14... | collective-permute-start | bytes 2359304 | tf_op jit(solution)/shard_map/ppermute | solution.py:384
  386.0 38.6 %collective-permute-start.45 = (bf16[2,512,384]{2,1,0:T(8,128)(2,1)}, bf16[2,512,384]{2,1,0:T(8,128)(2,1)}, u32[]{:S(2)}, u32[]{:S(2)}) collective-permute-start(bf16[2,512,384]{2,1,0:T(8,128)(2,1)} %collective-permute-done.44.refs_5_), channel_id=1, source_target_pairs={{0,2},{2,4},{4,6},{6,7},{7,5},{5,3},{3,1},{1,0},{8,10},{10,12},{12... | collective-permute-start | bytes 2359304 | tf_op jit(solution)/shard_map/ppermute | solution.py:384
  386.6 38.6 %collective-permute-start.52 = (bf16[2,512,384]{2,1,0:T(8,128)(2,1)}, bf16[2,512,384]{2,1,0:T(8,128)(2,1)}, u32[]{:S(2)}, u32[]{:S(2)}) collective-permute-start(bf16[2,512,384]{2,1,0:T(8,128)(2,1)} %collective-permute-done.51.refs_6_), channel_id=1, source_target_pairs={{2,0},{4,2},{6,4},{7,6},{5,7},{3,5},{1,3},{0,1},{10,8},{12,10},{14... | collective-permute-start | bytes 2359304 | tf_op jit(solution)/shard_map/ppermute | solution.py:384
  402.8 33.6 %collective-permute-start.17 = (bf16[2,512,384]{2,1,0:T(8,128)(2,1)}, bf16[2,512,384]{2,1,0:T(8,128)(2,1)S(1)}, u32[]{:S(2)}, u32[]{:S(2)}) collective-permute-start(bf16[2,512,384]{2,1,0:T(8,128)(2,1)} %collective-permute-done.16.refs_5_), channel_id=1, source_target_pairs={{0,2},{2,4},{4,6},{6,7},{7,5},{5,3},{3,1},{1,0},{8,10},{10,12},{12... | collective-permute-start | bytes 2359304 | tf_op jit(solution)/shard_map/ppermute | solution.py:384
  403.4 33.6 %collective-permute-start.24 = (bf16[2,512,384]{2,1,0:T(8,128)(2,1)}, bf16[2,512,384]{2,1,0:T(8,128)(2,1)S(1)}, u32[]{:S(2)}, u32[]{:S(2)}) collective-permute-start(bf16[2,512,384]{2,1,0:T(8,128)(2,1)} %collective-permute-done.23.refs_6_), channel_id=1, source_target_pairs={{2,0},{4,2},{6,4},{7,6},{5,7},{3,5},{1,3},{0,1},{10,8},{12,10},{14... | collective-permute-start | bytes 2359304 | tf_op jit(solution)/shard_map/ppermute | solution.py:384
  424.5 41.3 %collective-permute-start.46 = (bf16[2,512,384]{2,1,0:T(8,128)(2,1)}, bf16[2,512,384]{2,1,0:T(8,128)(2,1)S(1)}, u32[]{:S(2)}, u32[]{:S(2)}) collective-permute-start(bf16[2,512,384]{2,1,0:T(8,128)(2,1)} %collective-permute-done.45.refs_5_), channel_id=1, source_target_pairs={{0,2},{2,4},{4,6},{6,7},{7,5},{5,3},{3,1},{1,0},{8,10},{10,12},{12... | collective-permute-start | bytes 2359304 | tf_op jit(solution)/shard_map/ppermute | solution.py:384
  425.1 41.4 %collective-permute-start.53 = (bf16[2,512,384]{2,1,0:T(8,128)(2,1)}, bf16[2,512,384]{2,1,0:T(8,128)(2,1)S(1)}, u32[]{:S(2)}, u32[]{:S(2)}) collective-permute-start(bf16[2,512,384]{2,1,0:T(8,128)(2,1)} %collective-permute-done.52.refs_6_), channel_id=1, source_target_pairs={{2,0},{4,2},{6,4},{7,6},{5,7},{3,5},{1,3},{0,1},{10,8},{12,10},{14... | collective-permute-start | bytes 2359304 | tf_op jit(solution)/shard_map/ppermute | solution.py:384
  436.4 62.7 %copy-start.32 = (bf16[2,512,384]{2,1,0:T(8,128)(2,1)}, bf16[2,512,384]{2,1,0:T(8,128)(2,1)S(1)}, u32[]{:S(2)}) copy-start(bf16[2,512,384]{2,1,0:T(8,128)(2,1)S(1)} %collective-permute-done.17.refs_5_) | copy-start | bytes 2359300
  436.4 41.1 %collective-permute-start.18 = (bf16[2,512,384]{2,1,0:T(8,128)(2,1)S(1)}, bf16[2,512,384]{2,1,0:T(8,128)(2,1)S(1)}, u32[]{:S(2)}, u32[]{:S(2)}) collective-permute-start(bf16[2,512,384]{2,1,0:T(8,128)(2,1)S(1)} %collective-permute-done.17.refs_5_), channel_id=1, source_target_pairs={{0,2},{2,4},{4,6},{6,7},{7,5},{5,3},{3,1},{1,0},{8,10},{10,12},{12... | collective-permute-start | bytes 2359304 | tf_op jit(solution)/shard_map/ppermute | solution.py:384
  437.0 62.1 %copy-start.34 = (bf16[2,512,384]{2,1,0:T(8,128)(2,1)}, bf16[2,512,384]{2,1,0:T(8,128)(2,1)S(1)}, u32[]{:S(2)}) copy-start(bf16[2,512,384]{2,1,0:T(8,128)(2,1)S(1)} %collective-permute-done.24.refs_6_) | copy-start | bytes 2359300
  437.0 41.2 %collective-permute-start.25 = (bf16[2,512,384]{2,1,0:T(8,128)(2,1)S(1)}, bf16[2,512,384]{2,1,0:T(8,128)(2,1)S(1)}, u32[]{:S(2)}, u32[]{:S(2)}) collective-permute-start(bf16[2,512,384]{2,1,0:T(8,128)(2,1)S(1)} %collective-permute-done.24.refs_6_), channel_id=1, source_target_pairs={{2,0},{4,2},{6,4},{7,6},{5,7},{3,5},{1,3},{0,1},{10,8},{12,10},{14... | collective-permute-start | bytes 2359304 | tf_op jit(solution)/shard_map/ppermute | solution.py:384
  465.8 44.3 %copy-start.36 = (bf16[2,512,384]{2,1,0:T(8,128)(2,1)}, bf16[2,512,384]{2,1,0:T(8,128)(2,1)S(1)}, u32[]{:S(2)}) copy-start(bf16[2,512,384]{2,1,0:T(8,128)(2,1)S(1)} %collective-permute-done.46.refs_5_) | copy-start | bytes 2359300
  465.9 42.2 %collective-permute-start.47 = (bf16[2,512,384]{2,1,0:T(8,128)(2,1)S(1)}, bf16[2,512,384]{2,1,0:T(8,128)(2,1)S(1)}, u32[]{:S(2)}, u32[]{:S(2)}) collective-permute-start(bf16[2,512,384]{2,1,0:T(8,128)(2,1)S(1)} %collective-permute-done.46.refs_5_), channel_id=1, source_target_pairs={{0,2},{2,4},{4,6},{6,7},{7,5},{5,3},{3,1},{1,0},{8,10},{10,12},{12... | collective-permute-start | bytes 2359304 | tf_op jit(solution)/shard_map/ppermute | solution.py:384
  466.6 42.3 %collective-permute-start.54 = (bf16[2,512,384]{2,1,0:T(8,128)(2,1)S(1)}, bf16[2,512,384]{2,1,0:T(8,128)(2,1)S(1)}, u32[]{:S(2)}, u32[]{:S(2)}) collective-permute-start(bf16[2,512,384]{2,1,0:T(8,128)(2,1)S(1)} %collective-permute-done.53.refs_6_), channel_id=1, source_target_pairs={{2,0},{4,2},{6,4},{7,6},{5,7},{3,5},{1,3},{0,1},{10,8},{12,10},{14... | collective-permute-start | bytes 2359304 | tf_op jit(solution)/shard_map/ppermute | solution.py:384
  477.6 41.5 %collective-permute-start.19 = (bf16[2,512,384]{2,1,0:T(8,128)(2,1)S(1)}, bf16[2,512,384]{2,1,0:T(8,128)(2,1)S(1)}, u32[]{:S(2)}, u32[]{:S(2)}) collective-permute-start(bf16[2,512,384]{2,1,0:T(8,128)(2,1)S(1)} %collective-permute-done.18.refs_5_), channel_id=1, source_target_pairs={{0,2},{2,4},{4,6},{6,7},{7,5},{5,3},{3,1},{1,0},{8,10},{10,12},{12... | collective-permute-start | bytes 2359304 | tf_op jit(solution)/shard_map/ppermute | solution.py:384
  478.2 41.6 %collective-permute-start.26 = (bf16[2,512,384]{2,1,0:T(8,128)(2,1)S(1)}, bf16[2,512,384]{2,1,0:T(8,128)(2,1)S(1)}, u32[]{:S(2)}, u32[]{:S(2)}) collective-permute-start(bf16[2,512,384]{2,1,0:T(8,128)(2,1)S(1)} %collective-permute-done.25.refs_6_), channel_id=1, source_target_pairs={{2,0},{4,2},{6,4},{7,6},{5,7},{3,5},{1,3},{0,1},{10,8},{12,10},{14... | collective-permute-start | bytes 2359304 | tf_op jit(solution)/shard_map/ppermute | solution.py:384
  508.1 39.8 %collective-permute-start.48 = (bf16[2,512,384]{2,1,0:T(8,128)(2,1)S(1)}, bf16[2,512,384]{2,1,0:T(8,128)(2,1)S(1)}, u32[]{:S(2)}, u32[]{:S(2)}) collective-permute-start(bf16[2,512,384]{2,1,0:T(8,128)(2,1)S(1)} %collective-permute-done.47.refs_5_), channel_id=1, source_target_pairs={{0,2},{2,4},{4,6},{6,7},{7,5},{5,3},{3,1},{1,0},{8,10},{10,12},{12... | collective-permute-start | bytes 2359304 | tf_op jit(solution)/shard_map/ppermute | solution.py:384
  508.8 39.1 %collective-permute-start.55 = (bf16[2,512,384]{2,1,0:T(8,128)(2,1)S(1)}, bf16[2,512,384]{2,1,0:T(8,128)(2,1)S(1)}, u32[]{:S(2)}, u32[]{:S(2)}) collective-permute-start(bf16[2,512,384]{2,1,0:T(8,128)(2,1)S(1)} %collective-permute-done.54.refs_6_), channel_id=1, source_target_pairs={{2,0},{4,2},{6,4},{7,6},{5,7},{3,5},{1,3},{0,1},{10,8},{12,10},{14... | collective-permute-start | bytes 2359304 | tf_op jit(solution)/shard_map/ppermute | solution.py:384
  519.1 37.8 %collective-permute-start.20 = (bf16[2,512,384]{2,1,0:T(8,128)(2,1)S(1)}, bf16[2,512,384]{2,1,0:T(8,128)(2,1)S(1)}, u32[]{:S(2)}, u32[]{:S(2)}) collective-permute-start(bf16[2,512,384]{2,1,0:T(8,128)(2,1)S(1)} %collective-permute-done.19.refs_5_), channel_id=1, source_target_pairs={{0,2},{2,4},{4,6},{6,7},{7,5},{5,3},{3,1},{1,0},{8,10},{10,12},{12... | collective-permute-start | bytes 2359304 | tf_op jit(solution)/shard_map/ppermute | solution.py:384
  519.8 37.1 %collective-permute-start.27 = (bf16[2,512,384]{2,1,0:T(8,128)(2,1)S(1)}, bf16[2,512,384]{2,1,0:T(8,128)(2,1)S(1)}, u32[]{:S(2)}, u32[]{:S(2)}) collective-permute-start(bf16[2,512,384]{2,1,0:T(8,128)(2,1)S(1)} %collective-permute-done.26.refs_6_), channel_id=1, source_target_pairs={{2,0},{4,2},{6,4},{7,6},{5,7},{3,5},{1,3},{0,1},{10,8},{12,10},{14... | collective-permute-start | bytes 2359304 | tf_op jit(solution)/shard_map/ppermute | solution.py:384
  567.3 141.3 %reduce-scatter.5.cloned.1.call-start = ((), (), s32[]{:S(2)}) async-start(), calls=%async_computation.5 | async-start | bytes 1966080 | tf_op jit(solution)/shard_map/reduce_scatter | solution.py:408
  (100 other events, 1052.8 us)
Sparse Core Ops, SparseCore 0:
  10.1 21.0 all-gather.2
  32.8 19.6 all-gather.4
  567.4 28.1 reduce-scatter.2
  598.8 28.1 reduce-scatter.4

commit v2 on v0

v2 whole, which is shorter than its diff:
```python
import functools

import jax
import jax.numpy as jnp
from jax import lax
from jax.experimental import pallas as pl
from jax.experimental.pallas import tpu as pltpu
from jax.sharding import PartitionSpec as P

BLK = 128
Z_CHIPS = 4
ROOT_2_PI = 0.7978845608028654
CUBIC = 0.044715
VMEM_LIMIT = 48 << 20
FIRST_SHIFT = 20
SECOND_SHIFT = 14


def ring_of(n):
    if n % Z_CHIPS or n // Z_CHIPS < 2:
        return list(range(n))
    wide = n // Z_CHIPS
    order = [z * wide for z in range(Z_CHIPS)]
    for k, z in enumerate(reversed(range(Z_CHIPS))):
        ys = range(1, wide) if k % 2 == 0 else range(wide - 1, 0, -1)
        order += [z * wide + y for y in ys]
    return order


def gelu_pair(value, grad):
    inner = ROOT_2_PI * (value + CUBIC * (value * value * value))
    th = jnp.tanh(inner)
    half = 0.5 * (1.0 + th)
    slope = half + 0.5 * value * (1.0 - th * th) * (ROOT_2_PI * (1.0 + (3.0 * CUBIC) * (value * value)))
    return value * half, grad * slope


def slot_order(first, second, count, n_first):
    slots = first.shape[0]
    ids = jnp.arange(slots, dtype=jnp.int32)
    packed = (first << FIRST_SHIFT) | (second << SECOND_SHIFT) | ids
    key = jnp.where(ids < count, packed, jnp.iinfo(jnp.int32).max - slots + ids)
    rank = jnp.sum((key[None, :] < key[:, None]).astype(jnp.int32), axis=1)
    order = jnp.sum(jnp.where(rank[None, :] == ids[:, None], packed[None, :], 0), axis=1)
    edge = jnp.arange(n_first + 1, dtype=jnp.int32) << FIRST_SHIFT
    starts = jnp.sum((key[None, :] < edge[:, None]).astype(jnp.int32), axis=1)
    return starts, order


class Plan:
    def __init__(self, stream, shift, n, per, hidden_blocks, slots, width):
        self.stream, self.shift, self.n, self.per = tuple(stream), shift, n, per
        self.sizes = tuple(c for _, c, _ in stream)
        self.total = sum(self.sizes)
        self.width = width
        self.tokens = None
        self.start_at = (1, 2 + hidden_blocks)
        self.list_at = (3 + 2 * hidden_blocks, 3 + 2 * hidden_blocks + slots)

    def bases(self, meta):
        me = meta[0]
        return [lax.rem(me + (self.n - sign * self.shift) % self.n, self.n) * self.per + lo for lo, _, sign in self.stream]

    def each(self, meta, which, body):
        offset = 0
        for base, size in zip(self.bases(meta), self.sizes):
            lo = meta[self.start_at[which] + base]
            hi = meta[self.start_at[which] + base + size]

            def step(i, carry, base=base, offset=offset):
                entry = meta[self.list_at[which] + i]
                slot = entry & ((1 << SECOND_SHIFT) - 1)
                r = (entry >> SECOND_SHIFT) & ((1 << (FIRST_SHIFT - SECOND_SHIFT)) - 1)
                body(slot, (entry >> FIRST_SHIFT) - base + offset, r)
                return carry

            lax.fori_loop(lo, hi, step, 0)
            offset += size


def block_at(i):
    return pl.ds(pl.multiple_of(i * BLK, BLK), BLK)


def clear(buf):
    def step(i, carry):
        buf[block_at(i), :] = jnp.zeros((BLK, buf.shape[1]), buf.dtype)
        return carry

    lax.fori_loop(0, buf.shape[0] // BLK, step, 0)


def tile_start(plan, meta, vals, buf, sems, which):
    clear(buf)

    def go(slot, b, r):
        dst = buf.at[block_at(r), block_at(b)] if which == 0 else buf.at[block_at(b), block_at(r)]
        pltpu.make_async_copy(vals.at[slot], dst, sems.at[which, b, r]).start()

    plan.each(meta, which, go)


def tile_wait(plan, meta, vals, buf, sems, which):
    def go(slot, b, r):
        pltpu.make_async_copy(vals.at[slot], buf.at[pl.ds(0, BLK), pl.ds(0, BLK)], sems.at[which, b, r]).wait()

    plan.each(meta, which, go)


def dot_nn(a, b):
    return jnp.dot(a, b, preferred_element_type=jnp.float32)


def dot_nt(a, b):
    return lax.dot_general(a, b, (((1,), (1,)), ((), ())), preferred_element_type=jnp.float32)


def spans(plan):
    where = [(g, k) for g, size in enumerate(plan.sizes) for k in range(size)]
    return [(lo, where[lo : lo + 2]) for lo in range(0, plan.total, 2)]


def up_kernel(plan, has_in, last, *refs):
    meta, x, dy, vals1, vals2 = refs[:5]
    refs = refs[5:]
    n = len(plan.sizes)
    ins = refs[:n] if has_in else None
    refs = refs[n:] if has_in else refs
    outs, refs = refs[:n], refs[n:]
    if last:
        hid_ref, refs = refs[0], refs[1:]
    buf1, buf2, sems = refs
    tile_start(plan, meta, vals1, buf1, sems, 0)
    tile_start(plan, meta, vals2, buf2, sems, 1)
    tile_wait(plan, meta, vals1, buf1, sems, 0)
    for lo, pair in spans(plan):
        res = dot_nn(x[...], buf1[:, lo * BLK : (lo + len(pair)) * BLK])
        for i, (g, k) in enumerate(pair):
            at = slice(k * BLK, (k + 1) * BLK)
            h = res[:, i * BLK : (i + 1) * BLK]
            if has_in:
                h = h + ins[g][0, :, at].astype(jnp.float32)
            if last:
                hid_ref[:, (lo + i) * BLK : (lo + i + 1) * BLK] = h
            else:
                outs[g][0, :, at] = h.astype(jnp.bfloat16)
    tile_wait(plan, meta, vals2, buf2, sems, 1)
    for lo, pair in spans(plan):
        res = dot_nt(dy[...], buf2[lo * BLK : (lo + len(pair)) * BLK, :])
        for i, (g, k) in enumerate(pair):
            at = slice(k * BLK, (k + 1) * BLK)
            d = res[:, i * BLK : (i + 1) * BLK]
            if has_in:
                d = d + ins[g][1, :, at].astype(jnp.float32)
            if last:
                act, d = gelu_pair(hid_ref[:, (lo + i) * BLK : (lo + i + 1) * BLK], d)
                outs[g][0, :, at] = act.astype(jnp.bfloat16)
            outs[g][1, :, at] = d.astype(jnp.bfloat16)


def smem():
    return pl.BlockSpec(memory_space=pltpu.SMEM)


def vmem():
    return pl.BlockSpec(memory_space=pltpu.VMEM)


def hbm():
    return pl.BlockSpec(memory_space=pltpu.HBM)


def tile_scratch(total, width):
    return [
        pltpu.VMEM((width * BLK, total * BLK), jnp.bfloat16),
        pltpu.VMEM((total * BLK, width * BLK), jnp.bfloat16),
        pltpu.SemaphoreType.DMA((2, total, width)),
    ]


def up_call(plan, meta, x, dy, vals, ins, last):
    tokens = x.shape[0]
    n = len(plan.sizes)
    has_in = ins is not None
    total, width = plan.total, plan.width
    return pl.pallas_call(
        functools.partial(up_kernel, plan, has_in, last),
        out_shape=[jax.ShapeDtypeStruct((2, tokens, s * BLK), jnp.bfloat16) for s in plan.sizes],
        in_specs=[smem()] + [vmem()] * 2 + [hbm()] * 2 + [vmem()] * (n if has_in else 0),
        out_specs=[vmem()] * n,
        scratch_shapes=([pltpu.VMEM((tokens, total * BLK), jnp.float32)] if last else [])
        + tile_scratch(total, width),
        compiler_params=pltpu.CompilerParams(vmem_limit_bytes=VMEM_LIMIT),
        cost_estimate=pl.CostEstimate(
            flops=4 * tokens * width * total * BLK * BLK,
            bytes_accessed=4 * width * total * BLK * BLK + 8 * tokens * total * BLK,
            transcendentals=0,
        ),
        name="up_last" if last else "up",
    )(meta, x, dy, *vals, *(ins if has_in else ()))


def down_kernel(plan, first, last, *refs):
    meta, vals1, vals2 = refs[:3]
    refs = refs[3:]
    n = len(plan.sizes)
    acts, refs = refs[:n], refs[n:]
    if not first:
        olds, refs = refs[:2], refs[2:]
    n_out = 4 if last else 2
    outs, refs = refs[:n_out], refs[n_out:]
    act, grd, buf1, buf2, sems = refs
    tile_start(plan, meta, vals2, buf2, sems, 1)
    tile_start(plan, meta, vals1, buf1, sems, 0)
    at = 0
    for a, size in zip(acts, plan.sizes):
        act[:, at : at + size * BLK] = a[0]
        grd[:, at : at + size * BLK] = a[1]
        at += size * BLK
    tokens = act.shape[0]
    columns = plan.width * BLK
    wide = 256 if columns % 256 == 0 else BLK
    for which in (1, 0):
        tile_wait(plan, meta, (vals1, vals2)[which], (buf1, buf2)[which], sems, which)
        for lo in range(0, columns, wide):
            span = slice(lo, lo + wide)
            if which == 1:
                res = dot_nn(act[...], buf2[:, span])
            else:
                res = dot_nt(grd[...], buf1[span, :])
            k = 1 - which
            if not first:
                res = res + olds[k][:, span]
            if last:
                outs[2 * k][:, span] = res[: tokens // 2]
                outs[2 * k + 1][:, span] = res[tokens // 2 :].astype(jnp.bfloat16)
            else:
                outs[k][:, span] = res


def down_call(plan, meta, vals, acts, sums, last):
    total, width = plan.total, plan.width
    tokens = acts[0].shape[1]
    first = sums is None
    n = len(plan.sizes)
    if last:
        shapes = [
            jax.ShapeDtypeStruct((tokens // 2, width * BLK), jnp.float32),
            jax.ShapeDtypeStruct((tokens // 2, width * BLK), jnp.bfloat16),
        ] * 2
    else:
        shapes = [jax.ShapeDtypeStruct((tokens, width * BLK), jnp.float32)] * 2
    return pl.pallas_call(
        functools.partial(down_kernel, plan, first, last),
        out_shape=shapes,
        in_specs=[smem()] + [hbm()] * 2 + [vmem()] * (n if first else n + 2),
        out_specs=[vmem()] * len(shapes),
        input_output_aliases={} if first or last else {3 + n: 0, 4 + n: 1},
        scratch_shapes=[pltpu.VMEM((tokens, total * BLK), jnp.bfloat16)] * 2 + tile_scratch(total, width),
        compiler_params=pltpu.CompilerParams(vmem_limit_bytes=VMEM_LIMIT),
        cost_estimate=pl.CostEstimate(
            flops=4 * tokens * width * total * BLK * BLK,
            bytes_accessed=4 * width * total * BLK * BLK,
            transcendentals=0,
        ),
        name="down",
    )(meta, *vals, *acts, *(() if first else sums))


def grad_kernel(plan, *refs):
    meta, x_t, dy = refs[:3]
    refs = refs[3:]
    n = len(plan.sizes)
    acts, refs = refs[:n], refs[n:]
    _, _, first_o, second_o, grd, act_t, stage1, stage2, sems = refs
    at = 0
    for a, size in zip(acts, plan.sizes):
        act_t[at : at + size * BLK, :] = a[0].T
        grd[:, at : at + size * BLK] = a[1]
        at += size * BLK
    outs, stages = (first_o, second_o), (stage1, stage2)

    def send(which):
        def go(slot, b, r):
            src = stage1.at[block_at(r), block_at(b)] if which == 0 else stage2.at[block_at(b), block_at(r)]
            pltpu.make_async_copy(src, outs[which].at[slot], sems.at[which, b, r]).start()

        plan.each(meta, which, go)

    def drain(which):
        def go(slot, b, r):
            src = stages[which].at[pl.ds(0, BLK), pl.ds(0, BLK)]
            pltpu.make_async_copy(src, outs[which].at[slot], sems.at[which, b, r]).wait()

        plan.each(meta, which, go)

    for lo, pair in spans(plan):
        span = slice(lo * BLK, (lo + len(pair)) * BLK)
        stage1[:, span] = dot_nn(x_t[...], grd[:, span]).astype(jnp.bfloat16)
    send(0)
    columns = plan.width * BLK
    wide = 256 if columns % 256 == 0 else BLK
    for lo in range(0, columns, wide):
        stage2[:, lo : lo + wide] = dot_nn(act_t[...], dy[:, lo : lo + wide]).astype(jnp.bfloat16)
    send(1)
    drain(0)
    drain(1)


def grad_call(plan, meta, x_t, dy, acts, grads):
    total, width = plan.total, plan.width
    tokens = dy.shape[0]
    shape = jax.ShapeDtypeStruct(grads[0].shape, jnp.bfloat16)
    n = len(plan.sizes)
    return pl.pallas_call(
        functools.partial(grad_kernel, plan),
        out_shape=[shape, shape],
        in_specs=[smem()] + [vmem()] * (2 + n) + [hbm()] * 2,
        out_specs=[hbm(), hbm()],
        scratch_shapes=[
            pltpu.VMEM((tokens, total * BLK), jnp.bfloat16),
            pltpu.VMEM((total * BLK, tokens), jnp.bfloat16),
        ]
        + tile_scratch(total, width),
        input_output_aliases={3 + n: 0, 4 + n: 1},
        compiler_params=pltpu.CompilerParams(vmem_limit_bytes=VMEM_LIMIT),
        cost_estimate=pl.CostEstimate(
            flops=4 * tokens * width * total * BLK * BLK,
            bytes_accessed=2 * width * total * BLK * BLK,
            transcendentals=0,
        ),
        name="grads",
    )(meta, x_t, dy, *acts, *grads)


class Row:
    def __init__(self, size):
        self.cores = 2 if size % 2 == 0 else 1
        self.chips = size // self.cores

    def swap(self, value):
        if self.cores == 1:
            return value
        return lax.ppermute(value, "row", [(k, k ^ 1) for k in range(self.chips * 2)])

    def shift(self, value, step):
        pairs = []
        for x in range(self.chips):
            for c in range(self.cores):
                pairs.append((((x + step) % self.chips) * self.cores + c, x * self.cores + c))
        return lax.ppermute(value, "row", pairs)

    def gather(self, value):
        half = jnp.concatenate([value] + [self.shift(value, d) for d in range(1, self.chips)], axis=0)
        return jnp.concatenate([half, self.swap(half)], axis=0)

    def scatter(self, keep, send):
        total = keep + self.swap(send).astype(jnp.float32)
        rows = total.shape[0] // self.chips
        mine = total[:rows]
        for d in range(1, self.chips):
            part = total[d * rows : (d + 1) * rows].astype(jnp.bfloat16)
            mine = mine + self.shift(part, -d).astype(jnp.float32)
        return mine.astype(jnp.bfloat16)


def shards(
    inputs,
    out_grad,
    first_vals,
    first_rows,
    first_cols,
    first_count,
    second_vals,
    second_rows,
    second_cols,
    second_count,
    *,
    hidden_blocks,
):
    n = lax.axis_size("col")
    ring = ring_of(n)
    ahead = [(ring[k], ring[(k + 1) % n]) for k in range(n)]
    back = [(b, a) for a, b in ahead]
    place = [0] * n
    for k, dev in enumerate(ring):
        place[dev] = k
    me = jnp.asarray(place, jnp.int32)[lax.axis_index("col")]

    row = Row(lax.axis_size("row"))
    x = row.gather(inputs)
    dy = row.gather(out_grad)
    width = x.shape[1] // BLK
    per = hidden_blocks // n
    vals = (first_vals[0, 0], second_vals[0, 0])
    slots = vals[0].shape[0]
    starts1, order1 = slot_order(first_cols[0, 0], first_rows[0, 0], first_count[0, 0], hidden_blocks)
    starts2, order2 = slot_order(second_rows[0, 0], second_cols[0, 0], second_count[0, 0], hidden_blocks)
    meta = jnp.concatenate([me[None], starts1, starts2, order1, order2])

    n_ahead = (per + 1) // 2
    parts = []
    for lo, cnt, sign in ((0, n_ahead, 1), (n_ahead, per - n_ahead, -1)):
        half = (cnt + 1) // 2
        parts.append([(lo, half, sign), (lo + half, cnt - half, sign)])
    streams = [[part[s] for part in parts if part[s][1] > 0] for s in range(2)]
    streams = [s for s in streams if s]

    def plan_of(stream, shift):
        return Plan(stream, shift, n, per, hidden_blocks, slots, width)

    def hop(stream, arrays):
        return [
            lax.ppermute(a, "col", ahead if sign > 0 else back) for a, (_, _, sign) in zip(arrays, stream)
        ]

    held = [None] * len(streams)
    x_t = grads = None
    for t in range(n):
        for s, stream in enumerate(streams):
            ins = None if t == 0 else hop(stream, held[s])
            if t == 1 and s == 0:
                x_t = x.T
                ins, x_t = lax.optimization_barrier((ins, x_t))
            if t == 2 and s == 0:
                grads = (jnp.zeros_like(vals[0]), jnp.zeros_like(vals[1]))
                ins, grads = lax.optimization_barrier((ins, grads))
            held[s] = up_call(plan_of(stream, t + 1), meta, x, dy, vals, ins, t == n - 1)

    sums = None
    for t in range(n):
        for s, stream in enumerate(streams):
            if t > 0:
                held[s] = hop(stream, held[s])
                held[s], sums, grads = lax.optimization_barrier((held[s], sums, grads))
            last = t == n - 1 and s == len(streams) - 1
            plan = plan_of(stream, t)
            sums = down_call(plan, meta, vals, held[s], sums, last)
            grads = grad_call(plan, meta, x_t, dy, held[s], grads)

    out_sum = row.scatter(sums[0], sums[1])
    in_sum = row.scatter(sums[2], sums[3])
    return out_sum, in_sum, grads[0][None, None], grads[1][None, None]


def solution(mesh):
    hidden_blocks = 49152 // BLK // mesh.shape["row"]
    placed = (
        P("row", "col"),
        P("row", "col"),
        P("row", "col", None, None, None),
        P("row", "col", None),
        P("row", "col", None),
        P("row", "col"),
        P("row", "col", None, None, None),
        P("row", "col", None),
        P("row", "col", None),
        P("row", "col"),
    )
    return jax.shard_map(
        functools.partial(shards, hidden_blocks=hidden_blocks),
        mesh=mesh,
        in_specs=placed,
        out_specs=(
            P("row", "col"),
            P("row", "col"),
            P("row", "col", None, None, None),
            P("row", "col", None, None, None),
        ),
        check_vma=False,
    )
```

time: 1430 us -> 631 us (0.44)
  the two profiles are of different devices: /device:TPU:0 before, /device:TPU:12 now
where the time goes in v2:
time: 631 us; the launch traced here: 618 us
  Pallas kernels  414 us (66%)
  waiting for transfers between devices  104 us (16%)
  starting transfers between devices  63.3 us (10%)
  local copies, waits for them, and re-layouts  23.1 us (4%)
  other arithmetic  10.5 us (2%)
    pallas_call x16, Pallas kernels, down_call(): pl.pallas_call(functools.partial(down_kernel, plan, first, last), out_sha...  161 us
    pallas_call x16, Pallas kernels, up_call(): pl.pallas_call(functools.partial(up_kernel, plan, has_in, last), out_shap...  136 us
    pallas_call x16, Pallas kernels, grad_call(): pl.pallas_call(functools.partial(grad_kernel, plan), out_shape=[shape, sh...  117 us
    ppermute x56, waiting for transfers between devices, hop(): lax.ppermute(a, 'col', ahead if sign > 0 else back)  77.3 us
    ppermute x56, starting transfers between devices, hop(): lax.ppermute(a, 'col', ahead if sign > 0 else back)  58 us
    ppermute x4, waiting for transfers between devices, shift(): return lax.ppermute(value, 'row', pairs)  27.1 us
    unnamed x18, local copies, waits for them, and re-layouts  14.1 us
  transfers between devices with their start and end apart: 64, of which 27 were waited for; matrix products, arithmetic and copies ran while one was open for 4% of the time, Pallas kernels for 64%

profile of v2, /device:TPU:12, one launch (start us, length us, event | category | flops | bytes accessed | tf_op | source)
XLA Modules:
  0.0 618.4 jit_solution(12777468144813888618)
XLA Ops:
  8.9 11.3 %collective-permute-done = bf16[128,1536]{0,1:T(8,128)(2,1)S(1)} collective-permute-done((bf16[128,1536]{0,1:T(8,128)(2,1)S(1)}, bf16[128,1536]{0,1:T(8,128)(2,1)S(1)}, u32[]{:S(2)}, u32[]{:S(2)}) %collective-permute-start) | collective-permute-done | bytes 393248 | tf_op jit(solution)/shard_map/ppermute | solution.py:351
  30.6 7.4 %up.21 = (bf16[2,512,384]{2,1,0:T(8,128)(2,1)S(1)}, bf16[2,512,384]{2,1,0:T(8,128)(2,1)S(1)}) custom-call(s32[1219]{0:T(1024)S(1)} %concatenate.17.refs_0_, bf16[512,1536]{1,0:T(8,128)(2,1)S(1)} %copy.104.refs_1_, bf16[512,1536]{1,0:T(8,128)(2,1)S(1)} %constant_dynamic-update-slice_fusion.refs_2_, bf16[512,128,128]{2,1,0:T(8,128)(2,1)} %bitcast.12, ...), custom_call_target="tpu_custom_call" | custom-call | flops 2415919104 | bytes 7864320 | tf_op jit(solution)/shard_map/up/pallas_call | solution.py:186
  40.1 7.6 %up.14 = (bf16[2,512,384]{2,1,0:T(8,128)(2,1)S(1)}, bf16[2,512,384]{2,1,0:T(8,128)(2,1)S(1)}) custom-call(s32[1219]{0:T(1024)S(1)} %concatenate.17.refs_0_, bf16[512,1536]{1,0:T(8,128)(2,1)S(1)} %copy.104.refs_1_, bf16[512,1536]{1,0:T(8,128)(2,1)S(1)} %constant_dynamic-update-slice_fusion.refs_2_, bf16[512,128,128]{2,1,0:T(8,128)(2,1)} %bitcast.13, ...), custom_call_target="tpu_custom_call" | custom-call | flops 2415919104 | bytes 7864320 | tf_op jit(solution)/shard_map/up/pallas_call | solution.py:186
  49.8 8.8 %collective-permute-done.20.refs_5_ = bf16[2,512,384]{2,1,0:T(8,128)(2,1)S(1)} collective-permute-done((bf16[2,512,384]{2,1,0:T(8,128)(2,1)S(1)}, bf16[2,512,384]{2,1,0:T(8,128)(2,1)S(1)}, u32[]{:S(2)}, u32[]{:S(2)}) %collective-permute-start.20) | collective-permute-done | bytes 786464 | tf_op jit(solution)/shard_map/ppermute | solution.py:414
  58.6 8.5 %up.22 = (bf16[2,512,384]{2,1,0:T(8,128)(2,1)S(1)}, bf16[2,512,384]{2,1,0:T(8,128)(2,1)S(1)}) custom-call(s32[1219]{0:T(1024)S(1)} %concatenate.17.refs_0_, bf16[512,1536]{1,0:T(8,128)(2,1)S(1)} %copy.104.refs_1_, bf16[512,1536]{1,0:T(8,128)(2,1)} %copy-done, bf16[512,128,128]{2,1,0:T(8,128)(2,1)} %bitcast.14, bf16[512,128,128]{2,1,0:T(8,128)(2,1)} %bitcast.46, ...), custom_call_target="tpu_custom_call" | custom-call | flops 2415919104 | bytes 7864320 | tf_op jit(solution)/shard_map/up/pallas_call | solution.py:186
  69.3 6.2 collective-permute-done.4.refs_5_
  75.5 8.5 %up.15 = (bf16[2,512,384]{2,1,0:T(8,128)(2,1)S(1)}, bf16[2,512,384]{2,1,0:T(8,128)(2,1)S(1)}) custom-call(s32[1219]{0:T(1024)S(1)} %concatenate.17.refs_0_, bf16[512,1536]{1,0:T(8,128)(2,1)S(1)} %copy.104.refs_1_, bf16[512,1536]{1,0:T(8,128)(2,1)} %copy-done, bf16[512,128,128]{2,1,0:T(8,128)(2,1)} %bitcast.15, bf16[512,128,128]{2,1,0:T(8,128)(2,1)} %bitcast.47, ...), custom_call_target="tpu_custom_call" | custom-call | flops 2415919104 | bytes 7864320 | tf_op jit(solution)/shard_map/up/pallas_call | solution.py:186
  86.1 6.2 collective-permute-done.22.refs_5_
  92.3 8.4 %up.23 = (bf16[2,512,384]{2,1,0:T(8,128)(2,1)S(1)}, bf16[2,512,384]{2,1,0:T(8,128)(2,1)S(1)}) custom-call(s32[1219]{0:T(1024)S(1)} %concatenate.17.refs_0_, bf16[512,1536]{1,0:T(8,128)(2,1)S(1)} %copy.104.refs_1_, bf16[512,1536]{1,0:T(8,128)(2,1)} %copy-done, bf16[512,128,128]{2,1,0:T(8,128)(2,1)} %bitcast.16, bf16[512,128,128]{2,1,0:T(8,128)(2,1)} %bitcast.48, ...), custom_call_target="tpu_custom_call" | custom-call | flops 2415919104 | bytes 7864320 | tf_op jit(solution)/shard_map/up/pallas_call | solution.py:186
  102.8 6.4 %collective-permute-done.6.refs_5_ = bf16[2,512,384]{2,1,0:T(8,128)(2,1)S(1)} collective-permute-done((bf16[2,512,384]{2,1,0:T(8,128)(2,1)S(1)}, bf16[2,512,384]{2,1,0:T(8,128)(2,1)S(1)}, u32[]{:S(2)}, u32[]{:S(2)}) %collective-permute-start.6) | collective-permute-done | bytes 786464 | tf_op jit(solution)/shard_map/ppermute | solution.py:414
  109.2 8.3 %up.16 = (bf16[2,512,384]{2,1,0:T(8,128)(2,1)S(1)}, bf16[2,512,384]{2,1,0:T(8,128)(2,1)S(1)}) custom-call(s32[1219]{0:T(1024)S(1)} %concatenate.17.refs_0_, bf16[512,1536]{1,0:T(8,128)(2,1)S(1)} %copy.104.refs_1_, bf16[512,1536]{1,0:T(8,128)(2,1)} %copy-done, bf16[512,128,128]{2,1,0:T(8,128)(2,1)} %bitcast.17, bf16[512,128,128]{2,1,0:T(8,128)(2,1)} %bitcast.49, ...), custom_call_target="tpu_custom_call" | custom-call | flops 2415919104 | bytes 7864320 | tf_op jit(solution)/shard_map/up/pallas_call | solution.py:186
  119.6 6.4 %collective-permute-done.24.refs_5_ = bf16[2,512,384]{2,1,0:T(8,128)(2,1)S(1)} collective-permute-done((bf16[2,512,384]{2,1,0:T(8,128)(2,1)S(1)}, bf16[2,512,384]{2,1,0:T(8,128)(2,1)S(1)}, u32[]{:S(2)}, u32[]{:S(2)}) %collective-permute-start.24) | collective-permute-done | bytes 786464 | tf_op jit(solution)/shard_map/ppermute | solution.py:414
  126.0 8.6 %up.24 = (bf16[2,512,384]{2,1,0:T(8,128)(2,1)S(1)}, bf16[2,512,384]{2,1,0:T(8,128)(2,1)S(1)}) custom-call(s32[1219]{0:T(1024)S(1)} %concatenate.17.refs_0_, bf16[512,1536]{1,0:T(8,128)(2,1)S(1)} %copy.104.refs_1_, bf16[512,1536]{1,0:T(8,128)(2,1)} %copy-done, bf16[512,128,128]{2,1,0:T(8,128)(2,1)} %bitcast.18, bf16[512,128,128]{2,1,0:T(8,128)(2,1)} %bitcast.50, ...), custom_call_target="tpu_custom_call" | custom-call | flops 2415919104 | bytes 7864320 | tf_op jit(solution)/shard_map/up/pallas_call | solution.py:186
  136.7 6.1 collective-permute-done.8.refs_5_
  142.9 8.7 %up.17 = (bf16[2,512,384]{2,1,0:T(8,128)(2,1)S(1)}, bf16[2,512,384]{2,1,0:T(8,128)(2,1)S(1)}) custom-call(s32[1219]{0:T(1024)S(1)} %concatenate.17.refs_0_, bf16[512,1536]{1,0:T(8,128)(2,1)S(1)} %copy.104.refs_1_, bf16[512,1536]{1,0:T(8,128)(2,1)} %copy-done, bf16[512,128,128]{2,1,0:T(8,128)(2,1)} %bitcast.19, bf16[512,128,128]{2,1,0:T(8,128)(2,1)} %bitcast.51, ...), custom_call_target="tpu_custom_call" | custom-call | flops 2415919104 | bytes 7864320 | tf_op jit(solution)/shard_map/up/pallas_call | solution.py:186
  153.7 6.0 collective-permute-done.26.refs_5_
  159.7 8.3 %up.25 = (bf16[2,512,384]{2,1,0:T(8,128)(2,1)S(1)}, bf16[2,512,384]{2,1,0:T(8,128)(2,1)S(1)}) custom-call(s32[1219]{0:T(1024)S(1)} %concatenate.17.refs_0_, bf16[512,1536]{1,0:T(8,128)(2,1)S(1)} %copy.104.refs_1_, bf16[512,1536]{1,0:T(8,128)(2,1)} %copy-done, bf16[512,128,128]{2,1,0:T(8,128)(2,1)} %bitcast.20, bf16[512,128,128]{2,1,0:T(8,128)(2,1)} %bitcast.52, ...), custom_call_target="tpu_custom_call" | custom-call | flops 2415919104 | bytes 7864320 | tf_op jit(solution)/shard_map/up/pallas_call | solution.py:186
  170.1 6.4 %collective-permute-done.10.refs_5_ = bf16[2,512,384]{2,1,0:T(8,128)(2,1)S(1)} collective-permute-done((bf16[2,512,384]{2,1,0:T(8,128)(2,1)S(1)}, bf16[2,512,384]{2,1,0:T(8,128)(2,1)S(1)}, u32[]{:S(2)}, u32[]{:S(2)}) %collective-permute-start.10) | collective-permute-done | bytes 786464 | tf_op jit(solution)/shard_map/ppermute | solution.py:414
  176.6 8.5 %up.18 = (bf16[2,512,384]{2,1,0:T(8,128)(2,1)S(1)}, bf16[2,512,384]{2,1,0:T(8,128)(2,1)S(1)}) custom-call(s32[1219]{0:T(1024)S(1)} %concatenate.17.refs_0_, bf16[512,1536]{1,0:T(8,128)(2,1)S(1)} %copy.104.refs_1_, bf16[512,1536]{1,0:T(8,128)(2,1)} %copy-done, bf16[512,128,128]{2,1,0:T(8,128)(2,1)} %bitcast.21, bf16[512,128,128]{2,1,0:T(8,128)(2,1)} %bitcast.53, ...), custom_call_target="tpu_custom_call" | custom-call | flops 2415919104 | bytes 7864320 | tf_op jit(solution)/shard_map/up/pallas_call | solution.py:186
  187.2 6.2 collective-permute-done.28.refs_5_
  193.4 8.6 %up.26 = (bf16[2,512,384]{2,1,0:T(8,128)(2,1)S(1)}, bf16[2,512,384]{2,1,0:T(8,128)(2,1)S(1)}) custom-call(s32[1219]{0:T(1024)S(1)} %concatenate.17.refs_0_, bf16[512,1536]{1,0:T(8,128)(2,1)S(1)} %copy.104.refs_1_, bf16[512,1536]{1,0:T(8,128)(2,1)} %copy-done, bf16[512,128,128]{2,1,0:T(8,128)(2,1)} %bitcast.22, bf16[512,128,128]{2,1,0:T(8,128)(2,1)} %bitcast.54, ...), custom_call_target="tpu_custom_call" | custom-call | flops 2415919104 | bytes 7864320 | tf_op jit(solution)/shard_map/up/pallas_call | solution.py:186
  204.2 6.1 collective-permute-done.12.refs_5_
  210.3 8.8 %up.19 = (bf16[2,512,384]{2,1,0:T(8,128)(2,1)S(1)}, bf16[2,512,384]{2,1,0:T(8,128)(2,1)S(1)}) custom-call(s32[1219]{0:T(1024)S(1)} %concatenate.17.refs_0_, bf16[512,1536]{1,0:T(8,128)(2,1)S(1)} %copy.104.refs_1_, bf16[512,1536]{1,0:T(8,128)(2,1)} %copy-done, bf16[512,128,128]{2,1,0:T(8,128)(2,1)} %bitcast.23, bf16[512,128,128]{2,1,0:T(8,128)(2,1)} %bitcast.55, ...), custom_call_target="tpu_custom_call" | custom-call | flops 2415919104 | bytes 7864320 | tf_op jit(solution)/shard_map/up/pallas_call | solution.py:186
  221.2 5.9 collective-permute-done.30.refs_5_
  227.2 8.6 %up.27 = (bf16[2,512,384]{2,1,0:T(8,128)(2,1)S(1)}, bf16[2,512,384]{2,1,0:T(8,128)(2,1)S(1)}) custom-call(s32[1219]{0:T(1024)S(1)} %concatenate.17.refs_0_, bf16[512,1536]{1,0:T(8,128)(2,1)S(1)} %copy.104.refs_1_, bf16[512,1536]{1,0:T(8,128)(2,1)} %copy-done, bf16[512,128,128]{2,1,0:T(8,128)(2,1)} %bitcast.24, bf16[512,128,128]{2,1,0:T(8,128)(2,1)} %bitcast.56, ...), custom_call_target="tpu_custom_call" | custom-call | flops 2415919104 | bytes 7864320 | tf_op jit(solution)/shard_map/up/pallas_call | solution.py:186
  237.9 6.1 collective-permute-done.14.refs_5_
  244.0 8.2 %up.20 = (bf16[2,512,384]{2,1,0:T(8,128)(2,1)S(1)}, bf16[2,512,384]{2,1,0:T(8,128)(2,1)S(1)}) custom-call(s32[1219]{0:T(1024)S(1)} %concatenate.17.refs_0_, bf16[512,1536]{1,0:T(8,128)(2,1)S(1)} %copy.104.refs_1_, bf16[512,1536]{1,0:T(8,128)(2,1)} %copy-done, bf16[512,128,128]{2,1,0:T(8,128)(2,1)} %bitcast.25, bf16[512,128,128]{2,1,0:T(8,128)(2,1)} %bitcast.57, ...), custom_call_target="tpu_custom_call" | custom-call | flops 2415919104 | bytes 7864320 | tf_op jit(solution)/shard_map/up/pallas_call | solution.py:186
  258.4 6.2 %copy.118.refs_6_ = bf16[512,128,128]{2,1,0:T(8,128)(2,1)} copy(bf16[512,128,128]{2,1,0:T(8,128)(2,1)S(1)} %broadcast.105.refs_5_) | data formatting | bytes 33554432
  269.6 9.8 %up_last.3 = (bf16[2,512,384]{2,1,0:T(8,128)(2,1)}, bf16[2,512,384]{2,1,0:T(8,128)(2,1)}) custom-call(s32[1219]{0:T(1024)S(1)} %concatenate.17.refs_0_, bf16[512,1536]{1,0:T(8,128)(2,1)S(1)} %copy.104.refs_1_, bf16[512,1536]{1,0:T(8,128)(2,1)} %copy-done, bf16[512,128,128]{2,1,0:T(8,128)(2,1)} %bitcast.26, bf16[512,128,128]{2,1,0:T(8,128)(2,1)} %bitcast.58, ...), custom_call_target="tpu_custom_call" | custom-call | flops 2415919104 | bytes 7864320 | tf_op jit(solution)/shard_map/up_last/pallas_call | solution.py:186
  281.5 9.4 %down.16 = (f32[512,1536]{1,0:T(8,128)S(1)}, f32[512,1536]{1,0:T(8,128)}) custom-call(s32[1219]{0:T(1024)S(1)} %concatenate.17.refs_0_, bf16[512,128,128]{2,1,0:T(8,128)(2,1)} %bitcast.27, bf16[512,128,128]{2,1,0:T(8,128)(2,1)} %bitcast.59, bf16[2,512,384]{2,1,0:T(8,128)(2,1)} %get-tuple-element.227.refs_3_, bf16[2,512,384]{2,1,0:T(8,128)(2,1)} %get-tuple-element.228.refs_4_), custom_call_target="tpu_custom_call" | custom-call | flops 2415919104 | bytes 4718592 | tf_op jit(solution)/shard_map/down/pallas_call | solution.py:253
  290.9 9.0 %up_last.2 = (bf16[2,512,384]{2,1,0:T(8,128)(2,1)S(1)}, bf16[2,512,384]{2,1,0:T(8,128)(2,1)S(1)}) custom-call(s32[1219]{0:T(1024)S(1)} %concatenate.17.refs_0_, bf16[512,1536]{1,0:T(8,128)(2,1)S(1)} %copy.104.refs_1_, bf16[512,1536]{1,0:T(8,128)(2,1)} %copy-done, bf16[512,128,128]{2,1,0:T(8,128)(2,1)} %bitcast.28, bf16[512,128,128]{2,1,0:T(8,128)(2,1)} %bitcast.60, ...), custom_call_target="tpu_custom_call" | custom-call | flops 2415919104 | bytes 7864320 | tf_op jit(solution)/shard_map/up_last/pallas_call | solution.py:186
  302.0 7.8 %grads.16 = (bf16[512,128,128]{2,1,0:T(8,128)(2,1)}, bf16[512,128,128]{2,1,0:T(8,128)(2,1)}) custom-call(s32[1219]{0:T(1024)S(1)} %concatenate.17.refs_0_, bf16[1536,512]{1,0:T(8,128)(2,1)S(1)} %copy-done.3, bf16[512,1536]{1,0:T(8,128)(2,1)S(1)} %copy-done.1, ...), custom_call_target="tpu_custom_call", output_to_operand_aliasing={{0}: (5, {}), {1}: (6, {})} | custom-call | flops 2415919104 | bytes 2359296 | tf_op jit(solution)/shard_map/grads/pallas_call | solution.py:315
  309.8 7.1 %grads.17 = (bf16[512,128,128]{2,1,0:T(8,128)(2,1)}, bf16[512,128,128]{2,1,0:T(8,128)(2,1)}) custom-call(s32[1219]{0:T(1024)S(1)} %concatenate.17.refs_0_, bf16[1536,512]{1,0:T(8,128)(2,1)S(1)} %copy-done.3, bf16[512,1536]{1,0:T(8,128)(2,1)S(1)} %copy-done.1, ...), custom_call_target="tpu_custom_call", output_to_operand_aliasing={{0}: (5, {}), {1}: (6, {})} | custom-call | flops 2415919104 | bytes 2359296 | tf_op jit(solution)/shard_map/grads/pallas_call | solution.py:315
  316.9 10.0 %down.17 = (f32[512,1536]{1,0:T(8,128)S(1)}, f32[512,1536]{1,0:T(8,128)}) custom-call(s32[1219]{0:T(1024)S(1)} %concatenate.17.refs_0_, bf16[512,128,128]{2,1,0:T(8,128)(2,1)} %bitcast.29, bf16[512,128,128]{2,1,0:T(8,128)(2,1)} %bitcast.61, bf16[2,512,384]{2,1,0:T(8,128)(2,1)S(1)} %get-tuple-element.207.refs_3_, ...), custom_call_target="tpu_custom_call", output_to_operand_aliasing={{0}: (5, {}), {1}: (6, {})} | custom-call | flops 2415919104 | bytes 4718592 | tf_op jit(solution)/shard_map/down/pallas_call | solution.py:253
  329.0 7.1 %grads.18 = (bf16[512,128,128]{2,1,0:T(8,128)(2,1)}, bf16[512,128,128]{2,1,0:T(8,128)(2,1)}) custom-call(s32[1219]{0:T(1024)S(1)} %concatenate.17.refs_0_, bf16[1536,512]{1,0:T(8,128)(2,1)S(1)} %copy-done.3, bf16[512,1536]{1,0:T(8,128)(2,1)S(1)} %copy-done.1, ...), custom_call_target="tpu_custom_call", output_to_operand_aliasing={{0}: (5, {}), {1}: (6, {})} | custom-call | flops 2415919104 | bytes 2359296 | tf_op jit(solution)/shard_map/grads/pallas_call | solution.py:315
  336.1 9.8 %down.18 = (f32[512,1536]{1,0:T(8,128)S(1)}, f32[512,1536]{1,0:T(8,128)}) custom-call(s32[1219]{0:T(1024)S(1)} %concatenate.17.refs_0_, bf16[512,128,128]{2,1,0:T(8,128)(2,1)} %bitcast.30, bf16[512,128,128]{2,1,0:T(8,128)(2,1)} %bitcast.62, bf16[2,512,384]{2,1,0:T(8,128)(2,1)S(1)} %collective-permute-done.34.refs_3_, ...), custom_call_target="tpu_custom_call", output_to_operand_aliasing={{0}: (5, {}), {1}: (6, {})} | custom-call | flops 2415919104 | bytes 4718592 | tf_op jit(solution)/shard_map/down/pallas_call | solution.py:253
  348.0 7.2 %grads.19 = (bf16[512,128,128]{2,1,0:T(8,128)(2,1)}, bf16[512,128,128]{2,1,0:T(8,128)(2,1)}) custom-call(s32[1219]{0:T(1024)S(1)} %concatenate.17.refs_0_, bf16[1536,512]{1,0:T(8,128)(2,1)S(1)} %copy-done.3, bf16[512,1536]{1,0:T(8,128)(2,1)S(1)} %copy-done.1, ...), custom_call_target="tpu_custom_call", output_to_operand_aliasing={{0}: (5, {}), {1}: (6, {})} | custom-call | flops 2415919104 | bytes 2359296 | tf_op jit(solution)/shard_map/grads/pallas_call | solution.py:315
  355.2 10.4 %down.19 = (f32[512,1536]{1,0:T(8,128)S(1)}, f32[512,1536]{1,0:T(8,128)}) custom-call(s32[1219]{0:T(1024)S(1)} %concatenate.17.refs_0_, bf16[512,128,128]{2,1,0:T(8,128)(2,1)} %bitcast.31, bf16[512,128,128]{2,1,0:T(8,128)(2,1)} %bitcast.63, bf16[2,512,384]{2,1,0:T(8,128)(2,1)S(1)} %collective-permute-done.18.refs_3_, ...), custom_call_target="tpu_custom_call", output_to_operand_aliasing={{0}: (5, {}), {1}: (6, {})} | custom-call | flops 2415919104 | bytes 4718592 | tf_op jit(solution)/shard_map/down/pallas_call | solution.py:253
  367.7 7.3 %grads.20 = (bf16[512,128,128]{2,1,0:T(8,128)(2,1)}, bf16[512,128,128]{2,1,0:T(8,128)(2,1)}) custom-call(s32[1219]{0:T(1024)S(1)} %concatenate.17.refs_0_, bf16[1536,512]{1,0:T(8,128)(2,1)S(1)} %copy-done.3, bf16[512,1536]{1,0:T(8,128)(2,1)S(1)} %copy-done.1, ...), custom_call_target="tpu_custom_call", output_to_operand_aliasing={{0}: (5, {}), {1}: (6, {})} | custom-call | flops 2415919104 | bytes 2359296 | tf_op jit(solution)/shard_map/grads/pallas_call | solution.py:315
  375.1 10.1 %down.20 = (f32[512,1536]{1,0:T(8,128)S(1)}, f32[512,1536]{1,0:T(8,128)}) custom-call(s32[1219]{0:T(1024)S(1)} %concatenate.17.refs_0_, bf16[512,128,128]{2,1,0:T(8,128)(2,1)} %bitcast.32, bf16[512,128,128]{2,1,0:T(8,128)(2,1)} %bitcast.64, bf16[2,512,384]{2,1,0:T(8,128)(2,1)S(1)} %collective-permute-done.38.refs_3_, ...), custom_call_target="tpu_custom_call", output_to_operand_aliasing={{0}: (5, {}), {1}: (6, {})} | custom-call | flops 2415919104 | bytes 4718592 | tf_op jit(solution)/shard_map/down/pallas_call | solution.py:253
  387.2 7.2 %grads.21 = (bf16[512,128,128]{2,1,0:T(8,128)(2,1)}, bf16[512,128,128]{2,1,0:T(8,128)(2,1)}) custom-call(s32[1219]{0:T(1024)S(1)} %concatenate.17.refs_0_, bf16[1536,512]{1,0:T(8,128)(2,1)S(1)} %copy-done.3, bf16[512,1536]{1,0:T(8,128)(2,1)S(1)} %copy-done.1, ...), custom_call_target="tpu_custom_call", output_to_operand_aliasing={{0}: (5, {}), {1}: (6, {})} | custom-call | flops 2415919104 | bytes 2359296 | tf_op jit(solution)/shard_map/grads/pallas_call | solution.py:315
  394.4 10.1 %down.21 = (f32[512,1536]{1,0:T(8,128)S(1)}, f32[512,1536]{1,0:T(8,128)}) custom-call(s32[1219]{0:T(1024)S(1)} %concatenate.17.refs_0_, bf16[512,128,128]{2,1,0:T(8,128)(2,1)} %bitcast.33, bf16[512,128,128]{2,1,0:T(8,128)(2,1)} %bitcast.65, bf16[2,512,384]{2,1,0:T(8,128)(2,1)S(1)} %collective-permute-done.36.refs_3_, ...), custom_call_target="tpu_custom_call", output_to_operand_aliasing={{0}: (5, {}), {1}: (6, {})} | custom-call | flops 2415919104 | bytes 4718592 | tf_op jit(solution)/shard_map/down/pallas_call | solution.py:253
  406.6 7.2 %grads.22 = (bf16[512,128,128]{2,1,0:T(8,128)(2,1)}, bf16[512,128,128]{2,1,0:T(8,128)(2,1)}) custom-call(s32[1219]{0:T(1024)S(1)} %concatenate.17.refs_0_, bf16[1536,512]{1,0:T(8,128)(2,1)S(1)} %copy-done.3, bf16[512,1536]{1,0:T(8,128)(2,1)S(1)} %copy-done.1, ...), custom_call_target="tpu_custom_call", output_to_operand_aliasing={{0}: (5, {}), {1}: (6, {})} | custom-call | flops 2415919104 | bytes 2359296 | tf_op jit(solution)/shard_map/grads/pallas_call | solution.py:315
  413.8 9.9 %down.22 = (f32[512,1536]{1,0:T(8,128)S(1)}, f32[512,1536]{1,0:T(8,128)}) custom-call(s32[1219]{0:T(1024)S(1)} %concatenate.17.refs_0_, bf16[512,128,128]{2,1,0:T(8,128)(2,1)} %bitcast.34, bf16[512,128,128]{2,1,0:T(8,128)(2,1)} %bitcast.66, bf16[2,512,384]{2,1,0:T(8,128)(2,1)S(1)} %collective-permute-done.42.refs_3_, ...), custom_call_target="tpu_custom_call", output_to_operand_aliasing={{0}: (5, {}), {1}: (6, {})} | custom-call | flops 2415919104 | bytes 4718592 | tf_op jit(solution)/shard_map/down/pallas_call | solution.py:253
  425.8 7.1 %grads.23 = (bf16[512,128,128]{2,1,0:T(8,128)(2,1)}, bf16[512,128,128]{2,1,0:T(8,128)(2,1)}) custom-call(s32[1219]{0:T(1024)S(1)} %concatenate.17.refs_0_, bf16[1536,512]{1,0:T(8,128)(2,1)S(1)} %copy-done.3, bf16[512,1536]{1,0:T(8,128)(2,1)S(1)} %copy-done.1, ...), custom_call_target="tpu_custom_call", output_to_operand_aliasing={{0}: (5, {}), {1}: (6, {})} | custom-call | flops 2415919104 | bytes 2359296 | tf_op jit(solution)/shard_map/grads/pallas_call | solution.py:315
  432.9 10.1 %down.23 = (f32[512,1536]{1,0:T(8,128)S(1)}, f32[512,1536]{1,0:T(8,128)}) custom-call(s32[1219]{0:T(1024)S(1)} %concatenate.17.refs_0_, bf16[512,128,128]{2,1,0:T(8,128)(2,1)} %bitcast.35, bf16[512,128,128]{2,1,0:T(8,128)(2,1)} %bitcast.67, bf16[2,512,384]{2,1,0:T(8,128)(2,1)S(1)} %collective-permute-done.40.refs_3_, ...), custom_call_target="tpu_custom_call", output_to_operand_aliasing={{0}: (5, {}), {1}: (6, {})} | custom-call | flops 2415919104 | bytes 4718592 | tf_op jit(solution)/shard_map/down/pallas_call | solution.py:253
  445.1 7.4 %grads.24 = (bf16[512,128,128]{2,1,0:T(8,128)(2,1)}, bf16[512,128,128]{2,1,0:T(8,128)(2,1)}) custom-call(s32[1219]{0:T(1024)S(1)} %concatenate.17.refs_0_, bf16[1536,512]{1,0:T(8,128)(2,1)S(1)} %copy-done.3, bf16[512,1536]{1,0:T(8,128)(2,1)S(1)} %copy-done.1, ...), custom_call_target="tpu_custom_call", output_to_operand_aliasing={{0}: (5, {}), {1}: (6, {})} | custom-call | flops 2415919104 | bytes 2359296 | tf_op jit(solution)/shard_map/grads/pallas_call | solution.py:315
  452.5 10.2 %down.24 = (f32[512,1536]{1,0:T(8,128)S(1)}, f32[512,1536]{1,0:T(8,128)}) custom-call(s32[1219]{0:T(1024)S(1)} %concatenate.17.refs_0_, bf16[512,128,128]{2,1,0:T(8,128)(2,1)} %bitcast.36, bf16[512,128,128]{2,1,0:T(8,128)(2,1)} %bitcast.68, bf16[2,512,384]{2,1,0:T(8,128)(2,1)S(1)} %collective-permute-done.46.refs_3_, ...), custom_call_target="tpu_custom_call", output_to_operand_aliasing={{0}: (5, {}), {1}: (6, {})} | custom-call | flops 2415919104 | bytes 4718592 | tf_op jit(solution)/shard_map/down/pallas_call | solution.py:253
  464.8 7.3 %grads.25 = (bf16[512,128,128]{2,1,0:T(8,128)(2,1)}, bf16[512,128,128]{2,1,0:T(8,128)(2,1)}) custom-call(s32[1219]{0:T(1024)S(1)} %concatenate.17.refs_0_, bf16[1536,512]{1,0:T(8,128)(2,1)S(1)} %copy-done.3, bf16[512,1536]{1,0:T(8,128)(2,1)S(1)} %copy-done.1, ...), custom_call_target="tpu_custom_call", output_to_operand_aliasing={{0}: (5, {}), {1}: (6, {})} | custom-call | flops 2415919104 | bytes 2359296 | tf_op jit(solution)/shard_map/grads/pallas_call | solution.py:315
  472.1 10.4 %down.25 = (f32[512,1536]{1,0:T(8,128)S(1)}, f32[512,1536]{1,0:T(8,128)}) custom-call(s32[1219]{0:T(1024)S(1)} %concatenate.17.refs_0_, bf16[512,128,128]{2,1,0:T(8,128)(2,1)} %bitcast.37, bf16[512,128,128]{2,1,0:T(8,128)(2,1)} %bitcast.69, bf16[2,512,384]{2,1,0:T(8,128)(2,1)S(1)} %collective-permute-done.44.refs_3_, ...), custom_call_target="tpu_custom_call", output_to_operand_aliasing={{0}: (5, {}), {1}: (6, {})} | custom-call | flops 2415919104 | bytes 4718592 | tf_op jit(solution)/shard_map/down/pallas_call | solution.py:253
  484.6 7.1 %grads.26 = (bf16[512,128,128]{2,1,0:T(8,128)(2,1)}, bf16[512,128,128]{2,1,0:T(8,128)(2,1)}) custom-call(s32[1219]{0:T(1024)S(1)} %concatenate.17.refs_0_, bf16[1536,512]{1,0:T(8,128)(2,1)S(1)} %copy-done.3, bf16[512,1536]{1,0:T(8,128)(2,1)S(1)} %copy-done.1, ...), custom_call_target="tpu_custom_call", output_to_operand_aliasing={{0}: (5, {}), {1}: (6, {})} | custom-call | flops 2415919104 | bytes 2359296 | tf_op jit(solution)/shard_map/grads/pallas_call | solution.py:315
  491.7 9.8 %down.26 = (f32[512,1536]{1,0:T(8,128)S(1)}, f32[512,1536]{1,0:T(8,128)}) custom-call(s32[1219]{0:T(1024)S(1)} %concatenate.17.refs_0_, bf16[512,128,128]{2,1,0:T(8,128)(2,1)} %bitcast.38, bf16[512,128,128]{2,1,0:T(8,128)(2,1)} %bitcast.70, bf16[2,512,384]{2,1,0:T(8,128)(2,1)S(1)} %collective-permute-done.50.refs_3_, ...), custom_call_target="tpu_custom_call", output_to_operand_aliasing={{0}: (5, {}), {1}: (6, {})} | custom-call | flops 2415919104 | bytes 4718592 | tf_op jit(solution)/shard_map/down/pallas_call | solution.py:253
  503.7 7.3 %grads.27 = (bf16[512,128,128]{2,1,0:T(8,128)(2,1)}, bf16[512,128,128]{2,1,0:T(8,128)(2,1)}) custom-call(s32[1219]{0:T(1024)S(1)} %concatenate.17.refs_0_, bf16[1536,512]{1,0:T(8,128)(2,1)S(1)} %copy-done.3, bf16[512,1536]{1,0:T(8,128)(2,1)S(1)} %copy-done.1, ...), custom_call_target="tpu_custom_call", output_to_operand_aliasing={{0}: (5, {}), {1}: (6, {})} | custom-call | flops 2415919104 | bytes 2359296 | tf_op jit(solution)/shard_map/grads/pallas_call | solution.py:315
  511.0 10.2 %down.27 = (f32[512,1536]{1,0:T(8,128)S(1)}, f32[512,1536]{1,0:T(8,128)}) custom-call(s32[1219]{0:T(1024)S(1)} %concatenate.17.refs_0_, bf16[512,128,128]{2,1,0:T(8,128)(2,1)} %bitcast.39, bf16[512,128,128]{2,1,0:T(8,128)(2,1)} %bitcast.71, bf16[2,512,384]{2,1,0:T(8,128)(2,1)S(1)} %collective-permute-done.48.refs_3_, ...), custom_call_target="tpu_custom_call", output_to_operand_aliasing={{0}: (5, {}), {1}: (6, {})} | custom-call | flops 2415919104 | bytes 4718592 | tf_op jit(solution)/shard_map/down/pallas_call | solution.py:253
  523.4 7.4 %grads.28 = (bf16[512,128,128]{2,1,0:T(8,128)(2,1)}, bf16[512,128,128]{2,1,0:T(8,128)(2,1)}) custom-call(s32[1219]{0:T(1024)S(1)} %concatenate.17.refs_0_, bf16[1536,512]{1,0:T(8,128)(2,1)S(1)} %copy-done.3, bf16[512,1536]{1,0:T(8,128)(2,1)S(1)} %copy-done.1, ...), custom_call_target="tpu_custom_call", output_to_operand_aliasing={{0}: (5, {}), {1}: (6, {})} | custom-call | flops 2415919104 | bytes 2359296 | tf_op jit(solution)/shard_map/grads/pallas_call | solution.py:315
  530.8 10.2 %down.28 = (f32[512,1536]{1,0:T(8,128)S(1)}, f32[512,1536]{1,0:T(8,128)}) custom-call(s32[1219]{0:T(1024)S(1)} %concatenate.17.refs_0_, bf16[512,128,128]{2,1,0:T(8,128)(2,1)} %bitcast.40, bf16[512,128,128]{2,1,0:T(8,128)(2,1)} %bitcast.72, bf16[2,512,384]{2,1,0:T(8,128)(2,1)S(1)} %collective-permute-done.54.refs_3_, ...), custom_call_target="tpu_custom_call", output_to_operand_aliasing={{0}: (5, {}), {1}: (6, {})} | custom-call | flops 2415919104 | bytes 4718592 | tf_op jit(solution)/shard_map/down/pallas_call | solution.py:253
  543.1 7.2 %grads.29 = (bf16[512,128,128]{2,1,0:T(8,128)(2,1)}, bf16[512,128,128]{2,1,0:T(8,128)(2,1)}) custom-call(s32[1219]{0:T(1024)S(1)} %concatenate.17.refs_0_, bf16[1536,512]{1,0:T(8,128)(2,1)S(1)} %copy-done.3, bf16[512,1536]{1,0:T(8,128)(2,1)S(1)} %copy-done.1, ...), custom_call_target="tpu_custom_call", output_to_operand_aliasing={{0}: (5, {}), {1}: (6, {})} | custom-call | flops 2415919104 | bytes 2359296 | tf_op jit(solution)/shard_map/grads/pallas_call | solution.py:315
  550.3 10.2 %down.29 = (f32[512,1536]{1,0:T(8,128)S(1)}, f32[512,1536]{1,0:T(8,128)}) custom-call(s32[1219]{0:T(1024)S(1)} %concatenate.17.refs_0_, bf16[512,128,128]{2,1,0:T(8,128)(2,1)} %bitcast.41, bf16[512,128,128]{2,1,0:T(8,128)(2,1)} %bitcast.73, bf16[2,512,384]{2,1,0:T(8,128)(2,1)S(1)} %collective-permute-done.52.refs_3_, ...), custom_call_target="tpu_custom_call", output_to_operand_aliasing={{0}: (5, {}), {1}: (6, {})} | custom-call | flops 2415919104 | bytes 4718592 | tf_op jit(solution)/shard_map/down/pallas_call | solution.py:253
  560.5 7.4 %grads.30 = (bf16[512,128,128]{2,1,0:T(8,128)(2,1)}, bf16[512,128,128]{2,1,0:T(8,128)(2,1)}) custom-call(s32[1219]{0:T(1024)S(1)} %concatenate.17.refs_0_, bf16[1536,512]{1,0:T(8,128)(2,1)S(1)} %copy-done.3, bf16[512,1536]{1,0:T(8,128)(2,1)S(1)} %copy-done.1, ...), custom_call_target="tpu_custom_call", output_to_operand_aliasing={{0}: (5, {}), {1}: (6, {})} | custom-call | flops 2415919104 | bytes 2359296 | tf_op jit(solution)/shard_map/grads/pallas_call | solution.py:315
  567.9 10.2 %down.30 = (f32[512,1536]{1,0:T(8,128)S(1)}, f32[512,1536]{1,0:T(8,128)}) custom-call(s32[1219]{0:T(1024)S(1)} %concatenate.17.refs_0_, bf16[512,128,128]{2,1,0:T(8,128)(2,1)} %bitcast.42, bf16[512,128,128]{2,1,0:T(8,128)(2,1)} %bitcast.74, bf16[2,512,384]{2,1,0:T(8,128)(2,1)S(1)} %collective-permute-done.58.refs_3_, ...), custom_call_target="tpu_custom_call", output_to_operand_aliasing={{0}: (5, {}), {1}: (6, {})} | custom-call | flops 2415919104 | bytes 4718592 | tf_op jit(solution)/shard_map/down/pallas_call | solution.py:253
  579.7 10.2 %down.31 = (f32[256,1536]{1,0:T(8,128)S(1)}, bf16[256,1536]{1,0:T(8,128)(2,1)S(1)}, f32[256,1536]{1,0:T(8,128)}, bf16[256,1536]{1,0:T(8,128)(2,1)S(1)}) custom-call(s32[1219]{0:T(1024)S(1)} %concatenate.17.refs_0_, bf16[512,128,128]{2,1,0:T(8,128)(2,1)} %bitcast.43, bf16[512,128,128]{2,1,0:T(8,128)(2,1)} %bitcast.75, ...), custom_call_target="tpu_custom_call" | custom-call | flops 2415919104 | bytes 4718592 | tf_op jit(solution)/shard_map/down/pallas_call | solution.py:253
  590.5 7.3 %grads.31 = (bf16[512,128,128]{2,1,0:T(8,128)(2,1)}, bf16[512,128,128]{2,1,0:T(8,128)(2,1)}) custom-call(s32[1219]{0:T(1024)S(1)} %concatenate.17.refs_0_, bf16[1536,512]{1,0:T(8,128)(2,1)S(1)} %copy-done.3, bf16[512,1536]{1,0:T(8,128)(2,1)S(1)} %copy-done.1, ...), custom_call_target="tpu_custom_call", output_to_operand_aliasing={{0}: (5, {}), {1}: (6, {})} | custom-call | flops 2415919104 | bytes 2359296 | tf_op jit(solution)/shard_map/grads/pallas_call | solution.py:315
  600.5 9.7 %collective-permute-done.63 = bf16[128,1536]{1,0:T(8,128)(2,1)S(1)} collective-permute-done((bf16[128,1536]{1,0:T(8,128)(2,1)S(1)}, bf16[128,1536]{1,0:T(8,128)(2,1)S(1)}, u32[]{:S(2)}, u32[]{:S(2)}) %collective-permute-start.63) | collective-permute-done | bytes 393248 | tf_op jit(solution)/shard_map/ppermute | solution.py:351
  611.1 6.1 collective-permute-done.61
  (153 shorter events, 91.6 us)
Async XLA Ops:
  0.6 21.5 %collective-permute-start.2 = (bf16[128,1536]{1,0:T(8,128)(2,1)}, bf16[128,1536]{1,0:T(8,128)(2,1)S(1)}, u32[]{:S(2)}, u32[]{:S(2)}) collective-permute-start(bf16[128,1536]{1,0:T(8,128)(2,1)} %param.12), channel_id=1, source_target_pairs={{16,0},{24,8},{0,16},{8,24},{17,1},{25,9},{1,17},{9,25},{18,2},{26... | collective-permute-start | bytes 1179656 | tf_op jit(solution)/shard_map/ppermute | solution.py:351
  3.4 16.8 %collective-permute-start = (bf16[128,1536]{0,1:T(8,128)(2,1)S(1)}, bf16[128,1536]{0,1:T(8,128)(2,1)S(1)}, u32[]{:S(2)}, u32[]{:S(2)}) collective-permute-start(bf16[128,1536]{0,1:T(8,128)(2,1)S(1)} %copy.96), channel_id=1, source_target_pairs={{16,0},{24,8},{0,16},{8,24},{17,1},{25,9},{1,17},{9,25},{18,2},{26... | collective-permute-start | bytes 1179656 | tf_op jit(solution)/shard_map/ppermute | solution.py:351
  21.2 3.4 collective-permute-start.1
  24.0 5.3 collective-permute-start.3
  38.0 20.5 %collective-permute-start.20 = (bf16[2,512,384]{2,1,0:T(8,128)(2,1)S(1)}, bf16[2,512,384]{2,1,0:T(8,128)(2,1)S(1)}, u32[]{:S(2)}, u32[]{:S(2)}) collective-permute-start(bf16[2,512,384]{2,1,0:T(8,128)(2,1)S(1)} %get-tuple-element.209), channel_id=1, source_target_pairs={{0,2},{2,4},{4,6},{6,7},{7,5},{5,3},{3,1},{1,0},{8,10},{10,12},{12... | collective-permute-start | bytes 2359304 | tf_op jit(solution)/shard_map/ppermute | solution.py:414
  38.2 20.4 %collective-permute-start.21 = (bf16[2,512,384]{2,1,0:T(8,128)(2,1)S(1)}, bf16[2,512,384]{2,1,0:T(8,128)(2,1)S(1)}, u32[]{:S(2)}, u32[]{:S(2)}) collective-permute-start(bf16[2,512,384]{2,1,0:T(8,128)(2,1)S(1)} %get-tuple-element.210), channel_id=1, source_target_pairs={{2,0},{4,2},{6,4},{7,6},{5,7},{3,5},{1,3},{0,1},{10,8},{12,10},{14... | collective-permute-start | bytes 2359304 | tf_op jit(solution)/shard_map/ppermute | solution.py:414
  47.7 27.7 %collective-permute-start.4 = (bf16[2,512,384]{2,1,0:T(8,128)(2,1)S(1)}, bf16[2,512,384]{2,1,0:T(8,128)(2,1)S(1)}, u32[]{:S(2)}, u32[]{:S(2)}) collective-permute-start(bf16[2,512,384]{2,1,0:T(8,128)(2,1)S(1)} %get-tuple-element.193), channel_id=1, source_target_pairs={{0,2},{2,4},{4,6},{6,7},{7,5},{5,3},{3,1},{1,0},{8,10},{10,12},{12... | collective-permute-start | bytes 2359304 | tf_op jit(solution)/shard_map/ppermute | solution.py:414
  47.8 27.7 %collective-permute-start.5 = (bf16[2,512,384]{2,1,0:T(8,128)(2,1)S(1)}, bf16[2,512,384]{2,1,0:T(8,128)(2,1)S(1)}, u32[]{:S(2)}, u32[]{:S(2)}) collective-permute-start(bf16[2,512,384]{2,1,0:T(8,128)(2,1)S(1)} %get-tuple-element.194), channel_id=1, source_target_pairs={{2,0},{4,2},{6,4},{7,6},{5,7},{3,5},{1,3},{0,1},{10,8},{12,10},{14... | collective-permute-start | bytes 2359304 | tf_op jit(solution)/shard_map/ppermute | solution.py:414
  67.2 25.1 %collective-permute-start.22 = (bf16[2,512,384]{2,1,0:T(8,128)(2,1)S(1)}, bf16[2,512,384]{2,1,0:T(8,128)(2,1)S(1)}, u32[]{:S(2)}, u32[]{:S(2)}) collective-permute-start(bf16[2,512,384]{2,1,0:T(8,128)(2,1)S(1)} %get-tuple-element.213), channel_id=1, source_target_pairs={{0,2},{2,4},{4,6},{6,7},{7,5},{5,3},{3,1},{1,0},{8,10},{10,12},{12... | collective-permute-start | bytes 2359304 | tf_op jit(solution)/shard_map/ppermute | solution.py:414
  67.2 25.1 %collective-permute-start.23 = (bf16[2,512,384]{2,1,0:T(8,128)(2,1)S(1)}, bf16[2,512,384]{2,1,0:T(8,128)(2,1)S(1)}, u32[]{:S(2)}, u32[]{:S(2)}) collective-permute-start(bf16[2,512,384]{2,1,0:T(8,128)(2,1)S(1)} %get-tuple-element.214), channel_id=1, source_target_pairs={{2,0},{4,2},{6,4},{7,6},{5,7},{3,5},{1,3},{0,1},{10,8},{12,10},{14... | collective-permute-start | bytes 2359304 | tf_op jit(solution)/shard_map/ppermute | solution.py:414
  84.0 25.1 %collective-permute-start.6 = (bf16[2,512,384]{2,1,0:T(8,128)(2,1)S(1)}, bf16[2,512,384]{2,1,0:T(8,128)(2,1)S(1)}, u32[]{:S(2)}, u32[]{:S(2)}) collective-permute-start(bf16[2,512,384]{2,1,0:T(8,128)(2,1)S(1)} %get-tuple-element.195), channel_id=1, source_target_pairs={{0,2},{2,4},{4,6},{6,7},{7,5},{5,3},{3,1},{1,0},{8,10},{10,12},{12... | collective-permute-start | bytes 2359304 | tf_op jit(solution)/shard_map/ppermute | solution.py:414
  84.1 25.1 %collective-permute-start.7 = (bf16[2,512,384]{2,1,0:T(8,128)(2,1)S(1)}, bf16[2,512,384]{2,1,0:T(8,128)(2,1)S(1)}, u32[]{:S(2)}, u32[]{:S(2)}) collective-permute-start(bf16[2,512,384]{2,1,0:T(8,128)(2,1)S(1)} %get-tuple-element.196), channel_id=1, source_target_pairs={{2,0},{4,2},{6,4},{7,6},{5,7},{3,5},{1,3},{0,1},{10,8},{12,10},{14... | collective-permute-start | bytes 2359304 | tf_op jit(solution)/shard_map/ppermute | solution.py:414
  100.7 25.3 %collective-permute-start.24 = (bf16[2,512,384]{2,1,0:T(8,128)(2,1)S(1)}, bf16[2,512,384]{2,1,0:T(8,128)(2,1)S(1)}, u32[]{:S(2)}, u32[]{:S(2)}) collective-permute-start(bf16[2,512,384]{2,1,0:T(8,128)(2,1)S(1)} %get-tuple-element.217), channel_id=1, source_target_pairs={{0,2},{2,4},{4,6},{6,7},{7,5},{5,3},{3,1},{1,0},{8,10},{10,12},{12... | collective-permute-start | bytes 2359304 | tf_op jit(solution)/shard_map/ppermute | solution.py:414
  100.8 25.3 %collective-permute-start.25 = (bf16[2,512,384]{2,1,0:T(8,128)(2,1)S(1)}, bf16[2,512,384]{2,1,0:T(8,128)(2,1)S(1)}, u32[]{:S(2)}, u32[]{:S(2)}) collective-permute-start(bf16[2,512,384]{2,1,0:T(8,128)(2,1)S(1)} %get-tuple-element.218), channel_id=1, source_target_pairs={{2,0},{4,2},{6,4},{7,6},{5,7},{3,5},{1,3},{0,1},{10,8},{12,10},{14... | collective-permute-start | bytes 2359304 | tf_op jit(solution)/shard_map/ppermute | solution.py:414
  117.5 25.3 %collective-permute-start.8 = (bf16[2,512,384]{2,1,0:T(8,128)(2,1)S(1)}, bf16[2,512,384]{2,1,0:T(8,128)(2,1)S(1)}, u32[]{:S(2)}, u32[]{:S(2)}) collective-permute-start(bf16[2,512,384]{2,1,0:T(8,128)(2,1)S(1)} %get-tuple-element.197), channel_id=1, source_target_pairs={{0,2},{2,4},{4,6},{6,7},{7,5},{5,3},{3,1},{1,0},{8,10},{10,12},{12... | collective-permute-start | bytes 2359304 | tf_op jit(solution)/shard_map/ppermute | solution.py:414
  117.6 25.3 %collective-permute-start.9 = (bf16[2,512,384]{2,1,0:T(8,128)(2,1)S(1)}, bf16[2,512,384]{2,1,0:T(8,128)(2,1)S(1)}, u32[]{:S(2)}, u32[]{:S(2)}) collective-permute-start(bf16[2,512,384]{2,1,0:T(8,128)(2,1)S(1)} %get-tuple-element.198), channel_id=1, source_target_pairs={{2,0},{4,2},{6,4},{7,6},{5,7},{3,5},{1,3},{0,1},{10,8},{12,10},{14... | collective-permute-start | bytes 2359304 | tf_op jit(solution)/shard_map/ppermute | solution.py:414
  134.7 25.0 %collective-permute-start.26 = (bf16[2,512,384]{2,1,0:T(8,128)(2,1)S(1)}, bf16[2,512,384]{2,1,0:T(8,128)(2,1)S(1)}, u32[]{:S(2)}, u32[]{:S(2)}) collective-permute-start(bf16[2,512,384]{2,1,0:T(8,128)(2,1)S(1)} %get-tuple-element.219), channel_id=1, source_target_pairs={{0,2},{2,4},{4,6},{6,7},{7,5},{5,3},{3,1},{1,0},{8,10},{10,12},{12... | collective-permute-start | bytes 2359304 | tf_op jit(solution)/shard_map/ppermute | solution.py:414
  134.7 25.0 %collective-permute-start.27 = (bf16[2,512,384]{2,1,0:T(8,128)(2,1)S(1)}, bf16[2,512,384]{2,1,0:T(8,128)(2,1)S(1)}, u32[]{:S(2)}, u32[]{:S(2)}) collective-permute-start(bf16[2,512,384]{2,1,0:T(8,128)(2,1)S(1)} %get-tuple-element.220), channel_id=1, source_target_pairs={{2,0},{4,2},{6,4},{7,6},{5,7},{3,5},{1,3},{0,1},{10,8},{12,10},{14... | collective-permute-start | bytes 2359304 | tf_op jit(solution)/shard_map/ppermute | solution.py:414
  151.6 24.9 %collective-permute-start.10 = (bf16[2,512,384]{2,1,0:T(8,128)(2,1)S(1)}, bf16[2,512,384]{2,1,0:T(8,128)(2,1)S(1)}, u32[]{:S(2)}, u32[]{:S(2)}) collective-permute-start(bf16[2,512,384]{2,1,0:T(8,128)(2,1)S(1)} %get-tuple-element.199), channel_id=1, source_target_pairs={{0,2},{2,4},{4,6},{6,7},{7,5},{5,3},{3,1},{1,0},{8,10},{10,12},{12... | collective-permute-start | bytes 2359304 | tf_op jit(solution)/shard_map/ppermute | solution.py:414
  151.7 24.9 %collective-permute-start.11 = (bf16[2,512,384]{2,1,0:T(8,128)(2,1)S(1)}, bf16[2,512,384]{2,1,0:T(8,128)(2,1)S(1)}, u32[]{:S(2)}, u32[]{:S(2)}) collective-permute-start(bf16[2,512,384]{2,1,0:T(8,128)(2,1)S(1)} %get-tuple-element.200), channel_id=1, source_target_pairs={{2,0},{4,2},{6,4},{7,6},{5,7},{3,5},{1,3},{0,1},{10,8},{12,10},{14... | collective-permute-start | bytes 2359304 | tf_op jit(solution)/shard_map/ppermute | solution.py:414
  168.0 25.3 %collective-permute-start.28 = (bf16[2,512,384]{2,1,0:T(8,128)(2,1)S(1)}, bf16[2,512,384]{2,1,0:T(8,128)(2,1)S(1)}, u32[]{:S(2)}, u32[]{:S(2)}) collective-permute-start(bf16[2,512,384]{2,1,0:T(8,128)(2,1)S(1)} %get-tuple-element.221), channel_id=1, source_target_pairs={{0,2},{2,4},{4,6},{6,7},{7,5},{5,3},{3,1},{1,0},{8,10},{10,12},{12... | collective-permute-start | bytes 2359304 | tf_op jit(solution)/shard_map/ppermute | solution.py:414
  168.1 25.3 %collective-permute-start.29 = (bf16[2,512,384]{2,1,0:T(8,128)(2,1)S(1)}, bf16[2,512,384]{2,1,0:T(8,128)(2,1)S(1)}, u32[]{:S(2)}, u32[]{:S(2)}) collective-permute-start(bf16[2,512,384]{2,1,0:T(8,128)(2,1)S(1)} %get-tuple-element.222), channel_id=1, source_target_pairs={{2,0},{4,2},{6,4},{7,6},{5,7},{3,5},{1,3},{0,1},{10,8},{12,10},{14... | collective-permute-start | bytes 2359304 | tf_op jit(solution)/shard_map/ppermute | solution.py:414
  185.1 25.1 %collective-permute-start.12 = (bf16[2,512,384]{2,1,0:T(8,128)(2,1)S(1)}, bf16[2,512,384]{2,1,0:T(8,128)(2,1)S(1)}, u32[]{:S(2)}, u32[]{:S(2)}) collective-permute-start(bf16[2,512,384]{2,1,0:T(8,128)(2,1)S(1)} %get-tuple-element.201), channel_id=1, source_target_pairs={{0,2},{2,4},{4,6},{6,7},{7,5},{5,3},{3,1},{1,0},{8,10},{10,12},{12... | collective-permute-start | bytes 2359304 | tf_op jit(solution)/shard_map/ppermute | solution.py:414
  185.2 25.1 %collective-permute-start.13 = (bf16[2,512,384]{2,1,0:T(8,128)(2,1)S(1)}, bf16[2,512,384]{2,1,0:T(8,128)(2,1)S(1)}, u32[]{:S(2)}, u32[]{:S(2)}) collective-permute-start(bf16[2,512,384]{2,1,0:T(8,128)(2,1)S(1)} %get-tuple-element.202), channel_id=1, source_target_pairs={{2,0},{4,2},{6,4},{7,6},{5,7},{3,5},{1,3},{0,1},{10,8},{12,10},{14... | collective-permute-start | bytes 2359304 | tf_op jit(solution)/shard_map/ppermute | solution.py:414
  202.1 25.0 %collective-permute-start.30 = (bf16[2,512,384]{2,1,0:T(8,128)(2,1)S(1)}, bf16[2,512,384]{2,1,0:T(8,128)(2,1)S(1)}, u32[]{:S(2)}, u32[]{:S(2)}) collective-permute-start(bf16[2,512,384]{2,1,0:T(8,128)(2,1)S(1)} %get-tuple-element.223), channel_id=1, source_target_pairs={{0,2},{2,4},{4,6},{6,7},{7,5},{5,3},{3,1},{1,0},{8,10},{10,12},{12... | collective-permute-start | bytes 2359304 | tf_op jit(solution)/shard_map/ppermute | solution.py:414
  202.1 25.0 %collective-permute-start.31 = (bf16[2,512,384]{2,1,0:T(8,128)(2,1)S(1)}, bf16[2,512,384]{2,1,0:T(8,128)(2,1)S(1)}, u32[]{:S(2)}, u32[]{:S(2)}) collective-permute-start(bf16[2,512,384]{2,1,0:T(8,128)(2,1)S(1)} %get-tuple-element.224), channel_id=1, source_target_pairs={{2,0},{4,2},{6,4},{7,6},{5,7},{3,5},{1,3},{0,1},{10,8},{12,10},{14... | collective-permute-start | bytes 2359304 | tf_op jit(solution)/shard_map/ppermute | solution.py:414
  219.1 24.8 %collective-permute-start.14 = (bf16[2,512,384]{2,1,0:T(8,128)(2,1)S(1)}, bf16[2,512,384]{2,1,0:T(8,128)(2,1)S(1)}, u32[]{:S(2)}, u32[]{:S(2)}) collective-permute-start(bf16[2,512,384]{2,1,0:T(8,128)(2,1)S(1)} %get-tuple-element.203), channel_id=1, source_target_pairs={{0,2},{2,4},{4,6},{6,7},{7,5},{5,3},{3,1},{1,0},{8,10},{10,12},{12... | collective-permute-start | bytes 2359304 | tf_op jit(solution)/shard_map/ppermute | solution.py:414
  219.2 24.8 %collective-permute-start.15 = (bf16[2,512,384]{2,1,0:T(8,128)(2,1)S(1)}, bf16[2,512,384]{2,1,0:T(8,128)(2,1)S(1)}, u32[]{:S(2)}, u32[]{:S(2)}) collective-permute-start(bf16[2,512,384]{2,1,0:T(8,128)(2,1)S(1)} %get-tuple-element.204), channel_id=1, source_target_pairs={{2,0},{4,2},{6,4},{7,6},{5,7},{3,5},{1,3},{0,1},{10,8},{12,10},{14... | collective-permute-start | bytes 2359304 | tf_op jit(solution)/shard_map/ppermute | solution.py:414
  235.8 33.8 %collective-permute-start.32 = (bf16[2,512,384]{2,1,0:T(8,128)(2,1)S(1)}, bf16[2,512,384]{2,1,0:T(8,128)(2,1)S(1)}, u32[]{:S(2)}, u32[]{:S(2)}) collective-permute-start(bf16[2,512,384]{2,1,0:T(8,128)(2,1)S(1)} %get-tuple-element.225), channel_id=1, source_target_pairs={{0,2},{2,4},{4,6},{6,7},{7,5},{5,3},{3,1},{1,0},{8,10},{10,12},{12... | collective-permute-start | bytes 2359304 | tf_op jit(solution)/shard_map/ppermute | solution.py:414
  235.9 33.8 %collective-permute-start.33 = (bf16[2,512,384]{2,1,0:T(8,128)(2,1)S(1)}, bf16[2,512,384]{2,1,0:T(8,128)(2,1)S(1)}, u32[]{:S(2)}, u32[]{:S(2)}) collective-permute-start(bf16[2,512,384]{2,1,0:T(8,128)(2,1)S(1)} %get-tuple-element.226), channel_id=1, source_target_pairs={{2,0},{4,2},{6,4},{7,6},{5,7},{3,5},{1,3},{0,1},{10,8},{12,10},{14... | collective-permute-start | bytes 2359304 | tf_op jit(solution)/shard_map/ppermute | solution.py:414
  252.2 38.7 %collective-permute-start.16 = (bf16[2,512,384]{2,1,0:T(8,128)(2,1)S(1)}, bf16[2,512,384]{2,1,0:T(8,128)(2,1)S(1)}, u32[]{:S(2)}, u32[]{:S(2)}) collective-permute-start(bf16[2,512,384]{2,1,0:T(8,128)(2,1)S(1)} %get-tuple-element.205), channel_id=1, source_target_pairs={{0,2},{2,4},{4,6},{6,7},{7,5},{5,3},{3,1},{1,0},{8,10},{10,12},{12... | collective-permute-start | bytes 2359304 | tf_op jit(solution)/shard_map/ppermute | solution.py:414
  252.3 38.6 %collective-permute-start.17 = (bf16[2,512,384]{2,1,0:T(8,128)(2,1)S(1)}, bf16[2,512,384]{2,1,0:T(8,128)(2,1)S(1)}, u32[]{:S(2)}, u32[]{:S(2)}) collective-permute-start(bf16[2,512,384]{2,1,0:T(8,128)(2,1)S(1)} %get-tuple-element.206), channel_id=1, source_target_pairs={{2,0},{4,2},{6,4},{7,6},{5,7},{3,5},{1,3},{0,1},{10,8},{12,10},{14... | collective-permute-start | bytes 2359304 | tf_op jit(solution)/shard_map/ppermute | solution.py:414
  279.4 47.5 %collective-permute-start.34 = (bf16[2,512,384]{2,1,0:T(8,128)(2,1)}, bf16[2,512,384]{2,1,0:T(8,128)(2,1)S(1)}, u32[]{:S(2)}, u32[]{:S(2)}) collective-permute-start(bf16[2,512,384]{2,1,0:T(8,128)(2,1)} %get-tuple-element.227.refs_3_), channel_id=1, source_target_pairs={{0,2},{2,4},{4,6},{6,7},{7,5},{5,3},{3,1},{1,0},{8,10},{10,12},{12... | collective-permute-start | bytes 2359304 | tf_op jit(solution)/shard_map/ppermute | solution.py:414
  279.5 47.4 %collective-permute-start.35 = (bf16[2,512,384]{2,1,0:T(8,128)(2,1)}, bf16[2,512,384]{2,1,0:T(8,128)(2,1)S(1)}, u32[]{:S(2)}, u32[]{:S(2)}) collective-permute-start(bf16[2,512,384]{2,1,0:T(8,128)(2,1)} %get-tuple-element.228.refs_4_), channel_id=1, source_target_pairs={{2,0},{4,2},{6,4},{7,6},{5,7},{3,5},{1,3},{0,1},{10,8},{12,10},{14... | collective-permute-start | bytes 2359304 | tf_op jit(solution)/shard_map/ppermute | solution.py:414
  299.9 46.0 %collective-permute-start.18 = (bf16[2,512,384]{2,1,0:T(8,128)(2,1)S(1)}, bf16[2,512,384]{2,1,0:T(8,128)(2,1)S(1)}, u32[]{:S(2)}, u32[]{:S(2)}) collective-permute-start(bf16[2,512,384]{2,1,0:T(8,128)(2,1)S(1)} %get-tuple-element.207.refs_3_), channel_id=1, source_target_pairs={{0,2},{2,4},{4,6},{6,7},{7,5},{5,3},{3,1},{1,0},{8,10},{10,12},{12... | collective-permute-start | bytes 2359304 | tf_op jit(solution)/shard_map/ppermute | solution.py:414
  300.0 45.9 %collective-permute-start.19 = (bf16[2,512,384]{2,1,0:T(8,128)(2,1)S(1)}, bf16[2,512,384]{2,1,0:T(8,128)(2,1)S(1)}, u32[]{:S(2)}, u32[]{:S(2)}) collective-permute-start(bf16[2,512,384]{2,1,0:T(8,128)(2,1)S(1)} %get-tuple-element.208.refs_4_), channel_id=1, source_target_pairs={{2,0},{4,2},{6,4},{7,6},{5,7},{3,5},{1,3},{0,1},{10,8},{12,10},{14... | collective-permute-start | bytes 2359304 | tf_op jit(solution)/shard_map/ppermute | solution.py:414
  327.0 38.7 %collective-permute-start.38 = (bf16[2,512,384]{2,1,0:T(8,128)(2,1)S(1)}, bf16[2,512,384]{2,1,0:T(8,128)(2,1)S(1)}, u32[]{:S(2)}, u32[]{:S(2)}) collective-permute-start(bf16[2,512,384]{2,1,0:T(8,128)(2,1)S(1)} %collective-permute-done.34.refs_3_), channel_id=1, source_target_pairs={{0,2},{2,4},{4,6},{6,7},{7,5},{5,3},{3,1},{1,0},{8,10},{10,12},{12... | collective-permute-start | bytes 2359304 | tf_op jit(solution)/shard_map/ppermute | solution.py:414
  327.0 38.6 %collective-permute-start.39 = (bf16[2,512,384]{2,1,0:T(8,128)(2,1)S(1)}, bf16[2,512,384]{2,1,0:T(8,128)(2,1)S(1)}, u32[]{:S(2)}, u32[]{:S(2)}) collective-permute-start(bf16[2,512,384]{2,1,0:T(8,128)(2,1)S(1)} %collective-permute-done.35.refs_4_), channel_id=1, source_target_pairs={{2,0},{4,2},{6,4},{7,6},{5,7},{3,5},{1,3},{0,1},{10,8},{12,10},{14... | collective-permute-start | bytes 2359304 | tf_op jit(solution)/shard_map/ppermute | solution.py:414
  345.9 39.2 %collective-permute-start.36 = (bf16[2,512,384]{2,1,0:T(8,128)(2,1)S(1)}, bf16[2,512,384]{2,1,0:T(8,128)(2,1)S(1)}, u32[]{:S(2)}, u32[]{:S(2)}) collective-permute-start(bf16[2,512,384]{2,1,0:T(8,128)(2,1)S(1)} %collective-permute-done.18.refs_3_), channel_id=1, source_target_pairs={{0,2},{2,4},{4,6},{6,7},{7,5},{5,3},{3,1},{1,0},{8,10},{10,12},{12... | collective-permute-start | bytes 2359304 | tf_op jit(solution)/shard_map/ppermute | solution.py:414
  346.0 39.2 %collective-permute-start.37 = (bf16[2,512,384]{2,1,0:T(8,128)(2,1)S(1)}, bf16[2,512,384]{2,1,0:T(8,128)(2,1)S(1)}, u32[]{:S(2)}, u32[]{:S(2)}) collective-permute-start(bf16[2,512,384]{2,1,0:T(8,128)(2,1)S(1)} %collective-permute-done.19.refs_4_), channel_id=1, source_target_pairs={{2,0},{4,2},{6,4},{7,6},{5,7},{3,5},{1,3},{0,1},{10,8},{12,10},{14... | collective-permute-start | bytes 2359304 | tf_op jit(solution)/shard_map/ppermute | solution.py:414
  365.6 38.9 %collective-permute-start.42 = (bf16[2,512,384]{2,1,0:T(8,128)(2,1)S(1)}, bf16[2,512,384]{2,1,0:T(8,128)(2,1)S(1)}, u32[]{:S(2)}, u32[]{:S(2)}) collective-permute-start(bf16[2,512,384]{2,1,0:T(8,128)(2,1)S(1)} %collective-permute-done.38.refs_3_), channel_id=1, source_target_pairs={{0,2},{2,4},{4,6},{6,7},{7,5},{5,3},{3,1},{1,0},{8,10},{10,12},{12... | collective-permute-start | bytes 2359304 | tf_op jit(solution)/shard_map/ppermute | solution.py:414
  365.7 38.8 %collective-permute-start.43 = (bf16[2,512,384]{2,1,0:T(8,128)(2,1)S(1)}, bf16[2,512,384]{2,1,0:T(8,128)(2,1)S(1)}, u32[]{:S(2)}, u32[]{:S(2)}) collective-permute-start(bf16[2,512,384]{2,1,0:T(8,128)(2,1)S(1)} %collective-permute-done.39.refs_4_), channel_id=1, source_target_pairs={{2,0},{4,2},{6,4},{7,6},{5,7},{3,5},{1,3},{0,1},{10,8},{12,10},{14... | collective-permute-start | bytes 2359304 | tf_op jit(solution)/shard_map/ppermute | solution.py:414
  385.2 38.5 %collective-permute-start.40 = (bf16[2,512,384]{2,1,0:T(8,128)(2,1)S(1)}, bf16[2,512,384]{2,1,0:T(8,128)(2,1)S(1)}, u32[]{:S(2)}, u32[]{:S(2)}) collective-permute-start(bf16[2,512,384]{2,1,0:T(8,128)(2,1)S(1)} %collective-permute-done.36.refs_3_), channel_id=1, source_target_pairs={{0,2},{2,4},{4,6},{6,7},{7,5},{5,3},{3,1},{1,0},{8,10},{10,12},{12... | collective-permute-start | bytes 2359304 | tf_op jit(solution)/shard_map/ppermute | solution.py:414
  385.2 38.5 %collective-permute-start.41 = (bf16[2,512,384]{2,1,0:T(8,128)(2,1)S(1)}, bf16[2,512,384]{2,1,0:T(8,128)(2,1)S(1)}, u32[]{:S(2)}, u32[]{:S(2)}) collective-permute-start(bf16[2,512,384]{2,1,0:T(8,128)(2,1)S(1)} %collective-permute-done.37.refs_4_), channel_id=1, source_target_pairs={{2,0},{4,2},{6,4},{7,6},{5,7},{3,5},{1,3},{0,1},{10,8},{12,10},{14... | collective-permute-start | bytes 2359304 | tf_op jit(solution)/shard_map/ppermute | solution.py:414
  404.5 38.5 %collective-permute-start.46 = (bf16[2,512,384]{2,1,0:T(8,128)(2,1)S(1)}, bf16[2,512,384]{2,1,0:T(8,128)(2,1)S(1)}, u32[]{:S(2)}, u32[]{:S(2)}) collective-permute-start(bf16[2,512,384]{2,1,0:T(8,128)(2,1)S(1)} %collective-permute-done.42.refs_3_), channel_id=1, source_target_pairs={{0,2},{2,4},{4,6},{6,7},{7,5},{5,3},{3,1},{1,0},{8,10},{10,12},{12... | collective-permute-start | bytes 2359304 | tf_op jit(solution)/shard_map/ppermute | solution.py:414
  404.6 38.4 %collective-permute-start.47 = (bf16[2,512,384]{2,1,0:T(8,128)(2,1)S(1)}, bf16[2,512,384]{2,1,0:T(8,128)(2,1)S(1)}, u32[]{:S(2)}, u32[]{:S(2)}) collective-permute-start(bf16[2,512,384]{2,1,0:T(8,128)(2,1)S(1)} %collective-permute-done.43.refs_4_), channel_id=1, source_target_pairs={{2,0},{4,2},{6,4},{7,6},{5,7},{3,5},{1,3},{0,1},{10,8},{12,10},{14... | collective-permute-start | bytes 2359304 | tf_op jit(solution)/shard_map/ppermute | solution.py:414
  423.7 39.0 %collective-permute-start.44 = (bf16[2,512,384]{2,1,0:T(8,128)(2,1)S(1)}, bf16[2,512,384]{2,1,0:T(8,128)(2,1)S(1)}, u32[]{:S(2)}, u32[]{:S(2)}) collective-permute-start(bf16[2,512,384]{2,1,0:T(8,128)(2,1)S(1)} %collective-permute-done.40.refs_3_), channel_id=1, source_target_pairs={{0,2},{2,4},{4,6},{6,7},{7,5},{5,3},{3,1},{1,0},{8,10},{10,12},{12... | collective-permute-start | bytes 2359304 | tf_op jit(solution)/shard_map/ppermute | solution.py:414
  423.8 38.9 %collective-permute-start.45 = (bf16[2,512,384]{2,1,0:T(8,128)(2,1)S(1)}, bf16[2,512,384]{2,1,0:T(8,128)(2,1)S(1)}, u32[]{:S(2)}, u32[]{:S(2)}) collective-permute-start(bf16[2,512,384]{2,1,0:T(8,128)(2,1)S(1)} %collective-permute-done.41.refs_4_), channel_id=1, source_target_pairs={{2,0},{4,2},{6,4},{7,6},{5,7},{3,5},{1,3},{0,1},{10,8},{12,10},{14... | collective-permute-start | bytes 2359304 | tf_op jit(solution)/shard_map/ppermute | solution.py:414
  443.0 39.5 %collective-permute-start.50 = (bf16[2,512,384]{2,1,0:T(8,128)(2,1)S(1)}, bf16[2,512,384]{2,1,0:T(8,128)(2,1)S(1)}, u32[]{:S(2)}, u32[]{:S(2)}) collective-permute-start(bf16[2,512,384]{2,1,0:T(8,128)(2,1)S(1)} %collective-permute-done.46.refs_3_), channel_id=1, source_target_pairs={{0,2},{2,4},{4,6},{6,7},{7,5},{5,3},{3,1},{1,0},{8,10},{10,12},{12... | collective-permute-start | bytes 2359304 | tf_op jit(solution)/shard_map/ppermute | solution.py:414
  443.1 39.5 %collective-permute-start.51 = (bf16[2,512,384]{2,1,0:T(8,128)(2,1)S(1)}, bf16[2,512,384]{2,1,0:T(8,128)(2,1)S(1)}, u32[]{:S(2)}, u32[]{:S(2)}) collective-permute-start(bf16[2,512,384]{2,1,0:T(8,128)(2,1)S(1)} %collective-permute-done.47.refs_4_), channel_id=1, source_target_pairs={{2,0},{4,2},{6,4},{7,6},{5,7},{3,5},{1,3},{0,1},{10,8},{12,10},{14... | collective-permute-start | bytes 2359304 | tf_op jit(solution)/shard_map/ppermute | solution.py:414
  462.7 38.9 %collective-permute-start.48 = (bf16[2,512,384]{2,1,0:T(8,128)(2,1)S(1)}, bf16[2,512,384]{2,1,0:T(8,128)(2,1)S(1)}, u32[]{:S(2)}, u32[]{:S(2)}) collective-permute-start(bf16[2,512,384]{2,1,0:T(8,128)(2,1)S(1)} %collective-permute-done.44.refs_3_), channel_id=1, source_target_pairs={{0,2},{2,4},{4,6},{6,7},{7,5},{5,3},{3,1},{1,0},{8,10},{10,12},{12... | collective-permute-start | bytes 2359304 | tf_op jit(solution)/shard_map/ppermute | solution.py:414
  462.7 38.8 %collective-permute-start.49 = (bf16[2,512,384]{2,1,0:T(8,128)(2,1)S(1)}, bf16[2,512,384]{2,1,0:T(8,128)(2,1)S(1)}, u32[]{:S(2)}, u32[]{:S(2)}) collective-permute-start(bf16[2,512,384]{2,1,0:T(8,128)(2,1)S(1)} %collective-permute-done.45.refs_4_), channel_id=1, source_target_pairs={{2,0},{4,2},{6,4},{7,6},{5,7},{3,5},{1,3},{0,1},{10,8},{12,10},{14... | collective-permute-start | bytes 2359304 | tf_op jit(solution)/shard_map/ppermute | solution.py:414
  482.5 38.7 %collective-permute-start.54 = (bf16[2,512,384]{2,1,0:T(8,128)(2,1)S(1)}, bf16[2,512,384]{2,1,0:T(8,128)(2,1)S(1)}, u32[]{:S(2)}, u32[]{:S(2)}) collective-permute-start(bf16[2,512,384]{2,1,0:T(8,128)(2,1)S(1)} %collective-permute-done.50.refs_3_), channel_id=1, source_target_pairs={{0,2},{2,4},{4,6},{6,7},{7,5},{5,3},{3,1},{1,0},{8,10},{10,12},{12... | collective-permute-start | bytes 2359304 | tf_op jit(solution)/shard_map/ppermute | solution.py:414
  482.6 38.7 %collective-permute-start.55 = (bf16[2,512,384]{2,1,0:T(8,128)(2,1)S(1)}, bf16[2,512,384]{2,1,0:T(8,128)(2,1)S(1)}, u32[]{:S(2)}, u32[]{:S(2)}) collective-permute-start(bf16[2,512,384]{2,1,0:T(8,128)(2,1)S(1)} %collective-permute-done.51.refs_4_), channel_id=1, source_target_pairs={{2,0},{4,2},{6,4},{7,6},{5,7},{3,5},{1,3},{0,1},{10,8},{12,10},{14... | collective-permute-start | bytes 2359304 | tf_op jit(solution)/shard_map/ppermute | solution.py:414
  501.6 39.4 %collective-permute-start.52 = (bf16[2,512,384]{2,1,0:T(8,128)(2,1)S(1)}, bf16[2,512,384]{2,1,0:T(8,128)(2,1)S(1)}, u32[]{:S(2)}, u32[]{:S(2)}) collective-permute-start(bf16[2,512,384]{2,1,0:T(8,128)(2,1)S(1)} %collective-permute-done.48.refs_3_), channel_id=1, source_target_pairs={{0,2},{2,4},{4,6},{6,7},{7,5},{5,3},{3,1},{1,0},{8,10},{10,12},{12... | collective-permute-start | bytes 2359304 | tf_op jit(solution)/shard_map/ppermute | solution.py:414
  501.7 39.3 %collective-permute-start.53 = (bf16[2,512,384]{2,1,0:T(8,128)(2,1)S(1)}, bf16[2,512,384]{2,1,0:T(8,128)(2,1)S(1)}, u32[]{:S(2)}, u32[]{:S(2)}) collective-permute-start(bf16[2,512,384]{2,1,0:T(8,128)(2,1)S(1)} %collective-permute-done.49.refs_4_), channel_id=1, source_target_pairs={{2,0},{4,2},{6,4},{7,6},{5,7},{3,5},{1,3},{0,1},{10,8},{12,10},{14... | collective-permute-start | bytes 2359304 | tf_op jit(solution)/shard_map/ppermute | solution.py:414
  521.3 39.2 %collective-permute-start.58 = (bf16[2,512,384]{2,1,0:T(8,128)(2,1)S(1)}, bf16[2,512,384]{2,1,0:T(8,128)(2,1)S(1)}, u32[]{:S(2)}, u32[]{:S(2)}) collective-permute-start(bf16[2,512,384]{2,1,0:T(8,128)(2,1)S(1)} %collective-permute-done.54.refs_3_), channel_id=1, source_target_pairs={{0,2},{2,4},{4,6},{6,7},{7,5},{5,3},{3,1},{1,0},{8,10},{10,12},{12... | collective-permute-start | bytes 2359304 | tf_op jit(solution)/shard_map/ppermute | solution.py:414
  521.3 39.1 %collective-permute-start.59 = (bf16[2,512,384]{2,1,0:T(8,128)(2,1)S(1)}, bf16[2,512,384]{2,1,0:T(8,128)(2,1)S(1)}, u32[]{:S(2)}, u32[]{:S(2)}) collective-permute-start(bf16[2,512,384]{2,1,0:T(8,128)(2,1)S(1)} %collective-permute-done.55.refs_4_), channel_id=1, source_target_pairs={{2,0},{4,2},{6,4},{7,6},{5,7},{3,5},{1,3},{0,1},{10,8},{12,10},{14... | collective-permute-start | bytes 2359304 | tf_op jit(solution)/shard_map/ppermute | solution.py:414
  541.0 38.8 %collective-permute-start.56 = (bf16[2,512,384]{2,1,0:T(8,128)(2,1)S(1)}, bf16[2,512,384]{2,1,0:T(8,128)(2,1)S(1)}, u32[]{:S(2)}, u32[]{:S(2)}) collective-permute-start(bf16[2,512,384]{2,1,0:T(8,128)(2,1)S(1)} %collective-permute-done.52.refs_3_), channel_id=1, source_target_pairs={{0,2},{2,4},{4,6},{6,7},{7,5},{5,3},{3,1},{1,0},{8,10},{10,12},{12... | collective-permute-start | bytes 2359304 | tf_op jit(solution)/shard_map/ppermute | solution.py:414
  541.0 38.7 %collective-permute-start.57 = (bf16[2,512,384]{2,1,0:T(8,128)(2,1)S(1)}, bf16[2,512,384]{2,1,0:T(8,128)(2,1)S(1)}, u32[]{:S(2)}, u32[]{:S(2)}) collective-permute-start(bf16[2,512,384]{2,1,0:T(8,128)(2,1)S(1)} %collective-permute-done.53.refs_4_), channel_id=1, source_target_pairs={{2,0},{4,2},{6,4},{7,6},{5,7},{3,5},{1,3},{0,1},{10,8},{12,10},{14... | collective-permute-start | bytes 2359304 | tf_op jit(solution)/shard_map/ppermute | solution.py:414
  589.9 7.9 %collective-permute-start.62 = (bf16[256,1536]{1,0:T(8,128)(2,1)S(1)}, bf16[256,1536]{1,0:T(8,128)(2,1)S(1)}, u32[]{:S(2)}, u32[]{:S(2)}) collective-permute-start(bf16[256,1536]{1,0:T(8,128)(2,1)S(1)} %get-tuple-element.377), channel_id=1, source_target_pairs={{0,8},{8,0},{16,24},{24,16},{1,9},{9,1},{17,25},{25,17},{2,10},{10... | collective-permute-start | bytes 2359304 | tf_op jit(solution)/shard_map/ppermute | solution.py:344
  590.0 8.2 %collective-permute-start.60 = (bf16[256,1536]{1,0:T(8,128)(2,1)S(1)}, bf16[256,1536]{1,0:T(8,128)(2,1)S(1)}, u32[]{:S(2)}, u32[]{:S(2)}) collective-permute-start(bf16[256,1536]{1,0:T(8,128)(2,1)S(1)} %get-tuple-element.375), channel_id=1, source_target_pairs={{0,8},{8,0},{16,24},{24,16},{1,9},{9,1},{17,25},{25,17},{2,10},{10... | collective-permute-start | bytes 2359304 | tf_op jit(solution)/shard_map/ppermute | solution.py:344
  598.1 12.1 %collective-permute-start.63 = (bf16[128,1536]{1,0:T(8,128)(2,1)S(1)}, bf16[128,1536]{1,0:T(8,128)(2,1)S(1)}, u32[]{:S(2)}, u32[]{:S(2)}) collective-permute-start(bf16[128,1536]{1,0:T(8,128)(2,1)S(1)} %slice.30), channel_id=1, source_target_pairs={{16,0},{24,8},{0,16},{8,24},{17,1},{25,9},{1,17},{9,25},{18,2},{26... | collective-permute-start | bytes 1179656 | tf_op jit(solution)/shard_map/ppermute | solution.py:351
  598.4 18.7 %collective-permute-start.61 = (bf16[128,1536]{1,0:T(8,128)(2,1)S(1)}, bf16[128,1536]{1,0:T(8,128)(2,1)S(1)}, u32[]{:S(2)}, u32[]{:S(2)}) collective-permute-start(bf16[128,1536]{1,0:T(8,128)(2,1)S(1)} %slice.31), channel_id=1, source_target_pairs={{16,0},{24,8},{0,16},{8,24},{17,1},{25,9},{1,17},{9,25},{18,2},{26... | collective-permute-start | bytes 1179656 | tf_op jit(solution)/shard_map/ppermute | solution.py:351
  (7 other events, 76.4 us)

commit v3 on v2

v3 whole, which is shorter than its diff:
```python
import functools

import jax
import jax.numpy as jnp
from jax import lax
from jax.experimental import pallas as pl
from jax.experimental.pallas import tpu as pltpu
from jax.sharding import PartitionSpec as P

BLK = 128
Z_CHIPS = 4
ROOT_2_PI = 0.7978845608028654
CUBIC = 0.044715
VMEM_LIMIT = 40 << 20
FIRST_LIMIT = 60 << 20
FIRST_SHIFT = 20
SECOND_SHIFT = 14


def ring_of(n):
    if n % Z_CHIPS or n // Z_CHIPS < 2:
        return list(range(n))
    wide = n // Z_CHIPS
    order = [z * wide for z in range(Z_CHIPS)]
    for k, z in enumerate(reversed(range(Z_CHIPS))):
        ys = range(1, wide) if k % 2 == 0 else range(wide - 1, 0, -1)
        order += [z * wide + y for y in ys]
    return order


def gelu_pair(value, grad):
    inner = ROOT_2_PI * (value + CUBIC * (value * value * value))
    th = jnp.tanh(inner)
    half = 0.5 * (1.0 + th)
    slope = half + 0.5 * value * (1.0 - th * th) * (ROOT_2_PI * (1.0 + (3.0 * CUBIC) * (value * value)))
    return value * half, grad * slope


def slot_order(first, second, count, n_first):
    slots = first.shape[0]
    ids = jnp.arange(slots, dtype=jnp.int32)
    packed = (first << FIRST_SHIFT) | (second << SECOND_SHIFT) | ids
    key = jnp.where(ids < count, packed, jnp.iinfo(jnp.int32).max - slots + ids)
    rank = jnp.sum((key[None, :] < key[:, None]).astype(jnp.int32), axis=1)
    order = jnp.sum(jnp.where(rank[None, :] == ids[:, None], packed[None, :], 0), axis=1)
    edge = jnp.arange(n_first + 1, dtype=jnp.int32) << FIRST_SHIFT
    starts = jnp.sum((key[None, :] < edge[:, None]).astype(jnp.int32), axis=1)
    return starts, order


class Plan:
    def __init__(self, stream, shift, n, per, hidden_blocks, slots, width, parts=()):
        self.stream, self.shift, self.n, self.per = tuple(stream), shift, n, per
        self.sizes = tuple(c for _, c, _ in stream)
        self.total = sum(self.sizes)
        self.width = width
        self.parts = tuple(parts) if parts else (self,)
        self.start_at = (1, 2 + hidden_blocks)
        self.list_at = (3 + 2 * hidden_blocks, 3 + 2 * hidden_blocks + slots)

    def bases(self, meta):
        me = meta[0]
        return [lax.rem(me + (self.n - sign * self.shift) % self.n, self.n) * self.per + lo for lo, _, sign in self.stream]

    def each(self, meta, which, body):
        offset = 0
        for base, size in zip(self.bases(meta), self.sizes):
            lo = meta[self.start_at[which] + base]
            hi = meta[self.start_at[which] + base + size]

            def step(i, carry, base=base, offset=offset):
                entry = meta[self.list_at[which] + i]
                slot = entry & ((1 << SECOND_SHIFT) - 1)
                r = (entry >> SECOND_SHIFT) & ((1 << (FIRST_SHIFT - SECOND_SHIFT)) - 1)
                body(slot, (entry >> FIRST_SHIFT) - base + offset, r)
                return carry

            lax.fori_loop(lo, hi, step, 0)
            offset += size


def block_at(i):
    return pl.ds(pl.multiple_of(i * BLK, BLK), BLK)


def clear(buf):
    def step(i, carry):
        buf[block_at(i), :] = jnp.zeros((BLK, buf.shape[1]), buf.dtype)
        return carry

    lax.fori_loop(0, buf.shape[0] // BLK, step, 0)


def tile_start(plan, meta, vals, buf, sems, which):
    clear(buf)

    def go(slot, b, r):
        dst = buf.at[block_at(r), block_at(b)] if which == 0 else buf.at[block_at(b), block_at(r)]
        pltpu.make_async_copy(vals.at[slot], dst, sems.at[which, b, r]).start()

    plan.each(meta, which, go)


def tile_wait(plan, meta, vals, buf, sems, which):
    def go(slot, b, r):
        pltpu.make_async_copy(vals.at[slot], buf.at[pl.ds(0, BLK), pl.ds(0, BLK)], sems.at[which, b, r]).wait()

    plan.each(meta, which, go)


def dot_nn(a, b):
    return jnp.dot(a, b, preferred_element_type=jnp.float32)


def dot_nt(a, b):
    return lax.dot_general(a, b, (((1,), (1,)), ((), ())), preferred_element_type=jnp.float32)


def tile_loop(columns, body):
    wide = 2 * BLK if columns % (2 * BLK) == 0 else BLK
    if columns == wide:
        body(pl.ds(0, wide))
        return

    def step(i, carry):
        body(pl.ds(pl.multiple_of(i * wide, wide), wide))
        return carry

    lax.fori_loop(0, columns // wide, step, 0)


def row_loop(rows, body):
    def step(i, carry):
        body(block_at(i))
        return carry

    lax.fori_loop(0, rows // BLK, step, 0)


def group_slices(plan):
    at, out = 0, []
    for size in plan.sizes:
        out.append(slice(at, at + size * BLK))
        at += size * BLK
    return out


class Store:
    def __init__(self, plan):
        self.side, self.rows = plan.total * BLK, plan.width * BLK
        self.cuts = plan.width // plan.total
        self.shape = (plan.n, 2 * self.rows, self.side)

    def views(self, store, step, which, buf):
        if which == 0:
            return [(store.at[step, pl.ds(0, self.rows), :], buf)]
        return [
            (store.at[step, pl.ds(self.rows + i * self.side, self.side), :], buf.at[:, pl.ds(i * self.side, self.side)])
            for i in range(self.cuts)
        ]


def up_kernel(plan, n_pieces, has_in, last, *refs):
    meta, refs = refs[0], refs[1:]
    if n_pieces:
        pieces, refs = refs[: 2 * n_pieces], refs[2 * n_pieces :]
    else:
        x, dy, refs = refs[0], refs[1], refs[2:]
    vals1, vals2, refs = refs[0], refs[1], refs[2:]
    n = len(plan.sizes)
    ins = refs[:n] if has_in else None
    refs = refs[n + 1 :] if has_in else refs
    outs, refs = refs[:n], refs[n:]
    if n_pieces:
        x, dy, refs = refs[0], refs[1], refs[2:]
    store, refs = refs[0], refs[1:]
    buf1, buf2, sems, hid, grd, tile_sems = refs[:6]
    keep = [
        [
            pltpu.make_async_copy(src, dst, tile_sems.at[which, i])
            for i, (dst, src) in enumerate(Store(plan).views(store, plan.shift - 1, which, buf))
        ]
        for which, buf in enumerate((buf1, buf2))
    ]
    joins = []
    if n_pieces:
        rows = pieces[0].shape[0]
        for i in range(2 * n_pieces):
            dst = (x if i < n_pieces else dy).at[pl.ds(i % n_pieces * rows, rows), :]
            joins.append(pltpu.make_async_copy(pieces[i], dst, refs[6].at[i]))
    for join in joins:
        join.start()
    tile_start(plan, meta, vals1, buf1, sems, 0)
    tile_start(plan, meta, vals2, buf2, sems, 1)
    for join in joins:
        join.wait()
    columns = plan.total * BLK
    tile_wait(plan, meta, vals1, buf1, sems, 0)
    for copy in keep[0]:
        copy.start()

    def hid_tile(at):
        hid[:, at] = dot_nn(x[...], buf1[:, at])

    tile_loop(columns, hid_tile)
    tile_wait(plan, meta, vals2, buf2, sems, 1)
    for copy in keep[1]:
        copy.start()

    def grd_tile(at):
        grd[:, at] = dot_nt(dy[...], buf2[at, :])

    tile_loop(columns, grd_tile)

    def join_rows(part):
        for g, at in enumerate(group_slices(plan)):
            h, d = hid[part, at], grd[part, at]
            if has_in:
                h = h + ins[g][0, part, :].astype(jnp.float32)
                d = d + ins[g][1, part, :].astype(jnp.float32)
            if last:
                h, d = gelu_pair(h, d)
            outs[g][0, part, :] = h.astype(jnp.bfloat16)
            outs[g][1, part, :] = d.astype(jnp.bfloat16)

    row_loop(hid.shape[0], join_rows)
    for copy in keep[0] + keep[1]:
        copy.wait()


def smem():
    return pl.BlockSpec(memory_space=pltpu.SMEM)


def vmem():
    return pl.BlockSpec(memory_space=pltpu.VMEM)


def hbm():
    return pl.BlockSpec(memory_space=pltpu.HBM)


def tile_scratch(total, width):
    return [
        pltpu.VMEM((width * BLK, total * BLK), jnp.bfloat16),
        pltpu.VMEM((total * BLK, width * BLK), jnp.bfloat16),
        pltpu.SemaphoreType.DMA((2, total, width)),
    ]


def up_call(plan, meta, x, dy, vals, ins, store, last):
    pieces = isinstance(x, list)
    n_pieces = len(x) if pieces else 0
    given = (*x, *dy) if pieces else (x, dy)
    tokens = sum(p.shape[0] for p in x) if pieces else x.shape[0]
    n = len(plan.sizes)
    has_in = ins is not None
    total, width = plan.total, plan.width
    shapes = [jax.ShapeDtypeStruct((2, tokens, s * BLK), jnp.bfloat16) for s in plan.sizes]
    if pieces:
        shapes += [jax.ShapeDtypeStruct((tokens, width * BLK), jnp.bfloat16)] * 2
    in_vmem = len(shapes)
    shapes.append(jax.ShapeDtypeStruct(Store(plan).shape, jnp.bfloat16))
    n_in = 3 + len(given) + n
    res = pl.pallas_call(
        functools.partial(up_kernel, plan, n_pieces, has_in, last),
        out_shape=shapes,
        in_specs=[smem()]
        + [hbm() if pieces else vmem()] * len(given)
        + [hbm()] * 2
        + ([vmem()] * n + [hbm()] if has_in else []),
        out_specs=[vmem()] * in_vmem + [hbm()],
        input_output_aliases={n_in: in_vmem} if has_in else {},
        scratch_shapes=tile_scratch(total, width)
        + [pltpu.VMEM((tokens, total * BLK), jnp.float32)] * 2
        + [pltpu.SemaphoreType.DMA((2, Store(plan).cuts))]
        + ([pltpu.SemaphoreType.DMA((2 * n_pieces,))] if pieces else []),
        compiler_params=pltpu.CompilerParams(vmem_limit_bytes=FIRST_LIMIT if pieces else VMEM_LIMIT),
        cost_estimate=pl.CostEstimate(
            flops=4 * tokens * width * total * BLK * BLK,
            bytes_accessed=4 * width * total * BLK * BLK + 8 * tokens * total * BLK,
            transcendentals=0,
        ),
        name="up_last" if last else "up",
    )(meta, *given, *vals, *((*ins, store) if has_in else ()))
    return (res[:n], res[-1], res[n], res[n + 1]) if pieces else (res[:n], res[-1])


DEAD_GROUP = 16


def dead_kernel(which, plan, slots, meta, out, zeros, sems):
    zeros[...] = jnp.zeros_like(zeros)
    live = meta[plan.start_at[which] + plan.per * plan.n]
    edge = jnp.minimum((live + DEAD_GROUP - 1) // DEAD_GROUP * DEAD_GROUP, slots)

    def one(i):
        return pltpu.make_async_copy(zeros.at[0], out.at[i], sems.at[i % DEAD_GROUP])

    def many(i):
        return pltpu.make_async_copy(
            zeros, out.at[pl.ds(i * DEAD_GROUP, DEAD_GROUP)], sems.at[DEAD_GROUP + i]
        )

    def loop(lo, hi, body):
        def step(i, carry):
            body(i)
            return carry

        lax.fori_loop(lo, hi, step, 0)

    loop(edge // DEAD_GROUP, slots // DEAD_GROUP, lambda i: many(i).start())
    loop(live, edge, lambda i: one(i).start())
    loop(edge // DEAD_GROUP, slots // DEAD_GROUP, lambda i: many(i).wait())
    loop(live, edge, lambda i: one(i).wait())


def dead_call(which, plan, meta, like):
    slots = like.shape[0]
    return pl.pallas_call(
        functools.partial(dead_kernel, which, plan, slots),
        out_shape=jax.ShapeDtypeStruct(like.shape, like.dtype),
        in_specs=[smem()],
        out_specs=hbm(),
        scratch_shapes=[
            pltpu.VMEM((DEAD_GROUP, BLK, BLK), like.dtype),
            pltpu.SemaphoreType.DMA((DEAD_GROUP + slots // DEAD_GROUP,)),
        ],
        compiler_params=pltpu.CompilerParams(vmem_limit_bytes=VMEM_LIMIT),
        cost_estimate=pl.CostEstimate(flops=0, bytes_accessed=slots * BLK * BLK, transcendentals=0),
        name="dead",
    )(meta)


def back_kernel(plan, down, grads, first, last, *refs):
    meta, refs = refs[0], refs[1:]
    if grads:
        x_t, dy, refs = refs[0], refs[1], refs[2:]
    if down:
        stores, refs = refs[: len(plan.parts)], refs[len(plan.parts) :]
    n = len(plan.sizes)
    acts, refs = refs[:n], refs[n:]
    olds, outs = {}, {}
    if not first:
        for k in down:
            olds[k], refs = refs[0], refs[1:]
    if grads:
        refs = refs[2:]
    for k in down:
        outs[k], refs = (refs[:2], refs[2:]) if last else (refs[:1], refs[1:])
    if grads:
        slot_out, refs = refs[:2], refs[2:]
    act, grd = refs[:2]
    if down:
        bufs, sems = dict(zip(down, refs[2 : 2 + len(down)])), refs[2 + len(down)]
    if grads:
        act_t, stage1, stage2, out_sems = refs[-4:]
    tokens = act.shape[0]
    columns = plan.width * BLK
    loads = {}
    for k in down:
        at, loads[k] = 0, []
        for store, part in zip(stores, plan.parts):
            span = pl.ds(at * BLK, part.total * BLK)
            dst = bufs[k].at[span, :] if k == 0 else bufs[k].at[:, span]
            for src, to in Store(part).views(store, (plan.shift - 1) % plan.n, 1 - k, dst):
                loads[k].append(pltpu.make_async_copy(src, to, sems.at[k, len(loads[k])]))
            at += part.total
        for load in loads[k]:
            load.start()

    def split_rows(part):
        for a, at in zip(acts, group_slices(plan)):
            value = a[0, part, :]
            act[part, at] = value
            grd[part, at] = a[1, part, :]
            if grads:
                act_t[at, part] = value.T

    row_loop(tokens, split_rows)

    def block_of(which, b, r):
        if which == 0:
            return stage1.at[block_at(r), block_at(b)]
        return stage2.at[block_at(b), block_at(r)]

    def send(which):
        def go(slot, b, r):
            pltpu.make_async_copy(block_of(which, b, r), slot_out[which].at[slot], out_sems.at[which, b, r]).start()

        plan.each(meta, which, go)

    def drain(which):
        def go(slot, b, r):
            pltpu.make_async_copy(block_of(which, 0, 0), slot_out[which].at[slot], out_sems.at[which, b, r]).wait()

        plan.each(meta, which, go)

    def weigh(k):
        for load in loads[k]:
            load.wait()

        def tile(at):
            res = dot_nn(act[...], bufs[0][:, at]) if k == 0 else dot_nt(grd[...], bufs[1][at, :])
            if not first:
                res = res + olds[k][:, at]
            if last:
                outs[k][0][:, at] = res[: tokens // 2]
                outs[k][1][:, at] = res[tokens // 2 :].astype(jnp.bfloat16)
            else:
                outs[k][0][:, at] = res

        tile_loop(columns, tile)

    if grads:

        def first_tile(at):
            stage1[:, at] = dot_nn(x_t[...], grd[:, at]).astype(jnp.bfloat16)

        tile_loop(plan.total * BLK, first_tile)
        send(0)
    if 0 in down:
        weigh(0)
    if grads:

        def second_tile(at):
            stage2[:, at] = dot_nn(act_t[...], dy[:, at]).astype(jnp.bfloat16)

        tile_loop(columns, second_tile)
        send(1)
    if 1 in down:
        weigh(1)
    if grads:
        drain(0)
        drain(1)


def back_call(plan, meta, x_t, dy, stores, acts, sums, grads, *, down=(0, 1), with_grads=True, last=False):
    total, width = plan.total, plan.width
    tokens = acts[0].shape[1]
    n = len(plan.sizes)
    first = sums is None
    acc = jax.ShapeDtypeStruct((tokens, width * BLK), jnp.float32)
    half = [jax.ShapeDtypeStruct((tokens // 2, width * BLK), t) for t in (jnp.float32, jnp.bfloat16)]
    operands = [meta]
    specs = [smem()]
    if with_grads:
        operands += [x_t, dy]
        specs += [vmem()] * 2
    if down:
        operands += stores
        specs += [hbm()] * len(stores)
    operands += acts
    specs += [vmem()] * n
    shapes, outs, alias = [], [], {}
    for k in down:
        if not first:
            if not last:
                alias[len(operands)] = len(shapes)
            operands.append(sums[k])
            specs.append(vmem())
        shapes += half if last else [acc]
        outs += [vmem()] * (2 if last else 1)
    if with_grads:
        for k in (0, 1):
            alias[len(operands)] = len(shapes)
            operands.append(grads[k])
            specs.append(hbm())
            shapes.append(jax.ShapeDtypeStruct(grads[k].shape, jnp.bfloat16))
            outs.append(hbm())
    scratch = [pltpu.VMEM((tokens, total * BLK), jnp.bfloat16)] * 2
    if down:
        big = tile_scratch(total, width)
        scratch += [big[1 - k] for k in down] + [pltpu.SemaphoreType.DMA((2, sum(Store(p).cuts for p in plan.parts)))]
    if with_grads:
        stage1, stage2, sems = tile_scratch(total, width)
        scratch += [
            pltpu.VMEM((total * BLK, tokens), jnp.bfloat16),
            stage1,
            stage2,
            sems,
        ]
    parts = len(down) + (2 if with_grads else 0)
    return pl.pallas_call(
        functools.partial(back_kernel, plan, down, with_grads, first, last),
        out_shape=shapes,
        in_specs=specs,
        out_specs=outs,
        input_output_aliases=alias,
        scratch_shapes=scratch,
        compiler_params=pltpu.CompilerParams(vmem_limit_bytes=VMEM_LIMIT),
        cost_estimate=pl.CostEstimate(
            flops=2 * parts * tokens * width * total * BLK * BLK,
            bytes_accessed=parts * width * total * BLK * BLK,
            transcendentals=0,
        ),
        name="back",
    )(*operands)


class Row:
    def __init__(self, size):
        self.cores = 2 if size % 2 == 0 else 1
        self.chips = size // self.cores

    def swap(self, value):
        if self.cores == 1:
            return value
        return lax.ppermute(value, "row", [(k, k ^ 1) for k in range(self.chips * 2)])

    def shift(self, value, step):
        pairs = []
        for x in range(self.chips):
            for c in range(self.cores):
                pairs.append((((x + step) % self.chips) * self.cores + c, x * self.cores + c))
        return lax.ppermute(value, "row", pairs)

    def gather(self, value):
        near = [value] + [self.shift(value, d) for d in range(1, self.chips)]
        return near + ([self.swap(p) for p in near] if self.cores > 1 else [])

    def scatter_near(self, keep, send):
        return keep + self.swap(send).astype(jnp.float32)

    def scatter_far(self, total):
        rows = total.shape[0] // self.chips
        mine = total[:rows]
        for d in range(1, self.chips):
            part = total[d * rows : (d + 1) * rows].astype(jnp.bfloat16)
            mine = mine + self.shift(part, -d).astype(jnp.float32)
        return mine.astype(jnp.bfloat16)


def shards(
    inputs,
    out_grad,
    first_vals,
    first_rows,
    first_cols,
    first_count,
    second_vals,
    second_rows,
    second_cols,
    second_count,
    *,
    hidden_blocks,
):
    n = lax.axis_size("col")
    ring = ring_of(n)
    ahead = [(ring[k], ring[(k + 1) % n]) for k in range(n)]
    back = [(b, a) for a, b in ahead]
    place = [0] * n
    for k, dev in enumerate(ring):
        place[dev] = k
    me = jnp.asarray(place, jnp.int32)[lax.axis_index("col")]

    row = Row(lax.axis_size("row"))
    x = row.gather(inputs)
    dy = row.gather(out_grad)
    width = inputs.shape[1] // BLK
    per = hidden_blocks // n
    vals = (first_vals[0, 0], second_vals[0, 0])
    slots = vals[0].shape[0]
    starts1, order1 = slot_order(first_cols[0, 0], first_rows[0, 0], first_count[0, 0], hidden_blocks)
    starts2, order2 = slot_order(second_rows[0, 0], second_cols[0, 0], second_count[0, 0], hidden_blocks)
    meta = jnp.concatenate([me[None], starts1, starts2, order1, order2])

    n_ahead = (per + 1) // 2
    parts = []
    for lo, cnt, sign in ((0, n_ahead, 1), (n_ahead, per - n_ahead, -1)):
        half = (cnt + 1) // 2
        parts.append([(lo, half, sign), (lo + half, cnt - half, sign)])
    streams = [[part[s] for part in parts if part[s][1] > 0] for s in range(2)]
    streams = [s for s in streams if s]

    def plan_of(stream, shift, parts=()):
        return Plan(stream, shift, n, per, hidden_blocks, slots, width, parts)

    def hop(stream, arrays):
        return [
            lax.ppermute(a, "col", ahead if sign > 0 else back) for a, (_, _, sign) in zip(arrays, stream)
        ]

    held = [None] * len(streams)
    x_t, grads, stores = None, [], [None] * len(streams)
    for t in range(n):
        for s, stream in enumerate(streams):
            ins = None if t == 0 else hop(stream, held[s])
            if t == 1 and s == 0:
                x_t = x.T
                ins, x_t = lax.optimization_barrier((ins, x_t))
            if t in (2, 3) and s == 0:
                grads.append(dead_call(t - 2, plan_of(stream, 0), meta, vals[t - 2]))
                ins, grads = lax.optimization_barrier((ins, grads))
            res = up_call(plan_of(stream, t + 1), meta, x, dy, vals, ins, stores[s], t == n - 1)
            if isinstance(x, list):
                x, dy = res[2:]
            held[s], stores[s] = res[:2]

    sums = None
    for t in range(n):
        for s, stream in enumerate(streams):
            if t > 0:
                held[s] = hop(stream, held[s])
                held[s], sums, grads = lax.optimization_barrier((held[s], sums, grads))
            if t < n - 1:
                res = back_call(plan_of(stream, t), meta, x_t, dy, [stores[s]], held[s], sums, grads)
                sums, grads = res[:2], res[2:]

    parts = [plan_of(stream, n - 1) for stream in streams]
    plan, acts = plan_of(sum(streams, []), n - 1, parts), sum(held, [])
    args = (plan, meta, x_t, dy, stores)
    out_near = row.scatter_near(*back_call(*args, acts, sums, None, down=(0,), with_grads=False, last=True))
    out_near, acts = lax.optimization_barrier((out_near, acts))
    in_near = row.scatter_near(*back_call(*args, acts, sums, None, down=(1,), with_grads=False, last=True))
    in_near, acts = lax.optimization_barrier((in_near, acts))
    out_sum = row.scatter_far(out_near)
    in_sum = row.scatter_far(in_near)
    grads = back_call(*args, acts, sums, grads, down=(), with_grads=True)
    return out_sum, in_sum, grads[0][None, None], grads[1][None, None]


def solution(mesh):
    hidden_blocks = 49152 // BLK // mesh.shape["row"]
    placed = (
        P("row", "col"),
        P("row", "col"),
        P("row", "col", None, None, None),
        P("row", "col", None),
        P("row", "col", None),
        P("row", "col"),
        P("row", "col", None, None, None),
        P("row", "col", None),
        P("row", "col", None),
        P("row", "col"),
    )
    return jax.shard_map(
        functools.partial(shards, hidden_blocks=hidden_blocks),
        mesh=mesh,
        in_specs=placed,
        out_specs=(
            P("row", "col"),
            P("row", "col"),
            P("row", "col", None, None, None),
            P("row", "col", None, None, None),
        ),
        check_vma=False,
    )
```

time: 631 us -> 566 us (0.90)
  the two profiles are of different devices: /device:TPU:12 before, /device:TPU:0 now
where the time goes in v3:
time: 566 us; the launch traced here: 555 us
  Pallas kernels  342 us (60%)
  waiting for transfers between devices  133 us (23%)
  starting transfers between devices  62.9 us (11%)
  local copies, waits for them, and re-layouts  9.71 us (2%)
    pallas_call x17, Pallas kernels, back_call(): pl.pallas_call(functools.partial(back_kernel, plan, down, with_grads, fir...  206 us
    pallas_call x16, Pallas kernels, up_call(): pl.pallas_call(functools.partial(up_kernel, plan, n_pieces, has_in, last)...  132 us
    ppermute x56, waiting for transfers between devices, hop(): lax.ppermute(a, 'col', ahead if sign > 0 else back)  113 us
    ppermute x56, starting transfers between devices, hop(): lax.ppermute(a, 'col', ahead if sign > 0 else back)  57.9 us
    ppermute x4, waiting for transfers between devices, shift(): return lax.ppermute(value, 'row', pairs)  17.8 us
  transfers between devices with their start and end apart: 66, of which 40 were waited for; matrix products, arithmetic and copies ran while one was open for 1% of the time, Pallas kernels for 59%

profile of v3, /device:TPU:0, one launch (start us, length us, event | category | flops | bytes accessed | tf_op | source)
XLA Modules:
  0.0 555.2 jit_solution(6603103605181882475)
XLA Ops:
  0.6 3.0 collective-permute-start
  7.4 6.4 %collective-permute-done.refs_2_ = bf16[128,1536]{1,0:T(8,128)(2,1)S(1)} collective-permute-done((bf16[128,1536]{1,0:T(8,128)(2,1)}, bf16[128,1536]{1,0:T(8,128)(2,1)S(1)}, u32[]{:S(2)}, u32[]{:S(2)}) %collective-permute-start) | collective-permute-done | bytes 393248 | tf_op jit(solution)/shard_map/ppermute | solution.py:516
  13.8 7.6 %collective-permute-done.3.refs_6_ = bf16[128,1536]{1,0:T(8,128)(2,1)S(1)} collective-permute-done((bf16[128,1536]{1,0:T(8,128)(2,1)}, bf16[128,1536]{1,0:T(8,128)(2,1)S(1)}, u32[]{:S(2)}, u32[]{:S(2)}) %collective-permute-start.3) | collective-permute-done | bytes 393248 | tf_op jit(solution)/shard_map/ppermute | solution.py:516
  25.7 10.7 %up.14 = (bf16[2,512,384]{2,1,0:T(8,128)(2,1)}, bf16[2,512,384]{2,1,0:T(8,128)(2,1)}, bf16[512,1536]{1,0:T(8,128)(2,1)}, bf16[512,1536]{1,0:T(8,128)(2,1)}, bf16[8,3072,768]{2,1,0:T(8,128)(2,1)}) custom-call(s32[1219]{0:T(1024)} %concatenate.3.refs_0_.meta, bf16[128,1536]{1,0:T(8,128)(2,1)} %refs_1_.1, bf16[128,1536]{1,0:T(8,128)(2,1)} %copy-done.6, ...), custom_call_target="tpu_custom_call" | custom-call | flops 2415919104 | bytes 7864320 | tf_op jit(solution)/shard_map/up/pallas_call | solution.py:265
  41.3 8.7 %up.21 = (bf16[2,512,384]{2,1,0:T(8,128)(2,1)}, bf16[2,512,384]{2,1,0:T(8,128)(2,1)}, bf16[8,3072,768]{2,1,0:T(8,128)(2,1)}) custom-call(s32[1219]{0:T(1024)S(1)} %copy-done.5, bf16[512,1536]{1,0:T(8,128)(2,1)S(1)} %copy-done.2, bf16[512,1536]{1,0:T(8,128)(2,1)S(1)} %copy-done, bf16[512,128,128]{2,1,0:T(8,128)(2,1)} %bitcast.27, bf16[512,128,128]{2,1,0:T(8,128)(2,1)} %bitcast.43), custom_call_target="tpu_custom_call" | custom-call | flops 2415919104 | bytes 7864320 | tf_op jit(solution)/shard_map/up/pallas_call | solution.py:265
  53.9 3.3 collective-permute-done.6.refs_5_
  59.9 8.3 %up.15 = (bf16[2,512,384]{2,1,0:T(8,128)(2,1)S(1)}, bf16[2,512,384]{2,1,0:T(8,128)(2,1)S(1)}, bf16[8,3072,768]{2,1,0:T(8,128)(2,1)}) custom-call(s32[1219]{0:T(1024)S(1)} %copy-done.5, bf16[512,1536]{1,0:T(8,128)(2,1)S(1)} %copy-done.3, bf16[512,1536]{1,0:T(8,128)(2,1)S(1)} %copy-done.1, ...), custom_call_target="tpu_custom_call", output_to_operand_aliasing={{2}: (7, {})} | custom-call | flops 2415919104 | bytes 7864320 | tf_op jit(solution)/shard_map/up/pallas_call | solution.py:265
  70.3 3.7 collective-permute-done.20.refs_5_
  75.4 8.5 %up.22 = (bf16[2,512,384]{2,1,0:T(8,128)(2,1)S(1)}, bf16[2,512,384]{2,1,0:T(8,128)(2,1)S(1)}, bf16[8,3072,768]{2,1,0:T(8,128)(2,1)}) custom-call(s32[1219]{0:T(1024)S(1)} %copy-done.5, bf16[512,1536]{1,0:T(8,128)(2,1)S(1)} %copy-done.3, bf16[512,1536]{1,0:T(8,128)(2,1)S(1)} %copy-done.1, ...), custom_call_target="tpu_custom_call", output_to_operand_aliasing={{2}: (7, {})} | custom-call | flops 2415919104 | bytes 7864320 | tf_op jit(solution)/shard_map/up/pallas_call | solution.py:265
  87.1 3.7 collective-permute-done.8.refs_5_
  92.1 7.9 %up.16 = (bf16[2,512,384]{2,1,0:T(8,128)(2,1)S(1)}, bf16[2,512,384]{2,1,0:T(8,128)(2,1)S(1)}, bf16[8,3072,768]{2,1,0:T(8,128)(2,1)}) custom-call(s32[1219]{0:T(1024)S(1)} %copy-done.5, bf16[512,1536]{1,0:T(8,128)(2,1)S(1)} %copy-done.4, bf16[512,1536]{1,0:T(8,128)(2,1)S(1)} %copy-done.1, ...), custom_call_target="tpu_custom_call", output_to_operand_aliasing={{2}: (7, {})} | custom-call | flops 2415919104 | bytes 7864320 | tf_op jit(solution)/shard_map/up/pallas_call | solution.py:265
  102.0 5.6 %collective-permute-done.22.refs_5_ = bf16[2,512,384]{2,1,0:T(8,128)(2,1)S(1)} collective-permute-done((bf16[2,512,384]{2,1,0:T(8,128)(2,1)S(1)}, bf16[2,512,384]{2,1,0:T(8,128)(2,1)S(1)}, u32[]{:S(2)}, u32[]{:S(2)}) %collective-permute-start.22) | collective-permute-done | bytes 786464 | tf_op jit(solution)/shard_map/ppermute | solution.py:581
  109.0 7.8 %up.23 = (bf16[2,512,384]{2,1,0:T(8,128)(2,1)S(1)}, bf16[2,512,384]{2,1,0:T(8,128)(2,1)S(1)}, bf16[8,3072,768]{2,1,0:T(8,128)(2,1)}) custom-call(s32[1219]{0:T(1024)S(1)} %copy-done.5, bf16[512,1536]{1,0:T(8,128)(2,1)S(1)} %copy-done.4, bf16[512,1536]{1,0:T(8,128)(2,1)S(1)} %copy-done.1, ...), custom_call_target="tpu_custom_call", output_to_operand_aliasing={{2}: (7, {})} | custom-call | flops 2415919104 | bytes 7864320 | tf_op jit(solution)/shard_map/up/pallas_call | solution.py:265
  118.8 2.8 dead.3.refs_7_
  121.6 2.9 collective-permute-done.10.refs_5_
  125.8 8.0 %up.17 = (bf16[2,512,384]{2,1,0:T(8,128)(2,1)S(1)}, bf16[2,512,384]{2,1,0:T(8,128)(2,1)S(1)}, bf16[8,3072,768]{2,1,0:T(8,128)(2,1)}) custom-call(s32[1219]{0:T(1024)S(1)} %copy-done.5, bf16[512,1536]{1,0:T(8,128)(2,1)S(1)} %copy-done.4, bf16[512,1536]{1,0:T(8,128)(2,1)S(1)} %copy-done.1, ...), custom_call_target="tpu_custom_call", output_to_operand_aliasing={{2}: (7, {})} | custom-call | flops 2415919104 | bytes 7864320 | tf_op jit(solution)/shard_map/up/pallas_call | solution.py:265
  135.9 5.4 collective-permute-done.24.refs_5_
  142.7 7.6 %up.24 = (bf16[2,512,384]{2,1,0:T(8,128)(2,1)S(1)}, bf16[2,512,384]{2,1,0:T(8,128)(2,1)S(1)}, bf16[8,3072,768]{2,1,0:T(8,128)(2,1)}) custom-call(s32[1219]{0:T(1024)S(1)} %copy-done.5, bf16[512,1536]{1,0:T(8,128)(2,1)S(1)} %copy-done.4, bf16[512,1536]{1,0:T(8,128)(2,1)S(1)} %copy-done.1, ...), custom_call_target="tpu_custom_call", output_to_operand_aliasing={{2}: (7, {})} | custom-call | flops 2415919104 | bytes 7864320 | tf_op jit(solution)/shard_map/up/pallas_call | solution.py:265
  152.4 5.8 %collective-permute-done.12.refs_5_ = bf16[2,512,384]{2,1,0:T(8,128)(2,1)S(1)} collective-permute-done((bf16[2,512,384]{2,1,0:T(8,128)(2,1)S(1)}, bf16[2,512,384]{2,1,0:T(8,128)(2,1)S(1)}, u32[]{:S(2)}, u32[]{:S(2)}) %collective-permute-start.12) | collective-permute-done | bytes 786464 | tf_op jit(solution)/shard_map/ppermute | solution.py:581
  159.5 7.7 %up.18 = (bf16[2,512,384]{2,1,0:T(8,128)(2,1)S(1)}, bf16[2,512,384]{2,1,0:T(8,128)(2,1)S(1)}, bf16[8,3072,768]{2,1,0:T(8,128)(2,1)}) custom-call(s32[1219]{0:T(1024)S(1)} %copy-done.5, bf16[512,1536]{1,0:T(8,128)(2,1)S(1)} %copy-done.4, bf16[512,1536]{1,0:T(8,128)(2,1)S(1)} %copy-done.1, ...), custom_call_target="tpu_custom_call", output_to_operand_aliasing={{2}: (7, {})} | custom-call | flops 2415919104 | bytes 7864320 | tf_op jit(solution)/shard_map/up/pallas_call | solution.py:265
  169.3 5.7 %collective-permute-done.26.refs_5_ = bf16[2,512,384]{2,1,0:T(8,128)(2,1)S(1)} collective-permute-done((bf16[2,512,384]{2,1,0:T(8,128)(2,1)S(1)}, bf16[2,512,384]{2,1,0:T(8,128)(2,1)S(1)}, u32[]{:S(2)}, u32[]{:S(2)}) %collective-permute-start.26) | collective-permute-done | bytes 786464 | tf_op jit(solution)/shard_map/ppermute | solution.py:581
  176.4 7.6 %up.25 = (bf16[2,512,384]{2,1,0:T(8,128)(2,1)S(1)}, bf16[2,512,384]{2,1,0:T(8,128)(2,1)S(1)}, bf16[8,3072,768]{2,1,0:T(8,128)(2,1)}) custom-call(s32[1219]{0:T(1024)S(1)} %copy-done.5, bf16[512,1536]{1,0:T(8,128)(2,1)S(1)} %copy-done.4, bf16[512,1536]{1,0:T(8,128)(2,1)S(1)} %copy-done.1, ...), custom_call_target="tpu_custom_call", output_to_operand_aliasing={{2}: (7, {})} | custom-call | flops 2415919104 | bytes 7864320 | tf_op jit(solution)/shard_map/up/pallas_call | solution.py:265
  186.1 5.8 %collective-permute-done.14.refs_5_ = bf16[2,512,384]{2,1,0:T(8,128)(2,1)S(1)} collective-permute-done((bf16[2,512,384]{2,1,0:T(8,128)(2,1)S(1)}, bf16[2,512,384]{2,1,0:T(8,128)(2,1)S(1)}, u32[]{:S(2)}, u32[]{:S(2)}) %collective-permute-start.14) | collective-permute-done | bytes 786464 | tf_op jit(solution)/shard_map/ppermute | solution.py:581
  193.2 8.1 %up.19 = (bf16[2,512,384]{2,1,0:T(8,128)(2,1)S(1)}, bf16[2,512,384]{2,1,0:T(8,128)(2,1)S(1)}, bf16[8,3072,768]{2,1,0:T(8,128)(2,1)}) custom-call(s32[1219]{0:T(1024)S(1)} %copy-done.5, bf16[512,1536]{1,0:T(8,128)(2,1)S(1)} %copy-done.4, bf16[512,1536]{1,0:T(8,128)(2,1)S(1)} %copy-done.1, ...), custom_call_target="tpu_custom_call", output_to_operand_aliasing={{2}: (7, {})} | custom-call | flops 2415919104 | bytes 7864320 | tf_op jit(solution)/shard_map/up/pallas_call | solution.py:265
  203.4 5.4 collective-permute-done.28.refs_5_
  210.1 8.1 %up.26 = (bf16[2,512,384]{2,1,0:T(8,128)(2,1)S(1)}, bf16[2,512,384]{2,1,0:T(8,128)(2,1)S(1)}, bf16[8,3072,768]{2,1,0:T(8,128)(2,1)}) custom-call(s32[1219]{0:T(1024)S(1)} %copy-done.5, bf16[512,1536]{1,0:T(8,128)(2,1)S(1)} %copy-done.4, bf16[512,1536]{1,0:T(8,128)(2,1)S(1)} %copy-done.1, ...), custom_call_target="tpu_custom_call", output_to_operand_aliasing={{2}: (7, {})} | custom-call | flops 2415919104 | bytes 7864320 | tf_op jit(solution)/shard_map/up/pallas_call | solution.py:265
  220.3 5.3 collective-permute-done.16.refs_5_
  226.9 7.6 %up.20 = (bf16[2,512,384]{2,1,0:T(8,128)(2,1)S(1)}, bf16[2,512,384]{2,1,0:T(8,128)(2,1)S(1)}, bf16[8,3072,768]{2,1,0:T(8,128)(2,1)}) custom-call(s32[1219]{0:T(1024)S(1)} %copy-done.5, bf16[512,1536]{1,0:T(8,128)(2,1)S(1)} %copy-done.4, bf16[512,1536]{1,0:T(8,128)(2,1)S(1)} %copy-done.1, ...), custom_call_target="tpu_custom_call", output_to_operand_aliasing={{2}: (7, {})} | custom-call | flops 2415919104 | bytes 7864320 | tf_op jit(solution)/shard_map/up/pallas_call | solution.py:265
  236.6 5.8 %collective-permute-done.30.refs_5_ = bf16[2,512,384]{2,1,0:T(8,128)(2,1)S(1)} collective-permute-done((bf16[2,512,384]{2,1,0:T(8,128)(2,1)S(1)}, bf16[2,512,384]{2,1,0:T(8,128)(2,1)S(1)}, u32[]{:S(2)}, u32[]{:S(2)}) %collective-permute-start.30) | collective-permute-done | bytes 786464 | tf_op jit(solution)/shard_map/ppermute | solution.py:581
  243.8 8.0 %up.27 = (bf16[2,512,384]{2,1,0:T(8,128)(2,1)S(1)}, bf16[2,512,384]{2,1,0:T(8,128)(2,1)S(1)}, bf16[8,3072,768]{2,1,0:T(8,128)(2,1)}) custom-call(s32[1219]{0:T(1024)S(1)} %copy-done.5, bf16[512,1536]{1,0:T(8,128)(2,1)S(1)} %copy-done.4, bf16[512,1536]{1,0:T(8,128)(2,1)S(1)} %copy-done.1, ...), custom_call_target="tpu_custom_call", output_to_operand_aliasing={{2}: (7, {})} | custom-call | flops 2415919104 | bytes 7864320 | tf_op jit(solution)/shard_map/up/pallas_call | solution.py:265
  253.8 5.5 collective-permute-done.18.refs_5_
  260.6 8.9 %up_last.2 = (bf16[2,512,384]{2,1,0:T(8,128)(2,1)S(1)}, bf16[2,512,384]{2,1,0:T(8,128)(2,1)S(1)}, bf16[8,3072,768]{2,1,0:T(8,128)(2,1)}) custom-call(s32[1219]{0:T(1024)S(1)} %copy-done.5, bf16[512,1536]{1,0:T(8,128)(2,1)S(1)} %copy-done.4, bf16[512,1536]{1,0:T(8,128)(2,1)S(1)} %copy-done.1, ...), custom_call_target="tpu_custom_call", output_to_operand_aliasing={{2}: (7, {})} | custom-call | flops 2415919104 | bytes 7864320 | tf_op jit(solution)/shard_map/up_last/pallas_call | solution.py:265
  271.6 4.5 collective-permute-done.32.refs_5_
  277.5 8.9 %up_last.3 = (bf16[2,512,384]{2,1,0:T(8,128)(2,1)S(1)}, bf16[2,512,384]{2,1,0:T(8,128)(2,1)S(1)}, bf16[8,3072,768]{2,1,0:T(8,128)(2,1)}) custom-call(s32[1219]{0:T(1024)S(1)} %copy-done.5, bf16[512,1536]{1,0:T(8,128)(2,1)S(1)} %copy-done.4, bf16[512,1536]{1,0:T(8,128)(2,1)S(1)} %copy-done.1, ...), custom_call_target="tpu_custom_call", output_to_operand_aliasing={{2}: (7, {})} | custom-call | flops 2415919104 | bytes 7864320 | tf_op jit(solution)/shard_map/up_last/pallas_call | solution.py:265
  288.5 12.4 %back.17 = (f32[512,1536]{1,0:T(8,128)S(1)}, f32[512,1536]{1,0:T(8,128)S(1)}, bf16[512,128,128]{2,1,0:T(8,128)(2,1)}, bf16[512,128,128]{2,1,0:T(8,128)(2,1)}) custom-call(s32[1219]{0:T(1024)S(1)} %copy-done.5, bf16[1536,512]{1,0:T(8,128)(2,1)S(1)} %bitcast.11, bf16[512,1536]{1,0:T(8,128)(2,1)S(1)} %copy-done.1, ...), custom_call_target="tpu_custom_call", output_to_operand_aliasing={{2}: (6, {}), {3}: (7, {})} | custom-call | flops 4831838208 | bytes 4718592 | tf_op jit(solution)/shard_map/back/pallas_call | solution.py:484
  300.8 12.9 %back.18 = (f32[512,1536]{1,0:T(8,128)S(1)}, f32[512,1536]{1,0:T(8,128)S(1)}, bf16[512,128,128]{2,1,0:T(8,128)(2,1)}, bf16[512,128,128]{2,1,0:T(8,128)(2,1)}) custom-call(s32[1219]{0:T(1024)S(1)} %copy-done.5, bf16[1536,512]{1,0:T(8,128)(2,1)S(1)} %bitcast.12, ...), custom_call_target="tpu_custom_call", output_to_operand_aliasing={{0}: (6, {}), {1}: (7, {}), {2}: (8, {}), {3}: (9, {})} | custom-call | flops 4831838208 | bytes 4718592 | tf_op jit(solution)/shard_map/back/pallas_call | solution.py:484
  313.9 2.0 collective-permute-start.37
  315.9 12.8 %back.19 = (f32[512,1536]{1,0:T(8,128)S(1)}, f32[512,1536]{1,0:T(8,128)S(1)}, bf16[512,128,128]{2,1,0:T(8,128)(2,1)}, bf16[512,128,128]{2,1,0:T(8,128)(2,1)}) custom-call(s32[1219]{0:T(1024)S(1)} %copy-done.5, bf16[1536,512]{1,0:T(8,128)(2,1)S(1)} %bitcast.13, ...), custom_call_target="tpu_custom_call", output_to_operand_aliasing={{0}: (6, {}), {1}: (7, {}), {2}: (8, {}), {3}: (9, {})} | custom-call | flops 4831838208 | bytes 4718592 | tf_op jit(solution)/shard_map/back/pallas_call | solution.py:484
  328.8 2.0 collective-permute-start.43
  330.8 12.7 %back.20 = (f32[512,1536]{1,0:T(8,128)S(1)}, f32[512,1536]{1,0:T(8,128)S(1)}, bf16[512,128,128]{2,1,0:T(8,128)(2,1)}, bf16[512,128,128]{2,1,0:T(8,128)(2,1)}) custom-call(s32[1219]{0:T(1024)S(1)} %copy-done.5, bf16[1536,512]{1,0:T(8,128)(2,1)S(1)} %bitcast.14, ...), custom_call_target="tpu_custom_call", output_to_operand_aliasing={{0}: (6, {}), {1}: (7, {}), {2}: (8, {}), {3}: (9, {})} | custom-call | flops 4831838208 | bytes 4718592 | tf_op jit(solution)/shard_map/back/pallas_call | solution.py:484
  343.6 2.0 collective-permute-start.41
  345.6 12.7 %back.21 = (f32[512,1536]{1,0:T(8,128)S(1)}, f32[512,1536]{1,0:T(8,128)S(1)}, bf16[512,128,128]{2,1,0:T(8,128)(2,1)}, bf16[512,128,128]{2,1,0:T(8,128)(2,1)}) custom-call(s32[1219]{0:T(1024)S(1)} %copy-done.5, bf16[1536,512]{1,0:T(8,128)(2,1)S(1)} %bitcast.15, ...), custom_call_target="tpu_custom_call", output_to_operand_aliasing={{0}: (6, {}), {1}: (7, {}), {2}: (8, {}), {3}: (9, {})} | custom-call | flops 4831838208 | bytes 4718592 | tf_op jit(solution)/shard_map/back/pallas_call | solution.py:484
  358.4 2.0 collective-permute-start.47
  360.4 12.7 %back.22 = (f32[512,1536]{1,0:T(8,128)S(1)}, f32[512,1536]{1,0:T(8,128)S(1)}, bf16[512,128,128]{2,1,0:T(8,128)(2,1)}, bf16[512,128,128]{2,1,0:T(8,128)(2,1)}) custom-call(s32[1219]{0:T(1024)S(1)} %copy-done.5, bf16[1536,512]{1,0:T(8,128)(2,1)S(1)} %bitcast.16, ...), custom_call_target="tpu_custom_call", output_to_operand_aliasing={{0}: (6, {}), {1}: (7, {}), {2}: (8, {}), {3}: (9, {})} | custom-call | flops 4831838208 | bytes 4718592 | tf_op jit(solution)/shard_map/back/pallas_call | solution.py:484
  373.2 2.0 collective-permute-start.45
  375.2 12.8 %back.23 = (f32[512,1536]{1,0:T(8,128)S(1)}, f32[512,1536]{1,0:T(8,128)S(1)}, bf16[512,128,128]{2,1,0:T(8,128)(2,1)}, bf16[512,128,128]{2,1,0:T(8,128)(2,1)}) custom-call(s32[1219]{0:T(1024)S(1)} %copy-done.5, bf16[1536,512]{1,0:T(8,128)(2,1)S(1)} %bitcast.17, ...), custom_call_target="tpu_custom_call", output_to_operand_aliasing={{0}: (6, {}), {1}: (7, {}), {2}: (8, {}), {3}: (9, {})} | custom-call | flops 4831838208 | bytes 4718592 | tf_op jit(solution)/shard_map/back/pallas_call | solution.py:484
  388.1 2.0 collective-permute-start.51
  390.1 12.8 %back.24 = (f32[512,1536]{1,0:T(8,128)S(1)}, f32[512,1536]{1,0:T(8,128)S(1)}, bf16[512,128,128]{2,1,0:T(8,128)(2,1)}, bf16[512,128,128]{2,1,0:T(8,128)(2,1)}) custom-call(s32[1219]{0:T(1024)S(1)} %copy-done.5, bf16[1536,512]{1,0:T(8,128)(2,1)S(1)} %bitcast.18, ...), custom_call_target="tpu_custom_call", output_to_operand_aliasing={{0}: (6, {}), {1}: (7, {}), {2}: (8, {}), {3}: (9, {})} | custom-call | flops 4831838208 | bytes 4718592 | tf_op jit(solution)/shard_map/back/pallas_call | solution.py:484
  403.0 2.0 collective-permute-start.49
  405.0 12.8 %back.25 = (f32[512,1536]{1,0:T(8,128)S(1)}, f32[512,1536]{1,0:T(8,128)S(1)}, bf16[512,128,128]{2,1,0:T(8,128)(2,1)}, bf16[512,128,128]{2,1,0:T(8,128)(2,1)}) custom-call(s32[1219]{0:T(1024)S(1)} %copy-done.5, bf16[1536,512]{1,0:T(8,128)(2,1)S(1)} %bitcast.19, ...), custom_call_target="tpu_custom_call", output_to_operand_aliasing={{0}: (6, {}), {1}: (7, {}), {2}: (8, {}), {3}: (9, {})} | custom-call | flops 4831838208 | bytes 4718592 | tf_op jit(solution)/shard_map/back/pallas_call | solution.py:484
  421.0 12.9 %back.26 = (f32[512,1536]{1,0:T(8,128)S(1)}, f32[512,1536]{1,0:T(8,128)S(1)}, bf16[512,128,128]{2,1,0:T(8,128)(2,1)}, bf16[512,128,128]{2,1,0:T(8,128)(2,1)}) custom-call(s32[1219]{0:T(1024)S(1)} %copy-done.5, bf16[1536,512]{1,0:T(8,128)(2,1)S(1)} %bitcast.20, ...), custom_call_target="tpu_custom_call", output_to_operand_aliasing={{0}: (6, {}), {1}: (7, {}), {2}: (8, {}), {3}: (9, {})} | custom-call | flops 4831838208 | bytes 4718592 | tf_op jit(solution)/shard_map/back/pallas_call | solution.py:484
  437.8 12.7 %back.27 = (f32[512,1536]{1,0:T(8,128)S(1)}, f32[512,1536]{1,0:T(8,128)S(1)}, bf16[512,128,128]{2,1,0:T(8,128)(2,1)}, bf16[512,128,128]{2,1,0:T(8,128)(2,1)}) custom-call(s32[1219]{0:T(1024)S(1)} %copy-done.5, bf16[1536,512]{1,0:T(8,128)(2,1)S(1)} %bitcast.21, ...), custom_call_target="tpu_custom_call", output_to_operand_aliasing={{0}: (6, {}), {1}: (7, {}), {2}: (8, {}), {3}: (9, {})} | custom-call | flops 4831838208 | bytes 4718592 | tf_op jit(solution)/shard_map/back/pallas_call | solution.py:484
  450.5 2.1 collective-permute-done.55.refs_5_
  454.7 12.6 %back.28 = (f32[512,1536]{1,0:T(8,128)S(1)}, f32[512,1536]{1,0:T(8,128)S(1)}, bf16[512,128,128]{2,1,0:T(8,128)(2,1)}, bf16[512,128,128]{2,1,0:T(8,128)(2,1)}) custom-call(s32[1219]{0:T(1024)S(1)} %copy-done.5, bf16[1536,512]{1,0:T(8,128)(2,1)S(1)} %bitcast.22, ...), custom_call_target="tpu_custom_call", output_to_operand_aliasing={{0}: (6, {}), {1}: (7, {}), {2}: (8, {}), {3}: (9, {})} | custom-call | flops 4831838208 | bytes 4718592 | tf_op jit(solution)/shard_map/back/pallas_call | solution.py:484
  467.3 2.2 collective-permute-done.53.refs_5_
  471.5 13.0 %back.29 = (f32[512,1536]{1,0:T(8,128)S(1)}, f32[512,1536]{1,0:T(8,128)S(1)}, bf16[512,128,128]{2,1,0:T(8,128)(2,1)}, bf16[512,128,128]{2,1,0:T(8,128)(2,1)}) custom-call(s32[1219]{0:T(1024)S(1)} %copy-done.5, bf16[1536,512]{1,0:T(8,128)(2,1)S(1)} %bitcast.23, ...), custom_call_target="tpu_custom_call", output_to_operand_aliasing={{0}: (6, {}), {1}: (7, {}), {2}: (8, {}), {3}: (9, {})} | custom-call | flops 4831838208 | bytes 4718592 | tf_op jit(solution)/shard_map/back/pallas_call | solution.py:484
  488.4 13.1 %back.30 = (f32[512,1536]{1,0:T(8,128)S(1)}, f32[512,1536]{1,0:T(8,128)S(1)}, bf16[512,128,128]{2,1,0:T(8,128)(2,1)}, bf16[512,128,128]{2,1,0:T(8,128)(2,1)}) custom-call(s32[1219]{0:T(1024)S(1)} %copy-done.5, bf16[1536,512]{1,0:T(8,128)(2,1)S(1)} %bitcast.24, ...), custom_call_target="tpu_custom_call", output_to_operand_aliasing={{0}: (6, {}), {1}: (7, {}), {2}: (8, {}), {3}: (9, {})} | custom-call | flops 4831838208 | bytes 4718592 | tf_op jit(solution)/shard_map/back/pallas_call | solution.py:484
  503.2 12.5 %collective-permute-done.60.refs_5_ = bf16[2,512,384]{2,1,0:T(8,128)(2,1)S(1)} collective-permute-done((bf16[2,512,384]{2,1,0:T(8,128)(2,1)S(1)}, bf16[2,512,384]{2,1,0:T(8,128)(2,1)S(1)}, u32[]{:S(2)}, u32[]{:S(2)}) %collective-permute-start.60) | collective-permute-done | bytes 786464 | tf_op jit(solution)/shard_map/ppermute | solution.py:581
  515.7 2.2 collective-permute-done.61.refs_6_
  517.9 6.5 %back.31 = (f32[256,1536]{1,0:T(8,128)S(1)}, bf16[256,1536]{1,0:T(8,128)(2,1)S(1)}) custom-call(s32[1219]{0:T(1024)S(1)} %copy-done.5, bf16[8,3072,768]{2,1,0:T(8,128)(2,1)} %get-tuple-element.250.refs_3_.refs_1_, bf16[8,3072,768]{2,1,0:T(8,128)(2,1)} %get-tuple-element.272.refs_3_.refs_2_, bf16[2,512,384]{2,1,0:T(8,128)(2,1)S(1)} %collective-permute-done.56.refs_3_, ...), custom_call_target="tpu_custom_call" | custom-call | flops 2415919104 | bytes 2359296 | tf_op jit(solution)/shard_map/back/pallas_call | solution.py:484
  524.5 2.3 collective-permute-done.62
  527.7 6.7 %back.32 = (f32[256,1536]{1,0:T(8,128)S(1)}, bf16[256,1536]{1,0:T(8,128)(2,1)S(1)}) custom-call(s32[1219]{0:T(1024)S(1)} %copy-done.5, bf16[8,3072,768]{2,1,0:T(8,128)(2,1)} %get-tuple-element.250.refs_3_.refs_1_, bf16[8,3072,768]{2,1,0:T(8,128)(2,1)} %get-tuple-element.272.refs_3_.refs_2_, bf16[2,512,384]{2,1,0:T(8,128)(2,1)S(1)} %collective-permute-done.56.refs_3_, ...), custom_call_target="tpu_custom_call" | custom-call | flops 2415919104 | bytes 2359296 | tf_op jit(solution)/shard_map/back/pallas_call | solution.py:484
  534.5 3.8 collective-permute-done.63
  540.0 14.1 %back.33 = (bf16[512,128,128]{2,1,0:T(8,128)(2,1)}, bf16[512,128,128]{2,1,0:T(8,128)(2,1)}) custom-call(s32[1219]{0:T(1024)S(1)} %copy-done.5, bf16[1536,512]{1,0:T(8,128)(2,1)S(1)} %bitcast.25, bf16[512,1536]{1,0:T(8,128)(2,1)S(1)} %copy-done.1, ...), custom_call_target="tpu_custom_call", output_to_operand_aliasing={{0}: (7, {}), {1}: (8, {})} | custom-call | flops 4831838208 | bytes 4718592 | tf_op jit(solution)/shard_map/back/pallas_call | solution.py:484
  (145 shorter events, 86.5 us)
Async XLA Ops:
  0.6 13.2 %collective-permute-start = (bf16[128,1536]{1,0:T(8,128)(2,1)}, bf16[128,1536]{1,0:T(8,128)(2,1)S(1)}, u32[]{:S(2)}, u32[]{:S(2)}) collective-permute-start(bf16[128,1536]{1,0:T(8,128)(2,1)} %refs_1_.1), channel_id=1, source_target_pairs={{16,0},{24,8},{0,16},{8,24},{17,1},{25,9},{1,17},{9,25},{18,2},{26... | collective-permute-start | bytes 1179656 | tf_op jit(solution)/shard_map/ppermute | solution.py:516
  3.6 20.9 %collective-permute-start.1 = (bf16[128,1536]{1,0:T(8,128)(2,1)}, bf16[128,1536]{1,0:T(8,128)(2,1)S(1)}, u32[]{:S(2)}, u32[]{:S(2)}) collective-permute-start(bf16[128,1536]{1,0:T(8,128)(2,1)} %refs_1_.1), channel_id=1, source_target_pairs={{0,8},{8,0},{16,24},{24,16},{1,9},{9,1},{17,25},{25,17},{2,10},{10... | collective-permute-start | bytes 1179656 | tf_op jit(solution)/shard_map/ppermute | solution.py:509
  3.6 17.8 %collective-permute-start.3 = (bf16[128,1536]{1,0:T(8,128)(2,1)}, bf16[128,1536]{1,0:T(8,128)(2,1)S(1)}, u32[]{:S(2)}, u32[]{:S(2)}) collective-permute-start(bf16[128,1536]{1,0:T(8,128)(2,1)} %refs_5_.1), channel_id=1, source_target_pairs={{16,0},{24,8},{0,16},{8,24},{17,1},{25,9},{1,17},{9,25},{18,2},{26... | collective-permute-start | bytes 1179656 | tf_op jit(solution)/shard_map/ppermute | solution.py:516
  3.8 20.8 %collective-permute-start.4 = (bf16[128,1536]{1,0:T(8,128)(2,1)}, bf16[128,1536]{1,0:T(8,128)(2,1)S(1)}, u32[]{:S(2)}, u32[]{:S(2)}) collective-permute-start(bf16[128,1536]{1,0:T(8,128)(2,1)} %refs_5_.1), channel_id=1, source_target_pairs={{0,8},{8,0},{16,24},{24,16},{1,9},{9,1},{17,25},{25,17},{2,10},{10... | collective-permute-start | bytes 1179656 | tf_op jit(solution)/shard_map/ppermute | solution.py:509
  13.8 10.8 %collective-permute-start.2 = (bf16[128,1536]{1,0:T(8,128)(2,1)S(1)}, bf16[128,1536]{1,0:T(8,128)(2,1)S(1)}, u32[]{:S(2)}, u32[]{:S(2)}) collective-permute-start(bf16[128,1536]{1,0:T(8,128)(2,1)S(1)} %collective-permute-done.refs_2_), channel_id=1, source_target_pairs={{0,8},{8,0},{16,24},{24,16},{1,9},{9,1},{17,25},{25,17},{2,10},{10... | collective-permute-start | bytes 1179656 | tf_op jit(solution)/shard_map/ppermute | solution.py:509
  36.4 20.8 %collective-permute-start.6 = (bf16[2,512,384]{2,1,0:T(8,128)(2,1)}, bf16[2,512,384]{2,1,0:T(8,128)(2,1)}, u32[]{:S(2)}, u32[]{:S(2)}) collective-permute-start(bf16[2,512,384]{2,1,0:T(8,128)(2,1)} %get-tuple-element.222), channel_id=1, source_target_pairs={{0,2},{2,4},{4,6},{6,7},{7,5},{5,3},{3,1},{1,0},{8,10},{10,12},{12... | collective-permute-start | bytes 2359304 | tf_op jit(solution)/shard_map/ppermute | solution.py:581
  37.9 20.7 %collective-permute-start.7 = (bf16[2,512,384]{2,1,0:T(8,128)(2,1)}, bf16[2,512,384]{2,1,0:T(8,128)(2,1)}, u32[]{:S(2)}, u32[]{:S(2)}) collective-permute-start(bf16[2,512,384]{2,1,0:T(8,128)(2,1)} %get-tuple-element.223), channel_id=1, source_target_pairs={{2,0},{4,2},{6,4},{7,6},{5,7},{3,5},{1,3},{0,1},{10,8},{12,10},{14... | collective-permute-start | bytes 2359304 | tf_op jit(solution)/shard_map/ppermute | solution.py:581
  50.1 24.0 %collective-permute-start.20 = (bf16[2,512,384]{2,1,0:T(8,128)(2,1)}, bf16[2,512,384]{2,1,0:T(8,128)(2,1)}, u32[]{:S(2)}, u32[]{:S(2)}) collective-permute-start(bf16[2,512,384]{2,1,0:T(8,128)(2,1)} %get-tuple-element.251), channel_id=1, source_target_pairs={{0,2},{2,4},{4,6},{6,7},{7,5},{5,3},{3,1},{1,0},{8,10},{10,12},{12... | collective-permute-start | bytes 2359304 | tf_op jit(solution)/shard_map/ppermute | solution.py:581
  50.8 24.5 %collective-permute-start.21 = (bf16[2,512,384]{2,1,0:T(8,128)(2,1)}, bf16[2,512,384]{2,1,0:T(8,128)(2,1)}, u32[]{:S(2)}, u32[]{:S(2)}) collective-permute-start(bf16[2,512,384]{2,1,0:T(8,128)(2,1)} %get-tuple-element.252), channel_id=1, source_target_pairs={{2,0},{4,2},{6,4},{7,6},{5,7},{3,5},{1,3},{0,1},{10,8},{12,10},{14... | collective-permute-start | bytes 2359304 | tf_op jit(solution)/shard_map/ppermute | solution.py:581
  68.2 22.5 %collective-permute-start.8 = (bf16[2,512,384]{2,1,0:T(8,128)(2,1)S(1)}, bf16[2,512,384]{2,1,0:T(8,128)(2,1)S(1)}, u32[]{:S(2)}, u32[]{:S(2)}) collective-permute-start(bf16[2,512,384]{2,1,0:T(8,128)(2,1)S(1)} %get-tuple-element.227), channel_id=1, source_target_pairs={{0,2},{2,4},{4,6},{6,7},{7,5},{5,3},{3,1},{1,0},{8,10},{10,12},{12... | collective-permute-start | bytes 2359304 | tf_op jit(solution)/shard_map/ppermute | solution.py:581
  69.8 22.3 %collective-permute-start.9 = (bf16[2,512,384]{2,1,0:T(8,128)(2,1)S(1)}, bf16[2,512,384]{2,1,0:T(8,128)(2,1)S(1)}, u32[]{:S(2)}, u32[]{:S(2)}) collective-permute-start(bf16[2,512,384]{2,1,0:T(8,128)(2,1)S(1)} %get-tuple-element.228), channel_id=1, source_target_pairs={{2,0},{4,2},{6,4},{7,6},{5,7},{3,5},{1,3},{0,1},{10,8},{12,10},{14... | collective-permute-start | bytes 2359304 | tf_op jit(solution)/shard_map/ppermute | solution.py:581
  83.9 23.8 %collective-permute-start.22 = (bf16[2,512,384]{2,1,0:T(8,128)(2,1)S(1)}, bf16[2,512,384]{2,1,0:T(8,128)(2,1)S(1)}, u32[]{:S(2)}, u32[]{:S(2)}) collective-permute-start(bf16[2,512,384]{2,1,0:T(8,128)(2,1)S(1)} %get-tuple-element.254), channel_id=1, source_target_pairs={{0,2},{2,4},{4,6},{6,7},{7,5},{5,3},{3,1},{1,0},{8,10},{10,12},{12... | collective-permute-start | bytes 2359304 | tf_op jit(solution)/shard_map/ppermute | solution.py:581
  85.4 23.5 %collective-permute-start.23 = (bf16[2,512,384]{2,1,0:T(8,128)(2,1)S(1)}, bf16[2,512,384]{2,1,0:T(8,128)(2,1)S(1)}, u32[]{:S(2)}, u32[]{:S(2)}) collective-permute-start(bf16[2,512,384]{2,1,0:T(8,128)(2,1)S(1)} %get-tuple-element.255), channel_id=1, source_target_pairs={{2,0},{4,2},{6,4},{7,6},{5,7},{3,5},{1,3},{0,1},{10,8},{12,10},{14... | collective-permute-start | bytes 2359304 | tf_op jit(solution)/shard_map/ppermute | solution.py:581
  100.0 24.5 %collective-permute-start.10 = (bf16[2,512,384]{2,1,0:T(8,128)(2,1)S(1)}, bf16[2,512,384]{2,1,0:T(8,128)(2,1)S(1)}, u32[]{:S(2)}, u32[]{:S(2)}) collective-permute-start(bf16[2,512,384]{2,1,0:T(8,128)(2,1)S(1)} %get-tuple-element.232), channel_id=1, source_target_pairs={{0,2},{2,4},{4,6},{6,7},{7,5},{5,3},{3,1},{1,0},{8,10},{10,12},{12... | collective-permute-start | bytes 2359304 | tf_op jit(solution)/shard_map/ppermute | solution.py:581
  101.4 24.4 %collective-permute-start.11 = (bf16[2,512,384]{2,1,0:T(8,128)(2,1)S(1)}, bf16[2,512,384]{2,1,0:T(8,128)(2,1)S(1)}, u32[]{:S(2)}, u32[]{:S(2)}) collective-permute-start(bf16[2,512,384]{2,1,0:T(8,128)(2,1)S(1)} %get-tuple-element.233), channel_id=1, source_target_pairs={{2,0},{4,2},{6,4},{7,6},{5,7},{3,5},{1,3},{0,1},{10,8},{12,10},{14... | collective-permute-start | bytes 2359304 | tf_op jit(solution)/shard_map/ppermute | solution.py:581
  116.7 24.6 %collective-permute-start.24 = (bf16[2,512,384]{2,1,0:T(8,128)(2,1)S(1)}, bf16[2,512,384]{2,1,0:T(8,128)(2,1)S(1)}, u32[]{:S(2)}, u32[]{:S(2)}) collective-permute-start(bf16[2,512,384]{2,1,0:T(8,128)(2,1)S(1)} %get-tuple-element.257), channel_id=1, source_target_pairs={{0,2},{2,4},{4,6},{6,7},{7,5},{5,3},{3,1},{1,0},{8,10},{10,12},{12... | collective-permute-start | bytes 2359304 | tf_op jit(solution)/shard_map/ppermute | solution.py:581
  118.1 24.5 %collective-permute-start.25 = (bf16[2,512,384]{2,1,0:T(8,128)(2,1)S(1)}, bf16[2,512,384]{2,1,0:T(8,128)(2,1)S(1)}, u32[]{:S(2)}, u32[]{:S(2)}) collective-permute-start(bf16[2,512,384]{2,1,0:T(8,128)(2,1)S(1)} %get-tuple-element.258), channel_id=1, source_target_pairs={{2,0},{4,2},{6,4},{7,6},{5,7},{3,5},{1,3},{0,1},{10,8},{12,10},{14... | collective-permute-start | bytes 2359304 | tf_op jit(solution)/shard_map/ppermute | solution.py:581
  133.8 24.4 %collective-permute-start.12 = (bf16[2,512,384]{2,1,0:T(8,128)(2,1)S(1)}, bf16[2,512,384]{2,1,0:T(8,128)(2,1)S(1)}, u32[]{:S(2)}, u32[]{:S(2)}) collective-permute-start(bf16[2,512,384]{2,1,0:T(8,128)(2,1)S(1)} %get-tuple-element.238), channel_id=1, source_target_pairs={{0,2},{2,4},{4,6},{6,7},{7,5},{5,3},{3,1},{1,0},{8,10},{10,12},{12... | collective-permute-start | bytes 2359304 | tf_op jit(solution)/shard_map/ppermute | solution.py:581
  135.2 24.4 %collective-permute-start.13 = (bf16[2,512,384]{2,1,0:T(8,128)(2,1)S(1)}, bf16[2,512,384]{2,1,0:T(8,128)(2,1)S(1)}, u32[]{:S(2)}, u32[]{:S(2)}) collective-permute-start(bf16[2,512,384]{2,1,0:T(8,128)(2,1)S(1)} %get-tuple-element.239), channel_id=1, source_target_pairs={{2,0},{4,2},{6,4},{7,6},{5,7},{3,5},{1,3},{0,1},{10,8},{12,10},{14... | collective-permute-start | bytes 2359304 | tf_op jit(solution)/shard_map/ppermute | solution.py:581
  150.3 24.7 %collective-permute-start.26 = (bf16[2,512,384]{2,1,0:T(8,128)(2,1)S(1)}, bf16[2,512,384]{2,1,0:T(8,128)(2,1)S(1)}, u32[]{:S(2)}, u32[]{:S(2)}) collective-permute-start(bf16[2,512,384]{2,1,0:T(8,128)(2,1)S(1)} %get-tuple-element.260), channel_id=1, source_target_pairs={{0,2},{2,4},{4,6},{6,7},{7,5},{5,3},{3,1},{1,0},{8,10},{10,12},{12... | collective-permute-start | bytes 2359304 | tf_op jit(solution)/shard_map/ppermute | solution.py:581
  151.8 24.5 %collective-permute-start.27 = (bf16[2,512,384]{2,1,0:T(8,128)(2,1)S(1)}, bf16[2,512,384]{2,1,0:T(8,128)(2,1)S(1)}, u32[]{:S(2)}, u32[]{:S(2)}) collective-permute-start(bf16[2,512,384]{2,1,0:T(8,128)(2,1)S(1)} %get-tuple-element.261), channel_id=1, source_target_pairs={{2,0},{4,2},{6,4},{7,6},{5,7},{3,5},{1,3},{0,1},{10,8},{12,10},{14... | collective-permute-start | bytes 2359304 | tf_op jit(solution)/shard_map/ppermute | solution.py:581
  167.2 24.6 %collective-permute-start.14 = (bf16[2,512,384]{2,1,0:T(8,128)(2,1)S(1)}, bf16[2,512,384]{2,1,0:T(8,128)(2,1)S(1)}, u32[]{:S(2)}, u32[]{:S(2)}) collective-permute-start(bf16[2,512,384]{2,1,0:T(8,128)(2,1)S(1)} %get-tuple-element.241), channel_id=1, source_target_pairs={{0,2},{2,4},{4,6},{6,7},{7,5},{5,3},{3,1},{1,0},{8,10},{10,12},{12... | collective-permute-start | bytes 2359304 | tf_op jit(solution)/shard_map/ppermute | solution.py:581
  168.8 24.5 %collective-permute-start.15 = (bf16[2,512,384]{2,1,0:T(8,128)(2,1)S(1)}, bf16[2,512,384]{2,1,0:T(8,128)(2,1)S(1)}, u32[]{:S(2)}, u32[]{:S(2)}) collective-permute-start(bf16[2,512,384]{2,1,0:T(8,128)(2,1)S(1)} %get-tuple-element.242), channel_id=1, source_target_pairs={{2,0},{4,2},{6,4},{7,6},{5,7},{3,5},{1,3},{0,1},{10,8},{12,10},{14... | collective-permute-start | bytes 2359304 | tf_op jit(solution)/shard_map/ppermute | solution.py:581
  184.0 24.8 %collective-permute-start.28 = (bf16[2,512,384]{2,1,0:T(8,128)(2,1)S(1)}, bf16[2,512,384]{2,1,0:T(8,128)(2,1)S(1)}, u32[]{:S(2)}, u32[]{:S(2)}) collective-permute-start(bf16[2,512,384]{2,1,0:T(8,128)(2,1)S(1)} %get-tuple-element.263), channel_id=1, source_target_pairs={{0,2},{2,4},{4,6},{6,7},{7,5},{5,3},{3,1},{1,0},{8,10},{10,12},{12... | collective-permute-start | bytes 2359304 | tf_op jit(solution)/shard_map/ppermute | solution.py:581
  185.7 24.4 %collective-permute-start.29 = (bf16[2,512,384]{2,1,0:T(8,128)(2,1)S(1)}, bf16[2,512,384]{2,1,0:T(8,128)(2,1)S(1)}, u32[]{:S(2)}, u32[]{:S(2)}) collective-permute-start(bf16[2,512,384]{2,1,0:T(8,128)(2,1)S(1)} %get-tuple-element.264), channel_id=1, source_target_pairs={{2,0},{4,2},{6,4},{7,6},{5,7},{3,5},{1,3},{0,1},{10,8},{12,10},{14... | collective-permute-start | bytes 2359304 | tf_op jit(solution)/shard_map/ppermute | solution.py:581
  201.3 24.3 %collective-permute-start.16 = (bf16[2,512,384]{2,1,0:T(8,128)(2,1)S(1)}, bf16[2,512,384]{2,1,0:T(8,128)(2,1)S(1)}, u32[]{:S(2)}, u32[]{:S(2)}) collective-permute-start(bf16[2,512,384]{2,1,0:T(8,128)(2,1)S(1)} %get-tuple-element.244), channel_id=1, source_target_pairs={{0,2},{2,4},{4,6},{6,7},{7,5},{5,3},{3,1},{1,0},{8,10},{10,12},{12... | collective-permute-start | bytes 2359304 | tf_op jit(solution)/shard_map/ppermute | solution.py:581
  202.5 24.4 %collective-permute-start.17 = (bf16[2,512,384]{2,1,0:T(8,128)(2,1)S(1)}, bf16[2,512,384]{2,1,0:T(8,128)(2,1)S(1)}, u32[]{:S(2)}, u32[]{:S(2)}) collective-permute-start(bf16[2,512,384]{2,1,0:T(8,128)(2,1)S(1)} %get-tuple-element.245), channel_id=1, source_target_pairs={{2,0},{4,2},{6,4},{7,6},{5,7},{3,5},{1,3},{0,1},{10,8},{12,10},{14... | collective-permute-start | bytes 2359304 | tf_op jit(solution)/shard_map/ppermute | solution.py:581
  218.2 24.2 %collective-permute-start.30 = (bf16[2,512,384]{2,1,0:T(8,128)(2,1)S(1)}, bf16[2,512,384]{2,1,0:T(8,128)(2,1)S(1)}, u32[]{:S(2)}, u32[]{:S(2)}) collective-permute-start(bf16[2,512,384]{2,1,0:T(8,128)(2,1)S(1)} %get-tuple-element.266), channel_id=1, source_target_pairs={{0,2},{2,4},{4,6},{6,7},{7,5},{5,3},{3,1},{1,0},{8,10},{10,12},{12... | collective-permute-start | bytes 2359304 | tf_op jit(solution)/shard_map/ppermute | solution.py:581
  219.4 24.4 %collective-permute-start.31 = (bf16[2,512,384]{2,1,0:T(8,128)(2,1)S(1)}, bf16[2,512,384]{2,1,0:T(8,128)(2,1)S(1)}, u32[]{:S(2)}, u32[]{:S(2)}) collective-permute-start(bf16[2,512,384]{2,1,0:T(8,128)(2,1)S(1)} %get-tuple-element.267), channel_id=1, source_target_pairs={{2,0},{4,2},{6,4},{7,6},{5,7},{3,5},{1,3},{0,1},{10,8},{12,10},{14... | collective-permute-start | bytes 2359304 | tf_op jit(solution)/shard_map/ppermute | solution.py:581
  234.5 24.8 %collective-permute-start.18 = (bf16[2,512,384]{2,1,0:T(8,128)(2,1)S(1)}, bf16[2,512,384]{2,1,0:T(8,128)(2,1)S(1)}, u32[]{:S(2)}, u32[]{:S(2)}) collective-permute-start(bf16[2,512,384]{2,1,0:T(8,128)(2,1)S(1)} %get-tuple-element.247), channel_id=1, source_target_pairs={{0,2},{2,4},{4,6},{6,7},{7,5},{5,3},{3,1},{1,0},{8,10},{10,12},{12... | collective-permute-start | bytes 2359304 | tf_op jit(solution)/shard_map/ppermute | solution.py:581
  236.1 24.5 %collective-permute-start.19 = (bf16[2,512,384]{2,1,0:T(8,128)(2,1)S(1)}, bf16[2,512,384]{2,1,0:T(8,128)(2,1)S(1)}, u32[]{:S(2)}, u32[]{:S(2)}) collective-permute-start(bf16[2,512,384]{2,1,0:T(8,128)(2,1)S(1)} %get-tuple-element.248), channel_id=1, source_target_pairs={{2,0},{4,2},{6,4},{7,6},{5,7},{3,5},{1,3},{0,1},{10,8},{12,10},{14... | collective-permute-start | bytes 2359304 | tf_op jit(solution)/shard_map/ppermute | solution.py:581
  251.8 24.4 %collective-permute-start.32 = (bf16[2,512,384]{2,1,0:T(8,128)(2,1)S(1)}, bf16[2,512,384]{2,1,0:T(8,128)(2,1)S(1)}, u32[]{:S(2)}, u32[]{:S(2)}) collective-permute-start(bf16[2,512,384]{2,1,0:T(8,128)(2,1)S(1)} %get-tuple-element.269), channel_id=1, source_target_pairs={{0,2},{2,4},{4,6},{6,7},{7,5},{5,3},{3,1},{1,0},{8,10},{10,12},{12... | collective-permute-start | bytes 2359304 | tf_op jit(solution)/shard_map/ppermute | solution.py:581
  252.9 24.6 %collective-permute-start.33 = (bf16[2,512,384]{2,1,0:T(8,128)(2,1)S(1)}, bf16[2,512,384]{2,1,0:T(8,128)(2,1)S(1)}, u32[]{:S(2)}, u32[]{:S(2)}) collective-permute-start(bf16[2,512,384]{2,1,0:T(8,128)(2,1)S(1)} %get-tuple-element.270), channel_id=1, source_target_pairs={{2,0},{4,2},{6,4},{7,6},{5,7},{3,5},{1,3},{0,1},{10,8},{12,10},{14... | collective-permute-start | bytes 2359304 | tf_op jit(solution)/shard_map/ppermute | solution.py:581
  269.6 44.2 %collective-permute-start.34 = (bf16[2,512,384]{2,1,0:T(8,128)(2,1)S(1)}, bf16[2,512,384]{2,1,0:T(8,128)(2,1)S(1)}, u32[]{:S(2)}, u32[]{:S(2)}) collective-permute-start(bf16[2,512,384]{2,1,0:T(8,128)(2,1)S(1)} %get-tuple-element.273.refs_4_), channel_id=1, source_target_pairs={{0,2},{2,4},{4,6},{6,7},{7,5},{5,3},{3,1},{1,0},{8,10},{10,12},{12... | collective-permute-start | bytes 2359304 | tf_op jit(solution)/shard_map/ppermute | solution.py:581
  271.2 42.6 %collective-permute-start.35 = (bf16[2,512,384]{2,1,0:T(8,128)(2,1)S(1)}, bf16[2,512,384]{2,1,0:T(8,128)(2,1)S(1)}, u32[]{:S(2)}, u32[]{:S(2)}) collective-permute-start(bf16[2,512,384]{2,1,0:T(8,128)(2,1)S(1)} %get-tuple-element.274.refs_5_), channel_id=1, source_target_pairs={{2,0},{4,2},{6,4},{7,6},{5,7},{3,5},{1,3},{0,1},{10,8},{12,10},{14... | collective-permute-start | bytes 2359304 | tf_op jit(solution)/shard_map/ppermute | solution.py:581
  286.4 42.3 %collective-permute-start.38 = (bf16[2,512,384]{2,1,0:T(8,128)(2,1)S(1)}, bf16[2,512,384]{2,1,0:T(8,128)(2,1)S(1)}, u32[]{:S(2)}, u32[]{:S(2)}) collective-permute-start(bf16[2,512,384]{2,1,0:T(8,128)(2,1)S(1)} %get-tuple-element.276.refs_4_), channel_id=1, source_target_pairs={{0,2},{2,4},{4,6},{6,7},{7,5},{5,3},{3,1},{1,0},{8,10},{10,12},{12... | collective-permute-start | bytes 2359304 | tf_op jit(solution)/shard_map/ppermute | solution.py:581
  287.5 41.1 %collective-permute-start.39 = (bf16[2,512,384]{2,1,0:T(8,128)(2,1)S(1)}, bf16[2,512,384]{2,1,0:T(8,128)(2,1)S(1)}, u32[]{:S(2)}, u32[]{:S(2)}) collective-permute-start(bf16[2,512,384]{2,1,0:T(8,128)(2,1)S(1)} %get-tuple-element.277.refs_5_), channel_id=1, source_target_pairs={{2,0},{4,2},{6,4},{7,6},{5,7},{3,5},{1,3},{0,1},{10,8},{12,10},{14... | collective-permute-start | bytes 2359304 | tf_op jit(solution)/shard_map/ppermute | solution.py:581
  313.8 29.7 %collective-permute-start.36 = (bf16[2,512,384]{2,1,0:T(8,128)(2,1)S(1)}, bf16[2,512,384]{2,1,0:T(8,128)(2,1)S(1)}, u32[]{:S(2)}, u32[]{:S(2)}) collective-permute-start(bf16[2,512,384]{2,1,0:T(8,128)(2,1)S(1)} %collective-permute-done.34.refs_4_), channel_id=1, source_target_pairs={{0,2},{2,4},{4,6},{6,7},{7,5},{5,3},{3,1},{1,0},{8,10},{10,12},{12... | collective-permute-start | bytes 2359304 | tf_op jit(solution)/shard_map/ppermute | solution.py:581
  313.9 29.6 %collective-permute-start.37 = (bf16[2,512,384]{2,1,0:T(8,128)(2,1)S(1)}, bf16[2,512,384]{2,1,0:T(8,128)(2,1)S(1)}, u32[]{:S(2)}, u32[]{:S(2)}) collective-permute-start(bf16[2,512,384]{2,1,0:T(8,128)(2,1)S(1)} %collective-permute-done.35.refs_5_), channel_id=1, source_target_pairs={{2,0},{4,2},{6,4},{7,6},{5,7},{3,5},{1,3},{0,1},{10,8},{12,10},{14... | collective-permute-start | bytes 2359304 | tf_op jit(solution)/shard_map/ppermute | solution.py:581
  328.7 29.6 %collective-permute-start.42 = (bf16[2,512,384]{2,1,0:T(8,128)(2,1)S(1)}, bf16[2,512,384]{2,1,0:T(8,128)(2,1)S(1)}, u32[]{:S(2)}, u32[]{:S(2)}) collective-permute-start(bf16[2,512,384]{2,1,0:T(8,128)(2,1)S(1)} %collective-permute-done.38.refs_4_), channel_id=1, source_target_pairs={{0,2},{2,4},{4,6},{6,7},{7,5},{5,3},{3,1},{1,0},{8,10},{10,12},{12... | collective-permute-start | bytes 2359304 | tf_op jit(solution)/shard_map/ppermute | solution.py:581
  328.8 29.5 %collective-permute-start.43 = (bf16[2,512,384]{2,1,0:T(8,128)(2,1)S(1)}, bf16[2,512,384]{2,1,0:T(8,128)(2,1)S(1)}, u32[]{:S(2)}, u32[]{:S(2)}) collective-permute-start(bf16[2,512,384]{2,1,0:T(8,128)(2,1)S(1)} %collective-permute-done.39.refs_5_), channel_id=1, source_target_pairs={{2,0},{4,2},{6,4},{7,6},{5,7},{3,5},{1,3},{0,1},{10,8},{12,10},{14... | collective-permute-start | bytes 2359304 | tf_op jit(solution)/shard_map/ppermute | solution.py:581
  343.5 29.6 %collective-permute-start.40 = (bf16[2,512,384]{2,1,0:T(8,128)(2,1)S(1)}, bf16[2,512,384]{2,1,0:T(8,128)(2,1)S(1)}, u32[]{:S(2)}, u32[]{:S(2)}) collective-permute-start(bf16[2,512,384]{2,1,0:T(8,128)(2,1)S(1)} %collective-permute-done.36.refs_4_), channel_id=1, source_target_pairs={{0,2},{2,4},{4,6},{6,7},{7,5},{5,3},{3,1},{1,0},{8,10},{10,12},{12... | collective-permute-start | bytes 2359304 | tf_op jit(solution)/shard_map/ppermute | solution.py:581
  343.6 29.6 %collective-permute-start.41 = (bf16[2,512,384]{2,1,0:T(8,128)(2,1)S(1)}, bf16[2,512,384]{2,1,0:T(8,128)(2,1)S(1)}, u32[]{:S(2)}, u32[]{:S(2)}) collective-permute-start(bf16[2,512,384]{2,1,0:T(8,128)(2,1)S(1)} %collective-permute-done.37.refs_5_), channel_id=1, source_target_pairs={{2,0},{4,2},{6,4},{7,6},{5,7},{3,5},{1,3},{0,1},{10,8},{12,10},{14... | collective-permute-start | bytes 2359304 | tf_op jit(solution)/shard_map/ppermute | solution.py:581
  358.3 29.7 %collective-permute-start.46 = (bf16[2,512,384]{2,1,0:T(8,128)(2,1)S(1)}, bf16[2,512,384]{2,1,0:T(8,128)(2,1)S(1)}, u32[]{:S(2)}, u32[]{:S(2)}) collective-permute-start(bf16[2,512,384]{2,1,0:T(8,128)(2,1)S(1)} %collective-permute-done.42.refs_4_), channel_id=1, source_target_pairs={{0,2},{2,4},{4,6},{6,7},{7,5},{5,3},{3,1},{1,0},{8,10},{10,12},{12... | collective-permute-start | bytes 2359304 | tf_op jit(solution)/shard_map/ppermute | solution.py:581
  358.4 29.6 %collective-permute-start.47 = (bf16[2,512,384]{2,1,0:T(8,128)(2,1)S(1)}, bf16[2,512,384]{2,1,0:T(8,128)(2,1)S(1)}, u32[]{:S(2)}, u32[]{:S(2)}) collective-permute-start(bf16[2,512,384]{2,1,0:T(8,128)(2,1)S(1)} %collective-permute-done.43.refs_5_), channel_id=1, source_target_pairs={{2,0},{4,2},{6,4},{7,6},{5,7},{3,5},{1,3},{0,1},{10,8},{12,10},{14... | collective-permute-start | bytes 2359304 | tf_op jit(solution)/shard_map/ppermute | solution.py:581
  373.1 29.7 %collective-permute-start.44 = (bf16[2,512,384]{2,1,0:T(8,128)(2,1)S(1)}, bf16[2,512,384]{2,1,0:T(8,128)(2,1)S(1)}, u32[]{:S(2)}, u32[]{:S(2)}) collective-permute-start(bf16[2,512,384]{2,1,0:T(8,128)(2,1)S(1)} %collective-permute-done.40.refs_4_), channel_id=1, source_target_pairs={{0,2},{2,4},{4,6},{6,7},{7,5},{5,3},{3,1},{1,0},{8,10},{10,12},{12... | collective-permute-start | bytes 2359304 | tf_op jit(solution)/shard_map/ppermute | solution.py:581
  373.2 29.7 %collective-permute-start.45 = (bf16[2,512,384]{2,1,0:T(8,128)(2,1)S(1)}, bf16[2,512,384]{2,1,0:T(8,128)(2,1)S(1)}, u32[]{:S(2)}, u32[]{:S(2)}) collective-permute-start(bf16[2,512,384]{2,1,0:T(8,128)(2,1)S(1)} %collective-permute-done.41.refs_5_), channel_id=1, source_target_pairs={{2,0},{4,2},{6,4},{7,6},{5,7},{3,5},{1,3},{0,1},{10,8},{12,10},{14... | collective-permute-start | bytes 2359304 | tf_op jit(solution)/shard_map/ppermute | solution.py:581
  388.0 29.7 %collective-permute-start.50 = (bf16[2,512,384]{2,1,0:T(8,128)(2,1)S(1)}, bf16[2,512,384]{2,1,0:T(8,128)(2,1)S(1)}, u32[]{:S(2)}, u32[]{:S(2)}) collective-permute-start(bf16[2,512,384]{2,1,0:T(8,128)(2,1)S(1)} %collective-permute-done.46.refs_4_), channel_id=1, source_target_pairs={{0,2},{2,4},{4,6},{6,7},{7,5},{5,3},{3,1},{1,0},{8,10},{10,12},{12... | collective-permute-start | bytes 2359304 | tf_op jit(solution)/shard_map/ppermute | solution.py:581
  388.1 30.9 %collective-permute-start.51 = (bf16[2,512,384]{2,1,0:T(8,128)(2,1)S(1)}, bf16[2,512,384]{2,1,0:T(8,128)(2,1)S(1)}, u32[]{:S(2)}, u32[]{:S(2)}) collective-permute-start(bf16[2,512,384]{2,1,0:T(8,128)(2,1)S(1)} %collective-permute-done.47.refs_5_), channel_id=1, source_target_pairs={{2,0},{4,2},{6,4},{7,6},{5,7},{3,5},{1,3},{0,1},{10,8},{12,10},{14... | collective-permute-start | bytes 2359304 | tf_op jit(solution)/shard_map/ppermute | solution.py:581
  402.9 30.9 %collective-permute-start.48 = (bf16[2,512,384]{2,1,0:T(8,128)(2,1)S(1)}, bf16[2,512,384]{2,1,0:T(8,128)(2,1)S(1)}, u32[]{:S(2)}, u32[]{:S(2)}) collective-permute-start(bf16[2,512,384]{2,1,0:T(8,128)(2,1)S(1)} %collective-permute-done.44.refs_4_), channel_id=1, source_target_pairs={{0,2},{2,4},{4,6},{6,7},{7,5},{5,3},{3,1},{1,0},{8,10},{10,12},{12... | collective-permute-start | bytes 2359304 | tf_op jit(solution)/shard_map/ppermute | solution.py:581
  403.0 32.8 %collective-permute-start.49 = (bf16[2,512,384]{2,1,0:T(8,128)(2,1)S(1)}, bf16[2,512,384]{2,1,0:T(8,128)(2,1)S(1)}, u32[]{:S(2)}, u32[]{:S(2)}) collective-permute-start(bf16[2,512,384]{2,1,0:T(8,128)(2,1)S(1)} %collective-permute-done.45.refs_5_), channel_id=1, source_target_pairs={{2,0},{4,2},{6,4},{7,6},{5,7},{3,5},{1,3},{0,1},{10,8},{12,10},{14... | collective-permute-start | bytes 2359304 | tf_op jit(solution)/shard_map/ppermute | solution.py:581
  418.9 31.6 %collective-permute-start.54 = (bf16[2,512,384]{2,1,0:T(8,128)(2,1)S(1)}, bf16[2,512,384]{2,1,0:T(8,128)(2,1)S(1)}, u32[]{:S(2)}, u32[]{:S(2)}) collective-permute-start(bf16[2,512,384]{2,1,0:T(8,128)(2,1)S(1)} %collective-permute-done.50.refs_4_), channel_id=1, source_target_pairs={{0,2},{2,4},{4,6},{6,7},{7,5},{5,3},{3,1},{1,0},{8,10},{10,12},{12... | collective-permute-start | bytes 2359304 | tf_op jit(solution)/shard_map/ppermute | solution.py:581
  419.8 32.9 %collective-permute-start.55 = (bf16[2,512,384]{2,1,0:T(8,128)(2,1)S(1)}, bf16[2,512,384]{2,1,0:T(8,128)(2,1)S(1)}, u32[]{:S(2)}, u32[]{:S(2)}) collective-permute-start(bf16[2,512,384]{2,1,0:T(8,128)(2,1)S(1)} %collective-permute-done.51.refs_5_), channel_id=1, source_target_pairs={{2,0},{4,2},{6,4},{7,6},{5,7},{3,5},{1,3},{0,1},{10,8},{12,10},{14... | collective-permute-start | bytes 2359304 | tf_op jit(solution)/shard_map/ppermute | solution.py:581
  435.8 31.5 %collective-permute-start.52 = (bf16[2,512,384]{2,1,0:T(8,128)(2,1)S(1)}, bf16[2,512,384]{2,1,0:T(8,128)(2,1)S(1)}, u32[]{:S(2)}, u32[]{:S(2)}) collective-permute-start(bf16[2,512,384]{2,1,0:T(8,128)(2,1)S(1)} %collective-permute-done.48.refs_4_), channel_id=1, source_target_pairs={{0,2},{2,4},{4,6},{6,7},{7,5},{5,3},{3,1},{1,0},{8,10},{10,12},{12... | collective-permute-start | bytes 2359304 | tf_op jit(solution)/shard_map/ppermute | solution.py:581
  436.6 32.9 %collective-permute-start.53 = (bf16[2,512,384]{2,1,0:T(8,128)(2,1)S(1)}, bf16[2,512,384]{2,1,0:T(8,128)(2,1)S(1)}, u32[]{:S(2)}, u32[]{:S(2)}) collective-permute-start(bf16[2,512,384]{2,1,0:T(8,128)(2,1)S(1)} %collective-permute-done.49.refs_5_), channel_id=1, source_target_pairs={{2,0},{4,2},{6,4},{7,6},{5,7},{3,5},{1,3},{0,1},{10,8},{12,10},{14... | collective-permute-start | bytes 2359304 | tf_op jit(solution)/shard_map/ppermute | solution.py:581
  452.7 31.9 %collective-permute-start.58 = (bf16[2,512,384]{2,1,0:T(8,128)(2,1)S(1)}, bf16[2,512,384]{2,1,0:T(8,128)(2,1)S(1)}, u32[]{:S(2)}, u32[]{:S(2)}) collective-permute-start(bf16[2,512,384]{2,1,0:T(8,128)(2,1)S(1)} %collective-permute-done.54.refs_4_), channel_id=1, source_target_pairs={{0,2},{2,4},{4,6},{6,7},{7,5},{5,3},{3,1},{1,0},{8,10},{10,12},{12... | collective-permute-start | bytes 2359304 | tf_op jit(solution)/shard_map/ppermute | solution.py:581
  453.5 32.9 %collective-permute-start.59 = (bf16[2,512,384]{2,1,0:T(8,128)(2,1)S(1)}, bf16[2,512,384]{2,1,0:T(8,128)(2,1)S(1)}, u32[]{:S(2)}, u32[]{:S(2)}) collective-permute-start(bf16[2,512,384]{2,1,0:T(8,128)(2,1)S(1)} %collective-permute-done.55.refs_5_), channel_id=1, source_target_pairs={{2,0},{4,2},{6,4},{7,6},{5,7},{3,5},{1,3},{0,1},{10,8},{12,10},{14... | collective-permute-start | bytes 2359304 | tf_op jit(solution)/shard_map/ppermute | solution.py:581
  469.5 32.0 %collective-permute-start.56 = (bf16[2,512,384]{2,1,0:T(8,128)(2,1)S(1)}, bf16[2,512,384]{2,1,0:T(8,128)(2,1)S(1)}, u32[]{:S(2)}, u32[]{:S(2)}) collective-permute-start(bf16[2,512,384]{2,1,0:T(8,128)(2,1)S(1)} %collective-permute-done.52.refs_4_), channel_id=1, source_target_pairs={{0,2},{2,4},{4,6},{6,7},{7,5},{5,3},{3,1},{1,0},{8,10},{10,12},{12... | collective-permute-start | bytes 2359304 | tf_op jit(solution)/shard_map/ppermute | solution.py:581
  470.3 32.9 %collective-permute-start.57 = (bf16[2,512,384]{2,1,0:T(8,128)(2,1)S(1)}, bf16[2,512,384]{2,1,0:T(8,128)(2,1)S(1)}, u32[]{:S(2)}, u32[]{:S(2)}) collective-permute-start(bf16[2,512,384]{2,1,0:T(8,128)(2,1)S(1)} %collective-permute-done.53.refs_5_), channel_id=1, source_target_pairs={{2,0},{4,2},{6,4},{7,6},{5,7},{3,5},{1,3},{0,1},{10,8},{12,10},{14... | collective-permute-start | bytes 2359304 | tf_op jit(solution)/shard_map/ppermute | solution.py:581
  486.4 29.3 %collective-permute-start.60 = (bf16[2,512,384]{2,1,0:T(8,128)(2,1)S(1)}, bf16[2,512,384]{2,1,0:T(8,128)(2,1)S(1)}, u32[]{:S(2)}, u32[]{:S(2)}) collective-permute-start(bf16[2,512,384]{2,1,0:T(8,128)(2,1)S(1)} %collective-permute-done.58.refs_4_), channel_id=1, source_target_pairs={{0,2},{2,4},{4,6},{6,7},{7,5},{5,3},{3,1},{1,0},{8,10},{10,12},{12... | collective-permute-start | bytes 2359304 | tf_op jit(solution)/shard_map/ppermute | solution.py:581
  487.2 30.7 %collective-permute-start.61 = (bf16[2,512,384]{2,1,0:T(8,128)(2,1)S(1)}, bf16[2,512,384]{2,1,0:T(8,128)(2,1)S(1)}, u32[]{:S(2)}, u32[]{:S(2)}) collective-permute-start(bf16[2,512,384]{2,1,0:T(8,128)(2,1)S(1)} %collective-permute-done.59.refs_5_), channel_id=1, source_target_pairs={{2,0},{4,2},{6,4},{7,6},{5,7},{3,5},{1,3},{0,1},{10,8},{12,10},{14... | collective-permute-start | bytes 2359304 | tf_op jit(solution)/shard_map/ppermute | solution.py:581
  527.0 11.2 %collective-permute-start.63 = (bf16[128,1536]{1,0:T(8,128)(2,1)S(1)}, bf16[128,1536]{1,0:T(8,128)(2,1)S(1)}, u32[]{:S(2)}, u32[]{:S(2)}) collective-permute-start(bf16[128,1536]{1,0:T(8,128)(2,1)S(1)} %slice.25), channel_id=1, source_target_pairs={{16,0},{24,8},{0,16},{8,24},{17,1},{25,9},{1,17},{9,25},{18,2},{26... | collective-permute-start | bytes 1179656 | tf_op jit(solution)/shard_map/ppermute | solution.py:516
  534.4 4.7 collective-permute-start.64
  539.3 14.7 %collective-permute-start.65 = (bf16[128,1536]{1,0:T(8,128)(2,1)S(1)}, bf16[128,1536]{1,0:T(8,128)(2,1)S(1)}, u32[]{:S(2)}, u32[]{:S(2)}) collective-permute-start(bf16[128,1536]{1,0:T(8,128)(2,1)S(1)} %slice.24), channel_id=1, source_target_pairs={{16,0},{24,8},{0,16},{8,24},{17,1},{25,9},{1,17},{9,25},{18,2},{26... | collective-permute-start | bytes 1179656 | tf_op jit(solution)/shard_map/ppermute | solution.py:516
  (14 other events, 65.9 us)

commit v4 on v3

--- a/solution.py
+++ b/solution.py
@@ -129,12 +129,12 @@
     lax.fori_loop(0, columns // wide, step, 0)
 
 
-def row_loop(rows, body):
+def row_loop(rows, block, body):
     def step(i, carry):
-        body(block_at(i))
+        body(pl.ds(pl.multiple_of(i * block, block), block))
         return carry
 
-    lax.fori_loop(0, rows // BLK, step, 0)
+    lax.fori_loop(0, rows // block, step, 0)
 
 
 def group_slices(plan):
@@ -160,57 +160,56 @@
         ]
 
 
-def up_kernel(plan, n_pieces, has_in, last, *refs):
-    meta, refs = refs[0], refs[1:]
-    if n_pieces:
-        pieces, refs = refs[: 2 * n_pieces], refs[2 * n_pieces :]
-    else:
-        x, dy, refs = refs[0], refs[1], refs[2:]
-    vals1, vals2, refs = refs[0], refs[1], refs[2:]
+def keep_copies(plan, store, which, buf, sems):
+    return [
+        pltpu.make_async_copy(src, dst, sems.at[which, i])
+        for i, (dst, src) in enumerate(Store(plan).views(store, plan.shift - 1, which, buf))
+    ]
+
+
+def run(copies):
+    for copy in copies:
+        copy.start()
+
+
+def settle(copies):
+    for copy in copies:
+        copy.wait()
+
+
+def join_copies(pieces, whole, sems):
+    rows = pieces[0].shape[0]
+    return [
+        pltpu.make_async_copy(piece, whole.at[pl.ds(i * rows, rows), :], sems.at[i]) for i, piece in enumerate(pieces)
+    ]
+
+
+def up_kernel(plan, has_in, last, *refs):
+    meta, x, dy, vals1, vals2 = refs[:5]
+    refs = refs[5:]
     n = len(plan.sizes)
     ins = refs[:n] if has_in else None
     refs = refs[n + 1 :] if has_in else refs
     outs, refs = refs[:n], refs[n:]
-    if n_pieces:
-        x, dy, refs = refs[0], refs[1], refs[2:]
-    store, refs = refs[0], refs[1:]
-    buf1, buf2, sems, hid, grd, tile_sems = refs[:6]
-    keep = [
-        [
-            pltpu.make_async_copy(src, dst, tile_sems.at[which, i])
-            for i, (dst, src) in enumerate(Store(plan).views(store, plan.shift - 1, which, buf))
-        ]
-        for which, buf in enumerate((buf1, buf2))
-    ]
-    joins = []
-    if n_pieces:
-        rows = pieces[0].shape[0]
-        for i in range(2 * n_pieces):
-            dst = (x if i < n_pieces else dy).at[pl.ds(i % n_pieces * rows, rows), :]
-            joins.append(pltpu.make_async_copy(pieces[i], dst, refs[6].at[i]))
-    for join in joins:
-        join.start()
+    store, buf1, buf2, sems, hid, grd, keep_sems = refs
     tile_start(plan, meta, vals1, buf1, sems, 0)
     tile_start(plan, meta, vals2, buf2, sems, 1)
-    for join in joins:
-        join.wait()
-    columns = plan.total * BLK
     tile_wait(plan, meta, vals1, buf1, sems, 0)
-    for copy in keep[0]:
-        copy.start()
+    keep1 = keep_copies(plan, store, 0, buf1, keep_sems)
+    run(keep1)
 
     def hid_tile(at):
         hid[:, at] = dot_nn(x[...], buf1[:, at])
 
-    tile_loop(columns, hid_tile)
+    tile_loop(plan.total * BLK, hid_tile)
     tile_wait(plan, meta, vals2, buf2, sems, 1)
-    for copy in keep[1]:
-        copy.start()
+    keep2 = keep_copies(plan, store, 1, buf2, keep_sems)
+    run(keep2)
 
     def grd_tile(at):
         grd[:, at] = dot_nt(dy[...], buf2[at, :])
 
-    tile_loop(columns, grd_tile)
+    tile_loop(plan.total * BLK, grd_tile)
 
     def join_rows(part):
         for g, at in enumerate(group_slices(plan)):
@@ -223,9 +222,54 @@
             outs[g][0, part, :] = h.astype(jnp.bfloat16)
             outs[g][1, part, :] = d.astype(jnp.bfloat16)
 
-    row_loop(hid.shape[0], join_rows)
-    for copy in keep[0] + keep[1]:
-        copy.wait()
+    row_loop(hid.shape[0], BLK // 4, join_rows)
+    settle(keep1 + keep2)
+
+
+def first_hid_kernel(plan, n_pieces, *refs):
+    meta, pieces, refs = refs[0], refs[1 : 1 + n_pieces], refs[1 + n_pieces :]
+    vals1, x, hid, store, buf1, sems, keep_sems, join_sems = refs
+    joins = join_copies(pieces, x, join_sems)
+    run(joins)
+    tile_start(plan, meta, vals1, buf1, sems, 0)
+    settle(joins)
+    tile_wait(plan, meta, vals1, buf1, sems, 0)
+    keep = keep_copies(plan, store, 0, buf1, keep_sems)
+    run(keep)
+
+    def hid_tile(at):
+        hid[:, at] = dot_nn(x[...], buf1[:, at])
+
+    tile_loop(plan.total * BLK, hid_tile)
+    settle(keep)
+
+
+def first_grd_kernel(plan, n_pieces, *refs):
+    meta, pieces, refs = refs[0], refs[1 : 1 + n_pieces], refs[1 + n_pieces :]
+    vals2, hid, _, refs = refs[0], refs[1], refs[2], refs[3:]
+    n = len(plan.sizes)
+    outs, refs = refs[:n], refs[n:]
+    dy, store, buf2, sems, grd, keep_sems, join_sems = refs
+    joins = join_copies(pieces, dy, join_sems)
+    run(joins)
+    tile_start(plan, meta, vals2, buf2, sems, 1)
+    settle(joins)
+    tile_wait(plan, meta, vals2, buf2, sems, 1)
+    keep = keep_copies(plan, store, 1, buf2, keep_sems)
+    run(keep)
+
+    def grd_tile(at):
+        grd[:, at] = dot_nt(dy[...], buf2[at, :])
+
+    tile_loop(plan.total * BLK, grd_tile)
+
+    def join_rows(part):
+        for g, at in enumerate(group_slices(plan)):
+            outs[g][0, part, :] = hid[part, at].astype(jnp.bfloat16)
+            outs[g][1, part, :] = grd[part, at].astype(jnp.bfloat16)
+
+    row_loop(grd.shape[0], BLK // 4, join_rows)
+    settle(keep)
 
 
 def smem():
@@ -248,42 +292,76 @@
     ]
 
 
+def up_cost(plan, tokens, products):
+    side = plan.width * plan.total * BLK * BLK
+    return pl.CostEstimate(
+        flops=2 * products * tokens * side,
+        bytes_accessed=2 * products * side + 8 * tokens * plan.total * BLK,
+        transcendentals=0,
+    )
+
+
 def up_call(plan, meta, x, dy, vals, ins, store, last):
-    pieces = isinstance(x, list)
-    n_pieces = len(x) if pieces else 0
-    given = (*x, *dy) if pieces else (x, dy)
-    tokens = sum(p.shape[0] for p in x) if pieces else x.shape[0]
+    tokens = x.shape[0]
     n = len(plan.sizes)
     has_in = ins is not None
     total, width = plan.total, plan.width
     shapes = [jax.ShapeDtypeStruct((2, tokens, s * BLK), jnp.bfloat16) for s in plan.sizes]
-    if pieces:
-        shapes += [jax.ShapeDtypeStruct((tokens, width * BLK), jnp.bfloat16)] * 2
-    in_vmem = len(shapes)
     shapes.append(jax.ShapeDtypeStruct(Store(plan).shape, jnp.bfloat16))
-    n_in = 3 + len(given) + n
     res = pl.pallas_call(
-        functools.partial(up_kernel, plan, n_pieces, has_in, last),
+        functools.partial(up_kernel, plan, has_in, last),
         out_shape=shapes,
-        in_specs=[smem()]
-        + [hbm() if pieces else vmem()] * len(given)
-        + [hbm()] * 2
-        + ([vmem()] * n + [hbm()] if has_in else []),
-        out_specs=[vmem()] * in_vmem + [hbm()],
-        input_output_aliases={n_in: in_vmem} if has_in else {},
+        in_specs=[smem()] + [vmem()] * 2 + [hbm()] * 2 + ([vmem()] * n + [hbm()] if has_in else []),
+        out_specs=[vmem()] * n + [hbm()],
+        input_output_aliases={5 + n: n} if has_in else {},
         scratch_shapes=tile_scratch(total, width)
         + [pltpu.VMEM((tokens, total * BLK), jnp.float32)] * 2
-        + [pltpu.SemaphoreType.DMA((2, Store(plan).cuts))]
-        + ([pltpu.SemaphoreType.DMA((2 * n_pieces,))] if pieces else []),
-        compiler_params=pltpu.CompilerParams(vmem_limit_bytes=FIRST_LIMIT if pieces else VMEM_LIMIT),
-        cost_estimate=pl.CostEstimate(
-            flops=4 * tokens * width * total * BLK * BLK,
-            bytes_accessed=4 * width * total * BLK * BLK + 8 * tokens * total * BLK,
-            transcendentals=0,
-        ),
+        + [pltpu.SemaphoreType.DMA((2, Store(plan).cuts))],
+        compiler_params=pltpu.CompilerParams(vmem_limit_bytes=VMEM_LIMIT),
+        cost_estimate=up_cost(plan, tokens, 2),
         name="up_last" if last else "up",
-    )(meta, *given, *vals, *((*ins, store) if has_in else ()))
-    return (res[:n], res[-1], res[n], res[n + 1]) if pieces else (res[:n], res[-1])
+    )(meta, x, dy, *vals, *((*ins, store) if has_in else ()))
+    return res[:n], res[n]
+
+
+def first_call(plan, meta, x, dy, vals, gather_dy):
+    n_pieces = len(x)
+    tokens = sum(p.shape[0] for p in x)
+    n = len(plan.sizes)
+    total, width = plan.total, plan.width
+    buf1, buf2, sems = tile_scratch(total, width)
+    whole = jax.ShapeDtypeStruct((tokens, width * BLK), jnp.bfloat16)
+    store = jax.ShapeDtypeStruct(Store(plan).shape, jnp.bfloat16)
+    more_sems = [
+        pltpu.SemaphoreType.DMA((2, Store(plan).cuts)),
+        pltpu.SemaphoreType.DMA((n_pieces,)),
+    ]
+    params = pltpu.CompilerParams(vmem_limit_bytes=FIRST_LIMIT)
+    whole_x, hid, store = pl.pallas_call(
+        functools.partial(first_hid_kernel, plan, n_pieces),
+        out_shape=[whole, jax.ShapeDtypeStruct((tokens, total * BLK), jnp.float32), store],
+        in_specs=[smem()] + [hbm()] * (n_pieces + 1),
+        out_specs=[vmem(), vmem(), hbm()],
+        scratch_shapes=[buf1, sems] + more_sems,
+        compiler_params=params,
+        cost_estimate=up_cost(plan, tokens, 1),
+        name="first_hid",
+    )(meta, *x, vals[0])
+    late, hid = lax.optimization_barrier((dy[1:], hid))
+    dy = gather_dy(dy[:1] + late)
+    res = pl.pallas_call(
+        functools.partial(first_grd_kernel, plan, n_pieces),
+        out_shape=[jax.ShapeDtypeStruct((2, tokens, s * BLK), jnp.bfloat16) for s in plan.sizes]
+        + [whole, jax.ShapeDtypeStruct(store.shape, store.dtype)],
+        in_specs=[smem()] + [hbm()] * (n_pieces + 1) + [vmem(), hbm()],
+        out_specs=[vmem()] * (n + 1) + [hbm()],
+        input_output_aliases={3 + n_pieces: n + 1},
+        scratch_shapes=[buf2, sems, pltpu.VMEM((tokens, total * BLK), jnp.float32)] + more_sems,
+        compiler_params=params,
+        cost_estimate=up_cost(plan, tokens, 1),
+        name="first_grd",
+    )(meta, *dy, vals[1], hid, store)
+    return res[:n], res[n + 1], whole_x, res[n]
 
 
 DEAD_GROUP = 16
@@ -377,7 +455,7 @@
             if grads:
                 act_t[at, part] = value.T
 
-    row_loop(tokens, split_rows)
+    row_loop(tokens, BLK, split_rows)
 
     def block_of(which, b, r):
         if which == 0:
@@ -515,8 +593,10 @@
                 pairs.append((((x + step) % self.chips) * self.cores + c, x * self.cores + c))
         return lax.ppermute(value, "row", pairs)
 
-    def gather(self, value):
-        near = [value] + [self.shift(value, d) for d in range(1, self.chips)]
+    def near(self, value):
+        return [value] + [self.shift(value, d) for d in range(1, self.chips)]
+
+    def far(self, near):
         return near + ([self.swap(p) for p in near] if self.cores > 1 else [])
 
     def scatter_near(self, keep, send):
@@ -555,8 +635,8 @@
     me = jnp.asarray(place, jnp.int32)[lax.axis_index("col")]
 
     row = Row(lax.axis_size("row"))
-    x = row.gather(inputs)
-    dy = row.gather(out_grad)
+    x = row.near(inputs)
+    dy = row.near(out_grad)
     width = inputs.shape[1] // BLK
     per = hidden_blocks // n
     vals = (first_vals[0, 0], second_vals[0, 0])
@@ -564,6 +644,8 @@
     starts1, order1 = slot_order(first_cols[0, 0], first_rows[0, 0], first_count[0, 0], hidden_blocks)
     starts2, order2 = slot_order(second_rows[0, 0], second_cols[0, 0], second_count[0, 0], hidden_blocks)
     meta = jnp.concatenate([me[None], starts1, starts2, order1, order2])
+    late, meta = lax.optimization_barrier((x[1:], meta))
+    x = row.far(x[:1] + late)
 
     n_ahead = (per + 1) // 2
     parts = []
@@ -592,10 +674,11 @@
             if t in (2, 3) and s == 0:
                 grads.append(dead_call(t - 2, plan_of(stream, 0), meta, vals[t - 2]))
                 ins, grads = lax.optimization_barrier((ins, grads))
-            res = up_call(plan_of(stream, t + 1), meta, x, dy, vals, ins, stores[s], t == n - 1)
-            if isinstance(x, list):
-                x, dy = res[2:]
-            held[s], stores[s] = res[:2]
+            plan = plan_of(stream, t + 1)
+            if t == 0 and s == 0:
+                held[s], stores[s], x, dy = first_call(plan, meta, x, dy, vals, row.far)
+            else:
+                held[s], stores[s] = up_call(plan, meta, x, dy, vals, ins, stores[s], t == n - 1)
 
     sums = None
     for t in range(n):
@@ -603,13 +686,12 @@
             if t > 0:
                 held[s] = hop(stream, held[s])
                 held[s], sums, grads = lax.optimization_barrier((held[s], sums, grads))
-            if t < n - 1:
+            if t < n - 1 or s < len(streams) - 1:
                 res = back_call(plan_of(stream, t), meta, x_t, dy, [stores[s]], held[s], sums, grads)
                 sums, grads = res[:2], res[2:]
 
-    parts = [plan_of(stream, n - 1) for stream in streams]
-    plan, acts = plan_of(sum(streams, []), n - 1, parts), sum(held, [])
-    args = (plan, meta, x_t, dy, stores)
+    acts = held[-1]
+    args = (plan_of(streams[-1], n - 1), meta, x_t, dy, stores[-1:])
     out_near = row.scatter_near(*back_call(*args, acts, sums, None, down=(0,), with_grads=False, last=True))
     out_near, acts = lax.optimization_barrier((out_near, acts))
     in_near = row.scatter_near(*back_call(*args, acts, sums, None, down=(1,), with_grads=False, last=True))

time: 566 us -> 560 us (0.989)
  waiting for transfers between devices: 133 us -> 123 us
  starting transfers between devices: 62.9 us -> 70.7 us
    ppermute x4, starting transfers between devices: 4.52 us -> 10.8 us  [shift(): return lax.ppermute(value, 'row', pairs)]
    ppermute x56, waiting for transfers between devices: 113 us -> 107 us  [hop(): lax.ppermute(a, 'col', ahead if sign > 0 else back)]
    pallas_call x17 -> x18, Pallas kernels: 206 us -> 200 us  [back_call(): pl.pallas_call(functools.partial(back_kernel, plan, down, with_grads, fir...]
    pallas_call x16 -> x17, Pallas kernels: 132 us -> 131 us  [the longest x15 116 us: up_call(): pl.pallas_call(functools.partial(up_kernel, plan, has_in, last), out_shap...]
  transfers between devices with their start and end apart: 66 -> 66, of which waited for: 40 -> 47; matrix products, arithmetic and copies ran while one was open for 1% -> 1% of each run, Pallas kernels for 59% -> 58%
where the time goes in v4:
time: 560 us; the launch traced here: 550 us
  Pallas kernels  338 us (60%)
  waiting for transfers between devices  123 us (22%)
  starting transfers between devices  70.7 us (13%)
  local copies, waits for them, and re-layouts  10.2 us (2%)
    pallas_call x18, Pallas kernels, back_call(): pl.pallas_call(functools.partial(back_kernel, plan, down, with_grads, fir...  200 us
    pallas_call x15, Pallas kernels, up_call(): pl.pallas_call(functools.partial(up_kernel, plan, has_in, last), out_shap...  116 us
    ppermute x56, waiting for transfers between devices, hop(): lax.ppermute(a, 'col', ahead if sign > 0 else back)  107 us
    ppermute x56, starting transfers between devices, hop(): lax.ppermute(a, 'col', ahead if sign > 0 else back)  59.4 us
    ppermute x4, waiting for transfers between devices, shift(): return lax.ppermute(value, 'row', pairs)  12.6 us
  transfers between devices with their start and end apart: 66, of which 47 were waited for; matrix products, arithmetic and copies ran while one was open for 1% of the time, Pallas kernels for 58%

profile of v4, /device:TPU:0, one launch (start us, length us, event | category | flops | bytes accessed | tf_op | source)
XLA Modules:
  0.0 549.7 jit_solution(18286623790706484929)
XLA Ops:
  0.6 3.0 collective-permute-start
  10.0 3.0 collective-permute-done.refs_2_
  15.8 6.8 %first_hid.1 = (bf16[512,1536]{1,0:T(8,128)(2,1)}, f32[512,768]{1,0:T(8,128)}, bf16[8,3072,768]{2,1,0:T(8,128)(2,1)}) custom-call(s32[1219]{0:T(1024)} %concatenate.3.refs_0_.meta, bf16[128,1536]{1,0:T(8,128)(2,1)} %refs_1_.2, bf16[128,1536]{1,0:T(8,128)(2,1)} %copy-done.9, bf16[128,1536]{1,0:T(8,128)(2,1)} %copy-done.10, bf16[128,1536]{1,0:T(8,128)(2,1)} %copy-done.11, ...), custom_call_target="tpu_custom_call" | custom-call | flops 1207959552 | bytes 5505024 | tf_op jit(solution)/shard_map/first_hid/pallas_call | solution.py:340
  22.7 2.0 collective-permute-done.3.refs_2_
  27.2 8.2 %first_grd.1 = (bf16[2,512,384]{2,1,0:T(8,128)(2,1)}, bf16[2,512,384]{2,1,0:T(8,128)(2,1)}, bf16[512,1536]{1,0:T(8,128)(2,1)}, bf16[8,3072,768]{2,1,0:T(8,128)(2,1)}) custom-call(s32[1219]{0:T(1024)} %concatenate.3.refs_0_.meta, bf16[128,1536]{1,0:T(8,128)(2,1)} %refs_1_.3, bf16[128,1536]{1,0:T(8,128)(2,1)} %copy-done.6, ...), custom_call_target="tpu_custom_call", output_to_operand_aliasing={{3}: (7, {})} | custom-call | flops 1207959552 | bytes 5505024 | tf_op jit(solution)/shard_map/first_grd/pallas_call | solution.py:352
  40.3 8.3 %up.13 = (bf16[2,512,384]{2,1,0:T(8,128)(2,1)}, bf16[2,512,384]{2,1,0:T(8,128)(2,1)}, bf16[8,3072,768]{2,1,0:T(8,128)(2,1)}) custom-call(s32[1219]{0:T(1024)S(1)} %copy-done.5, bf16[512,1536]{1,0:T(8,128)(2,1)S(1)} %copy-done.2, bf16[512,1536]{1,0:T(8,128)(2,1)S(1)} %copy-done, bf16[512,128,128]{2,1,0:T(8,128)(2,1)} %bitcast.30, bf16[512,128,128]{2,1,0:T(8,128)(2,1)} %bitcast.46), custom_call_target="tpu_custom_call" | custom-call | flops 2415919104 | bytes 7864320 | tf_op jit(solution)/shard_map/up/pallas_call | solution.py:311
  52.4 3.7 collective-permute-done.22.refs_5_
  59.2 8.1 %up.20 = (bf16[2,512,384]{2,1,0:T(8,128)(2,1)S(1)}, bf16[2,512,384]{2,1,0:T(8,128)(2,1)S(1)}, bf16[8,3072,768]{2,1,0:T(8,128)(2,1)}) custom-call(s32[1219]{0:T(1024)S(1)} %copy-done.5, bf16[512,1536]{1,0:T(8,128)(2,1)S(1)} %copy-done.3, bf16[512,1536]{1,0:T(8,128)(2,1)S(1)} %copy-done.1, ...), custom_call_target="tpu_custom_call", output_to_operand_aliasing={{2}: (7, {})} | custom-call | flops 2415919104 | bytes 7864320 | tf_op jit(solution)/shard_map/up/pallas_call | solution.py:311
  69.5 3.5 collective-permute-done.6.refs_5_
  74.7 8.3 %up.14 = (bf16[2,512,384]{2,1,0:T(8,128)(2,1)S(1)}, bf16[2,512,384]{2,1,0:T(8,128)(2,1)S(1)}, bf16[8,3072,768]{2,1,0:T(8,128)(2,1)}) custom-call(s32[1219]{0:T(1024)S(1)} %copy-done.5, bf16[512,1536]{1,0:T(8,128)(2,1)S(1)} %copy-done.3, bf16[512,1536]{1,0:T(8,128)(2,1)S(1)} %copy-done.1, ...), custom_call_target="tpu_custom_call", output_to_operand_aliasing={{2}: (7, {})} | custom-call | flops 2415919104 | bytes 7864320 | tf_op jit(solution)/shard_map/up/pallas_call | solution.py:311
  85.0 6.0 %dead.2.refs_6_ = bf16[512,128,128]{2,1,0:T(8,128)(2,1)} custom-call(s32[1219]{0:T(1024)S(1)} %copy-done.5), custom_call_target="tpu_custom_call" | custom-call | bytes 8388608 | tf_op jit(solution)/shard_map/dead/pallas_call | solution.py:398
  91.4 7.4 %up.21 = (bf16[2,512,384]{2,1,0:T(8,128)(2,1)S(1)}, bf16[2,512,384]{2,1,0:T(8,128)(2,1)S(1)}, bf16[8,3072,768]{2,1,0:T(8,128)(2,1)}) custom-call(s32[1219]{0:T(1024)S(1)} %copy-done.5, bf16[512,1536]{1,0:T(8,128)(2,1)S(1)} %copy-done.4, bf16[512,1536]{1,0:T(8,128)(2,1)S(1)} %copy-done.1, ...), custom_call_target="tpu_custom_call", output_to_operand_aliasing={{2}: (7, {})} | custom-call | flops 2415919104 | bytes 7864320 | tf_op jit(solution)/shard_map/up/pallas_call | solution.py:311
  101.0 5.6 %collective-permute-done.8.refs_5_ = bf16[2,512,384]{2,1,0:T(8,128)(2,1)S(1)} collective-permute-done((bf16[2,512,384]{2,1,0:T(8,128)(2,1)S(1)}, bf16[2,512,384]{2,1,0:T(8,128)(2,1)S(1)}, u32[]{:S(2)}, u32[]{:S(2)}) %collective-permute-start.8) | collective-permute-done | bytes 786464 | tf_op jit(solution)/shard_map/ppermute | solution.py:663
  108.3 7.4 %up.15 = (bf16[2,512,384]{2,1,0:T(8,128)(2,1)S(1)}, bf16[2,512,384]{2,1,0:T(8,128)(2,1)S(1)}, bf16[8,3072,768]{2,1,0:T(8,128)(2,1)}) custom-call(s32[1219]{0:T(1024)S(1)} %copy-done.5, bf16[512,1536]{1,0:T(8,128)(2,1)S(1)} %copy-done.4, bf16[512,1536]{1,0:T(8,128)(2,1)S(1)} %copy-done.1, ...), custom_call_target="tpu_custom_call", output_to_operand_aliasing={{2}: (7, {})} | custom-call | flops 2415919104 | bytes 7864320 | tf_op jit(solution)/shard_map/up/pallas_call | solution.py:311
  118.9 4.5 collective-permute-done.26.refs_5_
  125.1 7.8 %up.22 = (bf16[2,512,384]{2,1,0:T(8,128)(2,1)S(1)}, bf16[2,512,384]{2,1,0:T(8,128)(2,1)S(1)}, bf16[8,3072,768]{2,1,0:T(8,128)(2,1)}) custom-call(s32[1219]{0:T(1024)S(1)} %copy-done.5, bf16[512,1536]{1,0:T(8,128)(2,1)S(1)} %copy-done.4, bf16[512,1536]{1,0:T(8,128)(2,1)S(1)} %copy-done.1, ...), custom_call_target="tpu_custom_call", output_to_operand_aliasing={{2}: (7, {})} | custom-call | flops 2415919104 | bytes 7864320 | tf_op jit(solution)/shard_map/up/pallas_call | solution.py:311
  135.1 5.2 collective-permute-done.10.refs_5_
  142.0 7.5 %up.16 = (bf16[2,512,384]{2,1,0:T(8,128)(2,1)S(1)}, bf16[2,512,384]{2,1,0:T(8,128)(2,1)S(1)}, bf16[8,3072,768]{2,1,0:T(8,128)(2,1)}) custom-call(s32[1219]{0:T(1024)S(1)} %copy-done.5, bf16[512,1536]{1,0:T(8,128)(2,1)S(1)} %copy-done.4, bf16[512,1536]{1,0:T(8,128)(2,1)S(1)} %copy-done.1, ...), custom_call_target="tpu_custom_call", output_to_operand_aliasing={{2}: (7, {})} | custom-call | flops 2415919104 | bytes 7864320 | tf_op jit(solution)/shard_map/up/pallas_call | solution.py:311
  151.6 5.5 %collective-permute-done.28.refs_5_ = bf16[2,512,384]{2,1,0:T(8,128)(2,1)S(1)} collective-permute-done((bf16[2,512,384]{2,1,0:T(8,128)(2,1)S(1)}, bf16[2,512,384]{2,1,0:T(8,128)(2,1)S(1)}, u32[]{:S(2)}, u32[]{:S(2)}) %collective-permute-start.28) | collective-permute-done | bytes 786464 | tf_op jit(solution)/shard_map/ppermute | solution.py:663
  158.8 7.4 %up.23 = (bf16[2,512,384]{2,1,0:T(8,128)(2,1)S(1)}, bf16[2,512,384]{2,1,0:T(8,128)(2,1)S(1)}, bf16[8,3072,768]{2,1,0:T(8,128)(2,1)}) custom-call(s32[1219]{0:T(1024)S(1)} %copy-done.5, bf16[512,1536]{1,0:T(8,128)(2,1)S(1)} %copy-done.4, bf16[512,1536]{1,0:T(8,128)(2,1)S(1)} %copy-done.1, ...), custom_call_target="tpu_custom_call", output_to_operand_aliasing={{2}: (7, {})} | custom-call | flops 2415919104 | bytes 7864320 | tf_op jit(solution)/shard_map/up/pallas_call | solution.py:311
  168.3 5.7 %collective-permute-done.12.refs_5_ = bf16[2,512,384]{2,1,0:T(8,128)(2,1)S(1)} collective-permute-done((bf16[2,512,384]{2,1,0:T(8,128)(2,1)S(1)}, bf16[2,512,384]{2,1,0:T(8,128)(2,1)S(1)}, u32[]{:S(2)}, u32[]{:S(2)}) %collective-permute-start.12) | collective-permute-done | bytes 786464 | tf_op jit(solution)/shard_map/ppermute | solution.py:663
  175.7 7.4 %up.17 = (bf16[2,512,384]{2,1,0:T(8,128)(2,1)S(1)}, bf16[2,512,384]{2,1,0:T(8,128)(2,1)S(1)}, bf16[8,3072,768]{2,1,0:T(8,128)(2,1)}) custom-call(s32[1219]{0:T(1024)S(1)} %copy-done.5, bf16[512,1536]{1,0:T(8,128)(2,1)S(1)} %copy-done.4, bf16[512,1536]{1,0:T(8,128)(2,1)S(1)} %copy-done.1, ...), custom_call_target="tpu_custom_call", output_to_operand_aliasing={{2}: (7, {})} | custom-call | flops 2415919104 | bytes 7864320 | tf_op jit(solution)/shard_map/up/pallas_call | solution.py:311
  185.2 5.7 %collective-permute-done.30.refs_5_ = bf16[2,512,384]{2,1,0:T(8,128)(2,1)S(1)} collective-permute-done((bf16[2,512,384]{2,1,0:T(8,128)(2,1)S(1)}, bf16[2,512,384]{2,1,0:T(8,128)(2,1)S(1)}, u32[]{:S(2)}, u32[]{:S(2)}) %collective-permute-start.30) | collective-permute-done | bytes 786464 | tf_op jit(solution)/shard_map/ppermute | solution.py:663
  192.5 7.4 %up.24 = (bf16[2,512,384]{2,1,0:T(8,128)(2,1)S(1)}, bf16[2,512,384]{2,1,0:T(8,128)(2,1)S(1)}, bf16[8,3072,768]{2,1,0:T(8,128)(2,1)}) custom-call(s32[1219]{0:T(1024)S(1)} %copy-done.5, bf16[512,1536]{1,0:T(8,128)(2,1)S(1)} %copy-done.4, bf16[512,1536]{1,0:T(8,128)(2,1)S(1)} %copy-done.1, ...), custom_call_target="tpu_custom_call", output_to_operand_aliasing={{2}: (7, {})} | custom-call | flops 2415919104 | bytes 7864320 | tf_op jit(solution)/shard_map/up/pallas_call | solution.py:311
  202.0 5.7 %collective-permute-done.14.refs_5_ = bf16[2,512,384]{2,1,0:T(8,128)(2,1)S(1)} collective-permute-done((bf16[2,512,384]{2,1,0:T(8,128)(2,1)S(1)}, bf16[2,512,384]{2,1,0:T(8,128)(2,1)S(1)}, u32[]{:S(2)}, u32[]{:S(2)}) %collective-permute-start.14) | collective-permute-done | bytes 786464 | tf_op jit(solution)/shard_map/ppermute | solution.py:663
  209.4 7.3 %up.18 = (bf16[2,512,384]{2,1,0:T(8,128)(2,1)S(1)}, bf16[2,512,384]{2,1,0:T(8,128)(2,1)S(1)}, bf16[8,3072,768]{2,1,0:T(8,128)(2,1)}) custom-call(s32[1219]{0:T(1024)S(1)} %copy-done.5, bf16[512,1536]{1,0:T(8,128)(2,1)S(1)} %copy-done.4, bf16[512,1536]{1,0:T(8,128)(2,1)S(1)} %copy-done.1, ...), custom_call_target="tpu_custom_call", output_to_operand_aliasing={{2}: (7, {})} | custom-call | flops 2415919104 | bytes 7864320 | tf_op jit(solution)/shard_map/up/pallas_call | solution.py:311
  218.8 5.8 %collective-permute-done.32.refs_5_ = bf16[2,512,384]{2,1,0:T(8,128)(2,1)S(1)} collective-permute-done((bf16[2,512,384]{2,1,0:T(8,128)(2,1)S(1)}, bf16[2,512,384]{2,1,0:T(8,128)(2,1)S(1)}, u32[]{:S(2)}, u32[]{:S(2)}) %collective-permute-start.32) | collective-permute-done | bytes 786464 | tf_op jit(solution)/shard_map/ppermute | solution.py:663
  226.3 7.4 %up.25 = (bf16[2,512,384]{2,1,0:T(8,128)(2,1)S(1)}, bf16[2,512,384]{2,1,0:T(8,128)(2,1)S(1)}, bf16[8,3072,768]{2,1,0:T(8,128)(2,1)}) custom-call(s32[1219]{0:T(1024)S(1)} %copy-done.5, bf16[512,1536]{1,0:T(8,128)(2,1)S(1)} %copy-done.4, bf16[512,1536]{1,0:T(8,128)(2,1)S(1)} %copy-done.1, ...), custom_call_target="tpu_custom_call", output_to_operand_aliasing={{2}: (7, {})} | custom-call | flops 2415919104 | bytes 7864320 | tf_op jit(solution)/shard_map/up/pallas_call | solution.py:311
  235.7 5.7 %collective-permute-done.16.refs_5_ = bf16[2,512,384]{2,1,0:T(8,128)(2,1)S(1)} collective-permute-done((bf16[2,512,384]{2,1,0:T(8,128)(2,1)S(1)}, bf16[2,512,384]{2,1,0:T(8,128)(2,1)S(1)}, u32[]{:S(2)}, u32[]{:S(2)}) %collective-permute-start.16) | collective-permute-done | bytes 786464 | tf_op jit(solution)/shard_map/ppermute | solution.py:663
  243.1 7.2 %up.19 = (bf16[2,512,384]{2,1,0:T(8,128)(2,1)S(1)}, bf16[2,512,384]{2,1,0:T(8,128)(2,1)S(1)}, bf16[8,3072,768]{2,1,0:T(8,128)(2,1)}) custom-call(s32[1219]{0:T(1024)S(1)} %copy-done.5, bf16[512,1536]{1,0:T(8,128)(2,1)S(1)} %copy-done.4, bf16[512,1536]{1,0:T(8,128)(2,1)S(1)} %copy-done.1, ...), custom_call_target="tpu_custom_call", output_to_operand_aliasing={{2}: (7, {})} | custom-call | flops 2415919104 | bytes 7864320 | tf_op jit(solution)/shard_map/up/pallas_call | solution.py:311
  252.4 5.8 %collective-permute-done.34.refs_5_ = bf16[2,512,384]{2,1,0:T(8,128)(2,1)S(1)} collective-permute-done((bf16[2,512,384]{2,1,0:T(8,128)(2,1)S(1)}, bf16[2,512,384]{2,1,0:T(8,128)(2,1)S(1)}, u32[]{:S(2)}, u32[]{:S(2)}) %collective-permute-start.34) | collective-permute-done | bytes 786464 | tf_op jit(solution)/shard_map/ppermute | solution.py:663
  260.0 8.3 %up_last.3 = (bf16[2,512,384]{2,1,0:T(8,128)(2,1)S(1)}, bf16[2,512,384]{2,1,0:T(8,128)(2,1)S(1)}, bf16[8,3072,768]{2,1,0:T(8,128)(2,1)}) custom-call(s32[1219]{0:T(1024)S(1)} %copy-done.5, bf16[512,1536]{1,0:T(8,128)(2,1)S(1)} %copy-done.4, bf16[512,1536]{1,0:T(8,128)(2,1)S(1)} %copy-done.1, ...), custom_call_target="tpu_custom_call", output_to_operand_aliasing={{2}: (7, {})} | custom-call | flops 2415919104 | bytes 7864320 | tf_op jit(solution)/shard_map/up_last/pallas_call | solution.py:311
  270.5 4.6 collective-permute-done.18.refs_5_
  276.8 8.4 %up_last.2 = (bf16[2,512,384]{2,1,0:T(8,128)(2,1)S(1)}, bf16[2,512,384]{2,1,0:T(8,128)(2,1)S(1)}, bf16[8,3072,768]{2,1,0:T(8,128)(2,1)}) custom-call(s32[1219]{0:T(1024)S(1)} %copy-done.5, bf16[512,1536]{1,0:T(8,128)(2,1)S(1)} %copy-done.4, bf16[512,1536]{1,0:T(8,128)(2,1)S(1)} %copy-done.1, ...), custom_call_target="tpu_custom_call", output_to_operand_aliasing={{2}: (7, {})} | custom-call | flops 2415919104 | bytes 7864320 | tf_op jit(solution)/shard_map/up_last/pallas_call | solution.py:311
  287.3 12.0 %back.18 = (f32[512,1536]{1,0:T(8,128)S(1)}, f32[512,1536]{1,0:T(8,128)S(1)}, bf16[512,128,128]{2,1,0:T(8,128)(2,1)}, bf16[512,128,128]{2,1,0:T(8,128)(2,1)}) custom-call(s32[1219]{0:T(1024)S(1)} %copy-done.5, bf16[1536,512]{1,0:T(8,128)(2,1)S(1)} %bitcast.11, bf16[512,1536]{1,0:T(8,128)(2,1)S(1)} %copy-done.1, ...), custom_call_target="tpu_custom_call", output_to_operand_aliasing={{2}: (6, {}), {3}: (7, {})} | custom-call | flops 4831838208 | bytes 4718592 | tf_op jit(solution)/shard_map/back/pallas_call | solution.py:562
  299.3 12.3 %back.19 = (f32[512,1536]{1,0:T(8,128)S(1)}, f32[512,1536]{1,0:T(8,128)S(1)}, bf16[512,128,128]{2,1,0:T(8,128)(2,1)}, bf16[512,128,128]{2,1,0:T(8,128)(2,1)}) custom-call(s32[1219]{0:T(1024)S(1)} %copy-done.5, bf16[1536,512]{1,0:T(8,128)(2,1)S(1)} %bitcast.12, ...), custom_call_target="tpu_custom_call", output_to_operand_aliasing={{0}: (6, {}), {1}: (7, {}), {2}: (8, {}), {3}: (9, {})} | custom-call | flops 4831838208 | bytes 4718592 | tf_op jit(solution)/shard_map/back/pallas_call | solution.py:562
  313.6 12.2 %back.20 = (f32[512,1536]{1,0:T(8,128)S(1)}, f32[512,1536]{1,0:T(8,128)S(1)}, bf16[512,128,128]{2,1,0:T(8,128)(2,1)}, bf16[512,128,128]{2,1,0:T(8,128)(2,1)}) custom-call(s32[1219]{0:T(1024)S(1)} %copy-done.5, bf16[1536,512]{1,0:T(8,128)(2,1)S(1)} %bitcast.13, ...), custom_call_target="tpu_custom_call", output_to_operand_aliasing={{0}: (6, {}), {1}: (7, {}), {2}: (8, {}), {3}: (9, {})} | custom-call | flops 4831838208 | bytes 4718592 | tf_op jit(solution)/shard_map/back/pallas_call | solution.py:562
  327.9 12.2 %back.21 = (f32[512,1536]{1,0:T(8,128)S(1)}, f32[512,1536]{1,0:T(8,128)S(1)}, bf16[512,128,128]{2,1,0:T(8,128)(2,1)}, bf16[512,128,128]{2,1,0:T(8,128)(2,1)}) custom-call(s32[1219]{0:T(1024)S(1)} %copy-done.5, bf16[1536,512]{1,0:T(8,128)(2,1)S(1)} %bitcast.14, ...), custom_call_target="tpu_custom_call", output_to_operand_aliasing={{0}: (6, {}), {1}: (7, {}), {2}: (8, {}), {3}: (9, {})} | custom-call | flops 4831838208 | bytes 4718592 | tf_op jit(solution)/shard_map/back/pallas_call | solution.py:562
  340.1 2.7 collective-permute-start.44
  342.8 12.2 %back.22 = (f32[512,1536]{1,0:T(8,128)S(1)}, f32[512,1536]{1,0:T(8,128)S(1)}, bf16[512,128,128]{2,1,0:T(8,128)(2,1)}, bf16[512,128,128]{2,1,0:T(8,128)(2,1)}) custom-call(s32[1219]{0:T(1024)S(1)} %copy-done.5, bf16[1536,512]{1,0:T(8,128)(2,1)S(1)} %bitcast.15, ...), custom_call_target="tpu_custom_call", output_to_operand_aliasing={{0}: (6, {}), {1}: (7, {}), {2}: (8, {}), {3}: (9, {})} | custom-call | flops 4831838208 | bytes 4718592 | tf_op jit(solution)/shard_map/back/pallas_call | solution.py:562
  355.1 2.2 collective-permute-start.42
  357.5 12.4 %back.23 = (f32[512,1536]{1,0:T(8,128)S(1)}, f32[512,1536]{1,0:T(8,128)S(1)}, bf16[512,128,128]{2,1,0:T(8,128)(2,1)}, bf16[512,128,128]{2,1,0:T(8,128)(2,1)}) custom-call(s32[1219]{0:T(1024)S(1)} %copy-done.5, bf16[1536,512]{1,0:T(8,128)(2,1)S(1)} %bitcast.16, ...), custom_call_target="tpu_custom_call", output_to_operand_aliasing={{0}: (6, {}), {1}: (7, {}), {2}: (8, {}), {3}: (9, {})} | custom-call | flops 4831838208 | bytes 4718592 | tf_op jit(solution)/shard_map/back/pallas_call | solution.py:562
  369.9 2.2 collective-permute-start.48
  372.1 12.3 %back.24 = (f32[512,1536]{1,0:T(8,128)S(1)}, f32[512,1536]{1,0:T(8,128)S(1)}, bf16[512,128,128]{2,1,0:T(8,128)(2,1)}, bf16[512,128,128]{2,1,0:T(8,128)(2,1)}) custom-call(s32[1219]{0:T(1024)S(1)} %copy-done.5, bf16[1536,512]{1,0:T(8,128)(2,1)S(1)} %bitcast.17, ...), custom_call_target="tpu_custom_call", output_to_operand_aliasing={{0}: (6, {}), {1}: (7, {}), {2}: (8, {}), {3}: (9, {})} | custom-call | flops 4831838208 | bytes 4718592 | tf_op jit(solution)/shard_map/back/pallas_call | solution.py:562
  384.5 2.4 collective-permute-start.46
  386.9 12.3 %back.25 = (f32[512,1536]{1,0:T(8,128)S(1)}, f32[512,1536]{1,0:T(8,128)S(1)}, bf16[512,128,128]{2,1,0:T(8,128)(2,1)}, bf16[512,128,128]{2,1,0:T(8,128)(2,1)}) custom-call(s32[1219]{0:T(1024)S(1)} %copy-done.5, bf16[1536,512]{1,0:T(8,128)(2,1)S(1)} %bitcast.18, ...), custom_call_target="tpu_custom_call", output_to_operand_aliasing={{0}: (6, {}), {1}: (7, {}), {2}: (8, {}), {3}: (9, {})} | custom-call | flops 4831838208 | bytes 4718592 | tf_op jit(solution)/shard_map/back/pallas_call | solution.py:562
  399.7 2.0 collective-permute-start.52
  401.8 12.2 %back.26 = (f32[512,1536]{1,0:T(8,128)S(1)}, f32[512,1536]{1,0:T(8,128)S(1)}, bf16[512,128,128]{2,1,0:T(8,128)(2,1)}, bf16[512,128,128]{2,1,0:T(8,128)(2,1)}) custom-call(s32[1219]{0:T(1024)S(1)} %copy-done.5, bf16[1536,512]{1,0:T(8,128)(2,1)S(1)} %bitcast.19, ...), custom_call_target="tpu_custom_call", output_to_operand_aliasing={{0}: (6, {}), {1}: (7, {}), {2}: (8, {}), {3}: (9, {})} | custom-call | flops 4831838208 | bytes 4718592 | tf_op jit(solution)/shard_map/back/pallas_call | solution.py:562
  418.6 12.4 %back.27 = (f32[512,1536]{1,0:T(8,128)S(1)}, f32[512,1536]{1,0:T(8,128)S(1)}, bf16[512,128,128]{2,1,0:T(8,128)(2,1)}, bf16[512,128,128]{2,1,0:T(8,128)(2,1)}) custom-call(s32[1219]{0:T(1024)S(1)} %copy-done.5, bf16[1536,512]{1,0:T(8,128)(2,1)S(1)} %bitcast.20, ...), custom_call_target="tpu_custom_call", output_to_operand_aliasing={{0}: (6, {}), {1}: (7, {}), {2}: (8, {}), {3}: (9, {})} | custom-call | flops 4831838208 | bytes 4718592 | tf_op jit(solution)/shard_map/back/pallas_call | solution.py:562
  433.4 2.0 collective-permute-start.56
  435.4 12.5 %back.28 = (f32[512,1536]{1,0:T(8,128)S(1)}, f32[512,1536]{1,0:T(8,128)S(1)}, bf16[512,128,128]{2,1,0:T(8,128)(2,1)}, bf16[512,128,128]{2,1,0:T(8,128)(2,1)}) custom-call(s32[1219]{0:T(1024)S(1)} %copy-done.5, bf16[1536,512]{1,0:T(8,128)(2,1)S(1)} %bitcast.21, ...), custom_call_target="tpu_custom_call", output_to_operand_aliasing={{0}: (6, {}), {1}: (7, {}), {2}: (8, {}), {3}: (9, {})} | custom-call | flops 4831838208 | bytes 4718592 | tf_op jit(solution)/shard_map/back/pallas_call | solution.py:562
  450.3 2.0 collective-permute-start.54
  452.3 12.3 %back.29 = (f32[512,1536]{1,0:T(8,128)S(1)}, f32[512,1536]{1,0:T(8,128)S(1)}, bf16[512,128,128]{2,1,0:T(8,128)(2,1)}, bf16[512,128,128]{2,1,0:T(8,128)(2,1)}) custom-call(s32[1219]{0:T(1024)S(1)} %copy-done.5, bf16[1536,512]{1,0:T(8,128)(2,1)S(1)} %bitcast.22, ...), custom_call_target="tpu_custom_call", output_to_operand_aliasing={{0}: (6, {}), {1}: (7, {}), {2}: (8, {}), {3}: (9, {})} | custom-call | flops 4831838208 | bytes 4718592 | tf_op jit(solution)/shard_map/back/pallas_call | solution.py:562
  467.1 2.0 collective-permute-start.60
  469.2 12.2 %back.30 = (f32[512,1536]{1,0:T(8,128)S(1)}, f32[512,1536]{1,0:T(8,128)S(1)}, bf16[512,128,128]{2,1,0:T(8,128)(2,1)}, bf16[512,128,128]{2,1,0:T(8,128)(2,1)}) custom-call(s32[1219]{0:T(1024)S(1)} %copy-done.5, bf16[1536,512]{1,0:T(8,128)(2,1)S(1)} %bitcast.23, ...), custom_call_target="tpu_custom_call", output_to_operand_aliasing={{0}: (6, {}), {1}: (7, {}), {2}: (8, {}), {3}: (9, {})} | custom-call | flops 4831838208 | bytes 4718592 | tf_op jit(solution)/shard_map/back/pallas_call | solution.py:562
  486.0 12.1 %back.31 = (f32[512,1536]{1,0:T(8,128)S(1)}, f32[512,1536]{1,0:T(8,128)S(1)}, bf16[512,128,128]{2,1,0:T(8,128)(2,1)}, bf16[512,128,128]{2,1,0:T(8,128)(2,1)}) custom-call(s32[1219]{0:T(1024)S(1)} %copy-done.5, bf16[1536,512]{1,0:T(8,128)(2,1)S(1)} %bitcast.24, ...), custom_call_target="tpu_custom_call", output_to_operand_aliasing={{0}: (6, {}), {1}: (7, {}), {2}: (8, {}), {3}: (9, {})} | custom-call | flops 4831838208 | bytes 4718592 | tf_op jit(solution)/shard_map/back/pallas_call | solution.py:562
  500.8 12.2 %back.32 = (f32[512,1536]{1,0:T(8,128)S(1)}, f32[512,1536]{1,0:T(8,128)S(1)}, bf16[512,128,128]{2,1,0:T(8,128)(2,1)}, bf16[512,128,128]{2,1,0:T(8,128)(2,1)}) custom-call(s32[1219]{0:T(1024)S(1)} %copy-done.5, bf16[1536,512]{1,0:T(8,128)(2,1)S(1)} %bitcast.25, ...), custom_call_target="tpu_custom_call", output_to_operand_aliasing={{0}: (6, {}), {1}: (7, {}), {2}: (8, {}), {3}: (9, {})} | custom-call | flops 4831838208 | bytes 4718592 | tf_op jit(solution)/shard_map/back/pallas_call | solution.py:562
  514.3 4.5 back.33
  518.9 2.3 collective-permute-done.62
  521.4 4.8 back.34
  526.4 4.0 collective-permute-start.63
  530.6 2.1 collective-permute-start.65
  532.7 7.6 %collective-permute-done.63 = bf16[128,1536]{1,0:T(8,128)(2,1)S(1)} collective-permute-done((bf16[128,1536]{1,0:T(8,128)(2,1)S(1)}, bf16[128,1536]{1,0:T(8,128)(2,1)S(1)}, u32[]{:S(2)}, u32[]{:S(2)}) %collective-permute-start.63) | collective-permute-done | bytes 393248 | tf_op jit(solution)/shard_map/ppermute | solution.py:594
  541.1 7.3 %back.35 = (bf16[512,128,128]{2,1,0:T(8,128)(2,1)}, bf16[512,128,128]{2,1,0:T(8,128)(2,1)}) custom-call(s32[1219]{0:T(1024)S(1)} %copy-done.5, bf16[1536,512]{1,0:T(8,128)(2,1)S(1)} %bitcast.26, bf16[512,1536]{1,0:T(8,128)(2,1)S(1)} %copy-done.1, ...), custom_call_target="tpu_custom_call", output_to_operand_aliasing={{0}: (5, {}), {1}: (6, {})} | custom-call | flops 2415919104 | bytes 2359296 | tf_op jit(solution)/shard_map/back/pallas_call | solution.py:562
  (147 shorter events, 101.0 us)
Async XLA Ops:
  0.6 12.3 %collective-permute-start = (bf16[128,1536]{1,0:T(8,128)(2,1)}, bf16[128,1536]{1,0:T(8,128)(2,1)S(1)}, u32[]{:S(2)}, u32[]{:S(2)}) collective-permute-start(bf16[128,1536]{1,0:T(8,128)(2,1)} %refs_1_.2), channel_id=1, source_target_pairs={{16,0},{24,8},{0,16},{8,24},{17,1},{25,9},{1,17},{9,25},{18,2},{26... | collective-permute-start | bytes 1179656 | tf_op jit(solution)/shard_map/ppermute | solution.py:594
  3.6 11.3 %collective-permute-start.1 = (bf16[128,1536]{1,0:T(8,128)(2,1)}, bf16[128,1536]{1,0:T(8,128)(2,1)S(1)}, u32[]{:S(2)}, u32[]{:S(2)}) collective-permute-start(bf16[128,1536]{1,0:T(8,128)(2,1)} %refs_1_.2), channel_id=1, source_target_pairs={{0,8},{8,0},{16,24},{24,16},{1,9},{9,1},{17,25},{25,17},{2,10},{10... | collective-permute-start | bytes 1179656 | tf_op jit(solution)/shard_map/ppermute | solution.py:587
  13.0 11.7 %collective-permute-start.3 = (bf16[128,1536]{1,0:T(8,128)(2,1)}, bf16[128,1536]{1,0:T(8,128)(2,1)S(1)}, u32[]{:S(2)}, u32[]{:S(2)}) collective-permute-start(bf16[128,1536]{1,0:T(8,128)(2,1)} %refs_1_.3), channel_id=1, source_target_pairs={{16,0},{24,8},{0,16},{8,24},{17,1},{25,9},{1,17},{9,25},{18,2},{26... | collective-permute-start | bytes 1179656 | tf_op jit(solution)/shard_map/ppermute | solution.py:594
  14.7 10.0 %collective-permute-start.4 = (bf16[128,1536]{1,0:T(8,128)(2,1)}, bf16[128,1536]{1,0:T(8,128)(2,1)S(1)}, u32[]{:S(2)}, u32[]{:S(2)}) collective-permute-start(bf16[128,1536]{1,0:T(8,128)(2,1)} %refs_1_.3), channel_id=1, source_target_pairs={{0,8},{8,0},{16,24},{24,16},{1,9},{9,1},{17,25},{25,17},{2,10},{10... | collective-permute-start | bytes 1179656 | tf_op jit(solution)/shard_map/ppermute | solution.py:587
  35.4 20.7 %collective-permute-start.22 = (bf16[2,512,384]{2,1,0:T(8,128)(2,1)}, bf16[2,512,384]{2,1,0:T(8,128)(2,1)}, u32[]{:S(2)}, u32[]{:S(2)}) collective-permute-start(bf16[2,512,384]{2,1,0:T(8,128)(2,1)} %get-tuple-element.258), channel_id=1, source_target_pairs={{0,2},{2,4},{4,6},{6,7},{7,5},{5,3},{3,1},{1,0},{8,10},{10,12},{12... | collective-permute-start | bytes 2359304 | tf_op jit(solution)/shard_map/ppermute | solution.py:663
  37.1 20.8 %collective-permute-start.23 = (bf16[2,512,384]{2,1,0:T(8,128)(2,1)}, bf16[2,512,384]{2,1,0:T(8,128)(2,1)}, u32[]{:S(2)}, u32[]{:S(2)}) collective-permute-start(bf16[2,512,384]{2,1,0:T(8,128)(2,1)} %get-tuple-element.259), channel_id=1, source_target_pairs={{2,0},{4,2},{6,4},{7,6},{5,7},{3,5},{1,3},{0,1},{10,8},{12,10},{14... | collective-permute-start | bytes 2359304 | tf_op jit(solution)/shard_map/ppermute | solution.py:663
  48.6 24.4 %collective-permute-start.6 = (bf16[2,512,384]{2,1,0:T(8,128)(2,1)}, bf16[2,512,384]{2,1,0:T(8,128)(2,1)}, u32[]{:S(2)}, u32[]{:S(2)}) collective-permute-start(bf16[2,512,384]{2,1,0:T(8,128)(2,1)} %get-tuple-element.234), channel_id=1, source_target_pairs={{0,2},{2,4},{4,6},{6,7},{7,5},{5,3},{3,1},{1,0},{8,10},{10,12},{12... | collective-permute-start | bytes 2359304 | tf_op jit(solution)/shard_map/ppermute | solution.py:663
  50.3 24.4 %collective-permute-start.7 = (bf16[2,512,384]{2,1,0:T(8,128)(2,1)}, bf16[2,512,384]{2,1,0:T(8,128)(2,1)}, u32[]{:S(2)}, u32[]{:S(2)}) collective-permute-start(bf16[2,512,384]{2,1,0:T(8,128)(2,1)} %get-tuple-element.235), channel_id=1, source_target_pairs={{2,0},{4,2},{6,4},{7,6},{5,7},{3,5},{1,3},{0,1},{10,8},{12,10},{14... | collective-permute-start | bytes 2359304 | tf_op jit(solution)/shard_map/ppermute | solution.py:663
  67.4 23.6 %collective-permute-start.24 = (bf16[2,512,384]{2,1,0:T(8,128)(2,1)S(1)}, bf16[2,512,384]{2,1,0:T(8,128)(2,1)S(1)}, u32[]{:S(2)}, u32[]{:S(2)}) collective-permute-start(bf16[2,512,384]{2,1,0:T(8,128)(2,1)S(1)} %get-tuple-element.264), channel_id=1, source_target_pairs={{0,2},{2,4},{4,6},{6,7},{7,5},{5,3},{3,1},{1,0},{8,10},{10,12},{12... | collective-permute-start | bytes 2359304 | tf_op jit(solution)/shard_map/ppermute | solution.py:663
  68.9 22.5 %collective-permute-start.25 = (bf16[2,512,384]{2,1,0:T(8,128)(2,1)S(1)}, bf16[2,512,384]{2,1,0:T(8,128)(2,1)S(1)}, u32[]{:S(2)}, u32[]{:S(2)}) collective-permute-start(bf16[2,512,384]{2,1,0:T(8,128)(2,1)S(1)} %get-tuple-element.265), channel_id=1, source_target_pairs={{2,0},{4,2},{6,4},{7,6},{5,7},{3,5},{1,3},{0,1},{10,8},{12,10},{14... | collective-permute-start | bytes 2359304 | tf_op jit(solution)/shard_map/ppermute | solution.py:663
  83.0 23.6 %collective-permute-start.8 = (bf16[2,512,384]{2,1,0:T(8,128)(2,1)S(1)}, bf16[2,512,384]{2,1,0:T(8,128)(2,1)S(1)}, u32[]{:S(2)}, u32[]{:S(2)}) collective-permute-start(bf16[2,512,384]{2,1,0:T(8,128)(2,1)S(1)} %get-tuple-element.237), channel_id=1, source_target_pairs={{0,2},{2,4},{4,6},{6,7},{7,5},{5,3},{3,1},{1,0},{8,10},{10,12},{12... | collective-permute-start | bytes 2359304 | tf_op jit(solution)/shard_map/ppermute | solution.py:663
  84.4 23.9 %collective-permute-start.9 = (bf16[2,512,384]{2,1,0:T(8,128)(2,1)S(1)}, bf16[2,512,384]{2,1,0:T(8,128)(2,1)S(1)}, u32[]{:S(2)}, u32[]{:S(2)}) collective-permute-start(bf16[2,512,384]{2,1,0:T(8,128)(2,1)S(1)} %get-tuple-element.238), channel_id=1, source_target_pairs={{2,0},{4,2},{6,4},{7,6},{5,7},{3,5},{1,3},{0,1},{10,8},{12,10},{14... | collective-permute-start | bytes 2359304 | tf_op jit(solution)/shard_map/ppermute | solution.py:663
  98.9 24.6 %collective-permute-start.26 = (bf16[2,512,384]{2,1,0:T(8,128)(2,1)S(1)}, bf16[2,512,384]{2,1,0:T(8,128)(2,1)S(1)}, u32[]{:S(2)}, u32[]{:S(2)}) collective-permute-start(bf16[2,512,384]{2,1,0:T(8,128)(2,1)S(1)} %get-tuple-element.269), channel_id=1, source_target_pairs={{0,2},{2,4},{4,6},{6,7},{7,5},{5,3},{3,1},{1,0},{8,10},{10,12},{12... | collective-permute-start | bytes 2359304 | tf_op jit(solution)/shard_map/ppermute | solution.py:663
  100.3 24.8 %collective-permute-start.27 = (bf16[2,512,384]{2,1,0:T(8,128)(2,1)S(1)}, bf16[2,512,384]{2,1,0:T(8,128)(2,1)S(1)}, u32[]{:S(2)}, u32[]{:S(2)}) collective-permute-start(bf16[2,512,384]{2,1,0:T(8,128)(2,1)S(1)} %get-tuple-element.270), channel_id=1, source_target_pairs={{2,0},{4,2},{6,4},{7,6},{5,7},{3,5},{1,3},{0,1},{10,8},{12,10},{14... | collective-permute-start | bytes 2359304 | tf_op jit(solution)/shard_map/ppermute | solution.py:663
  115.7 24.6 %collective-permute-start.10 = (bf16[2,512,384]{2,1,0:T(8,128)(2,1)S(1)}, bf16[2,512,384]{2,1,0:T(8,128)(2,1)S(1)}, u32[]{:S(2)}, u32[]{:S(2)}) collective-permute-start(bf16[2,512,384]{2,1,0:T(8,128)(2,1)S(1)} %get-tuple-element.240), channel_id=1, source_target_pairs={{0,2},{2,4},{4,6},{6,7},{7,5},{5,3},{3,1},{1,0},{8,10},{10,12},{12... | collective-permute-start | bytes 2359304 | tf_op jit(solution)/shard_map/ppermute | solution.py:663
  117.3 24.7 %collective-permute-start.11 = (bf16[2,512,384]{2,1,0:T(8,128)(2,1)S(1)}, bf16[2,512,384]{2,1,0:T(8,128)(2,1)S(1)}, u32[]{:S(2)}, u32[]{:S(2)}) collective-permute-start(bf16[2,512,384]{2,1,0:T(8,128)(2,1)S(1)} %get-tuple-element.241), channel_id=1, source_target_pairs={{2,0},{4,2},{6,4},{7,6},{5,7},{3,5},{1,3},{0,1},{10,8},{12,10},{14... | collective-permute-start | bytes 2359304 | tf_op jit(solution)/shard_map/ppermute | solution.py:663
  133.0 24.2 %collective-permute-start.28 = (bf16[2,512,384]{2,1,0:T(8,128)(2,1)S(1)}, bf16[2,512,384]{2,1,0:T(8,128)(2,1)S(1)}, u32[]{:S(2)}, u32[]{:S(2)}) collective-permute-start(bf16[2,512,384]{2,1,0:T(8,128)(2,1)S(1)} %get-tuple-element.275), channel_id=1, source_target_pairs={{0,2},{2,4},{4,6},{6,7},{7,5},{5,3},{3,1},{1,0},{8,10},{10,12},{12... | collective-permute-start | bytes 2359304 | tf_op jit(solution)/shard_map/ppermute | solution.py:663
  134.5 24.3 %collective-permute-start.29 = (bf16[2,512,384]{2,1,0:T(8,128)(2,1)S(1)}, bf16[2,512,384]{2,1,0:T(8,128)(2,1)S(1)}, u32[]{:S(2)}, u32[]{:S(2)}) collective-permute-start(bf16[2,512,384]{2,1,0:T(8,128)(2,1)S(1)} %get-tuple-element.276), channel_id=1, source_target_pairs={{2,0},{4,2},{6,4},{7,6},{5,7},{3,5},{1,3},{0,1},{10,8},{12,10},{14... | collective-permute-start | bytes 2359304 | tf_op jit(solution)/shard_map/ppermute | solution.py:663
  149.5 24.5 %collective-permute-start.12 = (bf16[2,512,384]{2,1,0:T(8,128)(2,1)S(1)}, bf16[2,512,384]{2,1,0:T(8,128)(2,1)S(1)}, u32[]{:S(2)}, u32[]{:S(2)}) collective-permute-start(bf16[2,512,384]{2,1,0:T(8,128)(2,1)S(1)} %get-tuple-element.243), channel_id=1, source_target_pairs={{0,2},{2,4},{4,6},{6,7},{7,5},{5,3},{3,1},{1,0},{8,10},{10,12},{12... | collective-permute-start | bytes 2359304 | tf_op jit(solution)/shard_map/ppermute | solution.py:663
  151.1 24.6 %collective-permute-start.13 = (bf16[2,512,384]{2,1,0:T(8,128)(2,1)S(1)}, bf16[2,512,384]{2,1,0:T(8,128)(2,1)S(1)}, u32[]{:S(2)}, u32[]{:S(2)}) collective-permute-start(bf16[2,512,384]{2,1,0:T(8,128)(2,1)S(1)} %get-tuple-element.244), channel_id=1, source_target_pairs={{2,0},{4,2},{6,4},{7,6},{5,7},{3,5},{1,3},{0,1},{10,8},{12,10},{14... | collective-permute-start | bytes 2359304 | tf_op jit(solution)/shard_map/ppermute | solution.py:663
  166.2 24.6 %collective-permute-start.30 = (bf16[2,512,384]{2,1,0:T(8,128)(2,1)S(1)}, bf16[2,512,384]{2,1,0:T(8,128)(2,1)S(1)}, u32[]{:S(2)}, u32[]{:S(2)}) collective-permute-start(bf16[2,512,384]{2,1,0:T(8,128)(2,1)S(1)} %get-tuple-element.278), channel_id=1, source_target_pairs={{0,2},{2,4},{4,6},{6,7},{7,5},{5,3},{3,1},{1,0},{8,10},{10,12},{12... | collective-permute-start | bytes 2359304 | tf_op jit(solution)/shard_map/ppermute | solution.py:663
  167.8 24.8 %collective-permute-start.31 = (bf16[2,512,384]{2,1,0:T(8,128)(2,1)S(1)}, bf16[2,512,384]{2,1,0:T(8,128)(2,1)S(1)}, u32[]{:S(2)}, u32[]{:S(2)}) collective-permute-start(bf16[2,512,384]{2,1,0:T(8,128)(2,1)S(1)} %get-tuple-element.279), channel_id=1, source_target_pairs={{2,0},{4,2},{6,4},{7,6},{5,7},{3,5},{1,3},{0,1},{10,8},{12,10},{14... | collective-permute-start | bytes 2359304 | tf_op jit(solution)/shard_map/ppermute | solution.py:663
  183.1 24.6 %collective-permute-start.14 = (bf16[2,512,384]{2,1,0:T(8,128)(2,1)S(1)}, bf16[2,512,384]{2,1,0:T(8,128)(2,1)S(1)}, u32[]{:S(2)}, u32[]{:S(2)}) collective-permute-start(bf16[2,512,384]{2,1,0:T(8,128)(2,1)S(1)} %get-tuple-element.246), channel_id=1, source_target_pairs={{0,2},{2,4},{4,6},{6,7},{7,5},{5,3},{3,1},{1,0},{8,10},{10,12},{12... | collective-permute-start | bytes 2359304 | tf_op jit(solution)/shard_map/ppermute | solution.py:663
  184.7 24.7 %collective-permute-start.15 = (bf16[2,512,384]{2,1,0:T(8,128)(2,1)S(1)}, bf16[2,512,384]{2,1,0:T(8,128)(2,1)S(1)}, u32[]{:S(2)}, u32[]{:S(2)}) collective-permute-start(bf16[2,512,384]{2,1,0:T(8,128)(2,1)S(1)} %get-tuple-element.247), channel_id=1, source_target_pairs={{2,0},{4,2},{6,4},{7,6},{5,7},{3,5},{1,3},{0,1},{10,8},{12,10},{14... | collective-permute-start | bytes 2359304 | tf_op jit(solution)/shard_map/ppermute | solution.py:663
  199.9 24.7 %collective-permute-start.32 = (bf16[2,512,384]{2,1,0:T(8,128)(2,1)S(1)}, bf16[2,512,384]{2,1,0:T(8,128)(2,1)S(1)}, u32[]{:S(2)}, u32[]{:S(2)}) collective-permute-start(bf16[2,512,384]{2,1,0:T(8,128)(2,1)S(1)} %get-tuple-element.281), channel_id=1, source_target_pairs={{0,2},{2,4},{4,6},{6,7},{7,5},{5,3},{3,1},{1,0},{8,10},{10,12},{12... | collective-permute-start | bytes 2359304 | tf_op jit(solution)/shard_map/ppermute | solution.py:663
  201.5 24.8 %collective-permute-start.33 = (bf16[2,512,384]{2,1,0:T(8,128)(2,1)S(1)}, bf16[2,512,384]{2,1,0:T(8,128)(2,1)S(1)}, u32[]{:S(2)}, u32[]{:S(2)}) collective-permute-start(bf16[2,512,384]{2,1,0:T(8,128)(2,1)S(1)} %get-tuple-element.282), channel_id=1, source_target_pairs={{2,0},{4,2},{6,4},{7,6},{5,7},{3,5},{1,3},{0,1},{10,8},{12,10},{14... | collective-permute-start | bytes 2359304 | tf_op jit(solution)/shard_map/ppermute | solution.py:663
  216.7 24.7 %collective-permute-start.16 = (bf16[2,512,384]{2,1,0:T(8,128)(2,1)S(1)}, bf16[2,512,384]{2,1,0:T(8,128)(2,1)S(1)}, u32[]{:S(2)}, u32[]{:S(2)}) collective-permute-start(bf16[2,512,384]{2,1,0:T(8,128)(2,1)S(1)} %get-tuple-element.249), channel_id=1, source_target_pairs={{0,2},{2,4},{4,6},{6,7},{7,5},{5,3},{3,1},{1,0},{8,10},{10,12},{12... | collective-permute-start | bytes 2359304 | tf_op jit(solution)/shard_map/ppermute | solution.py:663
  218.3 24.8 %collective-permute-start.17 = (bf16[2,512,384]{2,1,0:T(8,128)(2,1)S(1)}, bf16[2,512,384]{2,1,0:T(8,128)(2,1)S(1)}, u32[]{:S(2)}, u32[]{:S(2)}) collective-permute-start(bf16[2,512,384]{2,1,0:T(8,128)(2,1)S(1)} %get-tuple-element.250), channel_id=1, source_target_pairs={{2,0},{4,2},{6,4},{7,6},{5,7},{3,5},{1,3},{0,1},{10,8},{12,10},{14... | collective-permute-start | bytes 2359304 | tf_op jit(solution)/shard_map/ppermute | solution.py:663
  233.6 24.6 %collective-permute-start.34 = (bf16[2,512,384]{2,1,0:T(8,128)(2,1)S(1)}, bf16[2,512,384]{2,1,0:T(8,128)(2,1)S(1)}, u32[]{:S(2)}, u32[]{:S(2)}) collective-permute-start(bf16[2,512,384]{2,1,0:T(8,128)(2,1)S(1)} %get-tuple-element.284), channel_id=1, source_target_pairs={{0,2},{2,4},{4,6},{6,7},{7,5},{5,3},{3,1},{1,0},{8,10},{10,12},{12... | collective-permute-start | bytes 2359304 | tf_op jit(solution)/shard_map/ppermute | solution.py:663
  235.3 24.7 %collective-permute-start.35 = (bf16[2,512,384]{2,1,0:T(8,128)(2,1)S(1)}, bf16[2,512,384]{2,1,0:T(8,128)(2,1)S(1)}, u32[]{:S(2)}, u32[]{:S(2)}) collective-permute-start(bf16[2,512,384]{2,1,0:T(8,128)(2,1)S(1)} %get-tuple-element.285), channel_id=1, source_target_pairs={{2,0},{4,2},{6,4},{7,6},{5,7},{3,5},{1,3},{0,1},{10,8},{12,10},{14... | collective-permute-start | bytes 2359304 | tf_op jit(solution)/shard_map/ppermute | solution.py:663
  250.4 24.8 %collective-permute-start.18 = (bf16[2,512,384]{2,1,0:T(8,128)(2,1)S(1)}, bf16[2,512,384]{2,1,0:T(8,128)(2,1)S(1)}, u32[]{:S(2)}, u32[]{:S(2)}) collective-permute-start(bf16[2,512,384]{2,1,0:T(8,128)(2,1)S(1)} %get-tuple-element.252), channel_id=1, source_target_pairs={{0,2},{2,4},{4,6},{6,7},{7,5},{5,3},{3,1},{1,0},{8,10},{10,12},{12... | collective-permute-start | bytes 2359304 | tf_op jit(solution)/shard_map/ppermute | solution.py:663
  252.1 24.8 %collective-permute-start.19 = (bf16[2,512,384]{2,1,0:T(8,128)(2,1)S(1)}, bf16[2,512,384]{2,1,0:T(8,128)(2,1)S(1)}, u32[]{:S(2)}, u32[]{:S(2)}) collective-permute-start(bf16[2,512,384]{2,1,0:T(8,128)(2,1)S(1)} %get-tuple-element.253), channel_id=1, source_target_pairs={{2,0},{4,2},{6,4},{7,6},{5,7},{3,5},{1,3},{0,1},{10,8},{12,10},{14... | collective-permute-start | bytes 2359304 | tf_op jit(solution)/shard_map/ppermute | solution.py:663
  268.3 43.2 %collective-permute-start.36 = (bf16[2,512,384]{2,1,0:T(8,128)(2,1)S(1)}, bf16[2,512,384]{2,1,0:T(8,128)(2,1)S(1)}, u32[]{:S(2)}, u32[]{:S(2)}) collective-permute-start(bf16[2,512,384]{2,1,0:T(8,128)(2,1)S(1)} %get-tuple-element.288.refs_4_), channel_id=1, source_target_pairs={{0,2},{2,4},{4,6},{6,7},{7,5},{5,3},{3,1},{1,0},{8,10},{10,12},{12... | collective-permute-start | bytes 2359304 | tf_op jit(solution)/shard_map/ppermute | solution.py:663
  269.9 41.7 %collective-permute-start.37 = (bf16[2,512,384]{2,1,0:T(8,128)(2,1)S(1)}, bf16[2,512,384]{2,1,0:T(8,128)(2,1)S(1)}, u32[]{:S(2)}, u32[]{:S(2)}) collective-permute-start(bf16[2,512,384]{2,1,0:T(8,128)(2,1)S(1)} %get-tuple-element.289.refs_5_), channel_id=1, source_target_pairs={{2,0},{4,2},{6,4},{7,6},{5,7},{3,5},{1,3},{0,1},{10,8},{12,10},{14... | collective-permute-start | bytes 2359304 | tf_op jit(solution)/shard_map/ppermute | solution.py:663
  285.2 40.6 %collective-permute-start.20 = (bf16[2,512,384]{2,1,0:T(8,128)(2,1)S(1)}, bf16[2,512,384]{2,1,0:T(8,128)(2,1)S(1)}, u32[]{:S(2)}, u32[]{:S(2)}) collective-permute-start(bf16[2,512,384]{2,1,0:T(8,128)(2,1)S(1)} %get-tuple-element.256.refs_4_), channel_id=1, source_target_pairs={{0,2},{2,4},{4,6},{6,7},{7,5},{5,3},{3,1},{1,0},{8,10},{10,12},{12... | collective-permute-start | bytes 2359304 | tf_op jit(solution)/shard_map/ppermute | solution.py:663
  286.8 39.0 %collective-permute-start.21 = (bf16[2,512,384]{2,1,0:T(8,128)(2,1)S(1)}, bf16[2,512,384]{2,1,0:T(8,128)(2,1)S(1)}, u32[]{:S(2)}, u32[]{:S(2)}) collective-permute-start(bf16[2,512,384]{2,1,0:T(8,128)(2,1)S(1)} %get-tuple-element.257.refs_5_), channel_id=1, source_target_pairs={{2,0},{4,2},{6,4},{7,6},{5,7},{3,5},{1,3},{0,1},{10,8},{12,10},{14... | collective-permute-start | bytes 2359304 | tf_op jit(solution)/shard_map/ppermute | solution.py:663
  311.5 28.5 %collective-permute-start.40 = (bf16[2,512,384]{2,1,0:T(8,128)(2,1)S(1)}, bf16[2,512,384]{2,1,0:T(8,128)(2,1)S(1)}, u32[]{:S(2)}, u32[]{:S(2)}) collective-permute-start(bf16[2,512,384]{2,1,0:T(8,128)(2,1)S(1)} %collective-permute-done.36.refs_4_), channel_id=1, source_target_pairs={{0,2},{2,4},{4,6},{6,7},{7,5},{5,3},{3,1},{1,0},{8,10},{10,12},{12... | collective-permute-start | bytes 2359304 | tf_op jit(solution)/shard_map/ppermute | solution.py:663
  312.8 27.3 %collective-permute-start.41 = (bf16[2,512,384]{2,1,0:T(8,128)(2,1)S(1)}, bf16[2,512,384]{2,1,0:T(8,128)(2,1)S(1)}, u32[]{:S(2)}, u32[]{:S(2)}) collective-permute-start(bf16[2,512,384]{2,1,0:T(8,128)(2,1)S(1)} %collective-permute-done.37.refs_5_), channel_id=1, source_target_pairs={{2,0},{4,2},{6,4},{7,6},{5,7},{3,5},{1,3},{0,1},{10,8},{12,10},{14... | collective-permute-start | bytes 2359304 | tf_op jit(solution)/shard_map/ppermute | solution.py:663
  325.8 29.2 %collective-permute-start.38 = (bf16[2,512,384]{2,1,0:T(8,128)(2,1)S(1)}, bf16[2,512,384]{2,1,0:T(8,128)(2,1)S(1)}, u32[]{:S(2)}, u32[]{:S(2)}) collective-permute-start(bf16[2,512,384]{2,1,0:T(8,128)(2,1)S(1)} %collective-permute-done.20.refs_4_), channel_id=1, source_target_pairs={{0,2},{2,4},{4,6},{6,7},{7,5},{5,3},{3,1},{1,0},{8,10},{10,12},{12... | collective-permute-start | bytes 2359304 | tf_op jit(solution)/shard_map/ppermute | solution.py:663
  327.7 27.3 %collective-permute-start.39 = (bf16[2,512,384]{2,1,0:T(8,128)(2,1)S(1)}, bf16[2,512,384]{2,1,0:T(8,128)(2,1)S(1)}, u32[]{:S(2)}, u32[]{:S(2)}) collective-permute-start(bf16[2,512,384]{2,1,0:T(8,128)(2,1)S(1)} %collective-permute-done.21.refs_5_), channel_id=1, source_target_pairs={{2,0},{4,2},{6,4},{7,6},{5,7},{3,5},{1,3},{0,1},{10,8},{12,10},{14... | collective-permute-start | bytes 2359304 | tf_op jit(solution)/shard_map/ppermute | solution.py:663
  340.1 29.8 %collective-permute-start.44 = (bf16[2,512,384]{2,1,0:T(8,128)(2,1)S(1)}, bf16[2,512,384]{2,1,0:T(8,128)(2,1)S(1)}, u32[]{:S(2)}, u32[]{:S(2)}) collective-permute-start(bf16[2,512,384]{2,1,0:T(8,128)(2,1)S(1)} %collective-permute-done.40.refs_4_), channel_id=1, source_target_pairs={{0,2},{2,4},{4,6},{6,7},{7,5},{5,3},{3,1},{1,0},{8,10},{10,12},{12... | collective-permute-start | bytes 2359304 | tf_op jit(solution)/shard_map/ppermute | solution.py:663
  342.8 27.1 %collective-permute-start.45 = (bf16[2,512,384]{2,1,0:T(8,128)(2,1)S(1)}, bf16[2,512,384]{2,1,0:T(8,128)(2,1)S(1)}, u32[]{:S(2)}, u32[]{:S(2)}) collective-permute-start(bf16[2,512,384]{2,1,0:T(8,128)(2,1)S(1)} %collective-permute-done.41.refs_5_), channel_id=1, source_target_pairs={{2,0},{4,2},{6,4},{7,6},{5,7},{3,5},{1,3},{0,1},{10,8},{12,10},{14... | collective-permute-start | bytes 2359304 | tf_op jit(solution)/shard_map/ppermute | solution.py:663
  355.1 29.4 %collective-permute-start.42 = (bf16[2,512,384]{2,1,0:T(8,128)(2,1)S(1)}, bf16[2,512,384]{2,1,0:T(8,128)(2,1)S(1)}, u32[]{:S(2)}, u32[]{:S(2)}) collective-permute-start(bf16[2,512,384]{2,1,0:T(8,128)(2,1)S(1)} %collective-permute-done.38.refs_4_), channel_id=1, source_target_pairs={{0,2},{2,4},{4,6},{6,7},{7,5},{5,3},{3,1},{1,0},{8,10},{10,12},{12... | collective-permute-start | bytes 2359304 | tf_op jit(solution)/shard_map/ppermute | solution.py:663
  357.3 27.2 %collective-permute-start.43 = (bf16[2,512,384]{2,1,0:T(8,128)(2,1)S(1)}, bf16[2,512,384]{2,1,0:T(8,128)(2,1)S(1)}, u32[]{:S(2)}, u32[]{:S(2)}) collective-permute-start(bf16[2,512,384]{2,1,0:T(8,128)(2,1)S(1)} %collective-permute-done.39.refs_5_), channel_id=1, source_target_pairs={{2,0},{4,2},{6,4},{7,6},{5,7},{3,5},{1,3},{0,1},{10,8},{12,10},{14... | collective-permute-start | bytes 2359304 | tf_op jit(solution)/shard_map/ppermute | solution.py:663
  369.9 29.3 %collective-permute-start.48 = (bf16[2,512,384]{2,1,0:T(8,128)(2,1)S(1)}, bf16[2,512,384]{2,1,0:T(8,128)(2,1)S(1)}, u32[]{:S(2)}, u32[]{:S(2)}) collective-permute-start(bf16[2,512,384]{2,1,0:T(8,128)(2,1)S(1)} %collective-permute-done.44.refs_4_), channel_id=1, source_target_pairs={{0,2},{2,4},{4,6},{6,7},{7,5},{5,3},{3,1},{1,0},{8,10},{10,12},{12... | collective-permute-start | bytes 2359304 | tf_op jit(solution)/shard_map/ppermute | solution.py:663
  372.1 27.6 %collective-permute-start.49 = (bf16[2,512,384]{2,1,0:T(8,128)(2,1)S(1)}, bf16[2,512,384]{2,1,0:T(8,128)(2,1)S(1)}, u32[]{:S(2)}, u32[]{:S(2)}) collective-permute-start(bf16[2,512,384]{2,1,0:T(8,128)(2,1)S(1)} %collective-permute-done.45.refs_5_), channel_id=1, source_target_pairs={{2,0},{4,2},{6,4},{7,6},{5,7},{3,5},{1,3},{0,1},{10,8},{12,10},{14... | collective-permute-start | bytes 2359304 | tf_op jit(solution)/shard_map/ppermute | solution.py:663
  384.5 30.6 %collective-permute-start.46 = (bf16[2,512,384]{2,1,0:T(8,128)(2,1)S(1)}, bf16[2,512,384]{2,1,0:T(8,128)(2,1)S(1)}, u32[]{:S(2)}, u32[]{:S(2)}) collective-permute-start(bf16[2,512,384]{2,1,0:T(8,128)(2,1)S(1)} %collective-permute-done.42.refs_4_), channel_id=1, source_target_pairs={{0,2},{2,4},{4,6},{6,7},{7,5},{5,3},{3,1},{1,0},{8,10},{10,12},{12... | collective-permute-start | bytes 2359304 | tf_op jit(solution)/shard_map/ppermute | solution.py:663
  386.9 29.7 %collective-permute-start.47 = (bf16[2,512,384]{2,1,0:T(8,128)(2,1)S(1)}, bf16[2,512,384]{2,1,0:T(8,128)(2,1)S(1)}, u32[]{:S(2)}, u32[]{:S(2)}) collective-permute-start(bf16[2,512,384]{2,1,0:T(8,128)(2,1)S(1)} %collective-permute-done.43.refs_5_), channel_id=1, source_target_pairs={{2,0},{4,2},{6,4},{7,6},{5,7},{3,5},{1,3},{0,1},{10,8},{12,10},{14... | collective-permute-start | bytes 2359304 | tf_op jit(solution)/shard_map/ppermute | solution.py:663
  399.7 32.2 %collective-permute-start.52 = (bf16[2,512,384]{2,1,0:T(8,128)(2,1)S(1)}, bf16[2,512,384]{2,1,0:T(8,128)(2,1)S(1)}, u32[]{:S(2)}, u32[]{:S(2)}) collective-permute-start(bf16[2,512,384]{2,1,0:T(8,128)(2,1)S(1)} %collective-permute-done.48.refs_4_), channel_id=1, source_target_pairs={{0,2},{2,4},{4,6},{6,7},{7,5},{5,3},{3,1},{1,0},{8,10},{10,12},{12... | collective-permute-start | bytes 2359304 | tf_op jit(solution)/shard_map/ppermute | solution.py:663
  401.8 31.7 %collective-permute-start.53 = (bf16[2,512,384]{2,1,0:T(8,128)(2,1)S(1)}, bf16[2,512,384]{2,1,0:T(8,128)(2,1)S(1)}, u32[]{:S(2)}, u32[]{:S(2)}) collective-permute-start(bf16[2,512,384]{2,1,0:T(8,128)(2,1)S(1)} %collective-permute-done.49.refs_5_), channel_id=1, source_target_pairs={{2,0},{4,2},{6,4},{7,6},{5,7},{3,5},{1,3},{0,1},{10,8},{12,10},{14... | collective-permute-start | bytes 2359304 | tf_op jit(solution)/shard_map/ppermute | solution.py:663
  416.6 32.2 %collective-permute-start.50 = (bf16[2,512,384]{2,1,0:T(8,128)(2,1)S(1)}, bf16[2,512,384]{2,1,0:T(8,128)(2,1)S(1)}, u32[]{:S(2)}, u32[]{:S(2)}) collective-permute-start(bf16[2,512,384]{2,1,0:T(8,128)(2,1)S(1)} %collective-permute-done.46.refs_4_), channel_id=1, source_target_pairs={{0,2},{2,4},{4,6},{6,7},{7,5},{5,3},{3,1},{1,0},{8,10},{10,12},{12... | collective-permute-start | bytes 2359304 | tf_op jit(solution)/shard_map/ppermute | solution.py:663
  418.6 31.7 %collective-permute-start.51 = (bf16[2,512,384]{2,1,0:T(8,128)(2,1)S(1)}, bf16[2,512,384]{2,1,0:T(8,128)(2,1)S(1)}, u32[]{:S(2)}, u32[]{:S(2)}) collective-permute-start(bf16[2,512,384]{2,1,0:T(8,128)(2,1)S(1)} %collective-permute-done.47.refs_5_), channel_id=1, source_target_pairs={{2,0},{4,2},{6,4},{7,6},{5,7},{3,5},{1,3},{0,1},{10,8},{12,10},{14... | collective-permute-start | bytes 2359304 | tf_op jit(solution)/shard_map/ppermute | solution.py:663
  433.4 32.2 %collective-permute-start.56 = (bf16[2,512,384]{2,1,0:T(8,128)(2,1)S(1)}, bf16[2,512,384]{2,1,0:T(8,128)(2,1)S(1)}, u32[]{:S(2)}, u32[]{:S(2)}) collective-permute-start(bf16[2,512,384]{2,1,0:T(8,128)(2,1)S(1)} %collective-permute-done.52.refs_4_), channel_id=1, source_target_pairs={{0,2},{2,4},{4,6},{6,7},{7,5},{5,3},{3,1},{1,0},{8,10},{10,12},{12... | collective-permute-start | bytes 2359304 | tf_op jit(solution)/shard_map/ppermute | solution.py:663
  435.4 31.7 %collective-permute-start.57 = (bf16[2,512,384]{2,1,0:T(8,128)(2,1)S(1)}, bf16[2,512,384]{2,1,0:T(8,128)(2,1)S(1)}, u32[]{:S(2)}, u32[]{:S(2)}) collective-permute-start(bf16[2,512,384]{2,1,0:T(8,128)(2,1)S(1)} %collective-permute-done.53.refs_5_), channel_id=1, source_target_pairs={{2,0},{4,2},{6,4},{7,6},{5,7},{3,5},{1,3},{0,1},{10,8},{12,10},{14... | collective-permute-start | bytes 2359304 | tf_op jit(solution)/shard_map/ppermute | solution.py:663
  450.3 32.2 %collective-permute-start.54 = (bf16[2,512,384]{2,1,0:T(8,128)(2,1)S(1)}, bf16[2,512,384]{2,1,0:T(8,128)(2,1)S(1)}, u32[]{:S(2)}, u32[]{:S(2)}) collective-permute-start(bf16[2,512,384]{2,1,0:T(8,128)(2,1)S(1)} %collective-permute-done.50.refs_4_), channel_id=1, source_target_pairs={{0,2},{2,4},{4,6},{6,7},{7,5},{5,3},{3,1},{1,0},{8,10},{10,12},{12... | collective-permute-start | bytes 2359304 | tf_op jit(solution)/shard_map/ppermute | solution.py:663
  452.3 31.7 %collective-permute-start.55 = (bf16[2,512,384]{2,1,0:T(8,128)(2,1)S(1)}, bf16[2,512,384]{2,1,0:T(8,128)(2,1)S(1)}, u32[]{:S(2)}, u32[]{:S(2)}) collective-permute-start(bf16[2,512,384]{2,1,0:T(8,128)(2,1)S(1)} %collective-permute-done.51.refs_5_), channel_id=1, source_target_pairs={{2,0},{4,2},{6,4},{7,6},{5,7},{3,5},{1,3},{0,1},{10,8},{12,10},{14... | collective-permute-start | bytes 2359304 | tf_op jit(solution)/shard_map/ppermute | solution.py:663
  467.1 32.2 %collective-permute-start.60 = (bf16[2,512,384]{2,1,0:T(8,128)(2,1)S(1)}, bf16[2,512,384]{2,1,0:T(8,128)(2,1)S(1)}, u32[]{:S(2)}, u32[]{:S(2)}) collective-permute-start(bf16[2,512,384]{2,1,0:T(8,128)(2,1)S(1)} %collective-permute-done.56.refs_4_), channel_id=1, source_target_pairs={{0,2},{2,4},{4,6},{6,7},{7,5},{5,3},{3,1},{1,0},{8,10},{10,12},{12... | collective-permute-start | bytes 2359304 | tf_op jit(solution)/shard_map/ppermute | solution.py:663
  469.1 31.7 %collective-permute-start.61 = (bf16[2,512,384]{2,1,0:T(8,128)(2,1)S(1)}, bf16[2,512,384]{2,1,0:T(8,128)(2,1)S(1)}, u32[]{:S(2)}, u32[]{:S(2)}) collective-permute-start(bf16[2,512,384]{2,1,0:T(8,128)(2,1)S(1)} %collective-permute-done.57.refs_5_), channel_id=1, source_target_pairs={{2,0},{4,2},{6,4},{7,6},{5,7},{3,5},{1,3},{0,1},{10,8},{12,10},{14... | collective-permute-start | bytes 2359304 | tf_op jit(solution)/shard_map/ppermute | solution.py:663
  484.0 29.7 %collective-permute-start.58 = (bf16[2,512,384]{2,1,0:T(8,128)(2,1)S(1)}, bf16[2,512,384]{2,1,0:T(8,128)(2,1)S(1)}, u32[]{:S(2)}, u32[]{:S(2)}) collective-permute-start(bf16[2,512,384]{2,1,0:T(8,128)(2,1)S(1)} %collective-permute-done.54.refs_4_), channel_id=1, source_target_pairs={{0,2},{2,4},{4,6},{6,7},{7,5},{5,3},{3,1},{1,0},{8,10},{10,12},{12... | collective-permute-start | bytes 2359304 | tf_op jit(solution)/shard_map/ppermute | solution.py:663
  486.0 28.3 %collective-permute-start.59 = (bf16[2,512,384]{2,1,0:T(8,128)(2,1)S(1)}, bf16[2,512,384]{2,1,0:T(8,128)(2,1)S(1)}, u32[]{:S(2)}, u32[]{:S(2)}) collective-permute-start(bf16[2,512,384]{2,1,0:T(8,128)(2,1)S(1)} %collective-permute-done.55.refs_5_), channel_id=1, source_target_pairs={{2,0},{4,2},{6,4},{7,6},{5,7},{3,5},{1,3},{0,1},{10,8},{12,10},{14... | collective-permute-start | bytes 2359304 | tf_op jit(solution)/shard_map/ppermute | solution.py:663
  518.8 2.4 collective-permute-start.62
  526.1 4.2 collective-permute-start.64
  526.4 13.9 %collective-permute-start.63 = (bf16[128,1536]{1,0:T(8,128)(2,1)S(1)}, bf16[128,1536]{1,0:T(8,128)(2,1)S(1)}, u32[]{:S(2)}, u32[]{:S(2)}) collective-permute-start(bf16[128,1536]{1,0:T(8,128)(2,1)S(1)} %slice.25), channel_id=1, source_target_pairs={{16,0},{24,8},{0,16},{8,24},{17,1},{25,9},{1,17},{9,25},{18,2},{26... | collective-permute-start | bytes 1179656 | tf_op jit(solution)/shard_map/ppermute | solution.py:594
  530.6 17.9 %collective-permute-start.65 = (bf16[128,1536]{1,0:T(8,128)(2,1)S(1)}, bf16[128,1536]{1,0:T(8,128)(2,1)S(1)}, u32[]{:S(2)}, u32[]{:S(2)}) collective-permute-start(bf16[128,1536]{1,0:T(8,128)(2,1)S(1)} %slice.24), channel_id=1, source_target_pairs={{16,0},{24,8},{0,16},{8,24},{17,1},{25,9},{1,17},{9,25},{18,2},{26... | collective-permute-start | bytes 1179656 | tf_op jit(solution)/shard_map/ppermute | solution.py:594
  (14 other events, 52.1 us)

commit v5 on v4

--- a/solution.py
+++ b/solution.py
@@ -12,7 +12,7 @@
 ROOT_2_PI = 0.7978845608028654
 CUBIC = 0.044715
 VMEM_LIMIT = 40 << 20
-FIRST_LIMIT = 60 << 20
+FIRST_LIMIT = 44 << 20
 FIRST_SHIFT = 20
 SECOND_SHIFT = 14
 

time: 560 us -> 558 us (level)
  waiting for transfers between devices: 123 us -> 132 us
  transfers between devices with their start and end apart: 66 -> 66, of which waited for: 47 -> 48; matrix products, arithmetic and copies ran while one was open for 1% -> 1% of each run, Pallas kernels for 58% -> 58%
where the time goes in v5:
time: 558 us; the launch traced here: 548 us
  Pallas kernels  336 us (60%)
  waiting for transfers between devices  132 us (24%)
  starting transfers between devices  66.4 us (12%)
  local copies, waits for them, and re-layouts  6.19 us (1%)
    pallas_call x18, Pallas kernels, back_call(): pl.pallas_call(functools.partial(back_kernel, plan, down, with_grads, fir...  199 us
    pallas_call x15, Pallas kernels, up_call(): pl.pallas_call(functools.partial(up_kernel, plan, has_in, last), out_shap...  116 us
    ppermute x56, waiting for transfers between devices, hop(): lax.ppermute(a, 'col', ahead if sign > 0 else back)  110 us
    ppermute x56, starting transfers between devices, hop(): lax.ppermute(a, 'col', ahead if sign > 0 else back)  60.2 us
    ppermute x4, waiting for transfers between devices, shift(): return lax.ppermute(value, 'row', pairs)  15.8 us
  transfers between devices with their start and end apart: 66, of which 48 were waited for; matrix products, arithmetic and copies ran while one was open for 1% of the time, Pallas kernels for 58%

profile of v5, /device:TPU:0, one launch (start us, length us, event | category | flops | bytes accessed | tf_op | source)
XLA Modules:
  0.0 548.1 jit_solution(12710813680704094198)
XLA Ops:
  0.6 3.0 collective-permute-start
  9.4 3.6 collective-permute-done.refs_2_
  15.9 5.7 %first_hid.1 = (bf16[512,1536]{1,0:T(8,128)(2,1)S(1)}, f32[512,768]{1,0:T(8,128)S(1)}, bf16[8,3072,768]{2,1,0:T(8,128)(2,1)}) custom-call(s32[1219]{0:T(1024)S(1)} %concatenate.3.refs_0_.meta, bf16[128,1536]{1,0:T(8,128)(2,1)S(1)} %copy-done.4, bf16[128,1536]{1,0:T(8,128)(2,1)S(1)} %collective-permute-done.refs_2_, ...), custom_call_target="tpu_custom_call" | custom-call | flops 1207959552 | bytes 5505024 | tf_op jit(solution)/shard_map/first_hid/pallas_call | solution.py:340
  21.7 3.0 collective-permute-done.3.refs_2_
  26.4 7.3 %first_grd.1 = (bf16[2,512,384]{2,1,0:T(8,128)(2,1)}, bf16[2,512,384]{2,1,0:T(8,128)(2,1)}, bf16[512,1536]{1,0:T(8,128)(2,1)S(1)}, bf16[8,3072,768]{2,1,0:T(8,128)(2,1)}) custom-call(s32[1219]{0:T(1024)S(1)} %concatenate.3.refs_0_.meta, bf16[128,1536]{1,0:T(8,128)(2,1)S(1)} %copy-done.3, ...), custom_call_target="tpu_custom_call", output_to_operand_aliasing={{3}: (7, {})} | custom-call | flops 1207959552 | bytes 5505024 | tf_op jit(solution)/shard_map/first_grd/pallas_call | solution.py:352
  35.8 8.5 %up.13 = (bf16[2,512,384]{2,1,0:T(8,128)(2,1)}, bf16[2,512,384]{2,1,0:T(8,128)(2,1)}, bf16[8,3072,768]{2,1,0:T(8,128)(2,1)}) custom-call(s32[1219]{0:T(1024)S(1)} %concatenate.3.refs_0_.meta, bf16[512,1536]{1,0:T(8,128)(2,1)S(1)} %get-tuple-element.228.refs_1_, bf16[512,1536]{1,0:T(8,128)(2,1)S(1)} %get-tuple-element.233.refs_2_, ...), custom_call_target="tpu_custom_call" | custom-call | flops 2415919104 | bytes 7864320 | tf_op jit(solution)/shard_map/up/pallas_call | solution.py:311
  44.4 2.0 collective-permute-start.6
  48.2 6.3 %collective-permute-done.22.refs_5_ = bf16[2,512,384]{2,1,0:T(8,128)(2,1)} collective-permute-done((bf16[2,512,384]{2,1,0:T(8,128)(2,1)}, bf16[2,512,384]{2,1,0:T(8,128)(2,1)}, u32[]{:S(2)}, u32[]{:S(2)}) %collective-permute-start.22) | collective-permute-done | bytes 786464 | tf_op jit(solution)/shard_map/ppermute | solution.py:663
  57.8 8.1 %up.20 = (bf16[2,512,384]{2,1,0:T(8,128)(2,1)S(1)}, bf16[2,512,384]{2,1,0:T(8,128)(2,1)S(1)}, bf16[8,3072,768]{2,1,0:T(8,128)(2,1)}) custom-call(s32[1219]{0:T(1024)S(1)} %concatenate.3.refs_0_.meta, bf16[512,1536]{1,0:T(8,128)(2,1)S(1)} %copy-done.1, bf16[512,1536]{1,0:T(8,128)(2,1)S(1)} %get-tuple-element.233.refs_2_, ...), custom_call_target="tpu_custom_call", output_to_operand_aliasing={{2}: (7, {})} | custom-call | flops 2415919104 | bytes 7864320 | tf_op jit(solution)/shard_map/up/pallas_call | solution.py:311
  66.0 2.0 collective-permute-start.24
  68.1 3.2 collective-permute-done.6.refs_5_
  73.3 8.2 %up.14 = (bf16[2,512,384]{2,1,0:T(8,128)(2,1)S(1)}, bf16[2,512,384]{2,1,0:T(8,128)(2,1)S(1)}, bf16[8,3072,768]{2,1,0:T(8,128)(2,1)}) custom-call(s32[1219]{0:T(1024)S(1)} %concatenate.3.refs_0_.meta, bf16[512,1536]{1,0:T(8,128)(2,1)S(1)} %copy-done.1, bf16[512,1536]{1,0:T(8,128)(2,1)S(1)} %get-tuple-element.233.refs_2_, ...), custom_call_target="tpu_custom_call", output_to_operand_aliasing={{2}: (7, {})} | custom-call | flops 2415919104 | bytes 7864320 | tf_op jit(solution)/shard_map/up/pallas_call | solution.py:311
  83.6 4.5 dead.2.refs_6_
  90.0 7.3 %up.21 = (bf16[2,512,384]{2,1,0:T(8,128)(2,1)S(1)}, bf16[2,512,384]{2,1,0:T(8,128)(2,1)S(1)}, bf16[8,3072,768]{2,1,0:T(8,128)(2,1)}) custom-call(s32[1219]{0:T(1024)S(1)} %concatenate.3.refs_0_.meta, bf16[512,1536]{1,0:T(8,128)(2,1)S(1)} %copy-done.2, bf16[512,1536]{1,0:T(8,128)(2,1)S(1)} %get-tuple-element.233.refs_2_, ...), custom_call_target="tpu_custom_call", output_to_operand_aliasing={{2}: (7, {})} | custom-call | flops 2415919104 | bytes 7864320 | tf_op jit(solution)/shard_map/up/pallas_call | solution.py:311
  99.4 5.5 collective-permute-done.8.refs_5_
  104.9 2.0 collective-permute-done.9.refs_6_
  106.9 7.5 %up.15 = (bf16[2,512,384]{2,1,0:T(8,128)(2,1)S(1)}, bf16[2,512,384]{2,1,0:T(8,128)(2,1)S(1)}, bf16[8,3072,768]{2,1,0:T(8,128)(2,1)}) custom-call(s32[1219]{0:T(1024)S(1)} %concatenate.3.refs_0_.meta, bf16[512,1536]{1,0:T(8,128)(2,1)S(1)} %copy-done.2, bf16[512,1536]{1,0:T(8,128)(2,1)S(1)} %get-tuple-element.233.refs_2_, ...), custom_call_target="tpu_custom_call", output_to_operand_aliasing={{2}: (7, {})} | custom-call | flops 2415919104 | bytes 7864320 | tf_op jit(solution)/shard_map/up/pallas_call | solution.py:311
  116.5 3.7 dead.3.refs_7_
  121.8 2.0 collective-permute-done.27.refs_6_
  123.7 7.8 %up.22 = (bf16[2,512,384]{2,1,0:T(8,128)(2,1)S(1)}, bf16[2,512,384]{2,1,0:T(8,128)(2,1)S(1)}, bf16[8,3072,768]{2,1,0:T(8,128)(2,1)}) custom-call(s32[1219]{0:T(1024)S(1)} %concatenate.3.refs_0_.meta, bf16[512,1536]{1,0:T(8,128)(2,1)S(1)} %copy-done.2, bf16[512,1536]{1,0:T(8,128)(2,1)S(1)} %get-tuple-element.233.refs_2_, ...), custom_call_target="tpu_custom_call", output_to_operand_aliasing={{2}: (7, {})} | custom-call | flops 2415919104 | bytes 7864320 | tf_op jit(solution)/shard_map/up/pallas_call | solution.py:311
  133.7 4.9 collective-permute-done.10.refs_5_
  140.6 7.4 %up.16 = (bf16[2,512,384]{2,1,0:T(8,128)(2,1)S(1)}, bf16[2,512,384]{2,1,0:T(8,128)(2,1)S(1)}, bf16[8,3072,768]{2,1,0:T(8,128)(2,1)}) custom-call(s32[1219]{0:T(1024)S(1)} %concatenate.3.refs_0_.meta, bf16[512,1536]{1,0:T(8,128)(2,1)S(1)} %copy-done.2, bf16[512,1536]{1,0:T(8,128)(2,1)S(1)} %get-tuple-element.233.refs_2_, ...), custom_call_target="tpu_custom_call", output_to_operand_aliasing={{2}: (7, {})} | custom-call | flops 2415919104 | bytes 7864320 | tf_op jit(solution)/shard_map/up/pallas_call | solution.py:311
  150.1 5.4 collective-permute-done.28.refs_5_
  157.4 7.4 %up.23 = (bf16[2,512,384]{2,1,0:T(8,128)(2,1)S(1)}, bf16[2,512,384]{2,1,0:T(8,128)(2,1)S(1)}, bf16[8,3072,768]{2,1,0:T(8,128)(2,1)}) custom-call(s32[1219]{0:T(1024)S(1)} %concatenate.3.refs_0_.meta, bf16[512,1536]{1,0:T(8,128)(2,1)S(1)} %copy-done.2, bf16[512,1536]{1,0:T(8,128)(2,1)S(1)} %get-tuple-element.233.refs_2_, ...), custom_call_target="tpu_custom_call", output_to_operand_aliasing={{2}: (7, {})} | custom-call | flops 2415919104 | bytes 7864320 | tf_op jit(solution)/shard_map/up/pallas_call | solution.py:311
  166.9 5.4 collective-permute-done.12.refs_5_
  174.3 7.4 %up.17 = (bf16[2,512,384]{2,1,0:T(8,128)(2,1)S(1)}, bf16[2,512,384]{2,1,0:T(8,128)(2,1)S(1)}, bf16[8,3072,768]{2,1,0:T(8,128)(2,1)}) custom-call(s32[1219]{0:T(1024)S(1)} %concatenate.3.refs_0_.meta, bf16[512,1536]{1,0:T(8,128)(2,1)S(1)} %copy-done.2, bf16[512,1536]{1,0:T(8,128)(2,1)S(1)} %get-tuple-element.233.refs_2_, ...), custom_call_target="tpu_custom_call", output_to_operand_aliasing={{2}: (7, {})} | custom-call | flops 2415919104 | bytes 7864320 | tf_op jit(solution)/shard_map/up/pallas_call | solution.py:311
  183.8 5.4 collective-permute-done.30.refs_5_
  191.2 7.4 %up.24 = (bf16[2,512,384]{2,1,0:T(8,128)(2,1)S(1)}, bf16[2,512,384]{2,1,0:T(8,128)(2,1)S(1)}, bf16[8,3072,768]{2,1,0:T(8,128)(2,1)}) custom-call(s32[1219]{0:T(1024)S(1)} %concatenate.3.refs_0_.meta, bf16[512,1536]{1,0:T(8,128)(2,1)S(1)} %copy-done.2, bf16[512,1536]{1,0:T(8,128)(2,1)S(1)} %get-tuple-element.233.refs_2_, ...), custom_call_target="tpu_custom_call", output_to_operand_aliasing={{2}: (7, {})} | custom-call | flops 2415919104 | bytes 7864320 | tf_op jit(solution)/shard_map/up/pallas_call | solution.py:311
  200.7 5.4 collective-permute-done.14.refs_5_
  208.0 7.4 %up.18 = (bf16[2,512,384]{2,1,0:T(8,128)(2,1)S(1)}, bf16[2,512,384]{2,1,0:T(8,128)(2,1)S(1)}, bf16[8,3072,768]{2,1,0:T(8,128)(2,1)}) custom-call(s32[1219]{0:T(1024)S(1)} %concatenate.3.refs_0_.meta, bf16[512,1536]{1,0:T(8,128)(2,1)S(1)} %copy-done.2, bf16[512,1536]{1,0:T(8,128)(2,1)S(1)} %get-tuple-element.233.refs_2_, ...), custom_call_target="tpu_custom_call", output_to_operand_aliasing={{2}: (7, {})} | custom-call | flops 2415919104 | bytes 7864320 | tf_op jit(solution)/shard_map/up/pallas_call | solution.py:311
  217.5 5.4 collective-permute-done.32.refs_5_
  224.9 7.4 %up.25 = (bf16[2,512,384]{2,1,0:T(8,128)(2,1)S(1)}, bf16[2,512,384]{2,1,0:T(8,128)(2,1)S(1)}, bf16[8,3072,768]{2,1,0:T(8,128)(2,1)}) custom-call(s32[1219]{0:T(1024)S(1)} %concatenate.3.refs_0_.meta, bf16[512,1536]{1,0:T(8,128)(2,1)S(1)} %copy-done.2, bf16[512,1536]{1,0:T(8,128)(2,1)S(1)} %get-tuple-element.233.refs_2_, ...), custom_call_target="tpu_custom_call", output_to_operand_aliasing={{2}: (7, {})} | custom-call | flops 2415919104 | bytes 7864320 | tf_op jit(solution)/shard_map/up/pallas_call | solution.py:311
  234.3 5.4 collective-permute-done.16.refs_5_
  241.7 7.3 %up.19 = (bf16[2,512,384]{2,1,0:T(8,128)(2,1)S(1)}, bf16[2,512,384]{2,1,0:T(8,128)(2,1)S(1)}, bf16[8,3072,768]{2,1,0:T(8,128)(2,1)}) custom-call(s32[1219]{0:T(1024)S(1)} %concatenate.3.refs_0_.meta, bf16[512,1536]{1,0:T(8,128)(2,1)S(1)} %copy-done.2, bf16[512,1536]{1,0:T(8,128)(2,1)S(1)} %get-tuple-element.233.refs_2_, ...), custom_call_target="tpu_custom_call", output_to_operand_aliasing={{2}: (7, {})} | custom-call | flops 2415919104 | bytes 7864320 | tf_op jit(solution)/shard_map/up/pallas_call | solution.py:311
  251.1 5.5 %collective-permute-done.34.refs_5_ = bf16[2,512,384]{2,1,0:T(8,128)(2,1)S(1)} collective-permute-done((bf16[2,512,384]{2,1,0:T(8,128)(2,1)S(1)}, bf16[2,512,384]{2,1,0:T(8,128)(2,1)S(1)}, u32[]{:S(2)}, u32[]{:S(2)}) %collective-permute-start.34) | collective-permute-done | bytes 786464 | tf_op jit(solution)/shard_map/ppermute | solution.py:663
  258.6 8.3 %up_last.3 = (bf16[2,512,384]{2,1,0:T(8,128)(2,1)S(1)}, bf16[2,512,384]{2,1,0:T(8,128)(2,1)S(1)}, bf16[8,3072,768]{2,1,0:T(8,128)(2,1)}) custom-call(s32[1219]{0:T(1024)S(1)} %concatenate.3.refs_0_.meta, bf16[512,1536]{1,0:T(8,128)(2,1)S(1)} %copy-done.2, bf16[512,1536]{1,0:T(8,128)(2,1)S(1)} %get-tuple-element.233.refs_2_, ...), custom_call_target="tpu_custom_call", output_to_operand_aliasing={{2}: (7, {})} | custom-call | flops 2415919104 | bytes 7864320 | tf_op jit(solution)/shard_map/up_last/pallas_call | solution.py:311
  269.1 4.3 collective-permute-done.18.refs_5_
  275.4 8.4 %up_last.2 = (bf16[2,512,384]{2,1,0:T(8,128)(2,1)S(1)}, bf16[2,512,384]{2,1,0:T(8,128)(2,1)S(1)}, bf16[8,3072,768]{2,1,0:T(8,128)(2,1)}) custom-call(s32[1219]{0:T(1024)S(1)} %concatenate.3.refs_0_.meta, bf16[512,1536]{1,0:T(8,128)(2,1)S(1)} %copy-done.2, bf16[512,1536]{1,0:T(8,128)(2,1)S(1)} %get-tuple-element.233.refs_2_, ...), custom_call_target="tpu_custom_call", output_to_operand_aliasing={{2}: (7, {})} | custom-call | flops 2415919104 | bytes 7864320 | tf_op jit(solution)/shard_map/up_last/pallas_call | solution.py:311
  285.9 11.9 %back.18 = (f32[512,1536]{1,0:T(8,128)S(1)}, f32[512,1536]{1,0:T(8,128)S(1)}, bf16[512,128,128]{2,1,0:T(8,128)(2,1)}, bf16[512,128,128]{2,1,0:T(8,128)(2,1)}) custom-call(s32[1219]{0:T(1024)S(1)} %concatenate.3.refs_0_.meta, bf16[1536,512]{1,0:T(8,128)(2,1)S(1)} %bitcast.11, ...), custom_call_target="tpu_custom_call", output_to_operand_aliasing={{2}: (6, {}), {3}: (7, {})} | custom-call | flops 4831838208 | bytes 4718592 | tf_op jit(solution)/shard_map/back/pallas_call | solution.py:562
  297.8 12.1 %back.19 = (f32[512,1536]{1,0:T(8,128)S(1)}, f32[512,1536]{1,0:T(8,128)S(1)}, bf16[512,128,128]{2,1,0:T(8,128)(2,1)}, bf16[512,128,128]{2,1,0:T(8,128)(2,1)}) custom-call(s32[1219]{0:T(1024)S(1)} %concatenate.3.refs_0_.meta, bf16[1536,512]{1,0:T(8,128)(2,1)S(1)} %bitcast.12, ...), custom_call_target="tpu_custom_call", output_to_operand_aliasing={{0}: (6, {}), {1}: (7, {}), {2}: (8, {}), {3}: (9, {})} | custom-call | flops 4831838208 | bytes 4718592 | tf_op jit(solution)/shard_map/back/pallas_call | solution.py:562
  309.9 2.6 collective-permute-start.40
  312.5 12.3 %back.20 = (f32[512,1536]{1,0:T(8,128)S(1)}, f32[512,1536]{1,0:T(8,128)S(1)}, bf16[512,128,128]{2,1,0:T(8,128)(2,1)}, bf16[512,128,128]{2,1,0:T(8,128)(2,1)}) custom-call(s32[1219]{0:T(1024)S(1)} %concatenate.3.refs_0_.meta, bf16[1536,512]{1,0:T(8,128)(2,1)S(1)} %bitcast.13, ...), custom_call_target="tpu_custom_call", output_to_operand_aliasing={{0}: (6, {}), {1}: (7, {}), {2}: (8, {}), {3}: (9, {})} | custom-call | flops 4831838208 | bytes 4718592 | tf_op jit(solution)/shard_map/back/pallas_call | solution.py:562
  324.8 2.3 collective-permute-start.38
  327.1 12.2 %back.21 = (f32[512,1536]{1,0:T(8,128)S(1)}, f32[512,1536]{1,0:T(8,128)S(1)}, bf16[512,128,128]{2,1,0:T(8,128)(2,1)}, bf16[512,128,128]{2,1,0:T(8,128)(2,1)}) custom-call(s32[1219]{0:T(1024)S(1)} %concatenate.3.refs_0_.meta, bf16[1536,512]{1,0:T(8,128)(2,1)S(1)} %bitcast.14, ...), custom_call_target="tpu_custom_call", output_to_operand_aliasing={{0}: (6, {}), {1}: (7, {}), {2}: (8, {}), {3}: (9, {})} | custom-call | flops 4831838208 | bytes 4718592 | tf_op jit(solution)/shard_map/back/pallas_call | solution.py:562
  339.3 2.3 collective-permute-start.44
  341.6 12.2 %back.22 = (f32[512,1536]{1,0:T(8,128)S(1)}, f32[512,1536]{1,0:T(8,128)S(1)}, bf16[512,128,128]{2,1,0:T(8,128)(2,1)}, bf16[512,128,128]{2,1,0:T(8,128)(2,1)}) custom-call(s32[1219]{0:T(1024)S(1)} %concatenate.3.refs_0_.meta, bf16[1536,512]{1,0:T(8,128)(2,1)S(1)} %bitcast.15, ...), custom_call_target="tpu_custom_call", output_to_operand_aliasing={{0}: (6, {}), {1}: (7, {}), {2}: (8, {}), {3}: (9, {})} | custom-call | flops 4831838208 | bytes 4718592 | tf_op jit(solution)/shard_map/back/pallas_call | solution.py:562
  353.8 2.6 collective-permute-start.42
  356.6 12.2 %back.23 = (f32[512,1536]{1,0:T(8,128)S(1)}, f32[512,1536]{1,0:T(8,128)S(1)}, bf16[512,128,128]{2,1,0:T(8,128)(2,1)}, bf16[512,128,128]{2,1,0:T(8,128)(2,1)}) custom-call(s32[1219]{0:T(1024)S(1)} %concatenate.3.refs_0_.meta, bf16[1536,512]{1,0:T(8,128)(2,1)S(1)} %bitcast.16, ...), custom_call_target="tpu_custom_call", output_to_operand_aliasing={{0}: (6, {}), {1}: (7, {}), {2}: (8, {}), {3}: (9, {})} | custom-call | flops 4831838208 | bytes 4718592 | tf_op jit(solution)/shard_map/back/pallas_call | solution.py:562
  368.9 2.1 collective-permute-start.48
  370.9 12.1 %back.24 = (f32[512,1536]{1,0:T(8,128)S(1)}, f32[512,1536]{1,0:T(8,128)S(1)}, bf16[512,128,128]{2,1,0:T(8,128)(2,1)}, bf16[512,128,128]{2,1,0:T(8,128)(2,1)}) custom-call(s32[1219]{0:T(1024)S(1)} %concatenate.3.refs_0_.meta, bf16[1536,512]{1,0:T(8,128)(2,1)S(1)} %bitcast.17, ...), custom_call_target="tpu_custom_call", output_to_operand_aliasing={{0}: (6, {}), {1}: (7, {}), {2}: (8, {}), {3}: (9, {})} | custom-call | flops 4831838208 | bytes 4718592 | tf_op jit(solution)/shard_map/back/pallas_call | solution.py:562
  383.0 2.6 collective-permute-start.46
  385.7 12.4 %back.25 = (f32[512,1536]{1,0:T(8,128)S(1)}, f32[512,1536]{1,0:T(8,128)S(1)}, bf16[512,128,128]{2,1,0:T(8,128)(2,1)}, bf16[512,128,128]{2,1,0:T(8,128)(2,1)}) custom-call(s32[1219]{0:T(1024)S(1)} %concatenate.3.refs_0_.meta, bf16[1536,512]{1,0:T(8,128)(2,1)S(1)} %bitcast.18, ...), custom_call_target="tpu_custom_call", output_to_operand_aliasing={{0}: (6, {}), {1}: (7, {}), {2}: (8, {}), {3}: (9, {})} | custom-call | flops 4831838208 | bytes 4718592 | tf_op jit(solution)/shard_map/back/pallas_call | solution.py:562
  401.5 12.1 %back.26 = (f32[512,1536]{1,0:T(8,128)S(1)}, f32[512,1536]{1,0:T(8,128)S(1)}, bf16[512,128,128]{2,1,0:T(8,128)(2,1)}, bf16[512,128,128]{2,1,0:T(8,128)(2,1)}) custom-call(s32[1219]{0:T(1024)S(1)} %concatenate.3.refs_0_.meta, bf16[1536,512]{1,0:T(8,128)(2,1)S(1)} %bitcast.19, ...), custom_call_target="tpu_custom_call", output_to_operand_aliasing={{0}: (6, {}), {1}: (7, {}), {2}: (8, {}), {3}: (9, {})} | custom-call | flops 4831838208 | bytes 4718592 | tf_op jit(solution)/shard_map/back/pallas_call | solution.py:562
  418.4 12.1 %back.27 = (f32[512,1536]{1,0:T(8,128)S(1)}, f32[512,1536]{1,0:T(8,128)S(1)}, bf16[512,128,128]{2,1,0:T(8,128)(2,1)}, bf16[512,128,128]{2,1,0:T(8,128)(2,1)}) custom-call(s32[1219]{0:T(1024)S(1)} %concatenate.3.refs_0_.meta, bf16[1536,512]{1,0:T(8,128)(2,1)S(1)} %bitcast.20, ...), custom_call_target="tpu_custom_call", output_to_operand_aliasing={{0}: (6, {}), {1}: (7, {}), {2}: (8, {}), {3}: (9, {})} | custom-call | flops 4831838208 | bytes 4718592 | tf_op jit(solution)/shard_map/back/pallas_call | solution.py:562
  435.2 12.5 %back.28 = (f32[512,1536]{1,0:T(8,128)S(1)}, f32[512,1536]{1,0:T(8,128)S(1)}, bf16[512,128,128]{2,1,0:T(8,128)(2,1)}, bf16[512,128,128]{2,1,0:T(8,128)(2,1)}) custom-call(s32[1219]{0:T(1024)S(1)} %concatenate.3.refs_0_.meta, bf16[1536,512]{1,0:T(8,128)(2,1)S(1)} %bitcast.21, ...), custom_call_target="tpu_custom_call", output_to_operand_aliasing={{0}: (6, {}), {1}: (7, {}), {2}: (8, {}), {3}: (9, {})} | custom-call | flops 4831838208 | bytes 4718592 | tf_op jit(solution)/shard_map/back/pallas_call | solution.py:562
  452.1 12.2 %back.29 = (f32[512,1536]{1,0:T(8,128)S(1)}, f32[512,1536]{1,0:T(8,128)S(1)}, bf16[512,128,128]{2,1,0:T(8,128)(2,1)}, bf16[512,128,128]{2,1,0:T(8,128)(2,1)}) custom-call(s32[1219]{0:T(1024)S(1)} %concatenate.3.refs_0_.meta, bf16[1536,512]{1,0:T(8,128)(2,1)S(1)} %bitcast.22, ...), custom_call_target="tpu_custom_call", output_to_operand_aliasing={{0}: (6, {}), {1}: (7, {}), {2}: (8, {}), {3}: (9, {})} | custom-call | flops 4831838208 | bytes 4718592 | tf_op jit(solution)/shard_map/back/pallas_call | solution.py:562
  469.0 12.2 %back.30 = (f32[512,1536]{1,0:T(8,128)S(1)}, f32[512,1536]{1,0:T(8,128)S(1)}, bf16[512,128,128]{2,1,0:T(8,128)(2,1)}, bf16[512,128,128]{2,1,0:T(8,128)(2,1)}) custom-call(s32[1219]{0:T(1024)S(1)} %concatenate.3.refs_0_.meta, bf16[1536,512]{1,0:T(8,128)(2,1)S(1)} %bitcast.23, ...), custom_call_target="tpu_custom_call", output_to_operand_aliasing={{0}: (6, {}), {1}: (7, {}), {2}: (8, {}), {3}: (9, {})} | custom-call | flops 4831838208 | bytes 4718592 | tf_op jit(solution)/shard_map/back/pallas_call | solution.py:562
  485.8 12.2 %back.31 = (f32[512,1536]{1,0:T(8,128)S(1)}, f32[512,1536]{1,0:T(8,128)S(1)}, bf16[512,128,128]{2,1,0:T(8,128)(2,1)}, bf16[512,128,128]{2,1,0:T(8,128)(2,1)}) custom-call(s32[1219]{0:T(1024)S(1)} %concatenate.3.refs_0_.meta, bf16[1536,512]{1,0:T(8,128)(2,1)S(1)} %bitcast.24, ...), custom_call_target="tpu_custom_call", output_to_operand_aliasing={{0}: (6, {}), {1}: (7, {}), {2}: (8, {}), {3}: (9, {})} | custom-call | flops 4831838208 | bytes 4718592 | tf_op jit(solution)/shard_map/back/pallas_call | solution.py:562
  500.6 12.1 %back.32 = (f32[512,1536]{1,0:T(8,128)S(1)}, f32[512,1536]{1,0:T(8,128)S(1)}, bf16[512,128,128]{2,1,0:T(8,128)(2,1)}, bf16[512,128,128]{2,1,0:T(8,128)(2,1)}) custom-call(s32[1219]{0:T(1024)S(1)} %concatenate.3.refs_0_.meta, bf16[1536,512]{1,0:T(8,128)(2,1)S(1)} %bitcast.25, ...), custom_call_target="tpu_custom_call", output_to_operand_aliasing={{0}: (6, {}), {1}: (7, {}), {2}: (8, {}), {3}: (9, {})} | custom-call | flops 4831838208 | bytes 4718592 | tf_op jit(solution)/shard_map/back/pallas_call | solution.py:562
  514.5 4.5 back.33
  519.2 2.3 collective-permute-done.62
  521.6 4.8 back.34
  529.5 9.2 %collective-permute-done.63 = bf16[128,1536]{1,0:T(8,128)(2,1)S(1)} collective-permute-done((bf16[128,1536]{1,0:T(8,128)(2,1)S(1)}, bf16[128,1536]{1,0:T(8,128)(2,1)S(1)}, u32[]{:S(2)}, u32[]{:S(2)}) %collective-permute-start.63) | collective-permute-done | bytes 393248 | tf_op jit(solution)/shard_map/ppermute | solution.py:594
  539.5 7.4 %back.35 = (bf16[512,128,128]{2,1,0:T(8,128)(2,1)}, bf16[512,128,128]{2,1,0:T(8,128)(2,1)}) custom-call(s32[1219]{0:T(1024)S(1)} %concatenate.3.refs_0_.meta, bf16[1536,512]{1,0:T(8,128)(2,1)S(1)} %bitcast.26, bf16[512,1536]{1,0:T(8,128)(2,1)S(1)} %get-tuple-element.233.refs_2_, ...), custom_call_target="tpu_custom_call", output_to_operand_aliasing={{0}: (5, {}), {1}: (6, {})} | custom-call | flops 2415919104 | bytes 2359296 | tf_op jit(solution)/shard_map/back/pallas_call | solution.py:562
  (133 shorter events, 103.1 us)
Async XLA Ops:
  0.6 12.3 %collective-permute-start = (bf16[128,1536]{1,0:T(8,128)(2,1)}, bf16[128,1536]{1,0:T(8,128)(2,1)S(1)}, u32[]{:S(2)}, u32[]{:S(2)}) collective-permute-start(bf16[128,1536]{1,0:T(8,128)(2,1)} %refs_1_.2), channel_id=1, source_target_pairs={{16,0},{24,8},{0,16},{8,24},{17,1},{25,9},{1,17},{9,25},{18,2},{26... | collective-permute-start | bytes 1179656 | tf_op jit(solution)/shard_map/ppermute | solution.py:594
  3.6 11.3 %collective-permute-start.1 = (bf16[128,1536]{1,0:T(8,128)(2,1)}, bf16[128,1536]{1,0:T(8,128)(2,1)S(1)}, u32[]{:S(2)}, u32[]{:S(2)}) collective-permute-start(bf16[128,1536]{1,0:T(8,128)(2,1)} %refs_1_.2), channel_id=1, source_target_pairs={{0,8},{8,0},{16,24},{24,16},{1,9},{9,1},{17,25},{25,17},{2,10},{10... | collective-permute-start | bytes 1179656 | tf_op jit(solution)/shard_map/ppermute | solution.py:587
  13.0 11.7 %collective-permute-start.3 = (bf16[128,1536]{1,0:T(8,128)(2,1)}, bf16[128,1536]{1,0:T(8,128)(2,1)S(1)}, u32[]{:S(2)}, u32[]{:S(2)}) collective-permute-start(bf16[128,1536]{1,0:T(8,128)(2,1)} %refs_1_.3), channel_id=1, source_target_pairs={{16,0},{24,8},{0,16},{8,24},{17,1},{25,9},{1,17},{9,25},{18,2},{26... | collective-permute-start | bytes 1179656 | tf_op jit(solution)/shard_map/ppermute | solution.py:594
  14.7 10.0 %collective-permute-start.4 = (bf16[128,1536]{1,0:T(8,128)(2,1)}, bf16[128,1536]{1,0:T(8,128)(2,1)S(1)}, u32[]{:S(2)}, u32[]{:S(2)}) collective-permute-start(bf16[128,1536]{1,0:T(8,128)(2,1)} %refs_1_.3), channel_id=1, source_target_pairs={{0,8},{8,0},{16,24},{24,16},{1,9},{9,1},{17,25},{25,17},{2,10},{10... | collective-permute-start | bytes 1179656 | tf_op jit(solution)/shard_map/ppermute | solution.py:587
  33.7 20.7 %collective-permute-start.22 = (bf16[2,512,384]{2,1,0:T(8,128)(2,1)}, bf16[2,512,384]{2,1,0:T(8,128)(2,1)}, u32[]{:S(2)}, u32[]{:S(2)}) collective-permute-start(bf16[2,512,384]{2,1,0:T(8,128)(2,1)} %get-tuple-element.258), channel_id=1, source_target_pairs={{0,2},{2,4},{4,6},{6,7},{7,5},{5,3},{3,1},{1,0},{8,10},{10,12},{12... | collective-permute-start | bytes 2359304 | tf_op jit(solution)/shard_map/ppermute | solution.py:663
  35.7 20.8 %collective-permute-start.23 = (bf16[2,512,384]{2,1,0:T(8,128)(2,1)}, bf16[2,512,384]{2,1,0:T(8,128)(2,1)}, u32[]{:S(2)}, u32[]{:S(2)}) collective-permute-start(bf16[2,512,384]{2,1,0:T(8,128)(2,1)} %get-tuple-element.259), channel_id=1, source_target_pairs={{2,0},{4,2},{6,4},{7,6},{5,7},{3,5},{1,3},{0,1},{10,8},{12,10},{14... | collective-permute-start | bytes 2359304 | tf_op jit(solution)/shard_map/ppermute | solution.py:663
  44.4 27.0 %collective-permute-start.6 = (bf16[2,512,384]{2,1,0:T(8,128)(2,1)}, bf16[2,512,384]{2,1,0:T(8,128)(2,1)}, u32[]{:S(2)}, u32[]{:S(2)}) collective-permute-start(bf16[2,512,384]{2,1,0:T(8,128)(2,1)} %get-tuple-element.234), channel_id=1, source_target_pairs={{0,2},{2,4},{4,6},{6,7},{7,5},{5,3},{3,1},{1,0},{8,10},{10,12},{12... | collective-permute-start | bytes 2359304 | tf_op jit(solution)/shard_map/ppermute | solution.py:663
  46.4 26.9 %collective-permute-start.7 = (bf16[2,512,384]{2,1,0:T(8,128)(2,1)}, bf16[2,512,384]{2,1,0:T(8,128)(2,1)}, u32[]{:S(2)}, u32[]{:S(2)}) collective-permute-start(bf16[2,512,384]{2,1,0:T(8,128)(2,1)} %get-tuple-element.235), channel_id=1, source_target_pairs={{2,0},{4,2},{6,4},{7,6},{5,7},{3,5},{1,3},{0,1},{10,8},{12,10},{14... | collective-permute-start | bytes 2359304 | tf_op jit(solution)/shard_map/ppermute | solution.py:663
  66.0 22.1 %collective-permute-start.24 = (bf16[2,512,384]{2,1,0:T(8,128)(2,1)S(1)}, bf16[2,512,384]{2,1,0:T(8,128)(2,1)S(1)}, u32[]{:S(2)}, u32[]{:S(2)}) collective-permute-start(bf16[2,512,384]{2,1,0:T(8,128)(2,1)S(1)} %get-tuple-element.264), channel_id=1, source_target_pairs={{0,2},{2,4},{4,6},{6,7},{7,5},{5,3},{3,1},{1,0},{8,10},{10,12},{12... | collective-permute-start | bytes 2359304 | tf_op jit(solution)/shard_map/ppermute | solution.py:663
  68.0 22.0 %collective-permute-start.25 = (bf16[2,512,384]{2,1,0:T(8,128)(2,1)S(1)}, bf16[2,512,384]{2,1,0:T(8,128)(2,1)S(1)}, u32[]{:S(2)}, u32[]{:S(2)}) collective-permute-start(bf16[2,512,384]{2,1,0:T(8,128)(2,1)S(1)} %get-tuple-element.265), channel_id=1, source_target_pairs={{2,0},{4,2},{6,4},{7,6},{5,7},{3,5},{1,3},{0,1},{10,8},{12,10},{14... | collective-permute-start | bytes 2359304 | tf_op jit(solution)/shard_map/ppermute | solution.py:663
  81.5 23.4 %collective-permute-start.8 = (bf16[2,512,384]{2,1,0:T(8,128)(2,1)S(1)}, bf16[2,512,384]{2,1,0:T(8,128)(2,1)S(1)}, u32[]{:S(2)}, u32[]{:S(2)}) collective-permute-start(bf16[2,512,384]{2,1,0:T(8,128)(2,1)S(1)} %get-tuple-element.237), channel_id=1, source_target_pairs={{0,2},{2,4},{4,6},{6,7},{7,5},{5,3},{3,1},{1,0},{8,10},{10,12},{12... | collective-permute-start | bytes 2359304 | tf_op jit(solution)/shard_map/ppermute | solution.py:663
  83.1 23.8 %collective-permute-start.9 = (bf16[2,512,384]{2,1,0:T(8,128)(2,1)S(1)}, bf16[2,512,384]{2,1,0:T(8,128)(2,1)S(1)}, u32[]{:S(2)}, u32[]{:S(2)}) collective-permute-start(bf16[2,512,384]{2,1,0:T(8,128)(2,1)S(1)} %get-tuple-element.238), channel_id=1, source_target_pairs={{2,0},{4,2},{6,4},{7,6},{5,7},{3,5},{1,3},{0,1},{10,8},{12,10},{14... | collective-permute-start | bytes 2359304 | tf_op jit(solution)/shard_map/ppermute | solution.py:663
  97.4 24.4 %collective-permute-start.26 = (bf16[2,512,384]{2,1,0:T(8,128)(2,1)S(1)}, bf16[2,512,384]{2,1,0:T(8,128)(2,1)S(1)}, u32[]{:S(2)}, u32[]{:S(2)}) collective-permute-start(bf16[2,512,384]{2,1,0:T(8,128)(2,1)S(1)} %get-tuple-element.269), channel_id=1, source_target_pairs={{0,2},{2,4},{4,6},{6,7},{7,5},{5,3},{3,1},{1,0},{8,10},{10,12},{12... | collective-permute-start | bytes 2359304 | tf_op jit(solution)/shard_map/ppermute | solution.py:663
  99.3 24.4 %collective-permute-start.27 = (bf16[2,512,384]{2,1,0:T(8,128)(2,1)S(1)}, bf16[2,512,384]{2,1,0:T(8,128)(2,1)S(1)}, u32[]{:S(2)}, u32[]{:S(2)}) collective-permute-start(bf16[2,512,384]{2,1,0:T(8,128)(2,1)S(1)} %get-tuple-element.270), channel_id=1, source_target_pairs={{2,0},{4,2},{6,4},{7,6},{5,7},{3,5},{1,3},{0,1},{10,8},{12,10},{14... | collective-permute-start | bytes 2359304 | tf_op jit(solution)/shard_map/ppermute | solution.py:663
  114.4 24.2 %collective-permute-start.10 = (bf16[2,512,384]{2,1,0:T(8,128)(2,1)S(1)}, bf16[2,512,384]{2,1,0:T(8,128)(2,1)S(1)}, u32[]{:S(2)}, u32[]{:S(2)}) collective-permute-start(bf16[2,512,384]{2,1,0:T(8,128)(2,1)S(1)} %get-tuple-element.240), channel_id=1, source_target_pairs={{0,2},{2,4},{4,6},{6,7},{7,5},{5,3},{3,1},{1,0},{8,10},{10,12},{12... | collective-permute-start | bytes 2359304 | tf_op jit(solution)/shard_map/ppermute | solution.py:663
  116.0 24.6 %collective-permute-start.11 = (bf16[2,512,384]{2,1,0:T(8,128)(2,1)S(1)}, bf16[2,512,384]{2,1,0:T(8,128)(2,1)S(1)}, u32[]{:S(2)}, u32[]{:S(2)}) collective-permute-start(bf16[2,512,384]{2,1,0:T(8,128)(2,1)S(1)} %get-tuple-element.241), channel_id=1, source_target_pairs={{2,0},{4,2},{6,4},{7,6},{5,7},{3,5},{1,3},{0,1},{10,8},{12,10},{14... | collective-permute-start | bytes 2359304 | tf_op jit(solution)/shard_map/ppermute | solution.py:663
  131.6 23.9 %collective-permute-start.28 = (bf16[2,512,384]{2,1,0:T(8,128)(2,1)S(1)}, bf16[2,512,384]{2,1,0:T(8,128)(2,1)S(1)}, u32[]{:S(2)}, u32[]{:S(2)}) collective-permute-start(bf16[2,512,384]{2,1,0:T(8,128)(2,1)S(1)} %get-tuple-element.275), channel_id=1, source_target_pairs={{0,2},{2,4},{4,6},{6,7},{7,5},{5,3},{3,1},{1,0},{8,10},{10,12},{12... | collective-permute-start | bytes 2359304 | tf_op jit(solution)/shard_map/ppermute | solution.py:663
  133.4 24.1 %collective-permute-start.29 = (bf16[2,512,384]{2,1,0:T(8,128)(2,1)S(1)}, bf16[2,512,384]{2,1,0:T(8,128)(2,1)S(1)}, u32[]{:S(2)}, u32[]{:S(2)}) collective-permute-start(bf16[2,512,384]{2,1,0:T(8,128)(2,1)S(1)} %get-tuple-element.276), channel_id=1, source_target_pairs={{2,0},{4,2},{6,4},{7,6},{5,7},{3,5},{1,3},{0,1},{10,8},{12,10},{14... | collective-permute-start | bytes 2359304 | tf_op jit(solution)/shard_map/ppermute | solution.py:663
  148.0 24.3 %collective-permute-start.12 = (bf16[2,512,384]{2,1,0:T(8,128)(2,1)S(1)}, bf16[2,512,384]{2,1,0:T(8,128)(2,1)S(1)}, u32[]{:S(2)}, u32[]{:S(2)}) collective-permute-start(bf16[2,512,384]{2,1,0:T(8,128)(2,1)S(1)} %get-tuple-element.243), channel_id=1, source_target_pairs={{0,2},{2,4},{4,6},{6,7},{7,5},{5,3},{3,1},{1,0},{8,10},{10,12},{12... | collective-permute-start | bytes 2359304 | tf_op jit(solution)/shard_map/ppermute | solution.py:663
  149.7 24.6 %collective-permute-start.13 = (bf16[2,512,384]{2,1,0:T(8,128)(2,1)S(1)}, bf16[2,512,384]{2,1,0:T(8,128)(2,1)S(1)}, u32[]{:S(2)}, u32[]{:S(2)}) collective-permute-start(bf16[2,512,384]{2,1,0:T(8,128)(2,1)S(1)} %get-tuple-element.244), channel_id=1, source_target_pairs={{2,0},{4,2},{6,4},{7,6},{5,7},{3,5},{1,3},{0,1},{10,8},{12,10},{14... | collective-permute-start | bytes 2359304 | tf_op jit(solution)/shard_map/ppermute | solution.py:663
  164.9 24.3 %collective-permute-start.30 = (bf16[2,512,384]{2,1,0:T(8,128)(2,1)S(1)}, bf16[2,512,384]{2,1,0:T(8,128)(2,1)S(1)}, u32[]{:S(2)}, u32[]{:S(2)}) collective-permute-start(bf16[2,512,384]{2,1,0:T(8,128)(2,1)S(1)} %get-tuple-element.278), channel_id=1, source_target_pairs={{0,2},{2,4},{4,6},{6,7},{7,5},{5,3},{3,1},{1,0},{8,10},{10,12},{12... | collective-permute-start | bytes 2359304 | tf_op jit(solution)/shard_map/ppermute | solution.py:663
  166.4 24.7 %collective-permute-start.31 = (bf16[2,512,384]{2,1,0:T(8,128)(2,1)S(1)}, bf16[2,512,384]{2,1,0:T(8,128)(2,1)S(1)}, u32[]{:S(2)}, u32[]{:S(2)}) collective-permute-start(bf16[2,512,384]{2,1,0:T(8,128)(2,1)S(1)} %get-tuple-element.279), channel_id=1, source_target_pairs={{2,0},{4,2},{6,4},{7,6},{5,7},{3,5},{1,3},{0,1},{10,8},{12,10},{14... | collective-permute-start | bytes 2359304 | tf_op jit(solution)/shard_map/ppermute | solution.py:663
  181.7 24.3 %collective-permute-start.14 = (bf16[2,512,384]{2,1,0:T(8,128)(2,1)S(1)}, bf16[2,512,384]{2,1,0:T(8,128)(2,1)S(1)}, u32[]{:S(2)}, u32[]{:S(2)}) collective-permute-start(bf16[2,512,384]{2,1,0:T(8,128)(2,1)S(1)} %get-tuple-element.246), channel_id=1, source_target_pairs={{0,2},{2,4},{4,6},{6,7},{7,5},{5,3},{3,1},{1,0},{8,10},{10,12},{12... | collective-permute-start | bytes 2359304 | tf_op jit(solution)/shard_map/ppermute | solution.py:663
  183.5 24.5 %collective-permute-start.15 = (bf16[2,512,384]{2,1,0:T(8,128)(2,1)S(1)}, bf16[2,512,384]{2,1,0:T(8,128)(2,1)S(1)}, u32[]{:S(2)}, u32[]{:S(2)}) collective-permute-start(bf16[2,512,384]{2,1,0:T(8,128)(2,1)S(1)} %get-tuple-element.247), channel_id=1, source_target_pairs={{2,0},{4,2},{6,4},{7,6},{5,7},{3,5},{1,3},{0,1},{10,8},{12,10},{14... | collective-permute-start | bytes 2359304 | tf_op jit(solution)/shard_map/ppermute | solution.py:663
  198.6 24.3 %collective-permute-start.32 = (bf16[2,512,384]{2,1,0:T(8,128)(2,1)S(1)}, bf16[2,512,384]{2,1,0:T(8,128)(2,1)S(1)}, u32[]{:S(2)}, u32[]{:S(2)}) collective-permute-start(bf16[2,512,384]{2,1,0:T(8,128)(2,1)S(1)} %get-tuple-element.281), channel_id=1, source_target_pairs={{0,2},{2,4},{4,6},{6,7},{7,5},{5,3},{3,1},{1,0},{8,10},{10,12},{12... | collective-permute-start | bytes 2359304 | tf_op jit(solution)/shard_map/ppermute | solution.py:663
  200.3 24.6 %collective-permute-start.33 = (bf16[2,512,384]{2,1,0:T(8,128)(2,1)S(1)}, bf16[2,512,384]{2,1,0:T(8,128)(2,1)S(1)}, u32[]{:S(2)}, u32[]{:S(2)}) collective-permute-start(bf16[2,512,384]{2,1,0:T(8,128)(2,1)S(1)} %get-tuple-element.282), channel_id=1, source_target_pairs={{2,0},{4,2},{6,4},{7,6},{5,7},{3,5},{1,3},{0,1},{10,8},{12,10},{14... | collective-permute-start | bytes 2359304 | tf_op jit(solution)/shard_map/ppermute | solution.py:663
  215.4 24.3 %collective-permute-start.16 = (bf16[2,512,384]{2,1,0:T(8,128)(2,1)S(1)}, bf16[2,512,384]{2,1,0:T(8,128)(2,1)S(1)}, u32[]{:S(2)}, u32[]{:S(2)}) collective-permute-start(bf16[2,512,384]{2,1,0:T(8,128)(2,1)S(1)} %get-tuple-element.249), channel_id=1, source_target_pairs={{0,2},{2,4},{4,6},{6,7},{7,5},{5,3},{3,1},{1,0},{8,10},{10,12},{12... | collective-permute-start | bytes 2359304 | tf_op jit(solution)/shard_map/ppermute | solution.py:663
  217.0 24.7 %collective-permute-start.17 = (bf16[2,512,384]{2,1,0:T(8,128)(2,1)S(1)}, bf16[2,512,384]{2,1,0:T(8,128)(2,1)S(1)}, u32[]{:S(2)}, u32[]{:S(2)}) collective-permute-start(bf16[2,512,384]{2,1,0:T(8,128)(2,1)S(1)} %get-tuple-element.250), channel_id=1, source_target_pairs={{2,0},{4,2},{6,4},{7,6},{5,7},{3,5},{1,3},{0,1},{10,8},{12,10},{14... | collective-permute-start | bytes 2359304 | tf_op jit(solution)/shard_map/ppermute | solution.py:663
  232.2 24.4 %collective-permute-start.34 = (bf16[2,512,384]{2,1,0:T(8,128)(2,1)S(1)}, bf16[2,512,384]{2,1,0:T(8,128)(2,1)S(1)}, u32[]{:S(2)}, u32[]{:S(2)}) collective-permute-start(bf16[2,512,384]{2,1,0:T(8,128)(2,1)S(1)} %get-tuple-element.284), channel_id=1, source_target_pairs={{0,2},{2,4},{4,6},{6,7},{7,5},{5,3},{3,1},{1,0},{8,10},{10,12},{12... | collective-permute-start | bytes 2359304 | tf_op jit(solution)/shard_map/ppermute | solution.py:663
  233.9 24.7 %collective-permute-start.35 = (bf16[2,512,384]{2,1,0:T(8,128)(2,1)S(1)}, bf16[2,512,384]{2,1,0:T(8,128)(2,1)S(1)}, u32[]{:S(2)}, u32[]{:S(2)}) collective-permute-start(bf16[2,512,384]{2,1,0:T(8,128)(2,1)S(1)} %get-tuple-element.285), channel_id=1, source_target_pairs={{2,0},{4,2},{6,4},{7,6},{5,7},{3,5},{1,3},{0,1},{10,8},{12,10},{14... | collective-permute-start | bytes 2359304 | tf_op jit(solution)/shard_map/ppermute | solution.py:663
  249.0 24.4 %collective-permute-start.18 = (bf16[2,512,384]{2,1,0:T(8,128)(2,1)S(1)}, bf16[2,512,384]{2,1,0:T(8,128)(2,1)S(1)}, u32[]{:S(2)}, u32[]{:S(2)}) collective-permute-start(bf16[2,512,384]{2,1,0:T(8,128)(2,1)S(1)} %get-tuple-element.252), channel_id=1, source_target_pairs={{0,2},{2,4},{4,6},{6,7},{7,5},{5,3},{3,1},{1,0},{8,10},{10,12},{12... | collective-permute-start | bytes 2359304 | tf_op jit(solution)/shard_map/ppermute | solution.py:663
  250.8 24.6 %collective-permute-start.19 = (bf16[2,512,384]{2,1,0:T(8,128)(2,1)S(1)}, bf16[2,512,384]{2,1,0:T(8,128)(2,1)S(1)}, u32[]{:S(2)}, u32[]{:S(2)}) collective-permute-start(bf16[2,512,384]{2,1,0:T(8,128)(2,1)S(1)} %get-tuple-element.253), channel_id=1, source_target_pairs={{2,0},{4,2},{6,4},{7,6},{5,7},{3,5},{1,3},{0,1},{10,8},{12,10},{14... | collective-permute-start | bytes 2359304 | tf_op jit(solution)/shard_map/ppermute | solution.py:663
  266.9 43.0 %collective-permute-start.36 = (bf16[2,512,384]{2,1,0:T(8,128)(2,1)S(1)}, bf16[2,512,384]{2,1,0:T(8,128)(2,1)S(1)}, u32[]{:S(2)}, u32[]{:S(2)}) collective-permute-start(bf16[2,512,384]{2,1,0:T(8,128)(2,1)S(1)} %get-tuple-element.288.refs_4_), channel_id=1, source_target_pairs={{0,2},{2,4},{4,6},{6,7},{7,5},{5,3},{3,1},{1,0},{8,10},{10,12},{12... | collective-permute-start | bytes 2359304 | tf_op jit(solution)/shard_map/ppermute | solution.py:663
  268.8 41.1 %collective-permute-start.37 = (bf16[2,512,384]{2,1,0:T(8,128)(2,1)S(1)}, bf16[2,512,384]{2,1,0:T(8,128)(2,1)S(1)}, u32[]{:S(2)}, u32[]{:S(2)}) collective-permute-start(bf16[2,512,384]{2,1,0:T(8,128)(2,1)S(1)} %get-tuple-element.289.refs_5_), channel_id=1, source_target_pairs={{2,0},{4,2},{6,4},{7,6},{5,7},{3,5},{1,3},{0,1},{10,8},{12,10},{14... | collective-permute-start | bytes 2359304 | tf_op jit(solution)/shard_map/ppermute | solution.py:663
  283.8 41.0 %collective-permute-start.20 = (bf16[2,512,384]{2,1,0:T(8,128)(2,1)S(1)}, bf16[2,512,384]{2,1,0:T(8,128)(2,1)S(1)}, u32[]{:S(2)}, u32[]{:S(2)}) collective-permute-start(bf16[2,512,384]{2,1,0:T(8,128)(2,1)S(1)} %get-tuple-element.256.refs_4_), channel_id=1, source_target_pairs={{0,2},{2,4},{4,6},{6,7},{7,5},{5,3},{3,1},{1,0},{8,10},{10,12},{12... | collective-permute-start | bytes 2359304 | tf_op jit(solution)/shard_map/ppermute | solution.py:663
  285.5 39.3 %collective-permute-start.21 = (bf16[2,512,384]{2,1,0:T(8,128)(2,1)S(1)}, bf16[2,512,384]{2,1,0:T(8,128)(2,1)S(1)}, u32[]{:S(2)}, u32[]{:S(2)}) collective-permute-start(bf16[2,512,384]{2,1,0:T(8,128)(2,1)S(1)} %get-tuple-element.257.refs_5_), channel_id=1, source_target_pairs={{2,0},{4,2},{6,4},{7,6},{5,7},{3,5},{1,3},{0,1},{10,8},{12,10},{14... | collective-permute-start | bytes 2359304 | tf_op jit(solution)/shard_map/ppermute | solution.py:663
  309.9 29.4 %collective-permute-start.40 = (bf16[2,512,384]{2,1,0:T(8,128)(2,1)S(1)}, bf16[2,512,384]{2,1,0:T(8,128)(2,1)S(1)}, u32[]{:S(2)}, u32[]{:S(2)}) collective-permute-start(bf16[2,512,384]{2,1,0:T(8,128)(2,1)S(1)} %collective-permute-done.36.refs_4_), channel_id=1, source_target_pairs={{0,2},{2,4},{4,6},{6,7},{7,5},{5,3},{3,1},{1,0},{8,10},{10,12},{12... | collective-permute-start | bytes 2359304 | tf_op jit(solution)/shard_map/ppermute | solution.py:663
  312.5 26.8 %collective-permute-start.41 = (bf16[2,512,384]{2,1,0:T(8,128)(2,1)S(1)}, bf16[2,512,384]{2,1,0:T(8,128)(2,1)S(1)}, u32[]{:S(2)}, u32[]{:S(2)}) collective-permute-start(bf16[2,512,384]{2,1,0:T(8,128)(2,1)S(1)} %collective-permute-done.37.refs_5_), channel_id=1, source_target_pairs={{2,0},{4,2},{6,4},{7,6},{5,7},{3,5},{1,3},{0,1},{10,8},{12,10},{14... | collective-permute-start | bytes 2359304 | tf_op jit(solution)/shard_map/ppermute | solution.py:663
  324.8 28.9 %collective-permute-start.38 = (bf16[2,512,384]{2,1,0:T(8,128)(2,1)S(1)}, bf16[2,512,384]{2,1,0:T(8,128)(2,1)S(1)}, u32[]{:S(2)}, u32[]{:S(2)}) collective-permute-start(bf16[2,512,384]{2,1,0:T(8,128)(2,1)S(1)} %collective-permute-done.20.refs_4_), channel_id=1, source_target_pairs={{0,2},{2,4},{4,6},{6,7},{7,5},{5,3},{3,1},{1,0},{8,10},{10,12},{12... | collective-permute-start | bytes 2359304 | tf_op jit(solution)/shard_map/ppermute | solution.py:663
  327.1 26.7 %collective-permute-start.39 = (bf16[2,512,384]{2,1,0:T(8,128)(2,1)S(1)}, bf16[2,512,384]{2,1,0:T(8,128)(2,1)S(1)}, u32[]{:S(2)}, u32[]{:S(2)}) collective-permute-start(bf16[2,512,384]{2,1,0:T(8,128)(2,1)S(1)} %collective-permute-done.21.refs_5_), channel_id=1, source_target_pairs={{2,0},{4,2},{6,4},{7,6},{5,7},{3,5},{1,3},{0,1},{10,8},{12,10},{14... | collective-permute-start | bytes 2359304 | tf_op jit(solution)/shard_map/ppermute | solution.py:663
  339.3 29.5 %collective-permute-start.44 = (bf16[2,512,384]{2,1,0:T(8,128)(2,1)S(1)}, bf16[2,512,384]{2,1,0:T(8,128)(2,1)S(1)}, u32[]{:S(2)}, u32[]{:S(2)}) collective-permute-start(bf16[2,512,384]{2,1,0:T(8,128)(2,1)S(1)} %collective-permute-done.40.refs_4_), channel_id=1, source_target_pairs={{0,2},{2,4},{4,6},{6,7},{7,5},{5,3},{3,1},{1,0},{8,10},{10,12},{12... | collective-permute-start | bytes 2359304 | tf_op jit(solution)/shard_map/ppermute | solution.py:663
  341.6 27.3 %collective-permute-start.45 = (bf16[2,512,384]{2,1,0:T(8,128)(2,1)S(1)}, bf16[2,512,384]{2,1,0:T(8,128)(2,1)S(1)}, u32[]{:S(2)}, u32[]{:S(2)}) collective-permute-start(bf16[2,512,384]{2,1,0:T(8,128)(2,1)S(1)} %collective-permute-done.41.refs_5_), channel_id=1, source_target_pairs={{2,0},{4,2},{6,4},{7,6},{5,7},{3,5},{1,3},{0,1},{10,8},{12,10},{14... | collective-permute-start | bytes 2359304 | tf_op jit(solution)/shard_map/ppermute | solution.py:663
  353.8 29.3 %collective-permute-start.42 = (bf16[2,512,384]{2,1,0:T(8,128)(2,1)S(1)}, bf16[2,512,384]{2,1,0:T(8,128)(2,1)S(1)}, u32[]{:S(2)}, u32[]{:S(2)}) collective-permute-start(bf16[2,512,384]{2,1,0:T(8,128)(2,1)S(1)} %collective-permute-done.38.refs_4_), channel_id=1, source_target_pairs={{0,2},{2,4},{4,6},{6,7},{7,5},{5,3},{3,1},{1,0},{8,10},{10,12},{12... | collective-permute-start | bytes 2359304 | tf_op jit(solution)/shard_map/ppermute | solution.py:663
  356.4 26.6 %collective-permute-start.43 = (bf16[2,512,384]{2,1,0:T(8,128)(2,1)S(1)}, bf16[2,512,384]{2,1,0:T(8,128)(2,1)S(1)}, u32[]{:S(2)}, u32[]{:S(2)}) collective-permute-start(bf16[2,512,384]{2,1,0:T(8,128)(2,1)S(1)} %collective-permute-done.39.refs_5_), channel_id=1, source_target_pairs={{2,0},{4,2},{6,4},{7,6},{5,7},{3,5},{1,3},{0,1},{10,8},{12,10},{14... | collective-permute-start | bytes 2359304 | tf_op jit(solution)/shard_map/ppermute | solution.py:663
  368.9 29.3 %collective-permute-start.48 = (bf16[2,512,384]{2,1,0:T(8,128)(2,1)S(1)}, bf16[2,512,384]{2,1,0:T(8,128)(2,1)S(1)}, u32[]{:S(2)}, u32[]{:S(2)}) collective-permute-start(bf16[2,512,384]{2,1,0:T(8,128)(2,1)S(1)} %collective-permute-done.44.refs_4_), channel_id=1, source_target_pairs={{0,2},{2,4},{4,6},{6,7},{7,5},{5,3},{3,1},{1,0},{8,10},{10,12},{12... | collective-permute-start | bytes 2359304 | tf_op jit(solution)/shard_map/ppermute | solution.py:663
  370.9 28.6 %collective-permute-start.49 = (bf16[2,512,384]{2,1,0:T(8,128)(2,1)S(1)}, bf16[2,512,384]{2,1,0:T(8,128)(2,1)S(1)}, u32[]{:S(2)}, u32[]{:S(2)}) collective-permute-start(bf16[2,512,384]{2,1,0:T(8,128)(2,1)S(1)} %collective-permute-done.45.refs_5_), channel_id=1, source_target_pairs={{2,0},{4,2},{6,4},{7,6},{5,7},{3,5},{1,3},{0,1},{10,8},{12,10},{14... | collective-permute-start | bytes 2359304 | tf_op jit(solution)/shard_map/ppermute | solution.py:663
  383.0 31.7 %collective-permute-start.46 = (bf16[2,512,384]{2,1,0:T(8,128)(2,1)S(1)}, bf16[2,512,384]{2,1,0:T(8,128)(2,1)S(1)}, u32[]{:S(2)}, u32[]{:S(2)}) collective-permute-start(bf16[2,512,384]{2,1,0:T(8,128)(2,1)S(1)} %collective-permute-done.42.refs_4_), channel_id=1, source_target_pairs={{0,2},{2,4},{4,6},{6,7},{7,5},{5,3},{3,1},{1,0},{8,10},{10,12},{12... | collective-permute-start | bytes 2359304 | tf_op jit(solution)/shard_map/ppermute | solution.py:663
  385.7 30.7 %collective-permute-start.47 = (bf16[2,512,384]{2,1,0:T(8,128)(2,1)S(1)}, bf16[2,512,384]{2,1,0:T(8,128)(2,1)S(1)}, u32[]{:S(2)}, u32[]{:S(2)}) collective-permute-start(bf16[2,512,384]{2,1,0:T(8,128)(2,1)S(1)} %collective-permute-done.43.refs_5_), channel_id=1, source_target_pairs={{2,0},{4,2},{6,4},{7,6},{5,7},{3,5},{1,3},{0,1},{10,8},{12,10},{14... | collective-permute-start | bytes 2359304 | tf_op jit(solution)/shard_map/ppermute | solution.py:663
  399.5 32.1 %collective-permute-start.52 = (bf16[2,512,384]{2,1,0:T(8,128)(2,1)S(1)}, bf16[2,512,384]{2,1,0:T(8,128)(2,1)S(1)}, u32[]{:S(2)}, u32[]{:S(2)}) collective-permute-start(bf16[2,512,384]{2,1,0:T(8,128)(2,1)S(1)} %collective-permute-done.48.refs_4_), channel_id=1, source_target_pairs={{0,2},{2,4},{4,6},{6,7},{7,5},{5,3},{3,1},{1,0},{8,10},{10,12},{12... | collective-permute-start | bytes 2359304 | tf_op jit(solution)/shard_map/ppermute | solution.py:663
  400.4 32.8 %collective-permute-start.53 = (bf16[2,512,384]{2,1,0:T(8,128)(2,1)S(1)}, bf16[2,512,384]{2,1,0:T(8,128)(2,1)S(1)}, u32[]{:S(2)}, u32[]{:S(2)}) collective-permute-start(bf16[2,512,384]{2,1,0:T(8,128)(2,1)S(1)} %collective-permute-done.49.refs_5_), channel_id=1, source_target_pairs={{2,0},{4,2},{6,4},{7,6},{5,7},{3,5},{1,3},{0,1},{10,8},{12,10},{14... | collective-permute-start | bytes 2359304 | tf_op jit(solution)/shard_map/ppermute | solution.py:663
  416.4 32.1 %collective-permute-start.50 = (bf16[2,512,384]{2,1,0:T(8,128)(2,1)S(1)}, bf16[2,512,384]{2,1,0:T(8,128)(2,1)S(1)}, u32[]{:S(2)}, u32[]{:S(2)}) collective-permute-start(bf16[2,512,384]{2,1,0:T(8,128)(2,1)S(1)} %collective-permute-done.46.refs_4_), channel_id=1, source_target_pairs={{0,2},{2,4},{4,6},{6,7},{7,5},{5,3},{3,1},{1,0},{8,10},{10,12},{12... | collective-permute-start | bytes 2359304 | tf_op jit(solution)/shard_map/ppermute | solution.py:663
  417.3 32.8 %collective-permute-start.51 = (bf16[2,512,384]{2,1,0:T(8,128)(2,1)S(1)}, bf16[2,512,384]{2,1,0:T(8,128)(2,1)S(1)}, u32[]{:S(2)}, u32[]{:S(2)}) collective-permute-start(bf16[2,512,384]{2,1,0:T(8,128)(2,1)S(1)} %collective-permute-done.47.refs_5_), channel_id=1, source_target_pairs={{2,0},{4,2},{6,4},{7,6},{5,7},{3,5},{1,3},{0,1},{10,8},{12,10},{14... | collective-permute-start | bytes 2359304 | tf_op jit(solution)/shard_map/ppermute | solution.py:663
  433.2 32.1 %collective-permute-start.56 = (bf16[2,512,384]{2,1,0:T(8,128)(2,1)S(1)}, bf16[2,512,384]{2,1,0:T(8,128)(2,1)S(1)}, u32[]{:S(2)}, u32[]{:S(2)}) collective-permute-start(bf16[2,512,384]{2,1,0:T(8,128)(2,1)S(1)} %collective-permute-done.52.refs_4_), channel_id=1, source_target_pairs={{0,2},{2,4},{4,6},{6,7},{7,5},{5,3},{3,1},{1,0},{8,10},{10,12},{12... | collective-permute-start | bytes 2359304 | tf_op jit(solution)/shard_map/ppermute | solution.py:663
  434.1 32.8 %collective-permute-start.57 = (bf16[2,512,384]{2,1,0:T(8,128)(2,1)S(1)}, bf16[2,512,384]{2,1,0:T(8,128)(2,1)S(1)}, u32[]{:S(2)}, u32[]{:S(2)}) collective-permute-start(bf16[2,512,384]{2,1,0:T(8,128)(2,1)S(1)} %collective-permute-done.53.refs_5_), channel_id=1, source_target_pairs={{2,0},{4,2},{6,4},{7,6},{5,7},{3,5},{1,3},{0,1},{10,8},{12,10},{14... | collective-permute-start | bytes 2359304 | tf_op jit(solution)/shard_map/ppermute | solution.py:663
  450.1 32.1 %collective-permute-start.54 = (bf16[2,512,384]{2,1,0:T(8,128)(2,1)S(1)}, bf16[2,512,384]{2,1,0:T(8,128)(2,1)S(1)}, u32[]{:S(2)}, u32[]{:S(2)}) collective-permute-start(bf16[2,512,384]{2,1,0:T(8,128)(2,1)S(1)} %collective-permute-done.50.refs_4_), channel_id=1, source_target_pairs={{0,2},{2,4},{4,6},{6,7},{7,5},{5,3},{3,1},{1,0},{8,10},{10,12},{12... | collective-permute-start | bytes 2359304 | tf_op jit(solution)/shard_map/ppermute | solution.py:663
  451.0 32.8 %collective-permute-start.55 = (bf16[2,512,384]{2,1,0:T(8,128)(2,1)S(1)}, bf16[2,512,384]{2,1,0:T(8,128)(2,1)S(1)}, u32[]{:S(2)}, u32[]{:S(2)}) collective-permute-start(bf16[2,512,384]{2,1,0:T(8,128)(2,1)S(1)} %collective-permute-done.51.refs_5_), channel_id=1, source_target_pairs={{2,0},{4,2},{6,4},{7,6},{5,7},{3,5},{1,3},{0,1},{10,8},{12,10},{14... | collective-permute-start | bytes 2359304 | tf_op jit(solution)/shard_map/ppermute | solution.py:663
  466.9 32.1 %collective-permute-start.60 = (bf16[2,512,384]{2,1,0:T(8,128)(2,1)S(1)}, bf16[2,512,384]{2,1,0:T(8,128)(2,1)S(1)}, u32[]{:S(2)}, u32[]{:S(2)}) collective-permute-start(bf16[2,512,384]{2,1,0:T(8,128)(2,1)S(1)} %collective-permute-done.56.refs_4_), channel_id=1, source_target_pairs={{0,2},{2,4},{4,6},{6,7},{7,5},{5,3},{3,1},{1,0},{8,10},{10,12},{12... | collective-permute-start | bytes 2359304 | tf_op jit(solution)/shard_map/ppermute | solution.py:663
  467.8 32.8 %collective-permute-start.61 = (bf16[2,512,384]{2,1,0:T(8,128)(2,1)S(1)}, bf16[2,512,384]{2,1,0:T(8,128)(2,1)S(1)}, u32[]{:S(2)}, u32[]{:S(2)}) collective-permute-start(bf16[2,512,384]{2,1,0:T(8,128)(2,1)S(1)} %collective-permute-done.57.refs_5_), channel_id=1, source_target_pairs={{2,0},{4,2},{6,4},{7,6},{5,7},{3,5},{1,3},{0,1},{10,8},{12,10},{14... | collective-permute-start | bytes 2359304 | tf_op jit(solution)/shard_map/ppermute | solution.py:663
  483.8 29.9 %collective-permute-start.58 = (bf16[2,512,384]{2,1,0:T(8,128)(2,1)S(1)}, bf16[2,512,384]{2,1,0:T(8,128)(2,1)S(1)}, u32[]{:S(2)}, u32[]{:S(2)}) collective-permute-start(bf16[2,512,384]{2,1,0:T(8,128)(2,1)S(1)} %collective-permute-done.54.refs_4_), channel_id=1, source_target_pairs={{0,2},{2,4},{4,6},{6,7},{7,5},{5,3},{3,1},{1,0},{8,10},{10,12},{12... | collective-permute-start | bytes 2359304 | tf_op jit(solution)/shard_map/ppermute | solution.py:663
  484.7 29.9 %collective-permute-start.59 = (bf16[2,512,384]{2,1,0:T(8,128)(2,1)S(1)}, bf16[2,512,384]{2,1,0:T(8,128)(2,1)S(1)}, u32[]{:S(2)}, u32[]{:S(2)}) collective-permute-start(bf16[2,512,384]{2,1,0:T(8,128)(2,1)S(1)} %collective-permute-done.55.refs_5_), channel_id=1, source_target_pairs={{2,0},{4,2},{6,4},{7,6},{5,7},{3,5},{1,3},{0,1},{10,8},{12,10},{14... | collective-permute-start | bytes 2359304 | tf_op jit(solution)/shard_map/ppermute | solution.py:663
  519.1 2.4 collective-permute-start.62
  526.4 2.4 collective-permute-start.64
  526.7 12.0 %collective-permute-start.63 = (bf16[128,1536]{1,0:T(8,128)(2,1)S(1)}, bf16[128,1536]{1,0:T(8,128)(2,1)S(1)}, u32[]{:S(2)}, u32[]{:S(2)}) collective-permute-start(bf16[128,1536]{1,0:T(8,128)(2,1)S(1)} %slice.25), channel_id=1, source_target_pairs={{16,0},{24,8},{0,16},{8,24},{17,1},{25,9},{1,17},{9,25},{18,2},{26... | collective-permute-start | bytes 1179656 | tf_op jit(solution)/shard_map/ppermute | solution.py:594
  529.0 17.8 %collective-permute-start.65 = (bf16[128,1536]{1,0:T(8,128)(2,1)S(1)}, bf16[128,1536]{1,0:T(8,128)(2,1)S(1)}, u32[]{:S(2)}, u32[]{:S(2)}) collective-permute-start(bf16[128,1536]{1,0:T(8,128)(2,1)S(1)} %slice.24), channel_id=1, source_target_pairs={{16,0},{24,8},{0,16},{8,24},{17,1},{25,9},{1,17},{9,25},{18,2},{26... | collective-permute-start | bytes 1179656 | tf_op jit(solution)/shard_map/ppermute | solution.py:594
  (7 other events, 54.6 us)
